TPU v7x, 32 devices: a whole 2x2x4 slice. The times are simulated.
32 devices in a mesh: groups: 2 (over y), seq: 4 (over z), fsdp: 2 (over x), head: 2 (over core).
Axes of the slice: x: 2, y: 2, z: 4, core: 2. Of those that a mesh axis runs over, the one named last changes fastest.
Arguments:
- frames: bfloat16 [6144, 3072], P(('groups', 'seq')), parts along dimension 0, may hold values from -330 to 330
- modulation: float32 [4, 3072], P('groups'), parts along dimension 0, may hold values from -2.5 to 2.5
- w_qkv: bfloat16 [3072, 3, 2048], P('seq', None, ('fsdp', 'head')), may hold values from -0.109375 to 0.109375
- b_qkv: float32 [3, 2048], P(None, ('fsdp', 'head')), may hold values from -2.5 to 2.5
- qk_gain: float32 [2, 128], replicated, may hold values from 0.7 to 2.4
- block_lists: int32 [16, 27], P(('groups', 'seq')), parts along dimension 0, may hold values from -1 to 7, as said below
Outputs:
- attention: bfloat16 [6144, 2048], P(('groups', 'seq'), ('fsdp', 'head')), parts along dimension 0
There are 2 independent parts, one for each index of `groups`. A program takes and returns all parts, laid end to end along the dimension named above; an argument that names none is the same for every part. Nothing has to cross between parts.
Inputs may be any that keep to these rules, and one draw needn't show every extreme that they name: `block_lists`: tile g lies at width g // 2, time (g % 2) // 1 and height g % 1 of a 2 x 1 x 4 grid of tiles. Entry (a + 1) * 9 + (b + 1) * 3 + (c + 1) of row g, for a, b, c in -1, 0, 1, is the tile at time + a, height + b and width + c of tile g, or -1 where that tile is outside the grid or left out of the list. Entry 13 is always g.
All inputs are finite; a program needn't handle non-finite values.
Results may differ from a plain program's by a relative error of at most 0.0058.
Values may be sent and summed in bfloat16 or wider, within the bound.
No kernel may reach another device: no remote copies, remote signals or barrier semaphores. Data moves between devices by JAX's collectives and lax.ppermute only.
A program may use at most 128 MiB of HBM per device.

v0:
```python
import math

import jax
import jax.numpy as jnp
from jax import lax
from jax.sharding import PartitionSpec as P


def with_halo(shard, sides, width):
    for axis, dim in sides:
        devices, length = (lax.axis_size(axis), shard.shape[dim])
        up = [(i, (i + 1) % devices) for i in range(devices - 1)]
        down = [(j, i) for i, j in up]
        last = lax.slice_in_dim(shard, length - width, length, axis=dim)
        first = lax.slice_in_dim(shard, 0, width, axis=dim)
        before = lax.ppermute(last, axis, up)
        after = lax.ppermute(first, axis, down)
        shard = jnp.concatenate([before, shard, after], axis=dim)
    return shard


def normed_heads(tensor, gain_row, head_dim):
    shaped = tensor.reshape(tensor.shape[0], tensor.shape[1] // head_dim, head_dim)
    scaled = (
        shaped * lax.rsqrt(jnp.mean(shaped * shaped, axis=-1, keepdims=True) + 1e-06) * gain_row
    )
    return scaled.astype(jnp.bfloat16)


def reach_sides(key_rows, values):
    stacked = jnp.stack([key_rows, values], axis=0)
    return with_halo(stacked, (("seq", 1),), key_rows.shape[0])


def per_device(frames, modulation, w_qkv, b_qkv, qk_gain, block_lists):
    inputs = frames.astype(jnp.float32)
    average = jnp.mean(inputs, axis=-1, keepdims=True)
    centred = inputs - average
    variance = jnp.mean(centred * centred, axis=-1, keepdims=True)
    normed = centred * lax.rsqrt(variance + 1e-06) * (1.0 + modulation[0]) + modulation[1]
    normed = normed.astype(jnp.bfloat16)
    tokens = normed.shape[0]
    width_cols = w_qkv.shape[2]
    head_dim = qk_gain.shape[1]
    heads = width_cols // head_dim
    projected = jnp.einsum(
        "td,djc->tjc",
        normed,
        lax.all_gather(w_qkv, "seq", axis=0, tiled=True),
        preferred_element_type=jnp.float32,
    )
    projected = projected + b_qkv
    queries = normed_heads(projected[:, 0], qk_gain[0], head_dim)
    key_rows = normed_heads(projected[:, 1], qk_gain[1], head_dim)
    values = projected[:, 2].astype(jnp.bfloat16).reshape(tokens, heads, head_dim)
    neighbourhood = reach_sides(key_rows, values)
    position = lax.axis_index("seq")
    tile_dev = block_lists.shape[0]
    tile_len = tokens // tile_dev
    candidates = (position - 1) * tile_dev + jnp.arange(3 * tile_dev, dtype=jnp.int32)
    matches = (block_lists[:, :, None] == candidates[None, None, :]) & (
        block_lists[:, :, None] >= 0
    )
    allowed_tiles = jnp.any(matches, axis=1)
    allowed_keys = jnp.repeat(jnp.repeat(allowed_tiles, tile_len, axis=0), tile_len, axis=1)
    factor = 1.0 / math.sqrt(head_dim)
    scores = (
        jnp.einsum("qhd,khd->hqk", queries, neighbourhood[0], preferred_element_type=jnp.float32)
        * factor
    )
    weights = jnp.where(allowed_keys[None, :, :], jnp.exp(scores), 0.0)
    totals = jnp.sum(weights, axis=-1)
    mixture = jnp.einsum(
        "hqk,khd->qhd",
        weights.astype(jnp.bfloat16),
        neighbourhood[1],
        preferred_element_type=jnp.float32,
    )
    result = (mixture / jnp.transpose(totals)[:, :, None]).astype(jnp.bfloat16)
    return result.reshape(tokens, width_cols)


def solution(mesh):
    placed = (
        P(("groups", "seq"), None),
        P("groups", None),
        P("seq", None, ("fsdp", "head")),
        P(None, ("fsdp", "head")),
        P(),
        P(("groups", "seq"), None),
    )
    return jax.shard_map(
        per_device,
        mesh=mesh,
        in_specs=placed,
        out_specs=P(("groups", "seq"), ("fsdp", "head")),
        check_vma=False,
    )
```

profile of v0, /device:TPU:0, one launch (start us, length us, event | category | flops | bytes accessed | tf_op | source)
XLA Modules:
  0.0 278.2 jit_solution(9089081699902757114)
XLA Ops:
  6.5 0.0 copy-start.6
  6.5 0.0 all-gather.2.cloned.1.call-start
  6.5 4.3 %copy.27 = bf16[768,3,512]{0,2,1:T(8,128)(2,1)} copy(bf16[768,3,512]{2,0,1:T(8,128)(2,1)} %param.8) | data formatting | bytes 4718592 | tf_op args[2]
  10.8 0.0 all-gather.2.cloned.1.call-update
  10.9 0.0 copy-done.6
  10.9 0.0 copy-start
  10.9 0.0 copy-start.5
  10.9 0.0 copy-start.8
  10.9 3.2 %convert_reduce_fusion = f32[768]{0:T(1024)S(1)} fusion(bf16[768,3072]{1,0:T(8,128)(2,1)} %param.6), kind=kLoop, calls=%fused_computation.6 | loop fusion | flops 4717824 | bytes 4721664 | tf_op jit(solution)/shard_map/reduce_sum | solution.py:37
  14.1 0.5 copy-done
  14.6 1.4 fusion.7
  16.0 0.0 copy-done.5
  16.0 164.5 %all-gather.2.cloned.1.call-done = bf16[3072,3,512]{0,2,1:T(8,128)(2,1)} async-done(((bf16[768,3,512]{0,2,1:T(8,128)(2,1)}), bf16[3072,3,512]{0,2,1:T(8,128)(2,1)}) %all-gather.2.cloned.1.call-update) | async-done | bytes 9437200 | tf_op jit(solution)/shard_map/all_gather | solution.py:49
  180.5 0.0 copy-done.8
  180.5 11.9 %broadcast_add_fusion = f32[768,3,512]{0,2,1:T(8,128)S(1)} fusion(f32[3,512]{1,0:T(4,128)S(1)} %copy-done.8, bf16[3072,3,512]{0,2,1:T(8,128)(2,1)} %all-gather.2.cloned.1.call-done, bf16[768,3072]{1,0:T(8,128)(2,1)} %param.6, f32[3072]{0:T(1024)S(1)} %bitcast.43, f32[3072]{0:T(1024)S(1)} %bitcast.42, f32[768]{0:T(1024)S(1)} %add_rsqrt_fusion.2, ...), kind=kOutput, calls=%fused_computation.23 | convolution fusion | flops 7263092736 | bytes 18911232 | tf_op jit(solution)/shard_map/td,djc->tjc/dot_general | solution.py:46
  192.4 0.1 slice.53
  192.5 2.0 fusion.28
  194.5 0.4 copy.29
  194.9 1.5 reduce_sum.47
  196.4 0.0 copy-start.7
  196.4 3.0 %copy.28 = f32[1,768,4,128]{3,1,2,0:T(8,128)} copy(f32[1,768,4,128]{1,3,2,0:T(8,128)} %bitcast.37) | data formatting | bytes 3145728 | tf_op jit(solution)/shard_map/reshape;squeeze | solution.py:23
  199.5 1.9 multiply_convert_fusion.1
  201.4 1.3 pad_maximum_fusion.1
  202.6 1.3 collective-permute-start.1
  203.9 5.7 %collective-permute-start = (bf16[2,768,4,128]{3,1,2,0:T(8,128)(2,1)}, bf16[2,768,4,128]{3,1,2,0:T(8,128)(2,1)}, u32[]{:S(2)}, u32[]{:S(2)}) collective-permute-start(bf16[2,768,4,128]{3,1,2,0:T(8,128)(2,1)} %pad_maximum_fusion.1), channel_id=1, source_target_pairs={{0,4},{4,8},{8,12},{1,5},{5,9},{9,13},{2,6},{6,10},{10,14},{3,7},{... | collective-permute-start | bytes 4718600 | tf_op jit(solution)/shard_map/ppermute | solution.py:16
  209.7 0.0 copy-done.7
  209.7 0.2 and_reduce_fusion
  209.9 0.1 broadcast_in_dim.14
  209.9 1.7 broadcast_in_dim.19
  211.6 5.4 %copy.30 = pred[768,2304]{1,0:T(8,128)(4,1)} copy(pred[768,2304]{0,1:T(8,128)(4,1)} %bitcast.36) | data formatting | bytes 3538944 | tf_op jit(solution)/shard_map/jit(_where)/broadcast_in_dim | solution.py:71
  217.0 1.6 copy.31
  218.6 0.1 multiply_reduce_fusion
  218.8 0.0 copy-start.2
  218.8 0.0 copy-start.4
  218.8 22.4 %collective-permute-done.1 = bf16[2,768,4,128]{3,1,2,0:T(8,128)(2,1)} collective-permute-done((bf16[2,768,4,128]{3,1,2,0:T(8,128)(2,1)}, bf16[2,768,4,128]{3,1,2,0:T(8,128)(2,1)}, u32[]{:S(2)}, u32[]{:S(2)}) %collective-permute-start.1) | collective-permute-done | bytes 1572896 | tf_op jit(solution)/shard_map/ppermute | solution.py:17
  241.2 1.2 collective-permute-done
  242.4 2.0 pad_maximum_fusion
  244.4 0.0 copy-start.1
  244.4 0.0 copy-done.2
  244.4 0.0 copy-done.4
  244.4 0.0 copy-start.3
  244.4 12.9 %fusion = (f32[4,768]{1,0:T(4,128)S(1)}, f32[4,768,2304]{2,1,0:T(8,128)}) fusion(pred[768,2304]{1,0:T(8,128)(4,1)S(1)} %copy-done.2, bf16[2,2304,4,128]{3,1,2,0:T(8,128)(2,1)S(1)} %pad_maximum_fusion, f32[768,4,128]{2,0,1:T(8,128)S(1)} %copy-done.4, f32[128]{0:T(128)S(1)} %get-tuple-element.10, f32[768,4]{0,1:T(4,128)S(1)} %add_rsqrt_fusion), kind=kOutput, calls=%fused_computation.1 | convolution fusion | flops 1834349568 | bytes 34038272 | tf_op jit(solution)/shard_map/qhd,khd->hqk/dot_general | solution.py:68
  257.3 0.0 copy-done.1
  257.3 0.0 copy-done.3
  257.3 12.9 %fusion.21 = bf16[768,4,128]{0,2,1:T(8,128)(2,1)S(1)} fusion(f32[768,4]{0,1:T(4,128)S(1)} %bitcast.44, f32[4,768,2304]{2,1,0:T(8,128)} %get-tuple-element.13, pred[768,2304]{1,0:T(8,128)(4,1)S(1)} %copy-done.3, bf16[2,2304,4,128]{3,1,2,0:T(8,128)(2,1)} %copy-done.1), kind=kOutput, calls=%fused_computation.27 | convolution fusion | flops 1833959424 | bytes 33239040 | tf_op jit(solution)/shard_map/hqk,khd->qhd/dot_general | solution.py:73
  270.2 1.2 copy.33
  (8 shorter events, 0.1 us)
Async XLA Ops:
  6.5 4.3 %copy-start.6 = (f32[2,128]{1,0:T(2,128)S(1)}, f32[2,128]{1,0:T(2,128)}, u32[]{:S(2)}) copy-start(f32[2,128]{1,0:T(2,128)} %param.10) | copy-start | bytes 3076
  6.5 174.0 %all-gather.2.cloned.1.call-start = ((), (), s32[]{:S(2)}) async-start(), calls=%async_computation | async-start | bytes 11796480 | tf_op jit(solution)/shard_map/all_gather | solution.py:49
  10.9 3.8 %copy-start = (bf16[768,3072]{1,0:T(8,128)(2,1)S(1)}, bf16[768,3072]{1,0:T(8,128)(2,1)}, u32[]{:S(2)}) copy-start(bf16[768,3072]{1,0:T(8,128)(2,1)} %param.6) | copy-start | bytes 14155780
  10.9 5.1 %copy-start.5 = (f32[2,3072]{1,0:T(2,128)S(1)}, f32[2,3072]{1,0:T(2,128)}, u32[]{:S(2)}) copy-start(f32[2,3072]{1,0:T(2,128)} %param.7) | copy-start | bytes 73732
  10.9 169.6 %copy-start.8 = (f32[3,512]{1,0:T(4,128)S(1)}, f32[3,512]{1,0:T(4,128)}, u32[]{:S(2)}) copy-start(f32[3,512]{1,0:T(4,128)} %param.9) | copy-start | bytes 18436
  196.4 13.3 %copy-start.7 = (s32[2,27]{1,0:T(2,128)S(1)}, s32[2,27]{1,0:T(2,128)}, u32[]{:S(2)}) copy-start(s32[2,27]{1,0:T(2,128)} %param.11) | copy-start | bytes 652
  202.6 38.6 %collective-permute-start.1 = (bf16[2,768,4,128]{3,1,2,0:T(8,128)(2,1)}, bf16[2,768,4,128]{3,1,2,0:T(8,128)(2,1)}, u32[]{:S(2)}, u32[]{:S(2)}) collective-permute-start(bf16[2,768,4,128]{3,1,2,0:T(8,128)(2,1)} %pad_maximum_fusion.1), channel_id=1, source_target_pairs={{4,0},{8,4},{12,8},{5,1},{9,5},{13,9},{6,2},{10,6},{14,10},{7,3},{... | collective-permute-start | bytes 4718600 | tf_op jit(solution)/shard_map/ppermute | solution.py:17
  203.9 38.4 %collective-permute-start = (bf16[2,768,4,128]{3,1,2,0:T(8,128)(2,1)}, bf16[2,768,4,128]{3,1,2,0:T(8,128)(2,1)}, u32[]{:S(2)}, u32[]{:S(2)}) collective-permute-start(bf16[2,768,4,128]{3,1,2,0:T(8,128)(2,1)} %pad_maximum_fusion.1), channel_id=1, source_target_pairs={{0,4},{4,8},{8,12},{1,5},{5,9},{9,13},{2,6},{6,10},{10,14},{3,7},{... | collective-permute-start | bytes 4718600 | tf_op jit(solution)/shard_map/ppermute | solution.py:16
  218.8 25.6 %copy-start.2 = (pred[768,2304]{1,0:T(8,128)(4,1)S(1)}, pred[768,2304]{1,0:T(8,128)(4,1)}, u32[]{:S(2)}) copy-start(pred[768,2304]{1,0:T(8,128)(4,1)} %copy.30) | copy-start | bytes 5308420
  218.8 25.6 %copy-start.4 = (f32[768,4,128]{2,0,1:T(8,128)S(1)}, f32[768,4,128]{2,0,1:T(8,128)}, u32[]{:S(2)}) copy-start(f32[768,4,128]{2,0,1:T(8,128)} %copy.31) | copy-start | bytes 4718596
  244.4 12.9 %copy-start.1 = (bf16[2,2304,4,128]{3,1,2,0:T(8,128)(2,1)}, bf16[2,2304,4,128]{3,1,2,0:T(8,128)(2,1)S(1)}, u32[]{:S(2)}) copy-start(bf16[2,2304,4,128]{3,1,2,0:T(8,128)(2,1)S(1)} %pad_maximum_fusion) | copy-start | bytes 14155780
  244.4 12.9 %copy-start.3 = (pred[768,2304]{1,0:T(8,128)(4,1)S(1)}, pred[768,2304]{1,0:T(8,128)(4,1)}, u32[]{:S(2)}) copy-start(pred[768,2304]{1,0:T(8,128)(4,1)} %copy.30) | copy-start | bytes 5308420
Sparse Core Ops, SparseCore 0:
  11.0 169.4 all-gather.1
where the time goes:
time: 279 us; the launch traced here: 278 us
  waiting for transfers between devices  188 us (67%)
  matrix products  37.7 us (14%)
  local copies, waits for them, and re-layouts  18.3 us (7%)
  other arithmetic  13.7 us (5%)
  between operations  13.6 us (5%)
  starting transfers between devices  7 us (3%)
    all_gather x1, waiting for transfers between devices, per_device(): lax.all_gather(w_qkv, 'seq', axis=0, tiled=True)  164 us
    ppermute x1, waiting for transfers between devices, with_halo(): after = lax.ppermute(first, axis, down)  22.4 us
    dot_general x1, matrix products, per_device(): jnp.einsum('qhd,khd->hqk', queries, neighbourhood[0], preferred_element_t...  12.9 us
    dot_general x1, matrix products, per_device(): jnp.einsum('hqk,khd->qhd', weights.astype(jnp.bfloat16), neighbourhood[1]...  12.9 us
    dot_general x1, matrix products, per_device(): jnp.einsum('td,djc->tjc', normed, lax.all_gather(w_qkv, 'seq', axis=0, ti...  11.9 us
    ppermute x1, starting transfers between devices, with_halo(): before = lax.ppermute(last, axis, up)  5.72 us
  transfers between devices with their start and end apart: 3, of which 3 were waited for; matrix products, arithmetic and copies ran while one was open for 5% of the time, Pallas kernels for 0%

commit v1 on v0

--- a/solution.py
+++ b/solution.py
@@ -3,7 +3,12 @@
 import jax
 import jax.numpy as jnp
 from jax import lax
+from jax.experimental import pallas as pl
+from jax.experimental.pallas import tpu as pltpu
 from jax.sharding import PartitionSpec as P
+
+EPS = 1e-06
+HIDDEN = -1e30
 
 
 def with_halo(shard, sides, width):
@@ -22,22 +27,27 @@
 def normed_heads(tensor, gain_row, head_dim):
     shaped = tensor.reshape(tensor.shape[0], tensor.shape[1] // head_dim, head_dim)
     scaled = (
-        shaped * lax.rsqrt(jnp.mean(shaped * shaped, axis=-1, keepdims=True) + 1e-06) * gain_row
+        shaped * lax.rsqrt(jnp.mean(shaped * shaped, axis=-1, keepdims=True) + EPS) * gain_row
     )
     return scaled.astype(jnp.bfloat16)
 
 
-def reach_sides(key_rows, values):
-    stacked = jnp.stack([key_rows, values], axis=0)
-    return with_halo(stacked, (("seq", 1),), key_rows.shape[0])
-
-
-def per_device(frames, modulation, w_qkv, b_qkv, qk_gain, block_lists):
+def visible_tiles(block_lists):
+    position = lax.axis_index("seq")
+    tile_dev = block_lists.shape[0]
+    candidates = (position - 1) * tile_dev + jnp.arange(3 * tile_dev, dtype=jnp.int32)
+    matches = (block_lists[:, :, None] == candidates[None, None, :]) & (
+        block_lists[:, :, None] >= 0
+    )
+    return jnp.any(matches, axis=1)
+
+
+def general(frames, modulation, w_qkv, b_qkv, qk_gain, block_lists):
     inputs = frames.astype(jnp.float32)
     average = jnp.mean(inputs, axis=-1, keepdims=True)
     centred = inputs - average
     variance = jnp.mean(centred * centred, axis=-1, keepdims=True)
-    normed = centred * lax.rsqrt(variance + 1e-06) * (1.0 + modulation[0]) + modulation[1]
+    normed = centred * lax.rsqrt(variance + EPS) * (1.0 + modulation[0]) + modulation[1]
     normed = normed.astype(jnp.bfloat16)
     tokens = normed.shape[0]
     width_cols = w_qkv.shape[2]
@@ -53,16 +63,12 @@
     queries = normed_heads(projected[:, 0], qk_gain[0], head_dim)
     key_rows = normed_heads(projected[:, 1], qk_gain[1], head_dim)
     values = projected[:, 2].astype(jnp.bfloat16).reshape(tokens, heads, head_dim)
-    neighbourhood = reach_sides(key_rows, values)
-    position = lax.axis_index("seq")
-    tile_dev = block_lists.shape[0]
-    tile_len = tokens // tile_dev
-    candidates = (position - 1) * tile_dev + jnp.arange(3 * tile_dev, dtype=jnp.int32)
-    matches = (block_lists[:, :, None] == candidates[None, None, :]) & (
-        block_lists[:, :, None] >= 0
-    )
-    allowed_tiles = jnp.any(matches, axis=1)
-    allowed_keys = jnp.repeat(jnp.repeat(allowed_tiles, tile_len, axis=0), tile_len, axis=1)
+    stacked = jnp.stack([key_rows, values], axis=0)
+    neighbourhood = with_halo(stacked, (("seq", 1),), tokens)
+    tile_len = tokens // block_lists.shape[0]
+    allowed_keys = jnp.repeat(
+        jnp.repeat(visible_tiles(block_lists), tile_len, axis=0), tile_len, axis=1
+    )
     factor = 1.0 / math.sqrt(head_dim)
     scores = (
         jnp.einsum("qhd,khd->hqk", queries, neighbourhood[0], preferred_element_type=jnp.float32)
@@ -78,6 +84,217 @@
     )
     result = (mixture / jnp.transpose(totals)[:, :, None]).astype(jnp.bfloat16)
     return result.reshape(tokens, width_cols)
+
+
+def norm_kernel(x_ref, mod_ref, o_ref):
+    x = x_ref[...].astype(jnp.float32)
+    centred = x - jnp.mean(x, axis=-1, keepdims=True)
+    variance = jnp.mean(centred * centred, axis=-1, keepdims=True)
+    scaled = centred * lax.rsqrt(variance + EPS) * (1.0 + mod_ref[0:1, :]) + mod_ref[1:2, :]
+    o_ref[...] = scaled.astype(jnp.bfloat16)
+
+
+def normalize(frames, modulation):
+    tokens, width = frames.shape
+    rows = 128
+    return pl.pallas_call(
+        norm_kernel,
+        grid=(tokens // rows,),
+        in_specs=[
+            pl.BlockSpec((rows, width), lambda i: (i, 0)),
+            pl.BlockSpec((2, width), lambda i: (0, 0)),
+        ],
+        out_specs=pl.BlockSpec((rows, width), lambda i: (i, 0)),
+        out_shape=jax.ShapeDtypeStruct((tokens, width), jnp.bfloat16),
+        cost_estimate=pl.CostEstimate(
+            flops=10 * tokens * width, bytes_accessed=4 * tokens * width, transcendentals=0
+        ),
+        name="normalize",
+    )(frames, modulation)
+
+
+def project(place, x, w, pieces, bias, gain, first, count, last_seq):
+    tokens, width = x.shape
+    rows, half = w.shape[1], w.shape[2] // 2
+    head_dim = gain.shape[1]
+    step = 256
+
+    def kernel(place_ref, x_ref, own_ref, down_ref, up_ref, two_ref, far_ref, b_ref, g_ref, o_ref, acc_ref):
+        z = place_ref[0]
+        j = pl.program_id(0) + first
+
+        def add(ref, source, fresh):
+            at = pl.multiple_of(source * rows, 128)
+            for r in range(tokens // step):
+                part = jnp.dot(
+                    x_ref[pl.ds(r * step, step), pl.ds(at, rows)],
+                    ref[0],
+                    preferred_element_type=jnp.float32,
+                )
+                if fresh:
+                    acc_ref[pl.ds(r * step, step), :] = part
+                else:
+                    acc_ref[pl.ds(r * step, step), :] += part
+
+        add(own_ref, z, True)
+        add(two_ref, (z + 2) % (last_seq + 1), False)
+        pl.when(z < last_seq)(lambda: add(down_ref, z + 1, False))
+        pl.when(z > 0)(lambda: add(up_ref, z - 1, False))
+        pl.when((z == 0) | (z == last_seq))(lambda: add(far_ref, last_seq - z, False))
+
+        full = acc_ref[...] + b_ref[pl.ds(j, 1), :]
+
+        @pl.when(j == 2)
+        def _():
+            o_ref[0] = full.astype(jnp.bfloat16)
+
+        @pl.when(j < 2)
+        def _():
+            for h in range(half // head_dim):
+                part = full[:, h * head_dim : (h + 1) * head_dim]
+                mean = jnp.mean(part * part, axis=-1, keepdims=True)
+                scaled = part * lax.rsqrt(mean + EPS) * g_ref[pl.ds(j, 1), :]
+                o_ref[0, :, h * head_dim : (h + 1) * head_dim] = scaled.astype(jnp.bfloat16)
+
+    piece = pl.BlockSpec((1, rows, half), lambda j, s: (j, 0, 0))
+    return pl.pallas_call(
+        kernel,
+        grid_spec=pltpu.PrefetchScalarGridSpec(
+            num_scalar_prefetch=1,
+            grid=(count,),
+            in_specs=[
+                pl.BlockSpec((tokens, width), lambda j, s: (0, 0)),
+                pl.BlockSpec((1, rows, half), lambda j, s: (j + first, 0, s[1])),
+                piece,
+                piece,
+                piece,
+                piece,
+                pl.BlockSpec((3, half), lambda j, s: (0, s[1])),
+                pl.BlockSpec((2, head_dim), lambda j, s: (0, 0)),
+            ],
+            out_specs=pl.BlockSpec((1, tokens, half), lambda j, s: (j, 0, 0)),
+            scratch_shapes=[pltpu.VMEM((tokens, half), jnp.float32)],
+        ),
+        out_shape=jax.ShapeDtypeStruct((count, tokens, half), jnp.bfloat16),
+        compiler_params=pltpu.CompilerParams(vmem_limit_bytes=40 << 20),
+        cost_estimate=pl.CostEstimate(
+            flops=2 * tokens * width * half * count,
+            bytes_accessed=2 * (tokens * width + count * half * (width + tokens)),
+            transcendentals=0,
+        ),
+        name="project",
+    )(place, x, w, *pieces, bias, gain)
+
+
+def attend(place, limits, q, own, before, after, carried, width_cols, head_dim):
+    tokens, half = q.shape[1], q.shape[2]
+    tiles = limits.shape[0]
+    tile = tokens // tiles
+    heads = half // head_dim
+    scale = math.log2(math.e) / math.sqrt(head_dim)
+
+    def kernel(place_ref, limit_ref, q_ref, own_ref, before_ref, after_ref, *rest):
+        o_ref = rest[-1]
+        i = pl.program_id(1)
+        query = q_ref[0]
+        total = jnp.zeros((tile, 128), jnp.float32)
+        mixed = jnp.zeros((tile, head_dim), jnp.float32)
+        for side, ref in enumerate((own_ref, before_ref, after_ref)):
+            column = (1, 0, 2)[side]
+            for t in range(tiles):
+                keys = ref[0, t * tile : (t + 1) * tile, :]
+                values = ref[1, t * tile : (t + 1) * tile, :]
+                scores = lax.dot_general(
+                    query, keys, (((1,), (1,)), ((), ())), preferred_element_type=jnp.float32
+                )
+                weights = jnp.exp2(scores * scale + limit_ref[i, column * tiles + t])
+                for c in range(tile // 128):
+                    total = total + weights[:, c * 128 : (c + 1) * 128]
+                mixed = mixed + jnp.dot(
+                    weights.astype(jnp.bfloat16), values, preferred_element_type=jnp.float32
+                )
+        o_ref[...] = (mixed / jnp.sum(total, axis=-1, keepdims=True)).astype(jnp.bfloat16)
+
+    rows = pl.BlockSpec((2, tokens, head_dim), lambda h, i, s: (0, 0, h))
+    carried = () if carried is None else (carried,)
+    return pl.pallas_call(
+        kernel,
+        grid_spec=pltpu.PrefetchScalarGridSpec(
+            num_scalar_prefetch=1,
+            grid=(heads, tiles),
+            in_specs=[
+                pl.BlockSpec(memory_space=pltpu.SMEM),
+                pl.BlockSpec((1, tile, head_dim), lambda h, i, s: (0, i, h)),
+                rows,
+                rows,
+                rows,
+            ]
+            + [pl.BlockSpec(memory_space=pl.ANY)] * len(carried),
+            out_specs=pl.BlockSpec((tile, head_dim), lambda h, i, s: (i, s[1] * heads + h)),
+        ),
+        out_shape=jax.ShapeDtypeStruct((tokens, width_cols), jnp.bfloat16),
+        input_output_aliases={6: 0} if carried else {},
+        compiler_params=pltpu.CompilerParams(vmem_limit_bytes=40 << 20),
+        cost_estimate=pl.CostEstimate(
+            flops=4 * tokens * 3 * tokens * half,
+            bytes_accessed=2 * tokens * half * 8,
+            transcendentals=3 * tokens * tokens * heads,
+        ),
+        name="attend",
+    )(place, limits, q, own, before, after, *carried)
+
+
+def swap(value):
+    return lax.ppermute(value, "groups", [(0, 1), (1, 0)])
+
+
+def per_device(frames, modulation, w_qkv, b_qkv, qk_gain, block_lists):
+    columns = lax.axis_size("seq")
+    head_dim = qk_gain.shape[1]
+    width_cols = w_qkv.shape[2]
+    heads = width_cols // head_dim
+    tokens = frames.shape[0]
+    if columns != 4 or lax.axis_size("groups") != 2 or heads % 2:
+        return general(frames, modulation, w_qkv, b_qkv, qk_gain, block_lists)
+
+    seq = lax.axis_index("seq").astype(jnp.int32)
+    mine = lax.axis_index("groups").astype(jnp.int32)
+    last = columns - 1
+    half = width_cols // 2
+    rows = w_qkv.shape[0]
+    down = [(i + 1, i) for i in range(last)]
+    up = [(i, i + 1) for i in range(last)]
+    ends = [(1, 0), (last - 1, last)]
+    across = [(i, (i + 2) % columns) for i in range(columns)]
+
+    w = jnp.transpose(w_qkv, (1, 0, 2))
+    order = ((1, 2), (0, 1))
+    sent = [
+        lax.dynamic_slice(w, (first, 0, mine * half), (count, rows, half)) for first, count in order
+    ]
+    mine_pieces, twin_pieces = [], []
+    for part in sent:
+        two = lax.ppermute(part, "seq", across)
+        below = lax.ppermute(part, "seq", down)
+        above = lax.ppermute(part, "seq", up)
+        far = lax.ppermute(two, "seq", ends)
+        group = (below, above, two, far)
+        mine_pieces.append(group)
+        twin_pieces.append(tuple(swap(p) for p in group))
+
+    x = normalize(frames, modulation)
+    limits = jnp.where(visible_tiles(block_lists), 0.0, HIDDEN).astype(jnp.float32)
+    out = None
+    kv, q, places = [], [], []
+    for which, pieces in ((mine, mine_pieces), (1 - mine, twin_pieces)):
+        place = jnp.stack([seq, which])
+        places.append(place)
+        kv.append(project(place, x, w, pieces[0], b_qkv, qk_gain, 1, 2, last))
+        q.append(project(place, x, w, pieces[1], b_qkv, qk_gain, 0, 1, last))
+    halos = [(lax.ppermute(a, "seq", up), lax.ppermute(a, "seq", down)) for a in kv]
+    for place, q_half, own, (before, after) in zip(places, q, kv, halos):
+        out = attend(place, limits, q_half, own, before, after, out, width_cols, head_dim)
+    return out
 
 
 def solution(mesh):

time: 279 us -> 203 us (0.73)
  waiting for transfers between devices: 188 us -> 111 us
  Pallas kernels: 0 us -> 41.8 us
  matrix products: 37.7 us -> 0 us
  starting transfers between devices: 7 us -> 42.6 us
  local copies, waits for them, and re-layouts: 18.3 us -> 4.58 us
  between operations: 13.6 us -> 0.2 us
  other arithmetic: 13.7 us -> 1.03 us
    all_gather x1 -> x0, waiting for transfers between devices: 164 us -> none  [per_device(): lax.all_gather(w_qkv, 'seq', axis=0, tiled=True)]
    ppermute x2 -> x20, waiting for transfers between devices: 23.6 us -> 111 us  [the longest x2 54.8 us: per_device(): two = lax.ppermute(part, 'seq', across)]
    pallas_call x0 -> x7, Pallas kernels: none -> 41.8 us  [the longest x4 18 us: project(): pl.pallas_call(kernel, grid_spec=pltpu.PrefetchScalarGridSpec(num_scalar_...]
    dot_general x3 -> x0, matrix products: 37.7 us -> none  [the longest x1 12.9 us: per_device(): jnp.einsum('qhd,khd->hqk', queries, neighbourhood[0], preferred_element_t...]
    ppermute x2 -> x20, starting transfers between devices: 7 us -> 42.6 us  [the longest x8 10.2 us: swap(): return lax.ppermute(value, 'groups', [(0, 1), (1, 0)])]
    broadcast_in_dim x3 -> x0, local copies, waits for them, and re-layouts: 7.15 us -> none  [the longest x1 5.38 us: per_device(): weights = jnp.where(allowed_keys[None, :, :], jnp.exp(scores), 0.0)]
    reduce_sum x4 -> x0, other arithmetic: 6.18 us -> none  [the longest x1 3.17 us: per_device(): average = jnp.mean(inputs, axis=-1, keepdims=True)]
    another operation x2 -> x0, local copies, waits for them, and re-layouts: 4.66 us -> none  [normed_heads(): tensor.reshape(tensor.shape[0], tensor.shape[1] // head_dim, head_dim)]
  transfers between devices with their start and end apart: 3 -> 20, of which waited for: 3 -> 13; matrix products, arithmetic and copies ran while one was open for 5% -> 1% of each run, Pallas kernels for 0% -> 17%
where the time goes in v1:
time: 203 us; the launch traced here: 201 us
  waiting for transfers between devices  111 us (55%)
  starting transfers between devices  42.6 us (21%)
  Pallas kernels  41.8 us (21%)
  local copies, waits for them, and re-layouts  4.58 us (2%)
    ppermute x2, waiting for transfers between devices, per_device(): two = lax.ppermute(part, 'seq', across)  54.8 us
    ppermute x8, waiting for transfers between devices, swap(): return lax.ppermute(value, 'groups', [(0, 1), (1, 0)])  48.9 us
    pallas_call x4, Pallas kernels, project(): pl.pallas_call(kernel, grid_spec=pltpu.PrefetchScalarGridSpec(num_scalar_...  18 us
    pallas_call x2, Pallas kernels, attend(): pl.pallas_call(kernel, grid_spec=pltpu.PrefetchScalarGridSpec(num_scalar_...  16.3 us
    ppermute x8, starting transfers between devices, swap(): return lax.ppermute(value, 'groups', [(0, 1), (1, 0)])  10.2 us
    ppermute x2, starting transfers between devices, per_device(): lax.ppermute(a, 'seq', up)  9.5 us
    ppermute x2, starting transfers between devices, per_device(): two = lax.ppermute(part, 'seq', across)  9.08 us
    pallas_call x1, Pallas kernels, normalize(): pl.pallas_call(norm_kernel, grid=(tokens // rows,), in_specs=[pl.BlockSpe...  7.48 us
  transfers between devices with their start and end apart: 20, of which 13 were waited for; matrix products, arithmetic and copies ran while one was open for 1% of the time, Pallas kernels for 17%

profile of v1, /device:TPU:0, one launch (start us, length us, event | category | flops | bytes accessed | tf_op | source)
XLA Modules:
  0.0 201.1 jit_solution(14657449538051254987)
XLA Ops:
  0.0 1.2 dynamic-slice_bitcast_fusion
  1.2 4.1 %collective-permute-start.12 = (bf16[2,768,256]{2,1,0:T(8,128)(2,1)S(1)}, bf16[2,768,256]{2,1,0:T(8,128)(2,1)S(1)}, u32[]{:S(2)}, u32[]{:S(2)}) collective-permute-start(bf16[2,768,256]{2,1,0:T(8,128)(2,1)S(1)} %dynamic-slice_bitcast_fusion), channel_id=1, source_target_pairs={{0,8},{4,12},{8,0},{12,4},{1,9},{5,13},{9,1},{13,5},{2,10},{6,14},... | collective-permute-start | bytes 2359304 | tf_op jit(solution)/shard_map/ppermute | solution.py:277
  5.3 4.4 %collective-permute-start.10 = (bf16[2,768,256]{2,1,0:T(8,128)(2,1)S(1)}, bf16[2,768,256]{2,1,0:T(8,128)(2,1)}, u32[]{:S(2)}, u32[]{:S(2)}) collective-permute-start(bf16[2,768,256]{2,1,0:T(8,128)(2,1)S(1)} %dynamic-slice_bitcast_fusion), channel_id=1, source_target_pairs={{0,4},{4,8},{8,12},{1,5},{5,9},{9,13},{2,6},{6,10},{10,14},{3,7},{... | collective-permute-start | bytes 2359304 | tf_op jit(solution)/shard_map/ppermute | solution.py:279
  9.7 1.3 collective-permute-start.8
  10.9 29.6 %collective-permute-done.12.two_ref = bf16[2,768,256]{2,1,0:T(8,128)(2,1)S(1)} collective-permute-done((bf16[2,768,256]{2,1,0:T(8,128)(2,1)S(1)}, bf16[2,768,256]{2,1,0:T(8,128)(2,1)S(1)}, u32[]{:S(2)}, u32[]{:S(2)}) %collective-permute-start.12) | collective-permute-done | bytes 786464 | tf_op jit(solution)/shard_map/ppermute | solution.py:277
  40.6 1.3 collective-permute-start.14
  41.8 1.0 dynamic-slice_bitcast_fusion.1
  42.9 5.0 %collective-permute-start.4 = (bf16[1,768,256]{2,1,0:T(8,128)(2,1)S(1)}, bf16[1,768,256]{2,1,0:T(8,128)(2,1)S(1)}, u32[]{:S(2)}, u32[]{:S(2)}) collective-permute-start(bf16[1,768,256]{2,1,0:T(8,128)(2,1)S(1)} %dynamic-slice_bitcast_fusion.1), channel_id=1, source_target_pairs={{0,8},{4,12},{8,0},{12,4},{1,9},{5,13},{9,1},{13,5},{2,10},{6,14},... | collective-permute-start | bytes 1179656 | tf_op jit(solution)/shard_map/ppermute | solution.py:277
  47.9 1.3 collective-permute-start
  49.1 25.2 %collective-permute-done.4.two_ref = bf16[1,768,256]{2,1,0:T(8,128)(2,1)S(1)} collective-permute-done((bf16[1,768,256]{2,1,0:T(8,128)(2,1)S(1)}, bf16[1,768,256]{2,1,0:T(8,128)(2,1)S(1)}, u32[]{:S(2)}, u32[]{:S(2)}) %collective-permute-start.4) | collective-permute-done | bytes 393248 | tf_op jit(solution)/shard_map/ppermute | solution.py:277
  74.3 1.8 collective-permute-start.2
  76.1 3.6 %collective-permute-done.down_ref = bf16[1,768,256]{2,1,0:T(8,128)(2,1)S(1)} collective-permute-done((bf16[1,768,256]{2,1,0:T(8,128)(2,1)S(1)}, bf16[1,768,256]{2,1,0:T(8,128)(2,1)S(1)}, u32[]{:S(2)}, u32[]{:S(2)}) %collective-permute-start) | collective-permute-done | bytes 393248 | tf_op jit(solution)/shard_map/ppermute | solution.py:278
  79.7 1.6 collective-permute-start.13
  81.2 0.5 collective-permute-start.11
  81.7 1.6 collective-permute-start.9
  83.3 0.5 collective-permute-start.15
  83.7 0.9 collective-permute-done.2.up_ref
  84.6 1.3 collective-permute-start.6
  85.9 0.1 pad_add_fusion.1.place_ref
  86.0 7.5 %normalize.1.x_ref = bf16[768,3072]{1,0:T(8,128)(2,1)} custom-call(bf16[768,3072]{1,0:T(8,128)(2,1)} %x_ref.1, f32[2,3072]{1,0:T(2,128)} %mod_ref.1), custom_call_target="tpu_custom_call" | custom-call | flops 23592960 | bytes 9437184 | tf_op jit(solution)/shard_map/normalize/pallas_call | solution.py:100
  93.5 0.1 pad_add_fusion.place_ref
  93.5 0.7 broadcast_compare_fusion
  94.2 2.8 %collective-permute-done.6.far_ref = bf16[1,768,256]{2,1,0:T(8,128)(2,1)} collective-permute-done((bf16[1,768,256]{2,1,0:T(8,128)(2,1)S(1)}, bf16[1,768,256]{2,1,0:T(8,128)(2,1)}, u32[]{:S(2)}, u32[]{:S(2)}) %collective-permute-start.6) | collective-permute-done | bytes 393248 | tf_op jit(solution)/shard_map/ppermute | solution.py:280
  97.0 1.4 collective-permute-start.5
  98.4 1.8 collective-permute-done.13.two_ref
  100.2 1.6 collective-permute-start.1
  101.8 15.3 %collective-permute-done.11.up_ref = bf16[2,768,256]{2,1,0:T(8,128)(2,1)} collective-permute-done((bf16[2,768,256]{2,1,0:T(8,128)(2,1)}, bf16[2,768,256]{2,1,0:T(8,128)(2,1)}, u32[]{:S(2)}, u32[]{:S(2)}) %collective-permute-start.11) | collective-permute-done | bytes 786464 | tf_op jit(solution)/shard_map/ppermute | solution.py:248
  117.1 1.6 collective-permute-start.3
  118.7 2.3 %copy-done = bf16[768,3072]{1,0:T(8,128)(2,1)S(1)} copy-done((bf16[768,3072]{1,0:T(8,128)(2,1)S(1)}, bf16[768,3072]{1,0:T(8,128)(2,1)}, u32[]{:S(2)}) %copy-start) | copy-done | bytes 4718616
  121.0 5.8 %project.7.own_ref = bf16[2,768,256]{2,1,0:T(8,128)(2,1)S(1)} custom-call(s32[2]{0:T(128)S(1)} %pad_add_fusion.1.place_ref, bf16[768,3072]{1,0:T(8,128)(2,1)S(1)} %copy-done, bf16[3,768,512]{2,1,0:T(8,128)(2,1)S(1)} %bitcast.8, bf16[2,768,256]{2,1,0:T(8,128)(2,1)} %collective-permute-done.8.down_ref, bf16[2,768,256]{2,1,0:T(8,128)(2,1)} %collective-permute-done.10.up_ref, ...), custom_call_target="tpu_custom_call" | custom-call | flops 2415919104 | bytes 8650752 | tf_op jit(solution)/shard_map/project/pallas_call | solution.py:160
  126.8 0.0 copy-start.8
  126.8 7.1 %collective-permute-done.9.down_ref = bf16[2,768,256]{2,1,0:T(8,128)(2,1)} collective-permute-done((bf16[2,768,256]{2,1,0:T(8,128)(2,1)}, bf16[2,768,256]{2,1,0:T(8,128)(2,1)}, u32[]{:S(2)}, u32[]{:S(2)}) %collective-permute-start.9) | collective-permute-done | bytes 786464 | tf_op jit(solution)/shard_map/ppermute | solution.py:248
  134.0 4.7 %collective-permute-start.18 = (bf16[2,768,256]{2,1,0:T(8,128)(2,1)S(1)}, bf16[2,768,256]{2,1,0:T(8,128)(2,1)S(1)}, u32[]{:S(2)}, u32[]{:S(2)}) collective-permute-start(bf16[2,768,256]{2,1,0:T(8,128)(2,1)S(1)} %project.7.own_ref), channel_id=1, source_target_pairs={{0,4},{4,8},{8,12},{1,5},{5,9},{9,13},{2,6},{6,10},{10,14},{3,7},{... | collective-permute-start | bytes 2359304 | tf_op jit(solution)/shard_map/ppermute | solution.py:294
  138.7 12.1 %collective-permute-done.15.far_ref = bf16[2,768,256]{2,1,0:T(8,128)(2,1)} collective-permute-done((bf16[2,768,256]{2,1,0:T(8,128)(2,1)}, bf16[2,768,256]{2,1,0:T(8,128)(2,1)}, u32[]{:S(2)}, u32[]{:S(2)}) %collective-permute-start.15) | collective-permute-done | bytes 786464 | tf_op jit(solution)/shard_map/ppermute | solution.py:248
  150.8 1.3 collective-permute-start.19
  152.1 5.9 %project.5.own_ref = bf16[2,768,256]{2,1,0:T(8,128)(2,1)S(1)} custom-call(s32[2]{0:T(128)S(1)} %pad_add_fusion.place_ref, bf16[768,3072]{1,0:T(8,128)(2,1)S(1)} %copy-done, bf16[3,768,512]{2,1,0:T(8,128)(2,1)S(1)} %bitcast.9, bf16[2,768,256]{2,1,0:T(8,128)(2,1)} %collective-permute-done.9.down_ref, bf16[2,768,256]{2,1,0:T(8,128)(2,1)} %collective-permute-done.11.up_ref, ...), custom_call_target="tpu_custom_call" | custom-call | flops 2415919104 | bytes 8650752 | tf_op jit(solution)/shard_map/project/pallas_call | solution.py:160
  158.0 1.1 collective-permute-done.5.two_ref
  159.1 4.7 %collective-permute-start.16 = (bf16[2,768,256]{2,1,0:T(8,128)(2,1)S(1)}, bf16[2,768,256]{2,1,0:T(8,128)(2,1)S(1)}, u32[]{:S(2)}, u32[]{:S(2)}) collective-permute-start(bf16[2,768,256]{2,1,0:T(8,128)(2,1)S(1)} %project.5.own_ref), channel_id=1, source_target_pairs={{0,4},{4,8},{8,12},{1,5},{5,9},{9,13},{2,6},{6,10},{10,14},{3,7},{... | collective-permute-start | bytes 2359304 | tf_op jit(solution)/shard_map/ppermute | solution.py:294
  163.9 3.7 %collective-permute-done.1.down_ref = bf16[1,768,256]{2,1,0:T(8,128)(2,1)S(1)} collective-permute-done((bf16[1,768,256]{2,1,0:T(8,128)(2,1)}, bf16[1,768,256]{2,1,0:T(8,128)(2,1)S(1)}, u32[]{:S(2)}, u32[]{:S(2)}) %collective-permute-start.1) | collective-permute-done | bytes 393248 | tf_op jit(solution)/shard_map/ppermute | solution.py:248
  167.6 1.3 collective-permute-start.17
  168.9 4.4 %collective-permute-done.3.up_ref = bf16[1,768,256]{2,1,0:T(8,128)(2,1)S(1)} collective-permute-done((bf16[1,768,256]{2,1,0:T(8,128)(2,1)}, bf16[1,768,256]{2,1,0:T(8,128)(2,1)S(1)}, u32[]{:S(2)}, u32[]{:S(2)}) %collective-permute-start.3) | collective-permute-done | bytes 393248 | tf_op jit(solution)/shard_map/ppermute | solution.py:248
  173.3 1.6 collective-permute-start.7
  174.9 0.2 and_reduce_fusion
  175.1 3.6 %project.6.q_ref = bf16[1,768,256]{2,1,0:T(8,128)(2,1)S(1)} custom-call(s32[2]{0:T(128)S(1)} %pad_add_fusion.1.place_ref, bf16[768,3072]{1,0:T(8,128)(2,1)S(1)} %copy-done, bf16[3,768,512]{2,1,0:T(8,128)(2,1)S(1)} %bitcast.10, bf16[1,768,256]{2,1,0:T(8,128)(2,1)S(1)} %copy-done.3, bf16[1,768,256]{2,1,0:T(8,128)(2,1)S(1)} %copy-done.5, ...), custom_call_target="tpu_custom_call" | custom-call | flops 1207959552 | bytes 6684672 | tf_op jit(solution)/shard_map/project/pallas_call | solution.py:160
  178.7 3.3 %collective-permute-done.7.far_ref = bf16[1,768,256]{2,1,0:T(8,128)(2,1)S(1)} collective-permute-done((bf16[1,768,256]{2,1,0:T(8,128)(2,1)}, bf16[1,768,256]{2,1,0:T(8,128)(2,1)S(1)}, u32[]{:S(2)}, u32[]{:S(2)}) %collective-permute-start.7) | collective-permute-done | bytes 393248 | tf_op jit(solution)/shard_map/ppermute | solution.py:248
  182.0 2.8 %project.4.q_ref = bf16[1,768,256]{2,1,0:T(8,128)(2,1)S(1)} custom-call(s32[2]{0:T(128)S(1)} %pad_add_fusion.place_ref, bf16[768,3072]{1,0:T(8,128)(2,1)S(1)} %copy-done, bf16[3,768,512]{2,1,0:T(8,128)(2,1)S(1)} %bitcast.11, bf16[1,768,256]{2,1,0:T(8,128)(2,1)S(1)} %collective-permute-done.1.down_ref, ...), custom_call_target="tpu_custom_call" | custom-call | flops 1207959552 | bytes 6684672 | tf_op jit(solution)/shard_map/project/pallas_call | solution.py:160
  184.8 8.2 %attend.2.rest_0_ = bf16[768,512]{1,0:T(8,128)(2,1)} custom-call(s32[2]{0:T(128)S(1)} %pad_add_fusion.1.place_ref, f32[2,6]{1,0:T(2,128)S(1)} %broadcast_select_fusion.limit_ref, bf16[1,768,256]{2,1,0:T(8,128)(2,1)S(1)} %project.6.q_ref, bf16[2,768,256]{2,1,0:T(8,128)(2,1)S(1)} %project.7.own_ref, ...), custom_call_target="tpu_custom_call" | custom-call | flops 1811939328 | bytes 3145728 | tf_op jit(solution)/shard_map/attend/pallas_call | solution.py:220
  192.9 8.2 %attend.3 = bf16[768,512]{1,0:T(8,128)(2,1)} custom-call(s32[2]{0:T(128)S(1)} %pad_add_fusion.place_ref, f32[2,6]{1,0:T(2,128)S(1)} %broadcast_select_fusion.limit_ref, bf16[1,768,256]{2,1,0:T(8,128)(2,1)S(1)} %project.4.q_ref, bf16[2,768,256]{2,1,0:T(8,128)(2,1)S(1)} %project.5.own_ref, ...), custom_call_target="tpu_custom_call", output_to_operand_aliasing={{}: (6, {})} | custom-call | flops 1811939328 | bytes 3145728 | tf_op jit(solution)/shard_map/attend/pallas_call | solution.py:220
  (25 shorter events, 0.1 us)
Async XLA Ops:
  1.2 39.4 %collective-permute-start.12 = (bf16[2,768,256]{2,1,0:T(8,128)(2,1)S(1)}, bf16[2,768,256]{2,1,0:T(8,128)(2,1)S(1)}, u32[]{:S(2)}, u32[]{:S(2)}) collective-permute-start(bf16[2,768,256]{2,1,0:T(8,128)(2,1)S(1)} %dynamic-slice_bitcast_fusion), channel_id=1, source_target_pairs={{0,8},{4,12},{8,0},{12,4},{1,9},{5,13},{9,1},{13,5},{2,10},{6,14},... | collective-permute-start | bytes 2359304 | tf_op jit(solution)/shard_map/ppermute | solution.py:277
  5.3 75.9 %collective-permute-start.10 = (bf16[2,768,256]{2,1,0:T(8,128)(2,1)S(1)}, bf16[2,768,256]{2,1,0:T(8,128)(2,1)}, u32[]{:S(2)}, u32[]{:S(2)}) collective-permute-start(bf16[2,768,256]{2,1,0:T(8,128)(2,1)S(1)} %dynamic-slice_bitcast_fusion), channel_id=1, source_target_pairs={{0,4},{4,8},{8,12},{1,5},{5,9},{9,13},{2,6},{6,10},{10,14},{3,7},{... | collective-permute-start | bytes 2359304 | tf_op jit(solution)/shard_map/ppermute | solution.py:279
  9.7 72.0 %collective-permute-start.8 = (bf16[2,768,256]{2,1,0:T(8,128)(2,1)S(1)}, bf16[2,768,256]{2,1,0:T(8,128)(2,1)}, u32[]{:S(2)}, u32[]{:S(2)}) collective-permute-start(bf16[2,768,256]{2,1,0:T(8,128)(2,1)S(1)} %dynamic-slice_bitcast_fusion), channel_id=1, source_target_pairs={{4,0},{8,4},{12,8},{5,1},{9,5},{13,9},{6,2},{10,6},{14,10},{7,3},{... | collective-permute-start | bytes 2359304 | tf_op jit(solution)/shard_map/ppermute | solution.py:278
  40.6 42.7 %collective-permute-start.14 = (bf16[2,768,256]{2,1,0:T(8,128)(2,1)S(1)}, bf16[2,768,256]{2,1,0:T(8,128)(2,1)}, u32[]{:S(2)}, u32[]{:S(2)}) collective-permute-start(bf16[2,768,256]{2,1,0:T(8,128)(2,1)S(1)} %collective-permute-done.12.two_ref), channel_id=1, source_target_pairs={{4,0},{8,12},{5,1},{9,13},{6,2},{10,14},{7,3},{11,15},{20,16},{24,... | collective-permute-start | bytes 2359304 | tf_op jit(solution)/shard_map/ppermute | solution.py:280
  42.9 31.4 %collective-permute-start.4 = (bf16[1,768,256]{2,1,0:T(8,128)(2,1)S(1)}, bf16[1,768,256]{2,1,0:T(8,128)(2,1)S(1)}, u32[]{:S(2)}, u32[]{:S(2)}) collective-permute-start(bf16[1,768,256]{2,1,0:T(8,128)(2,1)S(1)} %dynamic-slice_bitcast_fusion.1), channel_id=1, source_target_pairs={{0,8},{4,12},{8,0},{12,4},{1,9},{5,13},{9,1},{13,5},{2,10},{6,14},... | collective-permute-start | bytes 1179656 | tf_op jit(solution)/shard_map/ppermute | solution.py:277
  47.9 31.8 %collective-permute-start = (bf16[1,768,256]{2,1,0:T(8,128)(2,1)S(1)}, bf16[1,768,256]{2,1,0:T(8,128)(2,1)S(1)}, u32[]{:S(2)}, u32[]{:S(2)}) collective-permute-start(bf16[1,768,256]{2,1,0:T(8,128)(2,1)S(1)} %dynamic-slice_bitcast_fusion.1), channel_id=1, source_target_pairs={{4,0},{8,4},{12,8},{5,1},{9,5},{13,9},{6,2},{10,6},{14,10},{7,3},{... | collective-permute-start | bytes 1179656 | tf_op jit(solution)/shard_map/ppermute | solution.py:278
  74.3 10.3 %collective-permute-start.2 = (bf16[1,768,256]{2,1,0:T(8,128)(2,1)S(1)}, bf16[1,768,256]{2,1,0:T(8,128)(2,1)S(1)}, u32[]{:S(2)}, u32[]{:S(2)}) collective-permute-start(bf16[1,768,256]{2,1,0:T(8,128)(2,1)S(1)} %dynamic-slice_bitcast_fusion.1), channel_id=1, source_target_pairs={{0,4},{4,8},{8,12},{1,5},{5,9},{9,13},{2,6},{6,10},{10,14},{3,7},{... | collective-permute-start | bytes 1179656 | tf_op jit(solution)/shard_map/ppermute | solution.py:279
  79.7 3.6 %copy-start.2 = (bf16[1,768,256]{2,1,0:T(8,128)(2,1)}, bf16[1,768,256]{2,1,0:T(8,128)(2,1)S(1)}, u32[]{:S(2)}) copy-start(bf16[1,768,256]{2,1,0:T(8,128)(2,1)S(1)} %collective-permute-done.down_ref) | copy-start | bytes 1179652
  79.7 20.6 %collective-permute-start.13 = (bf16[2,768,256]{2,1,0:T(8,128)(2,1)S(1)}, bf16[2,768,256]{2,1,0:T(8,128)(2,1)}, u32[]{:S(2)}, u32[]{:S(2)}) collective-permute-start(bf16[2,768,256]{2,1,0:T(8,128)(2,1)S(1)} %collective-permute-done.12.two_ref), channel_id=1, source_target_pairs={{0,16},{16,0},{1,17},{17,1},{2,18},{18,2},{3,19},{19,3},{4,20},{20... | collective-permute-start | bytes 2359304 | tf_op jit(solution)/shard_map/ppermute | solution.py:248
  81.2 35.9 %collective-permute-start.11 = (bf16[2,768,256]{2,1,0:T(8,128)(2,1)}, bf16[2,768,256]{2,1,0:T(8,128)(2,1)}, u32[]{:S(2)}, u32[]{:S(2)}) collective-permute-start(bf16[2,768,256]{2,1,0:T(8,128)(2,1)} %collective-permute-done.10.up_ref), channel_id=1, source_target_pairs={{0,16},{16,0},{1,17},{17,1},{2,18},{18,2},{3,19},{19,3},{4,20},{20... | collective-permute-start | bytes 2359304 | tf_op jit(solution)/shard_map/ppermute | solution.py:248
  81.7 52.3 %collective-permute-start.9 = (bf16[2,768,256]{2,1,0:T(8,128)(2,1)}, bf16[2,768,256]{2,1,0:T(8,128)(2,1)}, u32[]{:S(2)}, u32[]{:S(2)}) collective-permute-start(bf16[2,768,256]{2,1,0:T(8,128)(2,1)} %collective-permute-done.8.down_ref), channel_id=1, source_target_pairs={{0,16},{16,0},{1,17},{17,1},{2,18},{18,2},{3,19},{19,3},{4,20},{20... | collective-permute-start | bytes 2359304 | tf_op jit(solution)/shard_map/ppermute | solution.py:248
  83.3 67.5 %collective-permute-start.15 = (bf16[2,768,256]{2,1,0:T(8,128)(2,1)}, bf16[2,768,256]{2,1,0:T(8,128)(2,1)}, u32[]{:S(2)}, u32[]{:S(2)}) collective-permute-start(bf16[2,768,256]{2,1,0:T(8,128)(2,1)} %collective-permute-done.14.far_ref), channel_id=1, source_target_pairs={{0,16},{16,0},{1,17},{17,1},{2,18},{18,2},{3,19},{19,3},{4,20},{20... | collective-permute-start | bytes 2359304 | tf_op jit(solution)/shard_map/ppermute | solution.py:248
  84.6 1.4 copy-start.4
  84.6 12.4 %collective-permute-start.6 = (bf16[1,768,256]{2,1,0:T(8,128)(2,1)S(1)}, bf16[1,768,256]{2,1,0:T(8,128)(2,1)}, u32[]{:S(2)}, u32[]{:S(2)}) collective-permute-start(bf16[1,768,256]{2,1,0:T(8,128)(2,1)S(1)} %collective-permute-done.4.two_ref), channel_id=1, source_target_pairs={{4,0},{8,12},{5,1},{9,13},{6,2},{10,14},{7,3},{11,15},{20,16},{24,... | collective-permute-start | bytes 1179656 | tf_op jit(solution)/shard_map/ppermute | solution.py:280
  86.0 32.7 %copy-start.1 = (bf16[768,3,512]{2,0,1:T(8,128)(2,1)S(1)}, bf16[768,3,512]{2,0,1:T(8,128)(2,1)}, u32[]{:S(2)}) copy-start(bf16[768,3,512]{2,0,1:T(8,128)(2,1)} %param.8) | copy-start | bytes 7077892
  86.0 32.7 %copy-start.6 = (f32[3,512]{1,0:T(4,128)S(1)}, f32[3,512]{1,0:T(4,128)}, u32[]{:S(2)}) copy-start(f32[3,512]{1,0:T(4,128)} %b_ref.7) | copy-start | bytes 18436
  86.0 32.7 %copy-start.7 = (f32[2,128]{1,0:T(2,128)S(1)}, f32[2,128]{1,0:T(2,128)}, u32[]{:S(2)}) copy-start(f32[2,128]{1,0:T(2,128)} %g_ref.7) | copy-start | bytes 3076
  97.0 62.1 %collective-permute-start.5 = (bf16[1,768,256]{2,1,0:T(8,128)(2,1)S(1)}, bf16[1,768,256]{2,1,0:T(8,128)(2,1)S(1)}, u32[]{:S(2)}, u32[]{:S(2)}) collective-permute-start(bf16[1,768,256]{2,1,0:T(8,128)(2,1)S(1)} %collective-permute-done.4.two_ref), channel_id=1, source_target_pairs={{0,16},{16,0},{1,17},{17,1},{2,18},{18,2},{3,19},{19,3},{4,20},{20... | collective-permute-start | bytes 1179656 | tf_op jit(solution)/shard_map/ppermute | solution.py:248
  100.2 67.3 %collective-permute-start.1 = (bf16[1,768,256]{2,1,0:T(8,128)(2,1)}, bf16[1,768,256]{2,1,0:T(8,128)(2,1)S(1)}, u32[]{:S(2)}, u32[]{:S(2)}) collective-permute-start(bf16[1,768,256]{2,1,0:T(8,128)(2,1)} %copy-done.2), channel_id=1, source_target_pairs={{0,16},{16,0},{1,17},{17,1},{2,18},{18,2},{3,19},{19,3},{4,20},{20... | collective-permute-start | bytes 1179656 | tf_op jit(solution)/shard_map/ppermute | solution.py:248
  117.1 56.2 %collective-permute-start.3 = (bf16[1,768,256]{2,1,0:T(8,128)(2,1)}, bf16[1,768,256]{2,1,0:T(8,128)(2,1)S(1)}, u32[]{:S(2)}, u32[]{:S(2)}) collective-permute-start(bf16[1,768,256]{2,1,0:T(8,128)(2,1)} %copy-done.4), channel_id=1, source_target_pairs={{0,16},{16,0},{1,17},{17,1},{2,18},{18,2},{3,19},{19,3},{4,20},{20... | collective-permute-start | bytes 1179656 | tf_op jit(solution)/shard_map/ppermute | solution.py:248
  118.7 2.3 %copy-start = (bf16[768,3072]{1,0:T(8,128)(2,1)S(1)}, bf16[768,3072]{1,0:T(8,128)(2,1)}, u32[]{:S(2)}) copy-start(bf16[768,3072]{1,0:T(8,128)(2,1)} %normalize.1.x_ref) | copy-start | bytes 14155780
  126.8 48.1 %copy-start.8 = (s32[2,27]{1,0:T(2,128)S(1)}, s32[2,27]{1,0:T(2,128)}, u32[]{:S(2)}) copy-start(s32[2,27]{1,0:T(2,128)} %param.11) | copy-start | bytes 652
  126.8 48.3 %copy-start.3 = (bf16[1,768,256]{2,1,0:T(8,128)(2,1)S(1)}, bf16[1,768,256]{2,1,0:T(8,128)(2,1)}, u32[]{:S(2)}) copy-start(bf16[1,768,256]{2,1,0:T(8,128)(2,1)} %copy-done.2) | copy-start | bytes 1179652
  126.8 48.3 %copy-start.5 = (bf16[1,768,256]{2,1,0:T(8,128)(2,1)S(1)}, bf16[1,768,256]{2,1,0:T(8,128)(2,1)}, u32[]{:S(2)}) copy-start(bf16[1,768,256]{2,1,0:T(8,128)(2,1)} %copy-done.4) | copy-start | bytes 1179652
  134.0 50.8 %collective-permute-start.18 = (bf16[2,768,256]{2,1,0:T(8,128)(2,1)S(1)}, bf16[2,768,256]{2,1,0:T(8,128)(2,1)S(1)}, u32[]{:S(2)}, u32[]{:S(2)}) collective-permute-start(bf16[2,768,256]{2,1,0:T(8,128)(2,1)S(1)} %project.7.own_ref), channel_id=1, source_target_pairs={{0,4},{4,8},{8,12},{1,5},{5,9},{9,13},{2,6},{6,10},{10,14},{3,7},{... | collective-permute-start | bytes 2359304 | tf_op jit(solution)/shard_map/ppermute | solution.py:294
  150.8 33.9 %collective-permute-start.19 = (bf16[2,768,256]{2,1,0:T(8,128)(2,1)S(1)}, bf16[2,768,256]{2,1,0:T(8,128)(2,1)S(1)}, u32[]{:S(2)}, u32[]{:S(2)}) collective-permute-start(bf16[2,768,256]{2,1,0:T(8,128)(2,1)S(1)} %project.7.own_ref), channel_id=1, source_target_pairs={{4,0},{8,4},{12,8},{5,1},{9,5},{13,9},{6,2},{10,6},{14,10},{7,3},{... | collective-permute-start | bytes 2359304 | tf_op jit(solution)/shard_map/ppermute | solution.py:294
  159.1 33.8 %collective-permute-start.16 = (bf16[2,768,256]{2,1,0:T(8,128)(2,1)S(1)}, bf16[2,768,256]{2,1,0:T(8,128)(2,1)S(1)}, u32[]{:S(2)}, u32[]{:S(2)}) collective-permute-start(bf16[2,768,256]{2,1,0:T(8,128)(2,1)S(1)} %project.5.own_ref), channel_id=1, source_target_pairs={{0,4},{4,8},{8,12},{1,5},{5,9},{9,13},{2,6},{6,10},{10,14},{3,7},{... | collective-permute-start | bytes 2359304 | tf_op jit(solution)/shard_map/ppermute | solution.py:294
  167.6 25.4 %collective-permute-start.17 = (bf16[2,768,256]{2,1,0:T(8,128)(2,1)S(1)}, bf16[2,768,256]{2,1,0:T(8,128)(2,1)S(1)}, u32[]{:S(2)}, u32[]{:S(2)}) collective-permute-start(bf16[2,768,256]{2,1,0:T(8,128)(2,1)S(1)} %project.5.own_ref), channel_id=1, source_target_pairs={{4,0},{8,4},{12,8},{5,1},{9,5},{13,9},{6,2},{10,6},{14,10},{7,3},{... | collective-permute-start | bytes 2359304 | tf_op jit(solution)/shard_map/ppermute | solution.py:294
  173.3 8.7 %collective-permute-start.7 = (bf16[1,768,256]{2,1,0:T(8,128)(2,1)}, bf16[1,768,256]{2,1,0:T(8,128)(2,1)S(1)}, u32[]{:S(2)}, u32[]{:S(2)}) collective-permute-start(bf16[1,768,256]{2,1,0:T(8,128)(2,1)} %collective-permute-done.6.far_ref), channel_id=1, source_target_pairs={{0,16},{16,0},{1,17},{17,1},{2,18},{18,2},{3,19},{19,3},{4,20},{20... | collective-permute-start | bytes 1179656 | tf_op jit(solution)/shard_map/ppermute | solution.py:248

commit v2 on v0

--- a/solution.py
+++ b/solution.py
@@ -3,7 +3,14 @@
 import jax
 import jax.numpy as jnp
 from jax import lax
+from jax.experimental import pallas as pl
+from jax.experimental.pallas import tpu as pltpu
 from jax.sharding import PartitionSpec as P
+
+EPS = 1e-06
+HIDDEN = -1e30
+COST = pl.CostEstimate(flops=1 << 20, bytes_accessed=1 << 10, transcendentals=0)
+LONG = pl.CostEstimate(flops=1 << 37, bytes_accessed=1 << 10, transcendentals=0)
 
 
 def with_halo(shard, sides, width):
@@ -22,22 +29,27 @@
 def normed_heads(tensor, gain_row, head_dim):
     shaped = tensor.reshape(tensor.shape[0], tensor.shape[1] // head_dim, head_dim)
     scaled = (
-        shaped * lax.rsqrt(jnp.mean(shaped * shaped, axis=-1, keepdims=True) + 1e-06) * gain_row
+        shaped * lax.rsqrt(jnp.mean(shaped * shaped, axis=-1, keepdims=True) + EPS) * gain_row
     )
     return scaled.astype(jnp.bfloat16)
 
 
-def reach_sides(key_rows, values):
-    stacked = jnp.stack([key_rows, values], axis=0)
-    return with_halo(stacked, (("seq", 1),), key_rows.shape[0])
-
-
-def per_device(frames, modulation, w_qkv, b_qkv, qk_gain, block_lists):
+def visible_tiles(block_lists):
+    position = lax.axis_index("seq")
+    tile_dev = block_lists.shape[0]
+    candidates = (position - 1) * tile_dev + jnp.arange(3 * tile_dev, dtype=jnp.int32)
+    matches = (block_lists[:, :, None] == candidates[None, None, :]) & (
+        block_lists[:, :, None] >= 0
+    )
+    return jnp.any(matches, axis=1)
+
+
+def general(frames, modulation, w_qkv, b_qkv, qk_gain, block_lists):
     inputs = frames.astype(jnp.float32)
     average = jnp.mean(inputs, axis=-1, keepdims=True)
     centred = inputs - average
     variance = jnp.mean(centred * centred, axis=-1, keepdims=True)
-    normed = centred * lax.rsqrt(variance + 1e-06) * (1.0 + modulation[0]) + modulation[1]
+    normed = centred * lax.rsqrt(variance + EPS) * (1.0 + modulation[0]) + modulation[1]
     normed = normed.astype(jnp.bfloat16)
     tokens = normed.shape[0]
     width_cols = w_qkv.shape[2]
@@ -53,16 +65,12 @@
     queries = normed_heads(projected[:, 0], qk_gain[0], head_dim)
     key_rows = normed_heads(projected[:, 1], qk_gain[1], head_dim)
     values = projected[:, 2].astype(jnp.bfloat16).reshape(tokens, heads, head_dim)
-    neighbourhood = reach_sides(key_rows, values)
-    position = lax.axis_index("seq")
-    tile_dev = block_lists.shape[0]
-    tile_len = tokens // tile_dev
-    candidates = (position - 1) * tile_dev + jnp.arange(3 * tile_dev, dtype=jnp.int32)
-    matches = (block_lists[:, :, None] == candidates[None, None, :]) & (
-        block_lists[:, :, None] >= 0
-    )
-    allowed_tiles = jnp.any(matches, axis=1)
-    allowed_keys = jnp.repeat(jnp.repeat(allowed_tiles, tile_len, axis=0), tile_len, axis=1)
+    stacked = jnp.stack([key_rows, values], axis=0)
+    neighbourhood = with_halo(stacked, (("seq", 1),), tokens)
+    tile_len = tokens // block_lists.shape[0]
+    allowed_keys = jnp.repeat(
+        jnp.repeat(visible_tiles(block_lists), tile_len, axis=0), tile_len, axis=1
+    )
     factor = 1.0 / math.sqrt(head_dim)
     scores = (
         jnp.einsum("qhd,khd->hqk", queries, neighbourhood[0], preferred_element_type=jnp.float32)
@@ -78,6 +86,360 @@
     )
     result = (mixture / jnp.transpose(totals)[:, :, None]).astype(jnp.bfloat16)
     return result.reshape(tokens, width_cols)
+
+
+class Line:
+    def __init__(self):
+        self.held = []
+
+    def reached(self, *values):
+        boxes = [[v] for v in values]
+        self.held += boxes
+        return boxes
+
+    def after(self, *values):
+        out = lax.optimization_barrier((*values, *(box[0] for box in self.held)))
+        for box, value in zip(self.held, out[len(values) :]):
+            box[0] = value
+        return out[: len(values)]
+
+    def drop(self, *boxes):
+        self.held = [box for box in self.held if all(box is not b for b in boxes)]
+        return [box[0] for box in boxes]
+
+
+def norm_kernel(x_ref, mod_ref, o_ref):
+    x = x_ref[...].astype(jnp.float32)
+    centred = x - jnp.mean(x, axis=-1, keepdims=True)
+    variance = jnp.mean(centred * centred, axis=-1, keepdims=True)
+    scaled = centred * lax.rsqrt(variance + EPS) * (1.0 + mod_ref[0:1, :]) + mod_ref[1:2, :]
+    o_ref[...] = scaled.astype(jnp.bfloat16)
+
+
+def normalize(frames, modulation, rows, cost=COST):
+    tokens, width = frames.shape
+    return pl.pallas_call(
+        norm_kernel,
+        grid=(tokens // rows,),
+        in_specs=[
+            pl.BlockSpec((rows, width), lambda i: (i, 0)),
+            pl.BlockSpec((2, width), lambda i: (0, 0)),
+        ],
+        out_specs=pl.BlockSpec((rows, width), lambda i: (i, 0)),
+        out_shape=jax.ShapeDtypeStruct((tokens, width), jnp.bfloat16),
+        cost_estimate=cost,
+        name="normalize",
+    )(frames, modulation)
+
+
+def project(place, own_x, quarters, weights, bias, gain, norms, cost=COST):
+    sources = [own_x] * (own_x is not None) + list(quarters)
+    tokens = own_x.shape[0] if own_x is not None else 4 * quarters[0].shape[0]
+    rows, cols = weights[0].shape
+    head_dim = gain.shape[1]
+    outs = (own_x is not None) + bool(quarters)
+    step = 256
+
+    def kernel(place_ref, *refs):
+        x_refs, weight_refs = refs[: len(sources)], refs[len(sources) : len(sources) + 4]
+        b_ref, g_ref = refs[len(sources) + 4 : len(sources) + 6]
+        out_refs = refs[len(sources) + 6 :]
+        z, q = place_ref[0], place_ref[1]
+
+        def piece(ref, at, size, out_ref, to_row):
+            total = b_ref[...]
+            for s in range(4):
+                cut = pl.multiple_of((z ^ s) * rows, 128)
+                total = total + jnp.dot(
+                    ref[pl.ds(at, size), pl.ds(cut, rows)],
+                    weight_refs[s][...],
+                    preferred_element_type=jnp.float32,
+                )
+            for i, row in enumerate(norms):
+                part = total[:, i * head_dim : (i + 1) * head_dim]
+                if row is not None:
+                    mean = jnp.mean(part * part, axis=-1, keepdims=True)
+                    part = part * lax.rsqrt(mean + EPS) * g_ref[row : row + 1, :]
+                out_ref[pl.ds(to_row, size), i * head_dim : (i + 1) * head_dim] = part.astype(
+                    jnp.bfloat16
+                )
+
+        if own_x is not None:
+            for r in range(tokens // step):
+                piece(x_refs[0], r * step, step, out_refs[0], r * step)
+        for i, ref in enumerate(x_refs[len(sources) - len(quarters) :]):
+            size = ref.shape[0]
+            piece(ref, 0, size, out_refs[-1], pl.multiple_of((q ^ i) * size, 64))
+
+    vmem = pl.BlockSpec(memory_space=pltpu.VMEM)
+    out = jax.ShapeDtypeStruct((tokens, cols), jnp.bfloat16)
+    return pl.pallas_call(
+        kernel,
+        in_specs=[pl.BlockSpec(memory_space=pltpu.SMEM)] + [vmem] * (len(sources) + 6),
+        out_specs=[vmem] * outs,
+        out_shape=[out] * outs,
+        compiler_params=pltpu.CompilerParams(vmem_limit_bytes=40 << 20),
+        cost_estimate=cost,
+        name="project",
+    )(place, *sources, *weights, bias, gain)
+
+
+def tile_step(query, rows_ref, at, tile, head_dim, limit, total, mixed):
+    scale = math.log2(math.e) / math.sqrt(head_dim)
+    keys = rows_ref[at : at + tile, :head_dim]
+    values = rows_ref[at : at + tile, head_dim:]
+    scores = lax.dot_general(
+        query, keys, (((1,), (1,)), ((), ())), preferred_element_type=jnp.float32
+    )
+    weights = jnp.exp2(scores * scale + limit)
+    for c in range(tile // 128):
+        total = total + weights[:, c * 128 : (c + 1) * 128]
+    mixed = mixed + jnp.dot(
+        weights.astype(jnp.bfloat16), values, preferred_element_type=jnp.float32
+    )
+    return total, mixed
+
+
+def attend_pair(place, limits, queries, rows):
+    tokens, head_dim = queries[0].shape
+    tiles = limits.shape[1]
+    tile = tokens // tiles
+
+    def kernel(place_ref, limit_ref, q0_ref, q1_ref, rows0_ref, rows1_ref, done_ref, mixed_ref, total_ref):
+        is_mid = (place_ref[0] == 1) | (place_ref[0] == 2)
+        for column, q_ref in enumerate((q0_ref, q1_ref)):
+            for i in range(tiles):
+                here = slice(i * tile, (i + 1) * tile)
+                query = q_ref[here, :]
+                total = jnp.zeros((tile, 128), jnp.float32)
+                mixed = jnp.zeros((tile, head_dim), jnp.float32)
+                for side, ref in enumerate((rows0_ref, rows1_ref)):
+                    for t in range(tiles):
+                        limit = limit_ref[column, i, side * tiles + t]
+                        total, mixed = tile_step(
+                            query, ref, t * tile, tile, head_dim, limit, total, mixed
+                        )
+                is_edge = is_mid if column == 0 else jnp.logical_not(is_mid)
+
+                @pl.when(is_edge)
+                def _():
+                    mixed_ref[here, :] = mixed
+                    total_ref[here, :] = total
+
+                @pl.when(jnp.logical_not(is_edge))
+                def _():
+                    done_ref[here, :] = (mixed / jnp.sum(total, axis=-1, keepdims=True)).astype(
+                        jnp.bfloat16
+                    )
+
+    vmem = pl.BlockSpec(memory_space=pltpu.VMEM)
+    smem = pl.BlockSpec(memory_space=pltpu.SMEM)
+    return pl.pallas_call(
+        kernel,
+        in_specs=[smem, smem] + [vmem] * 4,
+        out_specs=[vmem] * 3,
+        out_shape=[
+            jax.ShapeDtypeStruct((tokens, head_dim), jnp.bfloat16),
+            jax.ShapeDtypeStruct((tokens, head_dim), jnp.float32),
+            jax.ShapeDtypeStruct((tokens, 128), jnp.float32),
+        ],
+        compiler_params=pltpu.CompilerParams(vmem_limit_bytes=40 << 20),
+        cost_estimate=COST,
+        name="attend_pair",
+    )(place, limits, *queries, *rows)
+
+
+def attend_halo(place, limits, queries, halo, done, mixed, total):
+    tokens, head_dim = queries[0].shape
+    tiles = limits.shape[1]
+    tile = tokens // tiles
+
+    def kernel(place_ref, limit_ref, q0_ref, q1_ref, halo_ref, done_ref, mixed_ref, total_ref, keep_ref, send_ref):
+        is_mid = (place_ref[0] == 1) | (place_ref[0] == 2)
+        column = jnp.where(is_mid, 0, 1)
+        for i in range(tiles):
+            here = slice(i * tile, (i + 1) * tile)
+            query = jnp.where(is_mid, q0_ref[here, :], q1_ref[here, :])
+            sums, rows = total_ref[here, :], mixed_ref[here, :]
+            for t in range(tiles):
+                limit = limit_ref[column, i, 2 * tiles + t]
+                sums, rows = tile_step(query, halo_ref, t * tile, tile, head_dim, limit, sums, rows)
+            edge = (rows / jnp.sum(sums, axis=-1, keepdims=True)).astype(jnp.bfloat16)
+            outer = done_ref[here, :]
+            keep_ref[here, :] = jnp.where(is_mid, edge, outer)
+            send_ref[here, :] = jnp.where(is_mid, outer, edge)
+
+    vmem = pl.BlockSpec(memory_space=pltpu.VMEM)
+    smem = pl.BlockSpec(memory_space=pltpu.SMEM)
+    out = jax.ShapeDtypeStruct((tokens, head_dim), jnp.bfloat16)
+    return pl.pallas_call(
+        kernel,
+        in_specs=[smem, smem] + [vmem] * 6,
+        out_specs=[vmem, vmem],
+        out_shape=[out, out],
+        compiler_params=pltpu.CompilerParams(vmem_limit_bytes=40 << 20),
+        cost_estimate=COST,
+        name="attend_halo",
+    )(place, limits, *queries, halo, done, mixed, total)
+
+
+def assemble(heads, parts):
+    tokens, head_dim = parts[0].shape
+
+    def kernel(head_ref, *refs):
+        for i, ref in enumerate(refs[:-1]):
+            refs[-1][:, pl.ds(pl.multiple_of(head_ref[i] * head_dim, 128), head_dim)] = ref[...]
+
+    vmem = pl.BlockSpec(memory_space=pltpu.VMEM)
+    return pl.pallas_call(
+        kernel,
+        in_specs=[pl.BlockSpec(memory_space=pltpu.SMEM)] + [vmem] * len(parts),
+        out_specs=vmem,
+        out_shape=jax.ShapeDtypeStruct((tokens, head_dim * len(parts)), jnp.bfloat16),
+        cost_estimate=COST,
+        name="assemble",
+    )(heads, *parts)
+
+
+def seen(lists, columns, tile_dev):
+    tiles = (columns[:, None] * tile_dev + jnp.arange(tile_dev, dtype=jnp.int32)).reshape(-1)
+    listed = jnp.any(
+        (lists[:, :, None] == tiles[None, None, :]) & (lists[:, :, None] >= 0), axis=1
+    )
+    return jnp.where(listed, 0.0, HIDDEN).astype(jnp.float32)
+
+
+def per_device(frames, modulation, w_qkv, b_qkv, qk_gain, block_lists):
+    sizes = tuple(lax.axis_size(a) for a in ("groups", "seq", "fsdp", "head"))
+    head_dim = qk_gain.shape[1]
+    width_cols = w_qkv.shape[2]
+    tokens = frames.shape[0]
+    if sizes != (2, 4, 2, 2) or width_cols != 4 * head_dim:
+        return general(frames, modulation, w_qkv, b_qkv, qk_gain, block_lists)
+
+    y, z, x, core = (lax.axis_index(a).astype(jnp.int32) for a in ("groups", "seq", "fsdp", "head"))
+    rows = w_qkv.shape[0]
+    quarter = tokens // 4
+    tile_dev = block_lists.shape[0]
+
+    def to(axis, value, bit):
+        return lax.ppermute(value, axis, [(i, i ^ bit) for i in range(lax.axis_size(axis))])
+
+    side = z % 2
+    mine, twin = 2 * side + y, 2 * side + 1 - y
+    other = 2 * (1 - side) + y
+    w = jnp.transpose(w_qkv, (1, 0, 2))
+
+    def cut(first, count, head):
+        parts = [
+            lax.dynamic_slice(w, (j, 0, head * head_dim), (1, rows, head_dim))[0]
+            for j in range(first, first + count)
+        ]
+        return jnp.concatenate(parts, axis=1)
+
+    def biases(first, count, head):
+        return lax.dynamic_slice(b_qkv, (first, head * head_dim), (count, head_dim)).reshape(1, -1)
+
+    KV, Q = (1, 2), (0, 1)
+    q_at = 2 * x + core
+    place = jnp.stack([z, q_at])
+
+    near = jnp.stack([z, z ^ 1, jnp.where(z < 2, 2, 1)])
+    is_mid = (z == 1) | (z == 2)
+    line = Line()
+
+    raw = lax.dynamic_slice(frames, (q_at * quarter, 0), (quarter, frames.shape[1]))
+    same, cross, own_twin, got = {}, {}, {}, {}
+    for part in (KV, Q):
+        same[part], cross[part] = cut(*part, mine), cut(*part, other)
+    cuts = line.reached(raw, *same.values(), *cross.values())
+    raw_other = to("seq", cuts[0][0], 1)
+    for i, part in enumerate((KV, Q)):
+        got[part] = [
+            to("seq", cuts[1 + i][0], 2),
+            to("seq", cuts[3 + i][0], 3),
+            to("seq", cuts[3 + i][0], 1),
+        ]
+    lists_other = to("seq", block_lists, 1)
+    (frames,) = line.after(frames)
+    own_x = line.reached(normalize(frames, modulation, 128, LONG))
+    line.drop(*cuts)
+
+    (raw_other,) = line.after(raw_other)
+    near_q = line.reached(normalize(raw_other, modulation, 96))
+    far_q = to("fsdp", near_q[0][0], 1)
+    near_c = to("head", near_q[0][0], 1)
+
+    def swaps(part):
+        arrived, back = [], []
+        for value in got[part]:
+            box = line.reached(value)[0]
+            (ready,) = line.after(box[0])
+            box[0] = ready
+            arrived.append(box)
+            back.append(to("groups", ready, 1))
+        return arrived, back
+
+    for part in (KV, Q):
+        own_twin[part] = cut(*part, twin)
+
+    def run(part, head, boxes, norms, own, far, cost=COST):
+        mine_w = (same if head is mine else own_twin)[part]
+        (mine_w,) = line.after(mine_w)
+        two, three, one = (box[0] for box in boxes)
+        return line.reached(
+            *project(
+                place, own_x[0][0] if own else None, [b[0] for b in quarters] if far else [],
+                [mine_w, one, two, three], biases(*part, head), qk_gain, norms, cost,
+            )
+        )
+
+    quarters = []
+    kv_boxes, kv_back = swaps(KV)
+    rows_mine = run(KV, mine, kv_boxes, (1, None), True, False, LONG)
+    far_box = line.reached(far_q)
+    (far_ready,) = line.after(far_box[0][0])
+    far_box[0][0] = far_ready
+    far_c = to("head", far_ready, 1)
+    quarters = near_q + line.reached(near_c) + far_box + line.reached(far_c)
+    rows_mine += run(KV, mine, kv_boxes, (1, None), False, True)
+    line.drop(*kv_boxes)
+
+    def send_edge(rows):
+        return to("seq", jnp.where(is_mid, rows[0][0], rows[1][0]), 2)
+
+    halo_mine = send_edge(rows_mine)
+    q_boxes, q_back = swaps(Q)
+    q_mine = run(Q, mine, q_boxes, (0,), True, True)
+    line.drop(*q_boxes)
+    kv_boxes = line.reached(*kv_back)
+    rows_twin = run(KV, twin, kv_boxes, (1, None), True, True)
+    line.drop(*kv_boxes)
+    halo_twin = send_edge(rows_twin)
+
+    limits = jnp.stack([seen(v, near, tile_dev) for v in (block_lists, lists_other)])
+
+    def pair(q, rows):
+        (limit,) = line.after(limits)
+        return line.reached(*attend_pair(place, limit, [b[0] for b in q], [b[0] for b in rows]))
+
+    parts_mine = pair(q_mine, rows_mine)
+    q_boxes = line.reached(*q_back)
+    q_twin = run(Q, twin, q_boxes, (0,), True, True)
+    line.drop(*q_boxes, *own_x, *quarters)
+    parts_twin = pair(q_twin, rows_twin)
+    line.drop(*rows_mine, *rows_twin)
+
+    keeps, sends = [], []
+    for q, halo, parts in ((q_mine, halo_mine, parts_mine), (q_twin, halo_twin, parts_twin)):
+        (limit,) = line.after(limits)
+        keep, send = attend_halo(place, limit, [b[0] for b in q], halo, *(b[0] for b in parts))
+        line.reached(keep)
+        keeps.append(keep)
+        sends.append(to("seq", send, 1))
+    across = 2 * (1 - side)
+    heads = jnp.stack([mine, twin, across + y, across + 1 - y])
+    return assemble(heads, [*keeps, *sends])
 
 
 def solution(mesh):

time: 279 us -> 173 us (0.62)
  waiting for transfers between devices: 188 us -> 74 us
  Pallas kernels: 0 us -> 43.9 us
  matrix products: 37.7 us -> 0 us
  starting transfers between devices: 7 us -> 26.9 us
  between operations: 13.6 us -> 0.29 us
  other arithmetic: 13.7 us -> 6.22 us
    all_gather x1 -> x0, waiting for transfers between devices: 164 us -> none  [per_device(): lax.all_gather(w_qkv, 'seq', axis=0, tiled=True)]
    ppermute x2 -> x21, waiting for transfers between devices: 23.6 us -> 74 us  [to(): lax.ppermute(value, axis, [(i, i ^ bit) for i in range(lax.axis_size(axis...]
    pallas_call x0 -> x12, Pallas kernels: none -> 43.9 us  [the longest x5 18.3 us: project(): pl.pallas_call(kernel, in_specs=[pl.BlockSpec(memory_space=pltpu.SMEM)] +...]
    dot_general x3 -> x0, matrix products: 37.7 us -> none  [the longest x1 12.9 us: per_device(): jnp.einsum('qhd,khd->hqk', queries, neighbourhood[0], preferred_element_t...]
    ppermute x2 -> x21, starting transfers between devices: 7 us -> 26.9 us  [to(): lax.ppermute(value, axis, [(i, i ^ bit) for i in range(lax.axis_size(axis...]
    unnamed x19 -> x54, local copies, waits for them, and re-layouts: 4.86 us -> 13.1 us
    broadcast_in_dim x3 -> x0, local copies, waits for them, and re-layouts: 7.15 us -> none  [the longest x1 5.38 us: per_device(): weights = jnp.where(allowed_keys[None, :, :], jnp.exp(scores), 0.0)]
    reduce_sum x4 -> x0, other arithmetic: 6.18 us -> none  [the longest x1 3.17 us: per_device(): average = jnp.mean(inputs, axis=-1, keepdims=True)]
  transfers between devices with their start and end apart: 3 -> 21, of which waited for: 3 -> 10; matrix products, arithmetic and copies ran while one was open for 5% -> 6% of each run, Pallas kernels for 0% -> 24%
where the time goes in v2:
time: 173 us; the launch traced here: 172 us
  waiting for transfers between devices  74 us (43%)
  Pallas kernels  43.9 us (25%)
  starting transfers between devices  26.9 us (16%)
  local copies, waits for them, and re-layouts  20.4 us (12%)
  other arithmetic  6.22 us (4%)
    ppermute x21, waiting for transfers between devices, to(): lax.ppermute(value, axis, [(i, i ^ bit) for i in range(lax.axis_size(axis...  74 us
    ppermute x21, starting transfers between devices, to(): lax.ppermute(value, axis, [(i, i ^ bit) for i in range(lax.axis_size(axis...  26.9 us
    pallas_call x5, Pallas kernels, project(): pl.pallas_call(kernel, in_specs=[pl.BlockSpec(memory_space=pltpu.SMEM)] +...  18.3 us
    unnamed x54, local copies, waits for them, and re-layouts  13.1 us
    pallas_call x2, Pallas kernels, normalize(): pl.pallas_call(norm_kernel, grid=(tokens // rows,), in_specs=[pl.BlockSpe...  10.1 us
    pallas_call x2, Pallas kernels, attend_pair(): pl.pallas_call(kernel, in_specs=[smem, smem] + [vmem] * 4, out_specs=[vme...  9.92 us
  transfers between devices with their start and end apart: 21, of which 10 were waited for; matrix products, arithmetic and copies ran while one was open for 6% of the time, Pallas kernels for 24%

profile of v2, /device:TPU:0, one launch (start us, length us, event | category | flops | bytes accessed | tf_op | source)
XLA Modules:
  0.0 171.7 jit_solution(13867000038691582111)
XLA Ops:
  0.0 2.7 %dynamic-slice_bitcast_fusion.1 = (bf16[768,128]{1,0:T(8,128)(2,1)S(1)}, bf16[768,128]{1,0:T(8,128)(2,1)}, bf16[768,128]{1,0:T(8,128)(2,1)}, bf16[768,128]{1,0:T...) fusion(bf16[768,3,512]{2,0,1:T(8,128)(2,1)} %param.8, ...), kind=kLoop, calls=%fused_computation.6 | loop fusion | bytes 3538956 | tf_op jit(solution)/shard_map/squeeze | solution.py:335
  3.5 3.0 %collective-permute-start.6 = (bf16[768,256]{1,0:T(8,128)(2,1)}, bf16[768,256]{1,0:T(8,128)(2,1)S(1)}, u32[]{:S(2)}, u32[]{:S(2)}) collective-permute-start(bf16[768,256]{1,0:T(8,128)(2,1)} %pad_maximum_fusion.2), channel_id=1, source_target_pairs={{0,4},{4,0},{8,12},{12,8},{1,5},{5,1},{9,13},{13,9},{2,6},{6,2},{1... | collective-permute-start | bytes 1179656 | tf_op jit(solution)/shard_map/ppermute | solution.py:326
  6.5 2.5 %collective-permute-start.7 = (bf16[768,256]{1,0:T(8,128)(2,1)}, bf16[768,256]{1,0:T(8,128)(2,1)S(1)}, u32[]{:S(2)}, u32[]{:S(2)}) collective-permute-start(bf16[768,256]{1,0:T(8,128)(2,1)} %pad_maximum_fusion.2), channel_id=1, source_target_pairs={{0,12},{4,8},{8,4},{12,0},{1,13},{5,9},{9,5},{13,1},{2,14},{6,10},... | collective-permute-start | bytes 1179656 | tf_op jit(solution)/shard_map/ppermute | solution.py:326
  9.0 1.4 constant_dynamic-slice_fusion.2
  11.2 1.3 collective-permute-start.8
  12.5 7.4 %normalize.2.refs_0_ = bf16[768,3072]{1,0:T(8,128)(2,1)} custom-call(bf16[768,3072]{1,0:T(8,128)(2,1)} %x_ref, f32[2,3072]{1,0:T(2,128)} %mod_ref.3), custom_call_target="tpu_custom_call" | custom-call | flops 137438953472 | bytes 1024 | tf_op jit(solution)/shard_map/normalize/pallas_call | solution.py:121
  20.7 37.3 %collective-permute-done.4.x_ref = bf16[192,3072]{1,0:T(8,128)(2,1)S(1)} collective-permute-done((bf16[192,3072]{1,0:T(8,128)(2,1)S(1)}, bf16[192,3072]{1,0:T(8,128)(2,1)S(1)}, u32[]{:S(2)}, u32[]{:S(2)}) %collective-permute-start.4) | collective-permute-done | bytes 1179680 | tf_op jit(solution)/shard_map/ppermute | solution.py:326
  58.0 1.0 copy-done.20
  59.0 2.8 %normalize.3.refs_0_.refs_1_ = bf16[192,3072]{1,0:T(8,128)(2,1)} custom-call(bf16[192,3072]{1,0:T(8,128)(2,1)} %copy-done.20, f32[2,3072]{1,0:T(2,128)} %mod_ref.3), custom_call_target="tpu_custom_call" | custom-call | flops 1048576 | bytes 1024 | tf_op jit(solution)/shard_map/normalize/pallas_call | solution.py:121
  61.8 1.7 collective-permute-start.5
  65.0 2.3 %copy-done = bf16[768,3072]{1,0:T(8,128)(2,1)S(1)} copy-done((bf16[768,3072]{1,0:T(8,128)(2,1)S(1)}, bf16[768,3072]{1,0:T(8,128)(2,1)}, u32[]{:S(2)}) %copy-start) | copy-done | bytes 4718616
  67.3 1.0 copy-done.4
  68.3 1.0 copy-done.10
  69.3 1.0 copy-done.13
  70.3 2.6 %project.5.rows0_ref = bf16[768,256]{1,0:T(8,128)(2,1)S(1)} custom-call(s32[2]{0:T(128)S(1)} %pad_add_fusion.1.place_ref, bf16[768,3072]{1,0:T(8,128)(2,1)S(1)} %copy-done, bf16[768,256]{1,0:T(8,128)(2,1)S(1)} %copy-done.4, bf16[768,256]{1,0:T(8,128)(2,1)S(1)} %copy-done.10, bf16[768,256]{1,0:T(8,128)(2,1)} %collective-permute-done.8.refs_3_.refs_6_, ...), custom_call_target="tpu_custom_call" | custom-call | flops 137438953472 | bytes 1024 | tf_op jit(solution)/shard_map/project/pallas_call | solution.py:176
  73.7 15.4 %collective-permute-done.5.refs_2_.refs_3_ = bf16[192,3072]{1,0:T(8,128)(2,1)S(1)} collective-permute-done((bf16[192,3072]{1,0:T(8,128)(2,1)}, bf16[192,3072]{1,0:T(8,128)(2,1)S(1)}, u32[]{:S(2)}, u32[]{:S(2)}) %collective-permute-start.5) | collective-permute-done | bytes 1179680 | tf_op jit(solution)/shard_map/ppermute | solution.py:326
  89.1 1.5 collective-permute-start.3
  90.7 2.5 %collective-permute-start = (s32[2,27]{1,0:T(2,128)}, s32[2,27]{1,0:T(2,128)}, u32[]{:S(2)}, u32[]{:S(2)}) collective-permute-start(s32[2,27]{1,0:T(2,128)} %param.11), channel_id=1, source_target_pairs={{0,4},{4,0},{8,12},{12,8},{1,5},{5,1},{9,13},{13,9},{2,6},{6,2},{1... | collective-permute-start | bytes 656 | tf_op jit(solution)/shard_map/ppermute | solution.py:326
  93.8 1.2 broadcast_compare_fusion.1
  95.1 1.5 collective-permute-start.11
  97.4 4.5 %collective-permute-done.3.refs_7_ = bf16[768,128]{1,0:T(8,128)(2,1)} collective-permute-done((bf16[768,128]{1,0:T(8,128)(2,1)}, bf16[768,128]{1,0:T(8,128)(2,1)}, u32[]{:S(2)}, u32[]{:S(2)}) %collective-permute-start.3) | collective-permute-done | bytes 196640 | tf_op jit(solution)/shard_map/ppermute | solution.py:326
  101.9 1.4 collective-permute-start.13
  103.3 1.3 constant_dynamic-slice_fusion
  104.5 1.2 add.79
  105.7 1.1 pad_maximum_fusion.refs_5_
  106.9 2.6 %collective-permute-start.2 = (bf16[768,128]{1,0:T(8,128)(2,1)}, bf16[768,128]{1,0:T(8,128)(2,1)S(1)}, u32[]{:S(2)}, u32[]{:S(2)}) collective-permute-start(bf16[768,128]{1,0:T(8,128)(2,1)} %get-tuple-element.330), channel_id=1, source_target_pairs={{0,12},{4,8},{8,4},{12,0},{1,13},{5,9},{9,5},{13,1},{2,14},{6,10},... | collective-permute-start | bytes 589832 | tf_op jit(solution)/shard_map/ppermute | solution.py:326
  110.2 1.0 copy-done.5
  111.2 1.0 copy-done.11
  112.2 1.0 copy-done.14
  113.2 3.0 %project.6.rows1_ref = bf16[768,256]{1,0:T(8,128)(2,1)S(1)} custom-call(s32[2]{0:T(128)S(1)} %pad_add_fusion.1.place_ref, bf16[192,3072]{1,0:T(8,128)(2,1)S(1)} %copy-done.2, bf16[192,3072]{1,0:T(8,128)(2,1)S(1)} %collective-permute-done.9.refs_1_.refs_2_, bf16[192,3072]{1,0:T(8,128)(2,1)S(1)} %collective-permute-done.5.refs_2_.refs_3_, ...), custom_call_target="tpu_custom_call" | custom-call | flops 1048576 | bytes 1024 | tf_op jit(solution)/shard_map/project/pallas_call | solution.py:176
  116.3 2.6 %collective-permute-done.2.refs_8_ = bf16[768,128]{1,0:T(8,128)(2,1)S(1)} collective-permute-done((bf16[768,128]{1,0:T(8,128)(2,1)}, bf16[768,128]{1,0:T(8,128)(2,1)S(1)}, u32[]{:S(2)}, u32[]{:S(2)}) %collective-permute-start.2) | collective-permute-done | bytes 196640 | tf_op jit(solution)/shard_map/ppermute | solution.py:326
  118.9 4.2 %project.7 = (bf16[768,128]{1,0:T(8,128)(2,1)S(1)}, bf16[768,128]{1,0:T(8,128)(2,1)S(1)}) custom-call(s32[2]{0:T(128)S(1)} %pad_add_fusion.1.place_ref, bf16[768,3072]{1,0:T(8,128)(2,1)S(1)} %copy-done.1, bf16[192,3072]{1,0:T(8,128)(2,1)S(1)} %copy-done.2, bf16[192,3072]{1,0:T(8,128)(2,1)S(1)} %collective-permute-done.9.refs_1_.refs_2_, ...), custom_call_target="tpu_custom_call" | custom-call | flops 1048576 | bytes 1024 | tf_op jit(solution)/shard_map/project/pallas_call | solution.py:176
  123.2 1.9 %collective-permute-start.17 = (bf16[768,256]{1,0:T(8,128)(2,1)S(1)}, bf16[768,256]{1,0:T(8,128)(2,1)S(1)}, u32[]{:S(2)}, u32[]{:S(2)}) collective-permute-start(bf16[768,256]{1,0:T(8,128)(2,1)S(1)} %broadcast_select_fusion.1), channel_id=1, source_target_pairs={{0,8},{4,12},{8,0},{12,4},{1,9},{5,13},{9,1},{13,5},{2,10},{6,14},... | collective-permute-start | bytes 1179656 | tf_op jit(solution)/shard_map/ppermute | solution.py:326
  125.1 4.4 %project.8 = (bf16[768,256]{1,0:T(8,128)(2,1)S(1)}, bf16[768,256]{1,0:T(8,128)(2,1)S(1)}) custom-call(s32[2]{0:T(128)S(1)} %pad_add_fusion.1.place_ref, bf16[768,3072]{1,0:T(8,128)(2,1)S(1)} %copy-done.1, bf16[192,3072]{1,0:T(8,128)(2,1)S(1)} %copy-done.2, bf16[192,3072]{1,0:T(8,128)(2,1)S(1)} %collective-permute-done.9.refs_1_.refs_2_, ...), custom_call_target="tpu_custom_call" | custom-call | flops 1048576 | bytes 1024 | tf_op jit(solution)/shard_map/project/pallas_call | solution.py:176
  129.7 1.1 collective-permute-start.18
  131.7 1.6 collective-permute-start.14
  133.8 1.5 collective-permute-start.16
  135.4 5.0 %attend_pair.2 = (bf16[768,128]{1,0:T(8,128)(2,1)S(1)}, f32[768,128]{1,0:T(8,128)S(1)}, f32[768,128]{1,0:T(8,128)S(1)}) custom-call(s32[2]{0:T(128)S(1)} %pad_add_fusion.1.place_ref, f32[2,2,6]{2,1,0:T(2,128)S(1)} %pad_maximum_fusion.3.limit_ref, bf16[768,128]{1,0:T(8,128)(2,1)S(1)} %get-tuple-element.305.q0_ref, ...), custom_call_target="tpu_custom_call" | custom-call | flops 1048576 | bytes 1024 | tf_op jit(solution)/shard_map/attend_pair/pallas_call | solution.py:237
  140.4 3.2 %collective-permute-done.15.refs_8_ = bf16[768,128]{1,0:T(8,128)(2,1)S(1)} collective-permute-done((bf16[768,128]{1,0:T(8,128)(2,1)S(1)}, bf16[768,128]{1,0:T(8,128)(2,1)S(1)}, u32[]{:S(2)}, u32[]{:S(2)}) %collective-permute-start.15) | collective-permute-done | bytes 196640 | tf_op jit(solution)/shard_map/ppermute | solution.py:326
  143.7 2.1 %collective-permute-done.16.refs_6_ = bf16[768,128]{1,0:T(8,128)(2,1)S(1)} collective-permute-done((bf16[768,128]{1,0:T(8,128)(2,1)S(1)}, bf16[768,128]{1,0:T(8,128)(2,1)S(1)}, u32[]{:S(2)}, u32[]{:S(2)}) %collective-permute-start.16) | collective-permute-done | bytes 196640 | tf_op jit(solution)/shard_map/ppermute | solution.py:326
  145.8 4.1 %project.9 = (bf16[768,128]{1,0:T(8,128)(2,1)S(1)}, bf16[768,128]{1,0:T(8,128)(2,1)S(1)}) custom-call(s32[2]{0:T(128)S(1)} %pad_add_fusion.1.place_ref, bf16[768,3072]{1,0:T(8,128)(2,1)S(1)} %copy-done.1, bf16[192,3072]{1,0:T(8,128)(2,1)S(1)} %copy-done.2, bf16[192,3072]{1,0:T(8,128)(2,1)S(1)} %collective-permute-done.9.refs_1_.refs_2_, ...), custom_call_target="tpu_custom_call" | custom-call | flops 1048576 | bytes 1024 | tf_op jit(solution)/shard_map/project/pallas_call | solution.py:176
  149.8 4.9 %attend_pair.3 = (bf16[768,128]{1,0:T(8,128)(2,1)S(1)}, f32[768,128]{1,0:T(8,128)S(1)}, f32[768,128]{1,0:T(8,128)S(1)}) custom-call(s32[2]{0:T(128)S(1)} %pad_add_fusion.1.place_ref, f32[2,2,6]{2,1,0:T(2,128)S(1)} %pad_maximum_fusion.3.limit_ref, bf16[768,128]{1,0:T(8,128)(2,1)S(1)} %get-tuple-element.317.q0_ref, ...), custom_call_target="tpu_custom_call" | custom-call | flops 1048576 | bytes 1024 | tf_op jit(solution)/shard_map/attend_pair/pallas_call | solution.py:237
  154.7 1.6 attend_halo.2
  157.0 2.7 %collective-permute-done.18.halo_ref = bf16[768,256]{1,0:T(8,128)(2,1)S(1)} collective-permute-done((bf16[768,256]{1,0:T(8,128)(2,1)S(1)}, bf16[768,256]{1,0:T(8,128)(2,1)S(1)}, u32[]{:S(2)}, u32[]{:S(2)}) %collective-permute-start.18) | collective-permute-done | bytes 393248 | tf_op jit(solution)/shard_map/ppermute | solution.py:326
  159.7 1.6 attend_halo.3
  162.7 1.1 collective-permute-done.19.refs_2_
  163.8 4.9 %collective-permute-done.20.refs_3_ = bf16[768,128]{1,0:T(8,128)(2,1)S(1)} collective-permute-done((bf16[768,128]{1,0:T(8,128)(2,1)S(1)}, bf16[768,128]{1,0:T(8,128)(2,1)S(1)}, u32[]{:S(2)}, u32[]{:S(2)}) %collective-permute-start.20) | collective-permute-done | bytes 196640 | tf_op jit(solution)/shard_map/ppermute | solution.py:326
  169.4 2.2 %assemble.1 = bf16[768,512]{1,0:T(8,128)(2,1)} custom-call(s32[4]{0:T(128)} %pad_add_fusion.head_ref, bf16[768,128]{1,0:T(8,128)(2,1)} %copy-done.15, bf16[768,128]{1,0:T(8,128)(2,1)} %copy-done.16, bf16[768,128]{1,0:T(8,128)(2,1)} %copy-done.23, bf16[768,128]{1,0:T(8,128)(2,1)} %copy-done.24), custom_call_target="tpu_custom_call" | custom-call | flops 1048576 | bytes 1024 | tf_op jit(solution)/shard_map/assemble/pallas_call | solution.py:294
  (79 shorter events, 11.4 us)
Async XLA Ops:
  3.5 60.8 %collective-permute-start.6 = (bf16[768,256]{1,0:T(8,128)(2,1)}, bf16[768,256]{1,0:T(8,128)(2,1)S(1)}, u32[]{:S(2)}, u32[]{:S(2)}) collective-permute-start(bf16[768,256]{1,0:T(8,128)(2,1)} %pad_maximum_fusion.2), channel_id=1, source_target_pairs={{0,4},{4,0},{8,12},{12,8},{1,5},{5,1},{9,13},{13,9},{2,6},{6,2},{1... | collective-permute-start | bytes 1179656 | tf_op jit(solution)/shard_map/ppermute | solution.py:326
  6.5 56.9 %collective-permute-start.7 = (bf16[768,256]{1,0:T(8,128)(2,1)}, bf16[768,256]{1,0:T(8,128)(2,1)S(1)}, u32[]{:S(2)}, u32[]{:S(2)}) collective-permute-start(bf16[768,256]{1,0:T(8,128)(2,1)} %pad_maximum_fusion.2), channel_id=1, source_target_pairs={{0,12},{4,8},{8,4},{12,0},{1,13},{5,9},{9,5},{13,1},{2,14},{6,10},... | collective-permute-start | bytes 1179656 | tf_op jit(solution)/shard_map/ppermute | solution.py:326
  9.0 2.2 %copy-start.21 = (bf16[768,128]{1,0:T(8,128)(2,1)S(1)}, bf16[768,128]{1,0:T(8,128)(2,1)}, u32[]{:S(2)}) copy-start(bf16[768,128]{1,0:T(8,128)(2,1)} %get-tuple-element.328) | copy-start | bytes 589828
  9.0 2.2 %copy-start.22 = (bf16[768,128]{1,0:T(8,128)(2,1)S(1)}, bf16[768,128]{1,0:T(8,128)(2,1)}, u32[]{:S(2)}) copy-start(bf16[768,128]{1,0:T(8,128)(2,1)} %get-tuple-element.329) | copy-start | bytes 589828
  10.4 47.6 %collective-permute-start.4 = (bf16[192,3072]{1,0:T(8,128)(2,1)S(1)}, bf16[192,3072]{1,0:T(8,128)(2,1)S(1)}, u32[]{:S(2)}, u32[]{:S(2)}) collective-permute-start(bf16[192,3072]{1,0:T(8,128)(2,1)S(1)} %constant_dynamic-slice_fusion.2), channel_id=1, source_target_pairs={{0,4},{4,0},{8,12},{12,8},{1,5},{5,1},{9,13},{13,9},{2,6},{6,2},{1... | collective-permute-start | bytes 3538952 | tf_op jit(solution)/shard_map/ppermute | solution.py:326
  11.2 8.7 %copy-start.3 = (bf16[768,256]{1,0:T(8,128)(2,1)}, bf16[768,256]{1,0:T(8,128)(2,1)S(1)}, u32[]{:S(2)}) copy-start(bf16[768,256]{1,0:T(8,128)(2,1)S(1)} %pad_maximum_fusion.1.refs_1_.refs_4_) | copy-start | bytes 1179652
  11.2 52.2 %collective-permute-start.8 = (bf16[768,256]{1,0:T(8,128)(2,1)S(1)}, bf16[768,256]{1,0:T(8,128)(2,1)}, u32[]{:S(2)}, u32[]{:S(2)}) collective-permute-start(bf16[768,256]{1,0:T(8,128)(2,1)S(1)} %pad_maximum_fusion.1.refs_1_.refs_4_), channel_id=1, source_target_pairs={{0,8},{4,12},{8,0},{12,4},{1,9},{5,13},{9,1},{13,5},{2,10},{6,14},... | collective-permute-start | bytes 1179656 | tf_op jit(solution)/shard_map/ppermute | solution.py:326
  20.7 44.3 %copy-start.17 = (f32[2,128]{1,0:T(2,128)S(1)}, f32[2,128]{1,0:T(2,128)}, u32[]{:S(2)}) copy-start(f32[2,128]{1,0:T(2,128)} %refs_10_.5) | copy-start | bytes 3076
  58.0 1.0 copy-start.20
  61.8 27.4 %collective-permute-start.5 = (bf16[192,3072]{1,0:T(8,128)(2,1)}, bf16[192,3072]{1,0:T(8,128)(2,1)S(1)}, u32[]{:S(2)}, u32[]{:S(2)}) collective-permute-start(bf16[192,3072]{1,0:T(8,128)(2,1)} %normalize.3.refs_0_.refs_1_), channel_id=1, source_target_pairs={{0,2},{2,0},{1,3},{3,1},{4,6},{6,4},{5,7},{7,5},{8,10},{10,8},{9,1... | collective-permute-start | bytes 3538952 | tf_op jit(solution)/shard_map/ppermute | solution.py:326
  63.4 43.4 %collective-permute-start.9 = (bf16[192,3072]{1,0:T(8,128)(2,1)}, bf16[192,3072]{1,0:T(8,128)(2,1)S(1)}, u32[]{:S(2)}, u32[]{:S(2)}) collective-permute-start(bf16[192,3072]{1,0:T(8,128)(2,1)} %normalize.3.refs_0_.refs_1_), channel_id=1, source_target_pairs={{0,1},{1,0},{2,3},{3,2},{4,5},{5,4},{6,7},{7,6},{8,9},{9,8},{10,11... | collective-permute-start | bytes 3538952 | tf_op jit(solution)/shard_map/ppermute | solution.py:326
  63.4 0.8 copy-start.12
  64.2 0.8 copy-start.9
  65.0 2.3 %copy-start = (bf16[768,3072]{1,0:T(8,128)(2,1)S(1)}, bf16[768,3072]{1,0:T(8,128)(2,1)}, u32[]{:S(2)}) copy-start(bf16[768,3072]{1,0:T(8,128)(2,1)} %normalize.2.refs_0_) | copy-start | bytes 14155780
  67.3 1.0 copy-start.4
  68.3 1.0 copy-start.10
  69.3 1.0 copy-start.13
  70.3 39.9 %copy-start.2 = (bf16[192,3072]{1,0:T(8,128)(2,1)S(1)}, bf16[192,3072]{1,0:T(8,128)(2,1)}, u32[]{:S(2)}) copy-start(bf16[192,3072]{1,0:T(8,128)(2,1)} %normalize.3.refs_0_.refs_1_) | copy-start | bytes 3538948
  72.9 0.8 copy-start.6
  89.1 17.8 %collective-permute-start.10 = (bf16[192,3072]{1,0:T(8,128)(2,1)S(1)}, bf16[192,3072]{1,0:T(8,128)(2,1)}, u32[]{:S(2)}, u32[]{:S(2)}) collective-permute-start(bf16[192,3072]{1,0:T(8,128)(2,1)S(1)} %collective-permute-done.5.refs_2_.refs_3_), channel_id=1, source_target_pairs={{0,1},{1,0},{2,3},{3,2},{4,5},{5,4},{6,7},{7,6},{8,9},{9,8},{10,11... | collective-permute-start | bytes 3538952 | tf_op jit(solution)/shard_map/ppermute | solution.py:326
  89.1 12.7 %collective-permute-start.3 = (bf16[768,128]{1,0:T(8,128)(2,1)}, bf16[768,128]{1,0:T(8,128)(2,1)}, u32[]{:S(2)}, u32[]{:S(2)}) collective-permute-start(bf16[768,128]{1,0:T(8,128)(2,1)} %get-tuple-element.237.refs_5_), channel_id=1, source_target_pairs={{0,8},{4,12},{8,0},{12,4},{1,9},{5,13},{9,1},{13,5},{2,10},{6,14},... | collective-permute-start | bytes 589832 | tf_op jit(solution)/shard_map/ppermute | solution.py:326
  90.7 5.9 %collective-permute-start = (s32[2,27]{1,0:T(2,128)}, s32[2,27]{1,0:T(2,128)}, u32[]{:S(2)}, u32[]{:S(2)}) collective-permute-start(s32[2,27]{1,0:T(2,128)} %param.11), channel_id=1, source_target_pairs={{0,4},{4,0},{8,12},{12,8},{1,5},{5,1},{9,13},{13,9},{2,6},{6,2},{1... | collective-permute-start | bytes 656 | tf_op jit(solution)/shard_map/ppermute | solution.py:326
  95.1 28.0 %collective-permute-start.11 = (bf16[768,256]{1,0:T(8,128)(2,1)}, bf16[768,256]{1,0:T(8,128)(2,1)}, u32[]{:S(2)}, u32[]{:S(2)}) collective-permute-start(bf16[768,256]{1,0:T(8,128)(2,1)} %collective-permute-done.8.refs_3_.refs_6_), channel_id=1, source_target_pairs={{0,16},{16,0},{1,17},{17,1},{2,18},{18,2},{3,19},{19,3},{4,20},{20... | collective-permute-start | bytes 1179656 | tf_op jit(solution)/shard_map/ppermute | solution.py:326
  96.6 26.5 %collective-permute-start.12 = (bf16[768,256]{1,0:T(8,128)(2,1)}, bf16[768,256]{1,0:T(8,128)(2,1)}, u32[]{:S(2)}, u32[]{:S(2)}) collective-permute-start(bf16[768,256]{1,0:T(8,128)(2,1)} %copy-done.12), channel_id=1, source_target_pairs={{0,16},{16,0},{1,17},{17,1},{2,18},{18,2},{3,19},{19,3},{4,20},{20... | collective-permute-start | bytes 1179656 | tf_op jit(solution)/shard_map/ppermute | solution.py:326
  101.9 21.3 %collective-permute-start.13 = (bf16[768,256]{1,0:T(8,128)(2,1)}, bf16[768,256]{1,0:T(8,128)(2,1)}, u32[]{:S(2)}, u32[]{:S(2)}) collective-permute-start(bf16[768,256]{1,0:T(8,128)(2,1)} %copy-done.9), channel_id=1, source_target_pairs={{0,16},{16,0},{1,17},{17,1},{2,18},{18,2},{3,19},{19,3},{4,20},{20... | collective-permute-start | bytes 1179656 | tf_op jit(solution)/shard_map/ppermute | solution.py:326
  106.8 12.0 %collective-permute-start.1 = (bf16[768,128]{1,0:T(8,128)(2,1)}, bf16[768,128]{1,0:T(8,128)(2,1)S(1)}, u32[]{:S(2)}, u32[]{:S(2)}) collective-permute-start(bf16[768,128]{1,0:T(8,128)(2,1)} %get-tuple-element.330), channel_id=1, source_target_pairs={{0,4},{4,0},{8,12},{12,8},{1,5},{5,1},{9,13},{13,9},{2,6},{6,2},{1... | collective-permute-start | bytes 589832 | tf_op jit(solution)/shard_map/ppermute | solution.py:326
  106.9 11.9 %collective-permute-start.2 = (bf16[768,128]{1,0:T(8,128)(2,1)}, bf16[768,128]{1,0:T(8,128)(2,1)S(1)}, u32[]{:S(2)}, u32[]{:S(2)}) collective-permute-start(bf16[768,128]{1,0:T(8,128)(2,1)} %get-tuple-element.330), channel_id=1, source_target_pairs={{0,12},{4,8},{8,4},{12,0},{1,13},{5,9},{9,5},{13,1},{2,14},{6,10},... | collective-permute-start | bytes 589832 | tf_op jit(solution)/shard_map/ppermute | solution.py:326
  110.2 1.0 copy-start.5
  111.2 1.0 copy-start.11
  112.2 1.0 copy-start.14
  113.2 5.6 %copy-start.1 = (bf16[768,3072]{1,0:T(8,128)(2,1)S(1)}, bf16[768,3072]{1,0:T(8,128)(2,1)}, u32[]{:S(2)}) copy-start(bf16[768,3072]{1,0:T(8,128)(2,1)} %normalize.2.refs_0_) | copy-start | bytes 14155780
  113.2 5.6 %copy-start.19 = (f32[1,128]{1,0:T(1,128)S(1)}, f32[1,128]{1,0:T(1,128)}, u32[]{:S(2)}) copy-start(f32[1,128]{1,0:T(1,128)} %get-tuple-element.337.refs_9_) | copy-start | bytes 1540
  118.9 4.3 %copy-start.7 = (bf16[768,256]{1,0:T(8,128)(2,1)S(1)}, bf16[768,256]{1,0:T(8,128)(2,1)}, u32[]{:S(2)}) copy-start(bf16[768,256]{1,0:T(8,128)(2,1)} %copy-done.6) | copy-start | bytes 1179652
  123.2 31.5 %collective-permute-start.17 = (bf16[768,256]{1,0:T(8,128)(2,1)S(1)}, bf16[768,256]{1,0:T(8,128)(2,1)S(1)}, u32[]{:S(2)}, u32[]{:S(2)}) collective-permute-start(bf16[768,256]{1,0:T(8,128)(2,1)S(1)} %broadcast_select_fusion.1), channel_id=1, source_target_pairs={{0,8},{4,12},{8,0},{12,4},{1,9},{5,13},{9,1},{13,5},{2,10},{6,14},... | collective-permute-start | bytes 1179656 | tf_op jit(solution)/shard_map/ppermute | solution.py:326
  129.6 1.2 copy-start.25
  129.6 1.2 copy-start.26
  129.6 16.2 %copy-start.8 = (bf16[768,128]{1,0:T(8,128)(2,1)S(1)}, bf16[768,128]{1,0:T(8,128)(2,1)}, u32[]{:S(2)}) copy-start(bf16[768,128]{1,0:T(8,128)(2,1)} %get-tuple-element.285.refs_5_) | copy-start | bytes 589828
  129.6 16.2 %copy-start.18 = (f32[1,128]{1,0:T(1,128)S(1)}, f32[1,128]{1,0:T(1,128)}, u32[]{:S(2)}) copy-start(f32[1,128]{1,0:T(1,128)} %get-tuple-element.336.refs_9_) | copy-start | bytes 1540
  129.7 30.0 %collective-permute-start.18 = (bf16[768,256]{1,0:T(8,128)(2,1)S(1)}, bf16[768,256]{1,0:T(8,128)(2,1)S(1)}, u32[]{:S(2)}, u32[]{:S(2)}) collective-permute-start(bf16[768,256]{1,0:T(8,128)(2,1)S(1)} %broadcast_select_fusion), channel_id=1, source_target_pairs={{0,8},{4,12},{8,0},{12,4},{1,9},{5,13},{9,1},{13,5},{2,10},{6,14},... | collective-permute-start | bytes 1179656 | tf_op jit(solution)/shard_map/ppermute | solution.py:326
  131.7 8.7 %collective-permute-start.14 = (bf16[768,128]{1,0:T(8,128)(2,1)}, bf16[768,128]{1,0:T(8,128)(2,1)S(1)}, u32[]{:S(2)}, u32[]{:S(2)}) collective-permute-start(bf16[768,128]{1,0:T(8,128)(2,1)} %collective-permute-done.3.refs_7_), channel_id=1, source_target_pairs={{0,16},{16,0},{1,17},{17,1},{2,18},{18,2},{3,19},{19,3},{4,20},{20... | collective-permute-start | bytes 589832 | tf_op jit(solution)/shard_map/ppermute | solution.py:326
  133.3 10.3 %collective-permute-start.15 = (bf16[768,128]{1,0:T(8,128)(2,1)S(1)}, bf16[768,128]{1,0:T(8,128)(2,1)S(1)}, u32[]{:S(2)}, u32[]{:S(2)}) collective-permute-start(bf16[768,128]{1,0:T(8,128)(2,1)S(1)} %collective-permute-done.2.refs_8_), channel_id=1, source_target_pairs={{0,16},{16,0},{1,17},{17,1},{2,18},{18,2},{3,19},{19,3},{4,20},{20... | collective-permute-start | bytes 589832 | tf_op jit(solution)/shard_map/ppermute | solution.py:326
  133.8 11.9 %collective-permute-start.16 = (bf16[768,128]{1,0:T(8,128)(2,1)S(1)}, bf16[768,128]{1,0:T(8,128)(2,1)S(1)}, u32[]{:S(2)}, u32[]{:S(2)}) collective-permute-start(bf16[768,128]{1,0:T(8,128)(2,1)S(1)} %collective-permute-done.1.refs_6_), channel_id=1, source_target_pairs={{0,16},{16,0},{1,17},{17,1},{2,18},{18,2},{3,19},{19,3},{4,20},{20... | collective-permute-start | bytes 589832 | tf_op jit(solution)/shard_map/ppermute | solution.py:326
  156.4 5.0 %copy-start.15 = (bf16[768,128]{1,0:T(8,128)(2,1)}, bf16[768,128]{1,0:T(8,128)(2,1)S(1)}, u32[]{:S(2)}) copy-start(bf16[768,128]{1,0:T(8,128)(2,1)S(1)} %get-tuple-element.310.refs_0_) | copy-start | bytes 589828
  156.4 7.4 %collective-permute-start.19 = (bf16[768,128]{1,0:T(8,128)(2,1)S(1)}, bf16[768,128]{1,0:T(8,128)(2,1)S(1)}, u32[]{:S(2)}, u32[]{:S(2)}) collective-permute-start(bf16[768,128]{1,0:T(8,128)(2,1)S(1)} %get-tuple-element.323), channel_id=1, source_target_pairs={{0,4},{4,0},{8,12},{12,8},{1,5},{5,1},{9,13},{13,9},{2,6},{6,2},{1... | collective-permute-start | bytes 589832 | tf_op jit(solution)/shard_map/ppermute | solution.py:326
  161.3 0.7 copy-start.16
  162.0 6.7 %collective-permute-start.20 = (bf16[768,128]{1,0:T(8,128)(2,1)S(1)}, bf16[768,128]{1,0:T(8,128)(2,1)S(1)}, u32[]{:S(2)}, u32[]{:S(2)}) collective-permute-start(bf16[768,128]{1,0:T(8,128)(2,1)S(1)} %get-tuple-element.324), channel_id=1, source_target_pairs={{0,4},{4,0},{8,12},{12,8},{1,5},{5,1},{9,13},{13,9},{2,6},{6,2},{1... | collective-permute-start | bytes 589832 | tf_op jit(solution)/shard_map/ppermute | solution.py:326
  163.8 5.0 %copy-start.23 = (bf16[768,128]{1,0:T(8,128)(2,1)}, bf16[768,128]{1,0:T(8,128)(2,1)S(1)}, u32[]{:S(2)}) copy-start(bf16[768,128]{1,0:T(8,128)(2,1)S(1)} %collective-permute-done.19.refs_2_) | copy-start | bytes 589828
  168.8 0.7 copy-start.24

commit v3 on v2

v3 whole, which is shorter than its diff:
```python
import math

import jax
import jax.numpy as jnp
from jax import lax
from jax.experimental import pallas as pl
from jax.experimental.pallas import tpu as pltpu
from jax.sharding import PartitionSpec as P

EPS = 1e-06
HIDDEN = -1e30
COST = pl.CostEstimate(flops=1 << 20, bytes_accessed=1 << 10, transcendentals=0)
MIDDLE = pl.CostEstimate(flops=1 << 33, bytes_accessed=1 << 10, transcendentals=0)
LONG = pl.CostEstimate(flops=1 << 37, bytes_accessed=1 << 10, transcendentals=0)


def with_halo(shard, sides, width):
    for axis, dim in sides:
        devices, length = (lax.axis_size(axis), shard.shape[dim])
        up = [(i, (i + 1) % devices) for i in range(devices - 1)]
        down = [(j, i) for i, j in up]
        last = lax.slice_in_dim(shard, length - width, length, axis=dim)
        first = lax.slice_in_dim(shard, 0, width, axis=dim)
        before = lax.ppermute(last, axis, up)
        after = lax.ppermute(first, axis, down)
        shard = jnp.concatenate([before, shard, after], axis=dim)
    return shard


def normed_heads(tensor, gain_row, head_dim):
    shaped = tensor.reshape(tensor.shape[0], tensor.shape[1] // head_dim, head_dim)
    scaled = (
        shaped * lax.rsqrt(jnp.mean(shaped * shaped, axis=-1, keepdims=True) + EPS) * gain_row
    )
    return scaled.astype(jnp.bfloat16)


def visible_tiles(block_lists):
    position = lax.axis_index("seq")
    tile_dev = block_lists.shape[0]
    candidates = (position - 1) * tile_dev + jnp.arange(3 * tile_dev, dtype=jnp.int32)
    matches = (block_lists[:, :, None] == candidates[None, None, :]) & (
        block_lists[:, :, None] >= 0
    )
    return jnp.any(matches, axis=1)


def general(frames, modulation, w_qkv, b_qkv, qk_gain, block_lists):
    inputs = frames.astype(jnp.float32)
    average = jnp.mean(inputs, axis=-1, keepdims=True)
    centred = inputs - average
    variance = jnp.mean(centred * centred, axis=-1, keepdims=True)
    normed = centred * lax.rsqrt(variance + EPS) * (1.0 + modulation[0]) + modulation[1]
    normed = normed.astype(jnp.bfloat16)
    tokens = normed.shape[0]
    width_cols = w_qkv.shape[2]
    head_dim = qk_gain.shape[1]
    heads = width_cols // head_dim
    projected = jnp.einsum(
        "td,djc->tjc",
        normed,
        lax.all_gather(w_qkv, "seq", axis=0, tiled=True),
        preferred_element_type=jnp.float32,
    )
    projected = projected + b_qkv
    queries = normed_heads(projected[:, 0], qk_gain[0], head_dim)
    key_rows = normed_heads(projected[:, 1], qk_gain[1], head_dim)
    values = projected[:, 2].astype(jnp.bfloat16).reshape(tokens, heads, head_dim)
    stacked = jnp.stack([key_rows, values], axis=0)
    neighbourhood = with_halo(stacked, (("seq", 1),), tokens)
    tile_len = tokens // block_lists.shape[0]
    allowed_keys = jnp.repeat(
        jnp.repeat(visible_tiles(block_lists), tile_len, axis=0), tile_len, axis=1
    )
    factor = 1.0 / math.sqrt(head_dim)
    scores = (
        jnp.einsum("qhd,khd->hqk", queries, neighbourhood[0], preferred_element_type=jnp.float32)
        * factor
    )
    weights = jnp.where(allowed_keys[None, :, :], jnp.exp(scores), 0.0)
    totals = jnp.sum(weights, axis=-1)
    mixture = jnp.einsum(
        "hqk,khd->qhd",
        weights.astype(jnp.bfloat16),
        neighbourhood[1],
        preferred_element_type=jnp.float32,
    )
    result = (mixture / jnp.transpose(totals)[:, :, None]).astype(jnp.bfloat16)
    return result.reshape(tokens, width_cols)


class Line:
    def __init__(self):
        self.held = []

    def reached(self, *values):
        boxes = [[v] for v in values]
        self.held += boxes
        return boxes

    def after(self, *values):
        out = lax.optimization_barrier((*values, *(box[0] for box in self.held)))
        for box, value in zip(self.held, out[len(values) :]):
            box[0] = value
        return out[: len(values)]

    def drop(self, *boxes):
        self.held = [box for box in self.held if all(box is not b for b in boxes)]
        return [box[0] for box in boxes]


def norm_kernel(x_ref, mod_ref, o_ref):
    x = x_ref[...].astype(jnp.float32)
    centred = x - jnp.mean(x, axis=-1, keepdims=True)
    variance = jnp.mean(centred * centred, axis=-1, keepdims=True)
    scaled = centred * lax.rsqrt(variance + EPS) * (1.0 + mod_ref[0:1, :]) + mod_ref[1:2, :]
    o_ref[...] = scaled.astype(jnp.bfloat16)


def normalize(frames, modulation, rows, cost=COST):
    tokens, width = frames.shape
    return pl.pallas_call(
        norm_kernel,
        grid=(tokens // rows,),
        in_specs=[
            pl.BlockSpec((rows, width), lambda i: (i, 0)),
            pl.BlockSpec((2, width), lambda i: (0, 0)),
        ],
        out_specs=pl.BlockSpec((rows, width), lambda i: (i, 0)),
        out_shape=jax.ShapeDtypeStruct((tokens, width), jnp.bfloat16),
        cost_estimate=cost,
        name="normalize",
    )(frames, modulation)


def cut_heads(at, w, groups, cost=COST):
    rows = w.shape[1]
    head_dim = 128
    widths = [head_dim * len(js) for _, js in groups]

    def kernel(at_ref, w_ref, *out_refs):
        for (index, js), ref in zip(groups, out_refs):
            cols = pl.ds(pl.multiple_of(at_ref[index] * head_dim, 128), head_dim)
            for i, j in enumerate(js):
                ref[:, i * head_dim : (i + 1) * head_dim] = w_ref[j, :, cols]

    return pl.pallas_call(
        kernel,
        in_specs=[pl.BlockSpec(memory_space=pltpu.SMEM), pl.BlockSpec()],
        out_specs=[pl.BlockSpec()] * len(groups),
        out_shape=[jax.ShapeDtypeStruct((rows, n), jnp.bfloat16) for n in widths],
        compiler_params=pltpu.CompilerParams(vmem_limit_bytes=24 << 20),
        cost_estimate=cost,
        name="cut_heads",
    )(at, w)


def see(at, lists, tile_dev):
    def kernel(at_ref, lists_ref, o_ref):
        lists = lists_ref[...]
        z = at_ref[0]
        lane = lax.broadcasted_iota(jnp.int32, o_ref.shape, 1)
        out = jnp.full(o_ref.shape, HIDDEN, jnp.float32)
        for c, column in enumerate((z, z ^ 1, jnp.where(z < 2, 2, 1))):
            for t in range(tile_dev):
                hit = (lists == column * tile_dev + t).astype(jnp.float32)
                listed = jnp.max(hit, axis=1, keepdims=True) > 0.0
                out = jnp.where((lane == c * tile_dev + t) & listed, 0.0, out)
        o_ref[...] = out

    return pl.pallas_call(
        kernel,
        in_specs=[pl.BlockSpec(memory_space=pltpu.SMEM), pl.BlockSpec()],
        out_specs=pl.BlockSpec(),
        out_shape=jax.ShapeDtypeStruct((lists.shape[0], 128), jnp.float32),
        cost_estimate=COST,
        name="see",
    )(at, lists)


def project(at, head_index, first, own_x, quarters, weights, bias, gain, norms, cost=COST):
    rows, cols = weights[0].shape
    head_dim = gain.shape[1]
    sources = [own_x] if quarters is None else list(quarters)
    tokens = own_x.shape[0] if quarters is None else 4 * quarters[0].shape[0]
    width = sources[0].shape[1]
    step = 256

    def kernel(at_ref, *refs):
        x_refs, weight_refs = refs[: len(sources)], refs[len(sources) : len(sources) + 4]
        b_ref, g_ref, out_ref = refs[len(sources) + 4 :]
        z, q = at_ref[0], at_ref[1]
        here = pl.ds(pl.multiple_of(at_ref[head_index] * head_dim, 128), head_dim)

        def piece(ref, to_row):
            total = None
            for s in range(4):
                cut = pl.multiple_of((z ^ s) * rows, 128)
                part = jnp.dot(
                    ref[:, pl.ds(cut, rows)],
                    weight_refs[s][...],
                    preferred_element_type=jnp.float32,
                )
                total = part if total is None else total + part
            for i, row in enumerate(norms):
                part = total[:, i * head_dim : (i + 1) * head_dim]
                part = part + b_ref[first + i : first + i + 1, here]
                if row is not None:
                    mean = jnp.mean(part * part, axis=-1, keepdims=True)
                    part = part * lax.rsqrt(mean + EPS) * g_ref[row : row + 1, :]
                out_ref[pl.ds(to_row, ref.shape[0]), i * head_dim : (i + 1) * head_dim] = (
                    part.astype(jnp.bfloat16)
                )

        if quarters is None:
            piece(x_refs[0], 0)
        else:
            for i, ref in enumerate(x_refs):
                piece(ref, pl.multiple_of((q ^ i) * ref.shape[0], 64))

    smem = pl.BlockSpec(memory_space=pltpu.SMEM)
    if quarters is None:
        grid = (tokens // step,)
        fixed = lambda shape: pl.BlockSpec(shape, lambda i: (0,) * len(shape))
        x_specs = [pl.BlockSpec((step, width), lambda i: (i, 0))]
        out_spec = pl.BlockSpec((step, cols), lambda i: (i, 0))
    else:
        grid = ()
        fixed = lambda shape: pl.BlockSpec()
        x_specs = [pl.BlockSpec()] * 4
        out_spec = pl.BlockSpec()
    return pl.pallas_call(
        kernel,
        grid=grid,
        in_specs=[smem, *x_specs, *(fixed(w.shape) for w in weights), fixed(bias.shape), fixed(gain.shape)],
        out_specs=out_spec,
        out_shape=jax.ShapeDtypeStruct((tokens, cols), jnp.bfloat16),
        compiler_params=pltpu.CompilerParams(vmem_limit_bytes=40 << 20),
        cost_estimate=cost,
        name="project",
    )(at, *sources, *weights, bias, gain)


def tile_step(query, rows_ref, at, tile, head_dim, limit, total, mixed):
    scale = math.log2(math.e) / math.sqrt(head_dim)
    keys = rows_ref[at : at + tile, :head_dim]
    values = rows_ref[at : at + tile, head_dim:]
    scores = lax.dot_general(
        query, keys, (((1,), (1,)), ((), ())), preferred_element_type=jnp.float32
    )
    weights = jnp.exp2(scores * scale + limit)
    for c in range(tile // 128):
        total = total + weights[:, c * 128 : (c + 1) * 128]
    mixed = mixed + jnp.dot(
        weights.astype(jnp.bfloat16), values, preferred_element_type=jnp.float32
    )
    return total, mixed


def attend_pair(place, limits, queries, rows):
    tokens, head_dim = queries[0].shape
    tiles = limits[0].shape[0]
    tile = tokens // tiles

    def kernel(place_ref, limit0_ref, limit1_ref, q0_ref, q1_ref, rows0_ref, rows1_ref, done_ref, mixed_ref, total_ref):
        is_mid = (place_ref[0] == 1) | (place_ref[0] == 2)
        for column, q_ref in enumerate((q0_ref, q1_ref)):
            for i in range(tiles):
                here = slice(i * tile, (i + 1) * tile)
                query = q_ref[here, :]
                total = jnp.zeros((tile, 128), jnp.float32)
                mixed = jnp.zeros((tile, head_dim), jnp.float32)
                for side, ref in enumerate((rows0_ref, rows1_ref)):
                    for t in range(tiles):
                        limit = (limit0_ref, limit1_ref)[column][i, (side ^ column) * tiles + t]
                        total, mixed = tile_step(
                            query, ref, t * tile, tile, head_dim, limit, total, mixed
                        )
                is_edge = is_mid if column == 0 else jnp.logical_not(is_mid)

                @pl.when(is_edge)
                def _():
                    mixed_ref[here, :] = mixed
                    total_ref[here, :] = total

                @pl.when(jnp.logical_not(is_edge))
                def _():
                    done_ref[here, :] = (mixed / jnp.sum(total, axis=-1, keepdims=True)).astype(
                        jnp.bfloat16
                    )

    vmem = pl.BlockSpec()
    smem = pl.BlockSpec(memory_space=pltpu.SMEM)
    return pl.pallas_call(
        kernel,
        in_specs=[smem, smem, smem] + [vmem] * 4,
        out_specs=[vmem] * 3,
        out_shape=[
            jax.ShapeDtypeStruct((tokens, head_dim), jnp.bfloat16),
            jax.ShapeDtypeStruct((tokens, head_dim), jnp.float32),
            jax.ShapeDtypeStruct((tokens, 128), jnp.float32),
        ],
        compiler_params=pltpu.CompilerParams(vmem_limit_bytes=40 << 20),
        cost_estimate=COST,
        name="attend_pair",
    )(place, *limits, *queries, *rows)


def attend_halo(place, limits, queries, halo, done, mixed, total):
    tokens, head_dim = queries[0].shape
    tiles = limits[0].shape[0]
    tile = tokens // tiles

    def kernel(place_ref, limit0_ref, limit1_ref, q0_ref, q1_ref, halo_ref, done_ref, mixed_ref, total_ref, keep_ref, send_ref):
        is_mid = (place_ref[0] == 1) | (place_ref[0] == 2)
        for i in range(tiles):
            here = slice(i * tile, (i + 1) * tile)
            query = jnp.where(is_mid, q0_ref[here, :], q1_ref[here, :])
            sums, rows = total_ref[here, :], mixed_ref[here, :]
            for t in range(tiles):
                limit = jnp.where(is_mid, limit0_ref[i, 2 * tiles + t], limit1_ref[i, 2 * tiles + t])
                sums, rows = tile_step(query, halo_ref, t * tile, tile, head_dim, limit, sums, rows)
            edge = (rows / jnp.sum(sums, axis=-1, keepdims=True)).astype(jnp.bfloat16)
            outer = done_ref[here, :]
            keep_ref[here, :] = jnp.where(is_mid, edge, outer)
            send_ref[here, :] = jnp.where(is_mid, outer, edge)

    vmem = pl.BlockSpec()
    smem = pl.BlockSpec(memory_space=pltpu.SMEM)
    out = jax.ShapeDtypeStruct((tokens, head_dim), jnp.bfloat16)
    return pl.pallas_call(
        kernel,
        in_specs=[smem, smem, smem] + [vmem] * 6,
        out_specs=[vmem, vmem],
        out_shape=[out, out],
        compiler_params=pltpu.CompilerParams(vmem_limit_bytes=40 << 20),
        cost_estimate=COST,
        name="attend_halo",
    )(place, *limits, *queries, halo, done, mixed, total)


def assemble(at, parts, carried=None, heads=4):
    indices, arrays = zip(*parts)
    tokens, head_dim = arrays[0].shape
    carried = () if carried is None else (carried,)

    def kernel(at_ref, *refs):
        out_ref, sems = refs[-2:]
        copies = []
        for i, (index, ref) in enumerate(zip(indices, refs)):
            cols = pl.ds(pl.multiple_of(at_ref[index] * head_dim, 128), head_dim)
            copies.append(pltpu.make_async_copy(ref, out_ref.at[:, cols], sems.at[i]))
            copies[-1].start()
        for copy in copies:
            copy.wait()

    anywhere = pl.BlockSpec(memory_space=pl.ANY)
    return pl.pallas_call(
        kernel,
        in_specs=[pl.BlockSpec(memory_space=pltpu.SMEM)] + [anywhere] * (len(arrays) + len(carried)),
        out_specs=anywhere,
        out_shape=jax.ShapeDtypeStruct((tokens, head_dim * heads), jnp.bfloat16),
        scratch_shapes=[pltpu.SemaphoreType.DMA((len(arrays),))],
        input_output_aliases={1 + len(arrays): 0} if carried else {},
        cost_estimate=COST,
        name="assemble",
    )(at, *arrays, *carried)


def per_device(frames, modulation, w_qkv, b_qkv, qk_gain, block_lists):
    sizes = tuple(lax.axis_size(a) for a in ("groups", "seq", "fsdp", "head"))
    head_dim = qk_gain.shape[1]
    width_cols = w_qkv.shape[2]
    tokens = frames.shape[0]
    if sizes != (2, 4, 2, 2) or width_cols != 4 * head_dim:
        return general(frames, modulation, w_qkv, b_qkv, qk_gain, block_lists)

    y, z, x, core = (lax.axis_index(a).astype(jnp.int32) for a in ("groups", "seq", "fsdp", "head"))
    rows = w_qkv.shape[0]
    quarter = tokens // 4
    tile_dev = block_lists.shape[0]

    def to(axis, value, bit):
        return lax.ppermute(value, axis, [(i, i ^ bit) for i in range(lax.axis_size(axis))])

    side = z % 2
    mine, twin = 2 * side + y, 2 * side + 1 - y
    across = 2 * (1 - side)
    at = jnp.stack([z, 2 * x + core, mine, twin, across + y, across + 1 - y])
    MINE, TWIN, CROSS, CROSS_TWIN = 2, 3, 4, 5
    KV, Q = (1, 2), (0,)
    NORMS = {KV: (1, None), Q: (0,)}
    is_mid = (z == 1) | (z == 2)
    w = jnp.transpose(w_qkv, (1, 0, 2))
    line = Line()

    raw = lax.dynamic_slice(frames, (at[1] * quarter, 0), (quarter, frames.shape[1]))
    raw_other = to("seq", raw, 1)
    w, raw = lax.optimization_barrier((w, raw))
    cuts = cut_heads(at, w, [(MINE, KV), (CROSS, KV), (MINE, Q), (CROSS, Q)], LONG)
    cuts = line.reached(*cuts)
    own_w = {(MINE, KV): cuts[0], (MINE, Q): cuts[2]}
    got = {}
    for part, same, cross in ((KV, *cuts[:2]), (Q, *cuts[2:])):
        got[part] = [to("seq", same[0], 2), to("seq", cross[0], 3), to("seq", cross[0], 1)]
    frames, modulation = line.after(frames, modulation)
    own_x = line.reached(normalize(frames, modulation, 128, MIDDLE))
    line.drop(cuts[1], cuts[3])
    (w,) = line.after(w)
    for key, box in zip(((TWIN, KV), (TWIN, Q)), line.reached(*cut_heads(at, w, [(TWIN, KV), (TWIN, Q)]))):
        own_w[key] = box
    own_limit = line.reached(see(at, block_lists, tile_dev))
    far_limit = to("seq", own_limit[0][0], 1)

    (raw_other,) = line.after(raw_other)
    near_q = line.reached(normalize(raw_other, modulation, 96))
    far_q = to("fsdp", near_q[0][0], 1)
    near_c = to("head", near_q[0][0], 1)

    def arrive(value):
        box = line.reached(value)[0]
        (box[0],) = line.after(box[0])
        return box

    def swaps(part):
        boxes = [arrive(value) for value in got[part]]
        return boxes, [to("groups", box[0], 1) for box in boxes]

    def run(head, part, boxes, own, cost=COST):
        (own_part,) = line.after(own_w[head, part][0])
        own_w[head, part][0] = own_part
        two, three, one = (box[0] for box in boxes)
        return line.reached(
            project(
                at, head, part[0], own_x[0][0] if own else None,
                None if own else [b[0] for b in quarters],
                [own_part, one, two, three], b_qkv, qk_gain, NORMS[part], cost,
            )
        )

    def send_edge(rows):
        return to("seq", jnp.where(is_mid, rows[0][0], rows[1][0]), 2)

    kv_boxes, kv_back = swaps(KV)
    rows_mine = run(MINE, KV, kv_boxes, True, LONG)
    far_box = arrive(far_q)
    far_c = to("head", far_box[0], 1)
    kv_twin = line.reached(*kv_back)
    rows_twin = run(TWIN, KV, kv_twin, True, LONG)
    quarters = near_q + line.reached(near_c) + [far_box] + line.reached(far_c)
    rows_mine += run(MINE, KV, kv_boxes, False)
    halo_mine = send_edge(rows_mine)
    rows_twin += run(TWIN, KV, kv_twin, False)
    halo_twin = send_edge(rows_twin)
    line.drop(*kv_boxes, *kv_twin)
    q_boxes, q_back = swaps(Q)
    q_mine = run(MINE, Q, q_boxes, True)
    q_mine += run(MINE, Q, q_boxes, False)
    line.drop(*q_boxes)

    limits = own_limit + line.reached(far_limit)

    def pair(q, rows):
        parts = attend_pair(at, [b[0] for b in limits], [b[0] for b in q], [b[0] for b in rows])
        return line.reached(*parts)

    def finish(q, halo, parts):
        keep, send = attend_halo(
            at, [b[0] for b in limits], [b[0] for b in q], halo, *(b[0] for b in parts)
        )
        return line.reached(keep)[0], to("seq", send, 1)

    parts_mine = pair(q_mine, rows_mine)
    q_twin_w = line.reached(*q_back)
    q_twin = run(TWIN, Q, q_twin_w, True)
    q_twin += run(TWIN, Q, q_twin_w, False)
    line.drop(*q_twin_w, *own_x, *quarters, *rows_mine)
    (halo_mine,) = line.after(halo_mine)
    keep_mine, back_mine = finish(q_mine, halo_mine, parts_mine)
    line.drop(*q_mine, *parts_mine)
    q_twin[0][0], q_twin[1][0] = line.after(q_twin[0][0], q_twin[1][0])
    parts_twin = pair(q_twin, rows_twin)
    (halo_twin,) = line.after(halo_twin)
    keep_twin, back_twin = finish(q_twin, halo_twin, parts_twin)
    parts = [(MINE, keep_mine[0]), (TWIN, keep_twin[0]), (CROSS, back_mine)]
    return assemble(at, [(CROSS_TWIN, back_twin)], assemble(at, parts))


def solution(mesh):
    placed = (
        P(("groups", "seq"), None),
        P("groups", None),
        P("seq", None, ("fsdp", "head")),
        P(None, ("fsdp", "head")),
        P(),
        P(("groups", "seq"), None),
    )
    return jax.shard_map(
        per_device,
        mesh=mesh,
        in_specs=placed,
        out_specs=P(("groups", "seq"), ("fsdp", "head")),
        check_vma=False,
    )
```

time: 173 us -> 174 us (level)
  Pallas kernels: 43.9 us -> 75.1 us
  waiting for transfers between devices: 74 us -> 60.9 us
  local copies, waits for them, and re-layouts: 20.4 us -> 7.76 us
  other arithmetic: 6.22 us -> 0.1 us
  starting transfers between devices: 26.9 us -> 29 us
    pallas_call x1 -> x2, Pallas kernels: 2.24 us -> 27.4 us  [assemble(): pl.pallas_call(kernel, in_specs=[pl.BlockSpec(memory_space=pltpu.SMEM)] +...]
    ppermute x21, waiting for transfers between devices: 74 us -> 60.9 us  [to(): lax.ppermute(value, axis, [(i, i ^ bit) for i in range(lax.axis_size(axis...]
    unnamed x54 -> x32, local copies, waits for them, and re-layouts: 13.1 us -> 5.17 us
    pallas_call x9 -> x15, Pallas kernels: 31.5 us -> 37.5 us  [the longest x8 20.7 us: project(): pl.pallas_call(kernel, grid=grid, in_specs=[smem, *x_specs, *(fixed(w.sha...]
    squeeze x1 -> x0, local copies, waits for them, and re-layouts: 2.65 us -> none  [cut(): lax.dynamic_slice(w, (j, 0, head * head_dim), (1, rows, head_dim))[0]]
    ppermute x21, starting transfers between devices: 26.9 us -> 29 us  [to(): lax.ppermute(value, axis, [(i, i ^ bit) for i in range(lax.axis_size(axis...]
    concatenate x3 -> x0, other arithmetic: 1.93 us -> none  [cut(): return jnp.concatenate(parts, axis=1)]
    ge x2 -> x0, other arithmetic: 1.88 us -> none  [seen(): lists[:, :, None] >= 0]
  transfers between devices with their start and end apart: 21 -> 21, of which waited for: 10 -> 7; matrix products, arithmetic and copies ran while one was open for 6% -> 0% of each run, Pallas kernels for 24% -> 39%
where the time goes in v3:
time: 174 us; the launch traced here: 173 us
  Pallas kernels  75.1 us (43%)
  waiting for transfers between devices  60.9 us (35%)
  starting transfers between devices  29 us (17%)
  local copies, waits for them, and re-layouts  7.76 us (4%)
    ppermute x21, waiting for transfers between devices, to(): lax.ppermute(value, axis, [(i, i ^ bit) for i in range(lax.axis_size(axis...  60.9 us
    ppermute x21, starting transfers between devices, to(): lax.ppermute(value, axis, [(i, i ^ bit) for i in range(lax.axis_size(axis...  29 us
    pallas_call x2, Pallas kernels, assemble(): pl.pallas_call(kernel, in_specs=[pl.BlockSpec(memory_space=pltpu.SMEM)] +...  27.4 us
    pallas_call x8, Pallas kernels, project(): pl.pallas_call(kernel, grid=grid, in_specs=[smem, *x_specs, *(fixed(w.sha...  20.7 us
    pallas_call x2, Pallas kernels, normalize(): pl.pallas_call(norm_kernel, grid=(tokens // rows,), in_specs=[pl.BlockSpe...  10.2 us
    pallas_call x2, Pallas kernels, attend_pair(): pl.pallas_call(kernel, in_specs=[smem, smem, smem] + [vmem] * 4, out_spec...  9.93 us
    unnamed x32, local copies, waits for them, and re-layouts  5.17 us
  transfers between devices with their start and end apart: 21, of which 7 were waited for; matrix products, arithmetic and copies ran while one was open for 0% of the time, Pallas kernels for 39%

profile of v3, /device:TPU:0, one launch (start us, length us, event | category | flops | bytes accessed | tf_op | source)
XLA Modules:
  0.0 173.3 jit_solution(1494646285481025189)
XLA Ops:
  0.0 2.5 %constant_dynamic-slice_fusion = bf16[192,3072]{1,0:T(8,128)(2,1)} fusion(bf16[768,3072]{1,0:T(8,128)(2,1)} %x_ref, s32[]{:T(128)S(6)} %select_n.24), kind=kLoop, calls=%fused_computation.2 | loop fusion | bytes 2359300 | tf_op jit(solution)/shard_map/dynamic_slice | solution.py:397
  2.5 3.0 %collective-permute-start = (bf16[192,3072]{1,0:T(8,128)(2,1)}, bf16[192,3072]{1,0:T(8,128)(2,1)}, u32[]{:S(2)}, u32[]{:S(2)}) collective-permute-start(bf16[192,3072]{1,0:T(8,128)(2,1)} %constant_dynamic-slice_fusion), channel_id=1, source_target_pairs={{0,4},{4,0},{8,12},{12,8},{1,5},{5,1},{9,13},{13,9},{2,6},{6,2},{1... | collective-permute-start | bytes 3538952 | tf_op jit(solution)/shard_map/ppermute | solution.py:384
  5.6 1.5 cut_heads.2
  7.1 2.5 %collective-permute-start.3 = (bf16[768,256]{1,0:T(8,128)(2,1)}, bf16[768,256]{1,0:T(8,128)(2,1)S(1)}, u32[]{:S(2)}, u32[]{:S(2)}) collective-permute-start(bf16[768,256]{1,0:T(8,128)(2,1)} %get-tuple-element.273), channel_id=1, source_target_pairs={{0,12},{4,8},{8,4},{12,0},{1,13},{5,9},{9,5},{13,1},{2,14},{6,10},... | collective-permute-start | bytes 1179656 | tf_op jit(solution)/shard_map/ppermute | solution.py:384
  9.6 0.7 collective-permute-start.2
  10.3 1.2 collective-permute-start.4
  11.5 1.7 collective-permute-start.14
  13.2 7.3 %normalize.2.refs_0_ = bf16[768,3072]{1,0:T(8,128)(2,1)} custom-call(bf16[768,3072]{1,0:T(8,128)(2,1)} %x_ref, f32[2,3072]{1,0:T(2,128)} %mod_ref.1), custom_call_target="tpu_custom_call" | custom-call | flops 8589934592 | bytes 1024 | tf_op jit(solution)/shard_map/normalize/pallas_call | solution.py:122
  20.6 0.6 cut_heads.3
  21.2 0.8 copy-done.3
  22.0 1.4 see.1.limit0_ref
  23.3 30.4 %collective-permute-done.x_ref = bf16[192,3072]{1,0:T(8,128)(2,1)} collective-permute-done((bf16[192,3072]{1,0:T(8,128)(2,1)}, bf16[192,3072]{1,0:T(8,128)(2,1)}, u32[]{:S(2)}, u32[]{:S(2)}) %collective-permute-start) | collective-permute-done | bytes 1179680 | tf_op jit(solution)/shard_map/ppermute | solution.py:384
  53.7 2.9 %normalize.3.refs_0_ = bf16[192,3072]{1,0:T(8,128)(2,1)} custom-call(bf16[192,3072]{1,0:T(8,128)(2,1)} %collective-permute-done.x_ref, f32[2,3072]{1,0:T(2,128)} %mod_ref.1), custom_call_target="tpu_custom_call" | custom-call | flops 1048576 | bytes 1024 | tf_op jit(solution)/shard_map/normalize/pallas_call | solution.py:122
  56.6 2.0 %collective-permute-start.1 = (bf16[192,3072]{1,0:T(8,128)(2,1)}, bf16[192,3072]{1,0:T(8,128)(2,1)S(1)}, u32[]{:S(2)}, u32[]{:S(2)}) collective-permute-start(bf16[192,3072]{1,0:T(8,128)(2,1)} %normalize.3.refs_0_), channel_id=1, source_target_pairs={{0,2},{2,0},{1,3},{3,1},{4,6},{6,4},{5,7},{7,5},{8,10},{10,8},{9,1... | collective-permute-start | bytes 3538952 | tf_op jit(solution)/shard_map/ppermute | solution.py:384
  58.6 2.7 %collective-permute-done.2.refs_2_.refs_5_ = bf16[768,256]{1,0:T(8,128)(2,1)} collective-permute-done((bf16[768,256]{1,0:T(8,128)(2,1)}, bf16[768,256]{1,0:T(8,128)(2,1)}, u32[]{:S(2)}, u32[]{:S(2)}) %collective-permute-start.2) | collective-permute-done | bytes 393248 | tf_op jit(solution)/shard_map/ppermute | solution.py:384
  61.3 1.7 collective-permute-start.5
  63.0 0.4 collective-permute-start.6
  63.3 1.7 collective-permute-start.7
  65.0 2.3 %copy-done.1 = bf16[768,3072]{1,0:T(8,128)(2,1)S(1)} copy-done((bf16[768,3072]{1,0:T(8,128)(2,1)S(1)}, bf16[768,3072]{1,0:T(8,128)(2,1)}, u32[]{:S(2)}) %copy-start.1) | copy-done | bytes 4718616
  67.4 3.2 %project.8.rows0_ref = bf16[768,256]{1,0:T(8,128)(2,1)S(1)} custom-call(s32[6]{0:T(128)S(1)} %copy-done.9, bf16[768,3072]{1,0:T(8,128)(2,1)S(1)} %copy-done.1, bf16[768,256]{1,0:T(8,128)(2,1)S(1)} %get-tuple-element.358.refs_1_.refs_4_, bf16[768,256]{1,0:T(8,128)(2,1)} %collective-permute-done.2.refs_2_.refs_5_, ...), custom_call_target="tpu_custom_call" | custom-call | flops 137438953472 | bytes 1024 | tf_op jit(solution)/shard_map/project/pallas_call | solution.py:232
  70.6 12.6 %collective-permute-done.1.refs_2_ = bf16[192,3072]{1,0:T(8,128)(2,1)S(1)} collective-permute-done((bf16[192,3072]{1,0:T(8,128)(2,1)}, bf16[192,3072]{1,0:T(8,128)(2,1)S(1)}, u32[]{:S(2)}, u32[]{:S(2)}) %collective-permute-start.1) | collective-permute-done | bytes 1179680 | tf_op jit(solution)/shard_map/ppermute | solution.py:384
  83.1 3.5 %collective-permute-start.13 = (bf16[768,128]{1,0:T(8,128)(2,1)S(1)}, bf16[768,128]{1,0:T(8,128)(2,1)S(1)}, u32[]{:S(2)}, u32[]{:S(2)}) collective-permute-start(bf16[768,128]{1,0:T(8,128)(2,1)S(1)} %get-tuple-element.275), channel_id=1, source_target_pairs={{0,12},{4,8},{8,4},{12,0},{1,13},{5,9},{9,5},{13,1},{2,14},{6,10},... | collective-permute-start | bytes 589832 | tf_op jit(solution)/shard_map/ppermute | solution.py:384
  86.7 2.0 %collective-permute-done.7.refs_2_.refs_5_ = bf16[768,256]{1,0:T(8,128)(2,1)S(1)} collective-permute-done((bf16[768,256]{1,0:T(8,128)(2,1)}, bf16[768,256]{1,0:T(8,128)(2,1)S(1)}, u32[]{:S(2)}, u32[]{:S(2)}) %collective-permute-start.7) | collective-permute-done | bytes 393248 | tf_op jit(solution)/shard_map/ppermute | solution.py:384
  88.7 2.6 %project.9.rows0_ref = bf16[768,256]{1,0:T(8,128)(2,1)S(1)} custom-call(s32[6]{0:T(128)S(1)} %copy-done.9, bf16[768,3072]{1,0:T(8,128)(2,1)S(1)} %copy-done.1, bf16[768,256]{1,0:T(8,128)(2,1)S(1)} %copy-done.4, bf16[768,256]{1,0:T(8,128)(2,1)S(1)} %collective-permute-done.7.refs_2_.refs_5_, bf16[768,256]{1,0:T(8,128)(2,1)S(1)} %collective-permute-done.5.refs_3_.refs_6_, ...), custom_call_target="tpu_custom_call" | custom-call | flops 137438953472 | bytes 1024 | tf_op jit(solution)/shard_map/project/pallas_call | solution.py:232
  91.5 2.7 %project.10.rows1_ref = bf16[768,256]{1,0:T(8,128)(2,1)S(1)} custom-call(s32[6]{0:T(128)S(1)} %copy-done.9, bf16[192,3072]{1,0:T(8,128)(2,1)S(1)} %copy-done, bf16[192,3072]{1,0:T(8,128)(2,1)S(1)} %collective-permute-done.8.refs_1_, bf16[192,3072]{1,0:T(8,128)(2,1)S(1)} %collective-permute-done.1.refs_2_, ...), custom_call_target="tpu_custom_call" | custom-call | flops 1048576 | bytes 1024 | tf_op jit(solution)/shard_map/project/pallas_call | solution.py:232
  94.3 1.6 collective-permute-start.11
  95.9 2.1 %project.11.rows1_ref = bf16[768,256]{1,0:T(8,128)(2,1)S(1)} custom-call(s32[6]{0:T(128)S(1)} %copy-done.9, bf16[192,3072]{1,0:T(8,128)(2,1)S(1)} %copy-done, bf16[192,3072]{1,0:T(8,128)(2,1)S(1)} %collective-permute-done.8.refs_1_, bf16[192,3072]{1,0:T(8,128)(2,1)S(1)} %collective-permute-done.1.refs_2_, ...), custom_call_target="tpu_custom_call" | custom-call | flops 1048576 | bytes 1024 | tf_op jit(solution)/shard_map/project/pallas_call | solution.py:232
  98.0 1.5 collective-permute-start.10
  99.5 1.6 collective-permute-start.15
  101.1 1.5 collective-permute-start.16
  102.6 0.5 collective-permute-start.17
  103.1 10.1 %collective-permute-done.15.limit1_ref = f32[2,128]{1,0:T(2,128)S(1)} collective-permute-done((f32[2,128]{1,0:T(2,128)S(1)}, f32[2,128]{1,0:T(2,128)S(1)}, u32[]{:S(2)}, u32[]{:S(2)}) %collective-permute-start.15) | collective-permute-done | bytes 1056 | tf_op jit(solution)/shard_map/ppermute | solution.py:384
  113.2 1.5 collective-permute-start.18
  114.7 3.1 %project.12.q0_ref = bf16[768,128]{1,0:T(8,128)(2,1)S(1)} custom-call(s32[6]{0:T(128)S(1)} %copy-done.9, bf16[768,3072]{1,0:T(8,128)(2,1)S(1)} %bitcast.8, bf16[768,128]{1,0:T(8,128)(2,1)} %get-tuple-element.448.refs_1_.refs_4_, bf16[768,128]{1,0:T(8,128)(2,1)S(1)} %collective-permute-done.12.refs_2_.refs_5_, ...), custom_call_target="tpu_custom_call" | custom-call | flops 1048576 | bytes 1024 | tf_op jit(solution)/shard_map/project/pallas_call | solution.py:232
  117.8 2.5 %project.13.q1_ref = bf16[768,128]{1,0:T(8,128)(2,1)S(1)} custom-call(s32[6]{0:T(128)S(1)} %copy-done.9, bf16[192,3072]{1,0:T(8,128)(2,1)S(1)} %copy-done, bf16[192,3072]{1,0:T(8,128)(2,1)S(1)} %collective-permute-done.8.refs_1_, bf16[192,3072]{1,0:T(8,128)(2,1)S(1)} %collective-permute-done.1.refs_2_, bf16[192,3072]{1,0:T(8,128)(2,1)S(1)} %collective-permute-done.9.refs_3_, ...), custom_call_target="tpu_custom_call" | custom-call | flops 1048576 | bytes 1024 | tf_op jit(solution)/shard_map/project/pallas_call | solution.py:232
  120.3 5.0 %attend_pair.2 = (bf16[768,128]{1,0:T(8,128)(2,1)S(1)}, f32[768,128]{1,0:T(8,128)S(1)}, f32[768,128]{1,0:T(8,128)S(1)}) custom-call(s32[6]{0:T(128)S(1)} %copy-done.9, f32[2,128]{1,0:T(2,128)S(1)} %copy-done.11, f32[2,128]{1,0:T(2,128)S(1)} %collective-permute-done.15.limit1_ref, bf16[768,128]{1,0:T(8,128)(2,1)S(1)} %project.12.q0_ref, ...), custom_call_target="tpu_custom_call" | custom-call | flops 1048576 | bytes 1024 | tf_op jit(solution)/shard_map/attend_pair/pallas_call | solution.py:294
  125.4 2.6 %project.14.q0_ref = bf16[768,128]{1,0:T(8,128)(2,1)S(1)} custom-call(s32[6]{0:T(128)S(1)} %copy-done.9, bf16[768,3072]{1,0:T(8,128)(2,1)S(1)} %bitcast.8, bf16[768,128]{1,0:T(8,128)(2,1)S(1)} %get-tuple-element.484.refs_1_.refs_4_, bf16[768,128]{1,0:T(8,128)(2,1)S(1)} %collective-permute-done.18.refs_2_.refs_5_, ...), custom_call_target="tpu_custom_call" | custom-call | flops 1048576 | bytes 1024 | tf_op jit(solution)/shard_map/project/pallas_call | solution.py:232
  128.0 2.0 %project.15.q1_ref = bf16[768,128]{1,0:T(8,128)(2,1)S(1)} custom-call(s32[6]{0:T(128)S(1)} %copy-done.9, bf16[192,3072]{1,0:T(8,128)(2,1)S(1)} %copy-done, bf16[192,3072]{1,0:T(8,128)(2,1)S(1)} %collective-permute-done.8.refs_1_, bf16[192,3072]{1,0:T(8,128)(2,1)S(1)} %collective-permute-done.1.refs_2_, bf16[192,3072]{1,0:T(8,128)(2,1)S(1)} %collective-permute-done.9.refs_3_, ...), custom_call_target="tpu_custom_call" | custom-call | flops 1048576 | bytes 1024 | tf_op jit(solution)/shard_map/project/pallas_call | solution.py:232
  130.0 1.6 attend_halo.2
  131.7 4.9 %attend_pair.3 = (bf16[768,128]{1,0:T(8,128)(2,1)S(1)}, f32[768,128]{1,0:T(8,128)S(1)}, f32[768,128]{1,0:T(8,128)S(1)}) custom-call(s32[6]{0:T(128)S(1)} %copy-done.9, f32[2,128]{1,0:T(2,128)S(1)} %copy-done.11, f32[2,128]{1,0:T(2,128)S(1)} %collective-permute-done.15.limit1_ref, bf16[768,128]{1,0:T(8,128)(2,1)S(1)} %project.14.q0_ref, ...), custom_call_target="tpu_custom_call" | custom-call | flops 1048576 | bytes 1024 | tf_op jit(solution)/shard_map/attend_pair/pallas_call | solution.py:294
  136.6 2.4 %collective-permute-start.20 = (bf16[768,128]{1,0:T(8,128)(2,1)S(1)}, bf16[768,128]{1,0:T(8,128)(2,1)S(1)}, u32[]{:S(2)}, u32[]{:S(2)}) collective-permute-start(bf16[768,128]{1,0:T(8,128)(2,1)S(1)} %get-tuple-element.536), channel_id=1, source_target_pairs={{0,4},{4,0},{8,12},{12,8},{1,5},{5,1},{9,13},{13,9},{2,6},{6,2},{1... | collective-permute-start | bytes 589832 | tf_op jit(solution)/shard_map/ppermute | solution.py:384
  139.0 1.6 attend_halo.3
  140.7 0.7 copy-done.7
  141.4 3.0 %collective-permute-done.20.refs_2_ = bf16[768,128]{1,0:T(8,128)(2,1)S(1)} collective-permute-done((bf16[768,128]{1,0:T(8,128)(2,1)S(1)}, bf16[768,128]{1,0:T(8,128)(2,1)S(1)}, u32[]{:S(2)}, u32[]{:S(2)}) %collective-permute-start.20) | collective-permute-done | bytes 196640 | tf_op jit(solution)/shard_map/ppermute | solution.py:384
  144.4 0.7 copy-done.12
  145.0 19.7 %assemble.2.refs_1_ = bf16[768,512]{1,0:T(8,128)(2,1)} custom-call(s32[6]{0:T(128)} %copy-done.8, bf16[768,128]{1,0:T(8,128)(2,1)} %copy-done.6, bf16[768,128]{1,0:T(8,128)(2,1)} %copy-done.7, bf16[768,128]{1,0:T(8,128)(2,1)} %copy-done.12), custom_call_target="tpu_custom_call" | custom-call | flops 1048576 | bytes 1024 | tf_op jit(solution)/shard_map/assemble/pallas_call | solution.py:358
  164.7 0.7 copy-done.13
  165.4 7.7 %assemble.3 = bf16[768,512]{1,0:T(8,128)(2,1)} custom-call(s32[6]{0:T(128)} %copy-done.8, bf16[768,128]{1,0:T(8,128)(2,1)} %copy-done.13, bf16[768,512]{1,0:T(8,128)(2,1)} %assemble.2.refs_1_), custom_call_target="tpu_custom_call", output_to_operand_aliasing={{}: (2, {})} | custom-call | flops 1048576 | bytes 1024 | tf_op jit(solution)/shard_map/assemble/pallas_call | solution.py:358
  (50 shorter events, 0.6 us)
Async XLA Ops:
  0.0 5.6 %copy-start.2 = (bf16[768,3,512]{2,0,1:T(8,128)(2,1)S(1)}, bf16[768,3,512]{2,0,1:T(8,128)(2,1)}, u32[]{:S(2)}) copy-start(bf16[768,3,512]{2,0,1:T(8,128)(2,1)} %param.8) | copy-start | bytes 7077892
  2.5 51.2 %collective-permute-start = (bf16[192,3072]{1,0:T(8,128)(2,1)}, bf16[192,3072]{1,0:T(8,128)(2,1)}, u32[]{:S(2)}, u32[]{:S(2)}) collective-permute-start(bf16[192,3072]{1,0:T(8,128)(2,1)} %constant_dynamic-slice_fusion), channel_id=1, source_target_pairs={{0,4},{4,0},{8,12},{12,8},{1,5},{5,1},{9,13},{13,9},{2,6},{6,2},{1... | collective-permute-start | bytes 3538952 | tf_op jit(solution)/shard_map/ppermute | solution.py:384
  5.6 14.9 %copy-start.8 = (s32[6]{0:T(128)}, s32[6]{0:T(128)S(1)}, u32[]{:S(2)}) copy-start(s32[6]{0:T(128)S(1)} %stack.27.at_ref.place_ref) | copy-start | bytes 76
  7.1 51.4 %collective-permute-start.3 = (bf16[768,256]{1,0:T(8,128)(2,1)}, bf16[768,256]{1,0:T(8,128)(2,1)S(1)}, u32[]{:S(2)}, u32[]{:S(2)}) collective-permute-start(bf16[768,256]{1,0:T(8,128)(2,1)} %get-tuple-element.273), channel_id=1, source_target_pairs={{0,12},{4,8},{8,4},{12,0},{1,13},{5,9},{9,5},{13,1},{2,14},{6,10},... | collective-permute-start | bytes 1179656 | tf_op jit(solution)/shard_map/ppermute | solution.py:384
  9.6 51.7 %collective-permute-start.2 = (bf16[768,256]{1,0:T(8,128)(2,1)}, bf16[768,256]{1,0:T(8,128)(2,1)}, u32[]{:S(2)}, u32[]{:S(2)}) collective-permute-start(bf16[768,256]{1,0:T(8,128)(2,1)} %get-tuple-element.273), channel_id=1, source_target_pairs={{0,4},{4,0},{8,12},{12,8},{1,5},{5,1},{9,13},{13,9},{2,6},{6,2},{1... | collective-permute-start | bytes 1179656 | tf_op jit(solution)/shard_map/ppermute | solution.py:384
  10.3 48.3 %collective-permute-start.4 = (bf16[768,256]{1,0:T(8,128)(2,1)S(1)}, bf16[768,256]{1,0:T(8,128)(2,1)}, u32[]{:S(2)}, u32[]{:S(2)}) collective-permute-start(bf16[768,256]{1,0:T(8,128)(2,1)S(1)} %get-tuple-element.358.refs_1_.refs_4_), channel_id=1, source_target_pairs={{0,8},{4,12},{8,0},{12,4},{1,9},{5,13},{9,1},{13,5},{2,10},{6,14},... | collective-permute-start | bytes 1179656 | tf_op jit(solution)/shard_map/ppermute | solution.py:384
  11.5 87.9 %collective-permute-start.14 = (bf16[768,128]{1,0:T(8,128)(2,1)}, bf16[768,128]{1,0:T(8,128)(2,1)}, u32[]{:S(2)}, u32[]{:S(2)}) collective-permute-start(bf16[768,128]{1,0:T(8,128)(2,1)} %get-tuple-element.448.refs_1_.refs_4_), channel_id=1, source_target_pairs={{0,8},{4,12},{8,0},{12,4},{1,9},{5,13},{9,1},{13,5},{2,10},{6,14},... | collective-permute-start | bytes 589832 | tf_op jit(solution)/shard_map/ppermute | solution.py:384
  21.2 0.8 copy-start.3
  53.7 11.3 %copy-start.5 = (f32[3,512]{1,0:T(4,128)S(1)}, f32[3,512]{1,0:T(4,128)}, u32[]{:S(2)}) copy-start(f32[3,512]{1,0:T(4,128)} %refs_8_.7) | copy-start | bytes 18436
  53.7 11.3 %copy-start.9 = (s32[6]{0:T(128)S(1)}, s32[6]{0:T(128)}, u32[]{:S(2)}) copy-start(s32[6]{0:T(128)} %copy-done.8) | copy-start | bytes 76
  53.7 11.3 %copy-start.10 = (f32[2,128]{1,0:T(2,128)S(1)}, f32[2,128]{1,0:T(2,128)}, u32[]{:S(2)}) copy-start(f32[2,128]{1,0:T(2,128)} %refs_9_.7) | copy-start | bytes 3076
  53.7 35.0 %copy-start.4 = (bf16[768,256]{1,0:T(8,128)(2,1)S(1)}, bf16[768,256]{1,0:T(8,128)(2,1)}, u32[]{:S(2)}) copy-start(bf16[768,256]{1,0:T(8,128)(2,1)} %copy-done.3) | copy-start | bytes 1179652
  56.6 30.0 %copy-start = (bf16[192,3072]{1,0:T(8,128)(2,1)S(1)}, bf16[192,3072]{1,0:T(8,128)(2,1)}, u32[]{:S(2)}) copy-start(bf16[192,3072]{1,0:T(8,128)(2,1)} %normalize.3.refs_0_) | copy-start | bytes 3538948
  56.6 26.5 %collective-permute-start.1 = (bf16[192,3072]{1,0:T(8,128)(2,1)}, bf16[192,3072]{1,0:T(8,128)(2,1)S(1)}, u32[]{:S(2)}, u32[]{:S(2)}) collective-permute-start(bf16[192,3072]{1,0:T(8,128)(2,1)} %normalize.3.refs_0_), channel_id=1, source_target_pairs={{0,2},{2,0},{1,3},{3,1},{4,6},{6,4},{5,7},{7,5},{8,10},{10,8},{9,1... | collective-permute-start | bytes 3538952 | tf_op jit(solution)/shard_map/ppermute | solution.py:384
  61.3 25.3 %collective-permute-start.5 = (bf16[768,256]{1,0:T(8,128)(2,1)}, bf16[768,256]{1,0:T(8,128)(2,1)S(1)}, u32[]{:S(2)}, u32[]{:S(2)}) collective-permute-start(bf16[768,256]{1,0:T(8,128)(2,1)} %collective-permute-done.4.refs_3_.refs_6_), channel_id=1, source_target_pairs={{0,16},{16,0},{1,17},{17,1},{2,18},{18,2},{3,19},{19,3},{4,20},{20... | collective-permute-start | bytes 1179656 | tf_op jit(solution)/shard_map/ppermute | solution.py:384
  63.0 23.6 %collective-permute-start.6 = (bf16[768,256]{1,0:T(8,128)(2,1)S(1)}, bf16[768,256]{1,0:T(8,128)(2,1)S(1)}, u32[]{:S(2)}, u32[]{:S(2)}) collective-permute-start(bf16[768,256]{1,0:T(8,128)(2,1)S(1)} %collective-permute-done.3.refs_4_.refs_7_), channel_id=1, source_target_pairs={{0,16},{16,0},{1,17},{17,1},{2,18},{18,2},{3,19},{19,3},{4,20},{20... | collective-permute-start | bytes 1179656 | tf_op jit(solution)/shard_map/ppermute | solution.py:384
  63.3 25.3 %collective-permute-start.7 = (bf16[768,256]{1,0:T(8,128)(2,1)}, bf16[768,256]{1,0:T(8,128)(2,1)S(1)}, u32[]{:S(2)}, u32[]{:S(2)}) collective-permute-start(bf16[768,256]{1,0:T(8,128)(2,1)} %collective-permute-done.2.refs_2_.refs_5_), channel_id=1, source_target_pairs={{0,16},{16,0},{1,17},{17,1},{2,18},{18,2},{3,19},{19,3},{4,20},{20... | collective-permute-start | bytes 1179656 | tf_op jit(solution)/shard_map/ppermute | solution.py:384
  65.0 2.3 %copy-start.1 = (bf16[768,3072]{1,0:T(8,128)(2,1)S(1)}, bf16[768,3072]{1,0:T(8,128)(2,1)}, u32[]{:S(2)}) copy-start(bf16[768,3072]{1,0:T(8,128)(2,1)} %normalize.2.refs_0_) | copy-start | bytes 14155780
  83.1 18.0 %collective-permute-start.13 = (bf16[768,128]{1,0:T(8,128)(2,1)S(1)}, bf16[768,128]{1,0:T(8,128)(2,1)S(1)}, u32[]{:S(2)}, u32[]{:S(2)}) collective-permute-start(bf16[768,128]{1,0:T(8,128)(2,1)S(1)} %get-tuple-element.275), channel_id=1, source_target_pairs={{0,12},{4,8},{8,4},{12,0},{1,13},{5,9},{9,5},{13,1},{2,14},{6,10},... | collective-permute-start | bytes 589832 | tf_op jit(solution)/shard_map/ppermute | solution.py:384
  86.6 14.5 %collective-permute-start.12 = (bf16[768,128]{1,0:T(8,128)(2,1)S(1)}, bf16[768,128]{1,0:T(8,128)(2,1)S(1)}, u32[]{:S(2)}, u32[]{:S(2)}) collective-permute-start(bf16[768,128]{1,0:T(8,128)(2,1)S(1)} %get-tuple-element.275), channel_id=1, source_target_pairs={{0,4},{4,0},{8,12},{12,8},{1,5},{5,1},{9,13},{13,9},{2,6},{6,2},{1... | collective-permute-start | bytes 589832 | tf_op jit(solution)/shard_map/ppermute | solution.py:384
  86.6 4.7 %collective-permute-start.8 = (bf16[192,3072]{1,0:T(8,128)(2,1)S(1)}, bf16[192,3072]{1,0:T(8,128)(2,1)S(1)}, u32[]{:S(2)}, u32[]{:S(2)}) collective-permute-start(bf16[192,3072]{1,0:T(8,128)(2,1)S(1)} %copy-done), channel_id=1, source_target_pairs={{0,1},{1,0},{2,3},{3,2},{4,5},{5,4},{6,7},{7,6},{8,9},{9,8},{10,11... | collective-permute-start | bytes 3538952 | tf_op jit(solution)/shard_map/ppermute | solution.py:384
  88.7 2.8 %collective-permute-start.9 = (bf16[192,3072]{1,0:T(8,128)(2,1)S(1)}, bf16[192,3072]{1,0:T(8,128)(2,1)S(1)}, u32[]{:S(2)}, u32[]{:S(2)}) collective-permute-start(bf16[192,3072]{1,0:T(8,128)(2,1)S(1)} %collective-permute-done.1.refs_2_), channel_id=1, source_target_pairs={{0,1},{1,0},{2,3},{3,2},{4,5},{5,4},{6,7},{7,6},{8,9},{9,8},{10,11... | collective-permute-start | bytes 3538952 | tf_op jit(solution)/shard_map/ppermute | solution.py:384
  94.2 20.5 %slice-start = ((s8[4718592]{0:T(1024)(128)(4,1)}), s8[4194304]{0:T(1024)(128)(4,1)S(1)}, s32[]{:S(2)}) async-start(s8[4718592]{0:T(1024)(128)(4,1)} %bitcast.7), calls=%async_computation | async-start | bytes 8388608
  94.3 20.5 %slice-start.1 = ((s8[4718592]{0:T(1024)(128)(4,1)}), s8[524288]{0:T(1024)(128)(4,1)S(1)}, s32[]{:S(2)}) async-start(s8[4718592]{0:T(1024)(128)(4,1)} %bitcast.7), calls=%async_computation.1 | async-start | bytes 1048576
  94.3 35.8 %collective-permute-start.11 = (bf16[768,256]{1,0:T(8,128)(2,1)S(1)}, bf16[768,256]{1,0:T(8,128)(2,1)S(1)}, u32[]{:S(2)}, u32[]{:S(2)}) collective-permute-start(bf16[768,256]{1,0:T(8,128)(2,1)S(1)} %broadcast_select_fusion), channel_id=1, source_target_pairs={{0,8},{4,12},{8,0},{12,4},{1,9},{5,13},{9,1},{13,5},{2,10},{6,14},... | collective-permute-start | bytes 1179656 | tf_op jit(solution)/shard_map/ppermute | solution.py:384
  97.9 1.5 copy-start.11
  98.0 38.6 %collective-permute-start.10 = (bf16[768,256]{1,0:T(8,128)(2,1)S(1)}, bf16[768,256]{1,0:T(8,128)(2,1)S(1)}, u32[]{:S(2)}, u32[]{:S(2)}) collective-permute-start(bf16[768,256]{1,0:T(8,128)(2,1)S(1)} %broadcast_select_fusion.1), channel_id=1, source_target_pairs={{0,8},{4,12},{8,0},{12,4},{1,9},{5,13},{9,1},{13,5},{2,10},{6,14},... | collective-permute-start | bytes 1179656 | tf_op jit(solution)/shard_map/ppermute | solution.py:384
  99.5 13.7 %collective-permute-start.15 = (f32[2,128]{1,0:T(2,128)S(1)}, f32[2,128]{1,0:T(2,128)S(1)}, u32[]{:S(2)}, u32[]{:S(2)}) collective-permute-start(f32[2,128]{1,0:T(2,128)S(1)} %copy-done.11), channel_id=1, source_target_pairs={{0,4},{4,0},{8,12},{12,8},{1,5},{5,1},{9,13},{13,9},{2,6},{6,2},{1... | collective-permute-start | bytes 3080 | tf_op jit(solution)/shard_map/ppermute | solution.py:384
  101.1 24.3 %collective-permute-start.16 = (bf16[768,128]{1,0:T(8,128)(2,1)}, bf16[768,128]{1,0:T(8,128)(2,1)S(1)}, u32[]{:S(2)}, u32[]{:S(2)}) collective-permute-start(bf16[768,128]{1,0:T(8,128)(2,1)} %collective-permute-done.14.refs_3_.refs_6_), channel_id=1, source_target_pairs={{0,16},{16,0},{1,17},{17,1},{2,18},{18,2},{3,19},{19,3},{4,20},{20... | collective-permute-start | bytes 589832 | tf_op jit(solution)/shard_map/ppermute | solution.py:384
  102.6 22.8 %collective-permute-start.17 = (bf16[768,128]{1,0:T(8,128)(2,1)S(1)}, bf16[768,128]{1,0:T(8,128)(2,1)S(1)}, u32[]{:S(2)}, u32[]{:S(2)}) collective-permute-start(bf16[768,128]{1,0:T(8,128)(2,1)S(1)} %collective-permute-done.13.refs_4_.refs_7_), channel_id=1, source_target_pairs={{0,16},{16,0},{1,17},{17,1},{2,18},{18,2},{3,19},{19,3},{4,20},{20... | collective-permute-start | bytes 589832 | tf_op jit(solution)/shard_map/ppermute | solution.py:384
  113.2 12.2 %collective-permute-start.18 = (bf16[768,128]{1,0:T(8,128)(2,1)S(1)}, bf16[768,128]{1,0:T(8,128)(2,1)S(1)}, u32[]{:S(2)}, u32[]{:S(2)}) collective-permute-start(bf16[768,128]{1,0:T(8,128)(2,1)S(1)} %collective-permute-done.12.refs_2_.refs_5_), channel_id=1, source_target_pairs={{0,16},{16,0},{1,17},{17,1},{2,18},{18,2},{3,19},{19,3},{4,20},{20... | collective-permute-start | bytes 589832 | tf_op jit(solution)/shard_map/ppermute | solution.py:384
  131.7 4.9 %copy-start.6 = (bf16[768,128]{1,0:T(8,128)(2,1)}, bf16[768,128]{1,0:T(8,128)(2,1)S(1)}, u32[]{:S(2)}) copy-start(bf16[768,128]{1,0:T(8,128)(2,1)S(1)} %get-tuple-element.534.refs_0_) | copy-start | bytes 589828
  136.6 7.8 %collective-permute-start.20 = (bf16[768,128]{1,0:T(8,128)(2,1)S(1)}, bf16[768,128]{1,0:T(8,128)(2,1)S(1)}, u32[]{:S(2)}, u32[]{:S(2)}) collective-permute-start(bf16[768,128]{1,0:T(8,128)(2,1)S(1)} %get-tuple-element.536), channel_id=1, source_target_pairs={{0,4},{4,0},{8,12},{12,8},{1,5},{5,1},{9,13},{13,9},{2,6},{6,2},{1... | collective-permute-start | bytes 589832 | tf_op jit(solution)/shard_map/ppermute | solution.py:384
  140.6 0.7 copy-start.7
  141.3 23.4 %collective-permute-start.19 = (bf16[768,128]{1,0:T(8,128)(2,1)S(1)}, bf16[768,128]{1,0:T(8,128)(2,1)S(1)}, u32[]{:S(2)}, u32[]{:S(2)}) collective-permute-start(bf16[768,128]{1,0:T(8,128)(2,1)S(1)} %get-tuple-element.533), channel_id=1, source_target_pairs={{0,4},{4,0},{8,12},{12,8},{1,5},{5,1},{9,13},{13,9},{2,6},{6,2},{1... | collective-permute-start | bytes 589832 | tf_op jit(solution)/shard_map/ppermute | solution.py:384
  144.4 0.7 copy-start.12
  164.7 0.7 copy-start.13

commit v4 on v3

--- a/solution.py
+++ b/solution.py
@@ -181,8 +181,8 @@
 def project(at, head_index, first, own_x, quarters, weights, bias, gain, norms, cost=COST):
     rows, cols = weights[0].shape
     head_dim = gain.shape[1]
-    sources = [own_x] if quarters is None else list(quarters)
-    tokens = own_x.shape[0] if quarters is None else 4 * quarters[0].shape[0]
+    sources = [own_x] if quarters is None else [part for _, _, part in quarters]
+    tokens = own_x.shape[0] if quarters is None else sum(part.shape[0] for part in sources)
     width = sources[0].shape[1]
     step = 256
 
@@ -215,8 +215,8 @@
         if quarters is None:
             piece(x_refs[0], 0)
         else:
-            for i, ref in enumerate(x_refs):
-                piece(ref, pl.multiple_of((q ^ i) * ref.shape[0], 64))
+            for (i, start, _), ref in zip(quarters, x_refs):
+                piece(ref, pl.multiple_of((q ^ i) * (tokens // 4) + start, 64))
 
     smem = pl.BlockSpec(memory_space=pltpu.SMEM)
     if quarters is None:
@@ -227,7 +227,7 @@
     else:
         grid = ()
         fixed = lambda shape: pl.BlockSpec()
-        x_specs = [pl.BlockSpec()] * 4
+        x_specs = [pl.BlockSpec()] * len(sources)
         out_spec = pl.BlockSpec()
     return pl.pallas_call(
         kernel,
@@ -339,32 +339,23 @@
     )(place, *limits, *queries, halo, done, mixed, total)
 
 
-def assemble(at, parts, carried=None, heads=4):
+def assemble(at, parts):
     indices, arrays = zip(*parts)
     tokens, head_dim = arrays[0].shape
-    carried = () if carried is None else (carried,)
 
     def kernel(at_ref, *refs):
-        out_ref, sems = refs[-2:]
-        copies = []
-        for i, (index, ref) in enumerate(zip(indices, refs)):
+        for index, ref in zip(indices, refs):
             cols = pl.ds(pl.multiple_of(at_ref[index] * head_dim, 128), head_dim)
-            copies.append(pltpu.make_async_copy(ref, out_ref.at[:, cols], sems.at[i]))
-            copies[-1].start()
-        for copy in copies:
-            copy.wait()
-
-    anywhere = pl.BlockSpec(memory_space=pl.ANY)
+            refs[-1][:, cols] = ref[...]
+
     return pl.pallas_call(
         kernel,
-        in_specs=[pl.BlockSpec(memory_space=pltpu.SMEM)] + [anywhere] * (len(arrays) + len(carried)),
-        out_specs=anywhere,
-        out_shape=jax.ShapeDtypeStruct((tokens, head_dim * heads), jnp.bfloat16),
-        scratch_shapes=[pltpu.SemaphoreType.DMA((len(arrays),))],
-        input_output_aliases={1 + len(arrays): 0} if carried else {},
+        in_specs=[pl.BlockSpec(memory_space=pltpu.SMEM)] + [pl.BlockSpec()] * len(arrays),
+        out_specs=pl.BlockSpec(),
+        out_shape=jax.ShapeDtypeStruct((tokens, head_dim * len(arrays)), jnp.bfloat16),
         cost_estimate=COST,
         name="assemble",
-    )(at, *arrays, *carried)
+    )(at, *arrays)
 
 
 def per_device(frames, modulation, w_qkv, b_qkv, qk_gain, block_lists):
@@ -394,37 +385,41 @@
     w = jnp.transpose(w_qkv, (1, 0, 2))
     line = Line()
 
-    raw = lax.dynamic_slice(frames, (at[1] * quarter, 0), (quarter, frames.shape[1]))
-    raw_other = to("seq", raw, 1)
-    w, raw = lax.optimization_barrier((w, raw))
+    cutting = (0, 2 * quarter // 3, quarter)
+    raws = [
+        lax.dynamic_slice(frames, (at[1] * quarter + lo, 0), (hi - lo, frames.shape[1]))
+        for lo, hi in zip(cutting, cutting[1:])
+    ]
+    raws_other = [to("seq", raw, 1) for raw in raws]
+    w, *_ = lax.optimization_barrier((w, *raws))
     cuts = cut_heads(at, w, [(MINE, KV), (CROSS, KV), (MINE, Q), (CROSS, Q)], LONG)
     cuts = line.reached(*cuts)
     own_w = {(MINE, KV): cuts[0], (MINE, Q): cuts[2]}
     got = {}
     for part, same, cross in ((KV, *cuts[:2]), (Q, *cuts[2:])):
         got[part] = [to("seq", same[0], 2), to("seq", cross[0], 3), to("seq", cross[0], 1)]
+    own_limit = line.reached(see(at, block_lists, tile_dev))
+    far_limit = to("seq", own_limit[0][0], 1)
     frames, modulation = line.after(frames, modulation)
     own_x = line.reached(normalize(frames, modulation, 128, MIDDLE))
     line.drop(cuts[1], cuts[3])
     (w,) = line.after(w)
     for key, box in zip(((TWIN, KV), (TWIN, Q)), line.reached(*cut_heads(at, w, [(TWIN, KV), (TWIN, Q)]))):
         own_w[key] = box
-    own_limit = line.reached(see(at, block_lists, tile_dev))
-    far_limit = to("seq", own_limit[0][0], 1)
-
-    (raw_other,) = line.after(raw_other)
-    near_q = line.reached(normalize(raw_other, modulation, 96))
-    far_q = to("fsdp", near_q[0][0], 1)
-    near_c = to("head", near_q[0][0], 1)
 
     def arrive(value):
         box = line.reached(value)[0]
         (box[0],) = line.after(box[0])
         return box
 
-    def swaps(part):
-        boxes = [arrive(value) for value in got[part]]
-        return boxes, [to("groups", box[0], 1) for box in boxes]
+    def take(i):
+        (raw,) = line.after(raws_other[i])
+        near = line.reached(normalize(raw, modulation, 64))[0]
+        return near, to("head", near[0], 1), to("fsdp", near[0], 1)
+
+    def swap(part, which, kept, back):
+        kept[which] = arrive(got[part][which])
+        back[which] = to("groups", kept[which][0], 1)
 
     def run(head, part, boxes, own, cost=COST):
         (own_part,) = line.after(own_w[head, part][0])
@@ -433,7 +428,7 @@
         return line.reached(
             project(
                 at, head, part[0], own_x[0][0] if own else None,
-                None if own else [b[0] for b in quarters],
+                None if own else [(i, start, box[0]) for i, start, box in quarters],
                 [own_part, one, two, three], b_qkv, qk_gain, NORMS[part], cost,
             )
         )
@@ -441,24 +436,33 @@
     def send_edge(rows):
         return to("seq", jnp.where(is_mid, rows[0][0], rows[1][0]), 2)
 
-    kv_boxes, kv_back = swaps(KV)
+    kv_boxes, kv_back, q_boxes, q_back = ([None] * 3 for _ in range(4))
+    near0, near_c0, far0 = take(0)
+    swap(KV, 0, kv_boxes, kv_back)
+    near1, near_c1, far1 = take(1)
+    swap(KV, 1, kv_boxes, kv_back)
+    swap(KV, 2, kv_boxes, kv_back)
+    limits = own_limit + [arrive(far_limit)]
+    far0 = arrive(far0)
+    far_c0 = to("head", far0[0], 1)
+    far1 = arrive(far1)
+    far_c1 = to("head", far1[0], 1)
+    for which in range(3):
+        swap(Q, which, q_boxes, q_back)
     rows_mine = run(MINE, KV, kv_boxes, True, LONG)
-    far_box = arrive(far_q)
-    far_c = to("head", far_box[0], 1)
     kv_twin = line.reached(*kv_back)
     rows_twin = run(TWIN, KV, kv_twin, True, LONG)
-    quarters = near_q + line.reached(near_c) + [far_box] + line.reached(far_c)
+    near_c0, far_c0, near_c1, far_c1 = line.reached(near_c0, far_c0, near_c1, far_c1)
+    quarters = [(0, 0, near0), (1, 0, near_c0), (2, 0, far0), (3, 0, far_c0)]
+    quarters += [(i, cutting[1], box) for i, box in enumerate((near1, near_c1, far1, far_c1))]
     rows_mine += run(MINE, KV, kv_boxes, False)
     halo_mine = send_edge(rows_mine)
     rows_twin += run(TWIN, KV, kv_twin, False)
     halo_twin = send_edge(rows_twin)
     line.drop(*kv_boxes, *kv_twin)
-    q_boxes, q_back = swaps(Q)
     q_mine = run(MINE, Q, q_boxes, True)
     q_mine += run(MINE, Q, q_boxes, False)
     line.drop(*q_boxes)
-
-    limits = own_limit + line.reached(far_limit)
 
     def pair(q, rows):
         parts = attend_pair(at, [b[0] for b in limits], [b[0] for b in q], [b[0] for b in rows])
@@ -474,7 +478,7 @@
     q_twin_w = line.reached(*q_back)
     q_twin = run(TWIN, Q, q_twin_w, True)
     q_twin += run(TWIN, Q, q_twin_w, False)
-    line.drop(*q_twin_w, *own_x, *quarters, *rows_mine)
+    line.drop(*q_twin_w, *own_x, *(box for *_, box in quarters), *rows_mine)
     (halo_mine,) = line.after(halo_mine)
     keep_mine, back_mine = finish(q_mine, halo_mine, parts_mine)
     line.drop(*q_mine, *parts_mine)
@@ -482,8 +486,8 @@
     parts_twin = pair(q_twin, rows_twin)
     (halo_twin,) = line.after(halo_twin)
     keep_twin, back_twin = finish(q_twin, halo_twin, parts_twin)
-    parts = [(MINE, keep_mine[0]), (TWIN, keep_twin[0]), (CROSS, back_mine)]
-    return assemble(at, [(CROSS_TWIN, back_twin)], assemble(at, parts))
+    parts = [(MINE, keep_mine[0]), (TWIN, keep_twin[0]), (CROSS, back_mine), (CROSS_TWIN, back_twin)]
+    return assemble(at, parts)
 
 
 def solution(mesh):

time: 174 us -> 148 us (0.85)
  Pallas kernels: 75.1 us -> 53.8 us
  waiting for transfers between devices: 60.9 us -> 51.6 us
  local copies, waits for them, and re-layouts: 7.76 us -> 10.8 us
    pallas_call x2 -> x1, Pallas kernels: 27.4 us -> 2.24 us  [assemble(): pl.pallas_call(kernel, in_specs=[pl.BlockSpec(memory_space=pltpu.SMEM)] +...]
    ppermute x21 -> x25, waiting for transfers between devices: 60.9 us -> 51.6 us  [to(): lax.ppermute(value, axis, [(i, i ^ bit) for i in range(lax.axis_size(axis...]
    pallas_call x8, Pallas kernels: 20.7 us -> 23.6 us  [project(): pl.pallas_call(kernel, grid=grid, in_specs=[smem, *x_specs, *(fixed(w.sha...]
    pallas_call x2 -> x3, Pallas kernels: 10.2 us -> 12.1 us  [normalize(): pl.pallas_call(norm_kernel, grid=(tokens // rows,), in_specs=[pl.BlockSpe...]
    unnamed x32 -> x54, local copies, waits for them, and re-layouts: 5.17 us -> 6.86 us
    ppermute x21 -> x25, starting transfers between devices: 29 us -> 30.6 us  [to(): lax.ppermute(value, axis, [(i, i ^ bit) for i in range(lax.axis_size(axis...]
    dynamic_slice x1 -> x2, local copies, waits for them, and re-layouts: 2.51 us -> 3.83 us  [per_device(): lax.dynamic_slice(frames, (at[1] * quarter + lo, 0), (hi - lo, frames.sha...]
  transfers between devices with their start and end apart: 21 -> 25, of which waited for: 7 -> 9; matrix products, arithmetic and copies ran while one was open for 0% -> 1% of each run, Pallas kernels for 39% -> 31%
where the time goes in v4:
time: 148 us; the launch traced here: 147 us
  Pallas kernels  53.8 us (36%)
  waiting for transfers between devices  51.6 us (35%)
  starting transfers between devices  30.6 us (21%)
  local copies, waits for them, and re-layouts  10.8 us (7%)
    ppermute x25, waiting for transfers between devices, to(): lax.ppermute(value, axis, [(i, i ^ bit) for i in range(lax.axis_size(axis...  51.6 us
    ppermute x25, starting transfers between devices, to(): lax.ppermute(value, axis, [(i, i ^ bit) for i in range(lax.axis_size(axis...  30.6 us
    pallas_call x8, Pallas kernels, project(): pl.pallas_call(kernel, grid=grid, in_specs=[smem, *x_specs, *(fixed(w.sha...  23.6 us
    pallas_call x3, Pallas kernels, normalize(): pl.pallas_call(norm_kernel, grid=(tokens // rows,), in_specs=[pl.BlockSpe...  12.1 us
    pallas_call x2, Pallas kernels, attend_pair(): pl.pallas_call(kernel, in_specs=[smem, smem, smem] + [vmem] * 4, out_spec...  9.93 us
    unnamed x54, local copies, waits for them, and re-layouts  6.86 us
    dynamic_slice x2, local copies, waits for them, and re-layouts, per_device(): lax.dynamic_slice(frames, (at[1] * quarter + lo, 0), (hi - lo, frames.sha...  3.83 us
    pallas_call x2, Pallas kernels, attend_halo(): pl.pallas_call(kernel, in_specs=[smem, smem, smem] + [vmem] * 6, out_spec...  3.26 us
  transfers between devices with their start and end apart: 25, of which 9 were waited for; matrix products, arithmetic and copies ran while one was open for 1% of the time, Pallas kernels for 31%

profile of v4, /device:TPU:0, one launch (start us, length us, event | category | flops | bytes accessed | tf_op | source)
XLA Modules:
  0.0 147.3 jit_solution(10506690085021309816)
XLA Ops:
  0.0 2.1 %constant_dynamic-slice_fusion.1 = bf16[128,3072]{1,0:T(8,128)(2,1)} fusion(bf16[768,3072]{1,0:T(8,128)(2,1)} %x_ref, s32[]{:T(128)S(6)} %select_n.27), kind=kLoop, calls=%fused_computation.3 | loop fusion | bytes 1572868 | tf_op jit(solution)/shard_map/dynamic_slice | solution.py:390
  2.1 3.0 %collective-permute-start.5 = (bf16[128,3072]{1,0:T(8,128)(2,1)}, bf16[128,3072]{1,0:T(8,128)(2,1)}, u32[]{:S(2)}, u32[]{:S(2)}) collective-permute-start(bf16[128,3072]{1,0:T(8,128)(2,1)} %constant_dynamic-slice_fusion.1), channel_id=1, source_target_pairs={{0,4},{4,0},{8,12},{12,8},{1,5},{5,1},{9,13},{13,9},{2,6},{6,2},{1... | collective-permute-start | bytes 2359304 | tf_op jit(solution)/shard_map/ppermute | solution.py:375
  5.1 1.8 %constant_dynamic-slice_fusion = bf16[64,3072]{1,0:T(8,128)(2,1)} fusion(bf16[768,3072]{1,0:T(8,128)(2,1)} %x_ref, s32[]{:T(128)S(6)} %select_n.28), kind=kLoop, calls=%fused_computation.2 | loop fusion | bytes 786436 | tf_op jit(solution)/shard_map/dynamic_slice | solution.py:390
  6.9 1.7 %copy-done.3 = bf16[768,3,512]{2,0,1:T(8,128)(2,1)S(1)} copy-done((bf16[768,3,512]{2,0,1:T(8,128)(2,1)S(1)}, bf16[768,3,512]{2,0,1:T(8,128)(2,1)}, u32[]{:S(2)}) %copy-start.3) | copy-done | bytes 2359320
  8.6 0.7 cut_heads.2
  10.1 2.6 %collective-permute-start.4 = (bf16[768,256]{1,0:T(8,128)(2,1)S(1)}, bf16[768,256]{1,0:T(8,128)(2,1)}, u32[]{:S(2)}, u32[]{:S(2)}) collective-permute-start(bf16[768,256]{1,0:T(8,128)(2,1)S(1)} %get-tuple-element.552.refs_1_.refs_8_), channel_id=1, source_target_pairs={{0,8},{4,12},{8,0},{12,4},{1,9},{5,13},{9,1},{13,5},{2,10},{6,14},... | collective-permute-start | bytes 1179656 | tf_op jit(solution)/shard_map/ppermute | solution.py:375
  12.6 1.3 see.1.limit0_ref
  14.0 7.5 %normalize.3.refs_0_ = bf16[768,3072]{1,0:T(8,128)(2,1)} custom-call(bf16[768,3072]{1,0:T(8,128)(2,1)} %x_ref, f32[2,3072]{1,0:T(2,128)} %mod_ref.2), custom_call_target="tpu_custom_call" | custom-call | flops 8589934592 | bytes 1024 | tf_op jit(solution)/shard_map/normalize/pallas_call | solution.py:122
  22.2 9.2 %collective-permute-done.5.x_ref = bf16[128,3072]{1,0:T(8,128)(2,1)} collective-permute-done((bf16[128,3072]{1,0:T(8,128)(2,1)}, bf16[128,3072]{1,0:T(8,128)(2,1)}, u32[]{:S(2)}, u32[]{:S(2)}) %collective-permute-start.5) | collective-permute-done | bytes 786464 | tf_op jit(solution)/shard_map/ppermute | solution.py:375
  31.4 2.5 %normalize.4.refs_0_ = bf16[128,3072]{1,0:T(8,128)(2,1)} custom-call(bf16[128,3072]{1,0:T(8,128)(2,1)} %collective-permute-done.5.x_ref, f32[2,3072]{1,0:T(2,128)} %mod_ref.2), custom_call_target="tpu_custom_call" | custom-call | flops 1048576 | bytes 1024 | tf_op jit(solution)/shard_map/normalize/pallas_call | solution.py:122
  33.8 1.7 %collective-permute-start.7 = (bf16[128,3072]{1,0:T(8,128)(2,1)}, bf16[128,3072]{1,0:T(8,128)(2,1)S(1)}, u32[]{:S(2)}, u32[]{:S(2)}) collective-permute-start(bf16[128,3072]{1,0:T(8,128)(2,1)} %normalize.4.refs_0_), channel_id=1, source_target_pairs={{0,2},{2,0},{1,3},{3,1},{4,6},{6,4},{5,7},{7,5},{8,10},{10,8},{9,1... | collective-permute-start | bytes 2359304 | tf_op jit(solution)/shard_map/ppermute | solution.py:375
  35.5 3.6 %collective-permute-start.10 = (bf16[768,256]{1,0:T(8,128)(2,1)}, bf16[768,256]{1,0:T(8,128)(2,1)S(1)}, u32[]{:S(2)}, u32[]{:S(2)}) collective-permute-start(bf16[768,256]{1,0:T(8,128)(2,1)} %copy-done.20), channel_id=1, source_target_pairs={{0,12},{4,8},{8,4},{12,0},{1,13},{5,9},{9,5},{13,1},{2,14},{6,10},... | collective-permute-start | bytes 1179656 | tf_op jit(solution)/shard_map/ppermute | solution.py:375
  39.1 1.1 collective-permute-start.9
  40.2 14.3 %collective-permute-done.3.x_ref = bf16[64,3072]{1,0:T(8,128)(2,1)S(1)} collective-permute-done((bf16[64,3072]{1,0:T(8,128)(2,1)}, bf16[64,3072]{1,0:T(8,128)(2,1)S(1)}, u32[]{:S(2)}, u32[]{:S(2)}) %collective-permute-start.3) | collective-permute-done | bytes 393248 | tf_op jit(solution)/shard_map/ppermute | solution.py:375
  54.5 0.8 copy-done.22
  55.3 2.1 %normalize.5.refs_4_ = bf16[64,3072]{1,0:T(8,128)(2,1)} custom-call(bf16[64,3072]{1,0:T(8,128)(2,1)} %copy-done.22, f32[2,3072]{1,0:T(2,128)} %mod_ref.2), custom_call_target="tpu_custom_call" | custom-call | flops 1048576 | bytes 1024 | tf_op jit(solution)/shard_map/normalize/pallas_call | solution.py:122
  57.6 4.8 %collective-permute-done.8.limit1_ref = f32[2,128]{1,0:T(2,128)S(1)} collective-permute-done((f32[2,128]{1,0:T(2,128)}, f32[2,128]{1,0:T(2,128)S(1)}, u32[]{:S(2)}, u32[]{:S(2)}) %collective-permute-start.8) | collective-permute-done | bytes 1056 | tf_op jit(solution)/shard_map/ppermute | solution.py:375
  62.4 3.1 %collective-permute-start.2 = (bf16[768,128]{1,0:T(8,128)(2,1)S(1)}, bf16[768,128]{1,0:T(8,128)(2,1)S(1)}, u32[]{:S(2)}, u32[]{:S(2)}) collective-permute-start(bf16[768,128]{1,0:T(8,128)(2,1)S(1)} %get-tuple-element.621.refs_1_.refs_8_), channel_id=1, source_target_pairs={{0,8},{4,12},{8,0},{12,4},{1,9},{5,13},{9,1},{13,5},{2,10},{6,14},... | collective-permute-start | bytes 589832 | tf_op jit(solution)/shard_map/ppermute | solution.py:375
  65.5 1.5 %collective-permute-start.1 = (bf16[768,128]{1,0:T(8,128)(2,1)}, bf16[768,128]{1,0:T(8,128)(2,1)S(1)}, u32[]{:S(2)}, u32[]{:S(2)}) collective-permute-start(bf16[768,128]{1,0:T(8,128)(2,1)} %copy-done.21), channel_id=1, source_target_pairs={{0,12},{4,8},{8,4},{12,0},{1,13},{5,9},{9,5},{13,1},{2,14},{6,10},... | collective-permute-start | bytes 589832 | tf_op jit(solution)/shard_map/ppermute | solution.py:375
  67.6 1.5 %collective-permute-start.13 = (bf16[768,256]{1,0:T(8,128)(2,1)}, bf16[768,256]{1,0:T(8,128)(2,1)S(1)}, u32[]{:S(2)}, u32[]{:S(2)}) collective-permute-start(bf16[768,256]{1,0:T(8,128)(2,1)} %collective-permute-done.9.refs_2_.refs_9_), channel_id=1, source_target_pairs={{0,16},{16,0},{1,17},{17,1},{2,18},{18,2},{3,19},{19,3},{4,20},{20... | collective-permute-start | bytes 1179656 | tf_op jit(solution)/shard_map/ppermute | solution.py:375
  69.6 8.1 %collective-permute-done.2.refs_3_.refs_10_ = bf16[768,128]{1,0:T(8,128)(2,1)S(1)} collective-permute-done((bf16[768,128]{1,0:T(8,128)(2,1)S(1)}, bf16[768,128]{1,0:T(8,128)(2,1)S(1)}, u32[]{:S(2)}, u32[]{:S(2)}) %collective-permute-start.2) | collective-permute-done | bytes 196640 | tf_op jit(solution)/shard_map/ppermute | solution.py:375
  77.7 1.5 %collective-permute-start.11 = (bf16[768,256]{1,0:T(8,128)(2,1)}, bf16[768,256]{1,0:T(8,128)(2,1)S(1)}, u32[]{:S(2)}, u32[]{:S(2)}) collective-permute-start(bf16[768,256]{1,0:T(8,128)(2,1)} %collective-permute-done.4.refs_3_.refs_10_), channel_id=1, source_target_pairs={{0,16},{16,0},{1,17},{17,1},{2,18},{18,2},{3,19},{19,3},{4,20},{20... | collective-permute-start | bytes 1179656 | tf_op jit(solution)/shard_map/ppermute | solution.py:375
  79.7 2.3 %copy-done.1 = bf16[768,3072]{1,0:T(8,128)(2,1)S(1)} copy-done((bf16[768,3072]{1,0:T(8,128)(2,1)S(1)}, bf16[768,3072]{1,0:T(8,128)(2,1)}, u32[]{:S(2)}) %copy-start.1) | copy-done | bytes 4718616
  82.1 3.2 %project.8.rows0_ref = bf16[768,256]{1,0:T(8,128)(2,1)S(1)} custom-call(s32[6]{0:T(128)S(1)} %copy-done.15, bf16[768,3072]{1,0:T(8,128)(2,1)S(1)} %copy-done.1, bf16[768,256]{1,0:T(8,128)(2,1)S(1)} %get-tuple-element.552.refs_1_.refs_8_, bf16[768,256]{1,0:T(8,128)(2,1)} %collective-permute-done.9.refs_2_.refs_9_, ...), custom_call_target="tpu_custom_call" | custom-call | flops 137438953472 | bytes 1024 | tf_op jit(solution)/shard_map/project/pallas_call | solution.py:232
  85.5 2.2 %collective-permute-done.12.refs_4_.refs_11_ = bf16[768,256]{1,0:T(8,128)(2,1)S(1)} collective-permute-done((bf16[768,256]{1,0:T(8,128)(2,1)S(1)}, bf16[768,256]{1,0:T(8,128)(2,1)S(1)}, u32[]{:S(2)}, u32[]{:S(2)}) %collective-permute-start.12) | collective-permute-done | bytes 393248 | tf_op jit(solution)/shard_map/ppermute | solution.py:375
  87.7 4.2 %collective-permute-done.11.refs_3_.refs_10_ = bf16[768,256]{1,0:T(8,128)(2,1)S(1)} collective-permute-done((bf16[768,256]{1,0:T(8,128)(2,1)}, bf16[768,256]{1,0:T(8,128)(2,1)S(1)}, u32[]{:S(2)}, u32[]{:S(2)}) %collective-permute-start.11) | collective-permute-done | bytes 393248 | tf_op jit(solution)/shard_map/ppermute | solution.py:375
  91.9 2.6 %project.9.rows0_ref = bf16[768,256]{1,0:T(8,128)(2,1)S(1)} custom-call(s32[6]{0:T(128)S(1)} %copy-done.15, bf16[768,3072]{1,0:T(8,128)(2,1)S(1)} %copy-done.1, bf16[768,256]{1,0:T(8,128)(2,1)S(1)} %get-tuple-element.586.refs_1_.refs_8_, bf16[768,256]{1,0:T(8,128)(2,1)S(1)} %collective-permute-done.13.refs_2_.refs_9_, ...), custom_call_target="tpu_custom_call" | custom-call | flops 137438953472 | bytes 1024 | tf_op jit(solution)/shard_map/project/pallas_call | solution.py:232
  94.6 3.7 %project.10.rows1_ref = bf16[768,256]{1,0:T(8,128)(2,1)S(1)} custom-call(s32[6]{0:T(128)S(1)} %copy-done.15, bf16[128,3072]{1,0:T(8,128)(2,1)S(1)} %copy-done, bf16[128,3072]{1,0:T(8,128)(2,1)} %collective-permute-done.14.refs_1_, bf16[128,3072]{1,0:T(8,128)(2,1)S(1)} %collective-permute-done.7.refs_2_, ...), custom_call_target="tpu_custom_call" | custom-call | flops 1048576 | bytes 1024 | tf_op jit(solution)/shard_map/project/pallas_call | solution.py:232
  98.4 2.7 %collective-permute-start.19 = (bf16[768,256]{1,0:T(8,128)(2,1)S(1)}, bf16[768,256]{1,0:T(8,128)(2,1)S(1)}, u32[]{:S(2)}, u32[]{:S(2)}) collective-permute-start(bf16[768,256]{1,0:T(8,128)(2,1)S(1)} %broadcast_select_fusion), channel_id=1, source_target_pairs={{0,8},{4,12},{8,0},{12,4},{1,9},{5,13},{9,1},{13,5},{2,10},{6,14},... | collective-permute-start | bytes 1179656 | tf_op jit(solution)/shard_map/ppermute | solution.py:375
  101.1 3.4 %project.11.rows1_ref = bf16[768,256]{1,0:T(8,128)(2,1)S(1)} custom-call(s32[6]{0:T(128)S(1)} %copy-done.15, bf16[128,3072]{1,0:T(8,128)(2,1)S(1)} %copy-done, bf16[128,3072]{1,0:T(8,128)(2,1)} %collective-permute-done.14.refs_1_, bf16[128,3072]{1,0:T(8,128)(2,1)S(1)} %collective-permute-done.7.refs_2_, ...), custom_call_target="tpu_custom_call" | custom-call | flops 1048576 | bytes 1024 | tf_op jit(solution)/shard_map/project/pallas_call | solution.py:232
  104.6 0.7 collective-permute-start.18
  105.3 1.5 %collective-permute-start.22 = (bf16[768,128]{1,0:T(8,128)(2,1)S(1)}, bf16[768,128]{1,0:T(8,128)(2,1)S(1)}, u32[]{:S(2)}, u32[]{:S(2)}) collective-permute-start(bf16[768,128]{1,0:T(8,128)(2,1)S(1)} %copy-done.10), channel_id=1, source_target_pairs={{0,16},{16,0},{1,17},{17,1},{2,18},{18,2},{3,19},{19,3},{4,20},{20... | collective-permute-start | bytes 589832 | tf_op jit(solution)/shard_map/ppermute | solution.py:375
  107.3 1.5 %collective-permute-start.20 = (bf16[768,128]{1,0:T(8,128)(2,1)S(1)}, bf16[768,128]{1,0:T(8,128)(2,1)S(1)}, u32[]{:S(2)}, u32[]{:S(2)}) collective-permute-start(bf16[768,128]{1,0:T(8,128)(2,1)S(1)} %copy-done.6), channel_id=1, source_target_pairs={{0,16},{16,0},{1,17},{17,1},{2,18},{18,2},{3,19},{19,3},{4,20},{20... | collective-permute-start | bytes 589832 | tf_op jit(solution)/shard_map/ppermute | solution.py:375
  108.9 2.5 %project.12.q0_ref = bf16[768,128]{1,0:T(8,128)(2,1)S(1)} custom-call(s32[6]{0:T(128)S(1)} %copy-done.15, bf16[768,3072]{1,0:T(8,128)(2,1)S(1)} %bitcast.8, bf16[768,128]{1,0:T(8,128)(2,1)S(1)} %get-tuple-element.621.refs_1_.refs_8_, bf16[768,128]{1,0:T(8,128)(2,1)S(1)} %copy-done.10, bf16[768,128]{1,0:T(8,128)(2,1)S(1)} %copy-done.6, ...), custom_call_target="tpu_custom_call" | custom-call | flops 1048576 | bytes 1024 | tf_op jit(solution)/shard_map/project/pallas_call | solution.py:232
  111.4 2.8 %project.13.q1_ref = bf16[768,128]{1,0:T(8,128)(2,1)S(1)} custom-call(s32[6]{0:T(128)S(1)} %copy-done.15, bf16[128,3072]{1,0:T(8,128)(2,1)S(1)} %copy-done, bf16[128,3072]{1,0:T(8,128)(2,1)} %collective-permute-done.14.refs_1_, bf16[128,3072]{1,0:T(8,128)(2,1)S(1)} %collective-permute-done.7.refs_2_, bf16[128,3072]{1,0:T(8,128)(2,1)S(1)} %collective-permute-done.15.refs_3_, ...), custom_call_target="tpu_custom_call" | custom-call | flops 1048576 | bytes 1024 | tf_op jit(solution)/shard_map/project/pallas_call | solution.py:232
  114.2 5.1 %attend_pair.2 = (bf16[768,128]{1,0:T(8,128)(2,1)S(1)}, f32[768,128]{1,0:T(8,128)S(1)}, f32[768,128]{1,0:T(8,128)S(1)}) custom-call(s32[6]{0:T(128)S(1)} %copy-done.15, f32[2,128]{1,0:T(2,128)S(1)} %copy-done.17, f32[2,128]{1,0:T(2,128)S(1)} %copy-done.19, bf16[768,128]{1,0:T(8,128)(2,1)S(1)} %project.12.q0_ref, bf16[768,128]{1,0:T(8,128)(2,1)S(1)} %project.13.q1_ref, ...), custom_call_target="tpu_custom_call" | custom-call | flops 1048576 | bytes 1024 | tf_op jit(solution)/shard_map/attend_pair/pallas_call | solution.py:294
  119.3 2.6 %project.14.q0_ref = bf16[768,128]{1,0:T(8,128)(2,1)S(1)} custom-call(s32[6]{0:T(128)S(1)} %copy-done.15, bf16[768,3072]{1,0:T(8,128)(2,1)S(1)} %bitcast.8, bf16[768,128]{1,0:T(8,128)(2,1)S(1)} %get-tuple-element.667.refs_1_.refs_8_, bf16[768,128]{1,0:T(8,128)(2,1)S(1)} %collective-permute-done.22.refs_2_.refs_9_, ...), custom_call_target="tpu_custom_call" | custom-call | flops 1048576 | bytes 1024 | tf_op jit(solution)/shard_map/project/pallas_call | solution.py:232
  121.9 2.8 %project.15.q1_ref = bf16[768,128]{1,0:T(8,128)(2,1)S(1)} custom-call(s32[6]{0:T(128)S(1)} %copy-done.15, bf16[128,3072]{1,0:T(8,128)(2,1)S(1)} %copy-done, bf16[128,3072]{1,0:T(8,128)(2,1)} %collective-permute-done.14.refs_1_, bf16[128,3072]{1,0:T(8,128)(2,1)S(1)} %collective-permute-done.7.refs_2_, bf16[128,3072]{1,0:T(8,128)(2,1)S(1)} %collective-permute-done.15.refs_3_, ...), custom_call_target="tpu_custom_call" | custom-call | flops 1048576 | bytes 1024 | tf_op jit(solution)/shard_map/project/pallas_call | solution.py:232
  124.6 1.6 %attend_halo.2 = (bf16[768,128]{1,0:T(8,128)(2,1)S(1)}, bf16[768,128]{1,0:T(8,128)(2,1)S(1)}) custom-call(s32[6]{0:T(128)S(1)} %copy-done.15, f32[2,128]{1,0:T(2,128)S(1)} %copy-done.17, f32[2,128]{1,0:T(2,128)S(1)} %copy-done.19, bf16[768,128]{1,0:T(8,128)(2,1)S(1)} %project.12.q0_ref, bf16[768,128]{1,0:T(8,128)(2,1)S(1)} %project.13.q1_ref, ...), custom_call_target="tpu_custom_call" | custom-call | flops 1048576 | bytes 1024 | tf_op jit(solution)/shard_map/attend_halo/pallas_call | solution.py:331
  126.3 4.9 %attend_pair.3 = (bf16[768,128]{1,0:T(8,128)(2,1)S(1)}, f32[768,128]{1,0:T(8,128)S(1)}, f32[768,128]{1,0:T(8,128)S(1)}) custom-call(s32[6]{0:T(128)S(1)} %copy-done.15, f32[2,128]{1,0:T(2,128)S(1)} %copy-done.17, f32[2,128]{1,0:T(2,128)S(1)} %copy-done.19, bf16[768,128]{1,0:T(8,128)(2,1)S(1)} %project.14.q0_ref, bf16[768,128]{1,0:T(8,128)(2,1)S(1)} %project.15.q1_ref, ...), custom_call_target="tpu_custom_call" | custom-call | flops 1048576 | bytes 1024 | tf_op jit(solution)/shard_map/attend_pair/pallas_call | solution.py:294
  131.2 0.8 collective-permute-done.18.halo_ref
  132.0 1.6 %attend_halo.3 = (bf16[768,128]{1,0:T(8,128)(2,1)S(1)}, bf16[768,128]{1,0:T(8,128)(2,1)S(1)}) custom-call(s32[6]{0:T(128)S(1)} %copy-done.15, f32[2,128]{1,0:T(2,128)S(1)} %copy-done.17, f32[2,128]{1,0:T(2,128)S(1)} %copy-done.19, bf16[768,128]{1,0:T(8,128)(2,1)S(1)} %project.14.q0_ref, bf16[768,128]{1,0:T(8,128)(2,1)S(1)} %project.15.q1_ref, ...), custom_call_target="tpu_custom_call" | custom-call | flops 1048576 | bytes 1024 | tf_op jit(solution)/shard_map/attend_halo/pallas_call | solution.py:331
  133.6 0.7 copy-done.13
  134.8 1.5 %collective-permute-start.23 = (bf16[768,128]{1,0:T(8,128)(2,1)S(1)}, bf16[768,128]{1,0:T(8,128)(2,1)S(1)}, u32[]{:S(2)}, u32[]{:S(2)}) collective-permute-start(bf16[768,128]{1,0:T(8,128)(2,1)S(1)} %get-tuple-element.721), channel_id=1, source_target_pairs={{0,4},{4,0},{8,12},{12,8},{1,5},{5,1},{9,13},{13,9},{2,6},{6,2},{1... | collective-permute-start | bytes 589832 | tf_op jit(solution)/shard_map/ppermute | solution.py:375
  136.3 5.8 %collective-permute-done.24.refs_3_ = bf16[768,128]{1,0:T(8,128)(2,1)S(1)} collective-permute-done((bf16[768,128]{1,0:T(8,128)(2,1)S(1)}, bf16[768,128]{1,0:T(8,128)(2,1)S(1)}, u32[]{:S(2)}, u32[]{:S(2)}) %collective-permute-start.24) | collective-permute-done | bytes 196640 | tf_op jit(solution)/shard_map/ppermute | solution.py:375
  142.1 2.2 %collective-permute-done.23.refs_2_ = bf16[768,128]{1,0:T(8,128)(2,1)S(1)} collective-permute-done((bf16[768,128]{1,0:T(8,128)(2,1)S(1)}, bf16[768,128]{1,0:T(8,128)(2,1)S(1)}, u32[]{:S(2)}, u32[]{:S(2)}) %collective-permute-start.23) | collective-permute-done | bytes 196640 | tf_op jit(solution)/shard_map/ppermute | solution.py:375
  144.3 0.7 copy-done.24
  145.0 2.2 %assemble.1 = bf16[768,512]{1,0:T(8,128)(2,1)} custom-call(s32[6]{0:T(128)} %copy-done.14, bf16[768,128]{1,0:T(8,128)(2,1)} %copy-done.12, bf16[768,128]{1,0:T(8,128)(2,1)} %copy-done.13, bf16[768,128]{1,0:T(8,128)(2,1)} %copy-done.24, bf16[768,128]{1,0:T(8,128)(2,1)} %copy-done.23), custom_call_target="tpu_custom_call" | custom-call | flops 1048576 | bytes 1024 | tf_op jit(solution)/shard_map/assemble/pallas_call | solution.py:351
  (81 shorter events, 4.6 us)
Async XLA Ops:
  2.1 29.3 %collective-permute-start.5 = (bf16[128,3072]{1,0:T(8,128)(2,1)}, bf16[128,3072]{1,0:T(8,128)(2,1)}, u32[]{:S(2)}, u32[]{:S(2)}) collective-permute-start(bf16[128,3072]{1,0:T(8,128)(2,1)} %constant_dynamic-slice_fusion.1), channel_id=1, source_target_pairs={{0,4},{4,0},{8,12},{12,8},{1,5},{5,1},{9,13},{13,9},{2,6},{6,2},{1... | collective-permute-start | bytes 2359304 | tf_op jit(solution)/shard_map/ppermute | solution.py:375
  6.9 1.7 %copy-start.3 = (bf16[768,3,512]{2,0,1:T(8,128)(2,1)S(1)}, bf16[768,3,512]{2,0,1:T(8,128)(2,1)}, u32[]{:S(2)}) copy-start(bf16[768,3,512]{2,0,1:T(8,128)(2,1)} %param.8) | copy-start | bytes 7077892
  8.6 0.8 copy-start.14
  10.1 3.9 %copy-start.20 = (bf16[768,256]{1,0:T(8,128)(2,1)}, bf16[768,256]{1,0:T(8,128)(2,1)S(1)}, u32[]{:S(2)}) copy-start(bf16[768,256]{1,0:T(8,128)(2,1)S(1)} %get-tuple-element.368) | copy-start | bytes 1179652
  10.1 30.2 %collective-permute-start.4 = (bf16[768,256]{1,0:T(8,128)(2,1)S(1)}, bf16[768,256]{1,0:T(8,128)(2,1)}, u32[]{:S(2)}, u32[]{:S(2)}) collective-permute-start(bf16[768,256]{1,0:T(8,128)(2,1)S(1)} %get-tuple-element.552.refs_1_.refs_8_), channel_id=1, source_target_pairs={{0,8},{4,12},{8,0},{12,4},{1,9},{5,13},{9,1},{13,5},{2,10},{6,14},... | collective-permute-start | bytes 1179656 | tf_op jit(solution)/shard_map/ppermute | solution.py:375
  13.9 7.5 %copy-start.4 = (bf16[768,3,512]{2,0,1:T(8,128)(2,1)S(1)}, bf16[768,3,512]{2,0,1:T(8,128)(2,1)}, u32[]{:S(2)}) copy-start(bf16[768,3,512]{2,0,1:T(8,128)(2,1)} %param.8) | copy-start | bytes 7077892
  14.0 7.5 %copy-start.15 = (s32[6]{0:T(128)S(1)}, s32[6]{0:T(128)}, u32[]{:S(2)}) copy-start(s32[6]{0:T(128)} %copy-done.14) | copy-start | bytes 76
  21.5 58.2 %copy-start.11 = (f32[3,512]{1,0:T(4,128)S(1)}, f32[3,512]{1,0:T(4,128)}, u32[]{:S(2)}) copy-start(f32[3,512]{1,0:T(4,128)} %refs_12_.7) | copy-start | bytes 18436
  21.5 58.2 %copy-start.16 = (f32[2,128]{1,0:T(2,128)S(1)}, f32[2,128]{1,0:T(2,128)}, u32[]{:S(2)}) copy-start(f32[2,128]{1,0:T(2,128)} %refs_13_.7) | copy-start | bytes 3076
  33.8 33.8 %collective-permute-start.7 = (bf16[128,3072]{1,0:T(8,128)(2,1)}, bf16[128,3072]{1,0:T(8,128)(2,1)S(1)}, u32[]{:S(2)}, u32[]{:S(2)}) collective-permute-start(bf16[128,3072]{1,0:T(8,128)(2,1)} %normalize.4.refs_0_), channel_id=1, source_target_pairs={{0,2},{2,0},{1,3},{3,1},{4,6},{6,4},{5,7},{7,5},{8,10},{10,8},{9,1... | collective-permute-start | bytes 2359304 | tf_op jit(solution)/shard_map/ppermute | solution.py:375
  35.5 19.1 %collective-permute-start.3 = (bf16[64,3072]{1,0:T(8,128)(2,1)}, bf16[64,3072]{1,0:T(8,128)(2,1)S(1)}, u32[]{:S(2)}, u32[]{:S(2)}) collective-permute-start(bf16[64,3072]{1,0:T(8,128)(2,1)} %constant_dynamic-slice_fusion), channel_id=1, source_target_pairs={{0,4},{4,0},{8,12},{12,8},{1,5},{5,1},{9,13},{13,9},{2,6},{6,2},{1... | collective-permute-start | bytes 1179656 | tf_op jit(solution)/shard_map/ppermute | solution.py:375
  35.5 30.0 %collective-permute-start.10 = (bf16[768,256]{1,0:T(8,128)(2,1)}, bf16[768,256]{1,0:T(8,128)(2,1)S(1)}, u32[]{:S(2)}, u32[]{:S(2)}) collective-permute-start(bf16[768,256]{1,0:T(8,128)(2,1)} %copy-done.20), channel_id=1, source_target_pairs={{0,12},{4,8},{8,4},{12,0},{1,13},{5,9},{9,5},{13,1},{2,14},{6,10},... | collective-permute-start | bytes 1179656 | tf_op jit(solution)/shard_map/ppermute | solution.py:375
  39.1 27.9 %collective-permute-start.9 = (bf16[768,256]{1,0:T(8,128)(2,1)}, bf16[768,256]{1,0:T(8,128)(2,1)}, u32[]{:S(2)}, u32[]{:S(2)}) collective-permute-start(bf16[768,256]{1,0:T(8,128)(2,1)} %copy-done.20), channel_id=1, source_target_pairs={{0,4},{4,0},{8,12},{12,8},{1,5},{5,1},{9,13},{13,9},{2,6},{6,2},{1... | collective-permute-start | bytes 1179656 | tf_op jit(solution)/shard_map/ppermute | solution.py:375
  57.4 11.7 %collective-permute-start.6 = (bf16[64,3072]{1,0:T(8,128)(2,1)}, bf16[64,3072]{1,0:T(8,128)(2,1)S(1)}, u32[]{:S(2)}, u32[]{:S(2)}) collective-permute-start(bf16[64,3072]{1,0:T(8,128)(2,1)} %normalize.5.refs_4_), channel_id=1, source_target_pairs={{0,2},{2,0},{1,3},{3,1},{4,6},{6,4},{5,7},{7,5},{8,10},{10,8},{9,1... | collective-permute-start | bytes 1179656 | tf_op jit(solution)/shard_map/ppermute | solution.py:375
  57.6 4.8 %collective-permute-start.8 = (f32[2,128]{1,0:T(2,128)}, f32[2,128]{1,0:T(2,128)S(1)}, u32[]{:S(2)}, u32[]{:S(2)}) collective-permute-start(f32[2,128]{1,0:T(2,128)} %see.1.limit0_ref), channel_id=1, source_target_pairs={{0,4},{4,0},{8,12},{12,8},{1,5},{5,1},{9,13},{13,9},{2,6},{6,2},{1... | collective-permute-start | bytes 3080 | tf_op jit(solution)/shard_map/ppermute | solution.py:375
  62.4 22.9 %copy-start.18 = (f32[2,128]{1,0:T(2,128)}, f32[2,128]{1,0:T(2,128)S(1)}, u32[]{:S(2)}) copy-start(f32[2,128]{1,0:T(2,128)S(1)} %collective-permute-done.8.limit1_ref) | copy-start | bytes 3076
  62.4 15.3 %collective-permute-start.2 = (bf16[768,128]{1,0:T(8,128)(2,1)S(1)}, bf16[768,128]{1,0:T(8,128)(2,1)S(1)}, u32[]{:S(2)}, u32[]{:S(2)}) collective-permute-start(bf16[768,128]{1,0:T(8,128)(2,1)S(1)} %get-tuple-element.621.refs_1_.refs_8_), channel_id=1, source_target_pairs={{0,8},{4,12},{8,0},{12,4},{1,9},{5,13},{9,1},{13,5},{2,10},{6,14},... | collective-permute-start | bytes 589832 | tf_op jit(solution)/shard_map/ppermute | solution.py:375
  65.5 13.7 %collective-permute-start.1 = (bf16[768,128]{1,0:T(8,128)(2,1)}, bf16[768,128]{1,0:T(8,128)(2,1)S(1)}, u32[]{:S(2)}, u32[]{:S(2)}) collective-permute-start(bf16[768,128]{1,0:T(8,128)(2,1)} %copy-done.21), channel_id=1, source_target_pairs={{0,12},{4,8},{8,4},{12,0},{1,13},{5,9},{9,5},{13,1},{2,14},{6,10},... | collective-permute-start | bytes 589832 | tf_op jit(solution)/shard_map/ppermute | solution.py:375
  67.0 12.2 %collective-permute-start = (bf16[768,128]{1,0:T(8,128)(2,1)}, bf16[768,128]{1,0:T(8,128)(2,1)S(1)}, u32[]{:S(2)}, u32[]{:S(2)}) collective-permute-start(bf16[768,128]{1,0:T(8,128)(2,1)} %copy-done.21), channel_id=1, source_target_pairs={{0,4},{4,0},{8,12},{12,8},{1,5},{5,1},{9,13},{13,9},{2,6},{6,2},{1... | collective-permute-start | bytes 589832 | tf_op jit(solution)/shard_map/ppermute | solution.py:375
  67.6 17.8 %collective-permute-start.13 = (bf16[768,256]{1,0:T(8,128)(2,1)}, bf16[768,256]{1,0:T(8,128)(2,1)S(1)}, u32[]{:S(2)}, u32[]{:S(2)}) collective-permute-start(bf16[768,256]{1,0:T(8,128)(2,1)} %collective-permute-done.9.refs_2_.refs_9_), channel_id=1, source_target_pairs={{0,16},{16,0},{1,17},{17,1},{2,18},{18,2},{3,19},{19,3},{4,20},{20... | collective-permute-start | bytes 1179656 | tf_op jit(solution)/shard_map/ppermute | solution.py:375
  69.1 18.6 %collective-permute-start.12 = (bf16[768,256]{1,0:T(8,128)(2,1)S(1)}, bf16[768,256]{1,0:T(8,128)(2,1)S(1)}, u32[]{:S(2)}, u32[]{:S(2)}) collective-permute-start(bf16[768,256]{1,0:T(8,128)(2,1)S(1)} %collective-permute-done.10.refs_4_.refs_11_), channel_id=1, source_target_pairs={{0,16},{16,0},{1,17},{17,1},{2,18},{18,2},{3,19},{19,3},{4,20},{20... | collective-permute-start | bytes 1179656 | tf_op jit(solution)/shard_map/ppermute | solution.py:375
  77.7 7.6 %copy-start.5 = (bf16[768,128]{1,0:T(8,128)(2,1)}, bf16[768,128]{1,0:T(8,128)(2,1)S(1)}, u32[]{:S(2)}) copy-start(bf16[768,128]{1,0:T(8,128)(2,1)S(1)} %collective-permute-done.2.refs_3_.refs_10_) | copy-start | bytes 589828
  77.7 14.2 %collective-permute-start.11 = (bf16[768,256]{1,0:T(8,128)(2,1)}, bf16[768,256]{1,0:T(8,128)(2,1)S(1)}, u32[]{:S(2)}, u32[]{:S(2)}) collective-permute-start(bf16[768,256]{1,0:T(8,128)(2,1)} %collective-permute-done.4.refs_3_.refs_10_), channel_id=1, source_target_pairs={{0,16},{16,0},{1,17},{17,1},{2,18},{18,2},{3,19},{19,3},{4,20},{20... | collective-permute-start | bytes 1179656 | tf_op jit(solution)/shard_map/ppermute | solution.py:375
  79.2 6.1 %copy-start.7 = (bf16[768,128]{1,0:T(8,128)(2,1)}, bf16[768,128]{1,0:T(8,128)(2,1)S(1)}, u32[]{:S(2)}) copy-start(bf16[768,128]{1,0:T(8,128)(2,1)S(1)} %collective-permute-done.1.refs_4_.refs_11_) | copy-start | bytes 589828
  79.2 15.3 %collective-permute-start.16 = (bf16[64,3072]{1,0:T(8,128)(2,1)}, bf16[64,3072]{1,0:T(8,128)(2,1)}, u32[]{:S(2)}, u32[]{:S(2)}) collective-permute-start(bf16[64,3072]{1,0:T(8,128)(2,1)} %normalize.5.refs_4_), channel_id=1, source_target_pairs={{0,1},{1,0},{2,3},{3,2},{4,5},{5,4},{6,7},{7,6},{8,9},{9,8},{10,11... | collective-permute-start | bytes 1179656 | tf_op jit(solution)/shard_map/ppermute | solution.py:375
  79.2 6.1 %copy-start.9 = (bf16[768,128]{1,0:T(8,128)(2,1)}, bf16[768,128]{1,0:T(8,128)(2,1)S(1)}, u32[]{:S(2)}) copy-start(bf16[768,128]{1,0:T(8,128)(2,1)S(1)} %collective-permute-done.refs_2_.refs_9_) | copy-start | bytes 589828
  79.2 15.3 %collective-permute-start.14 = (bf16[128,3072]{1,0:T(8,128)(2,1)}, bf16[128,3072]{1,0:T(8,128)(2,1)}, u32[]{:S(2)}, u32[]{:S(2)}) collective-permute-start(bf16[128,3072]{1,0:T(8,128)(2,1)} %normalize.4.refs_0_), channel_id=1, source_target_pairs={{0,1},{1,0},{2,3},{3,2},{4,5},{5,4},{6,7},{7,6},{8,9},{9,8},{10,11... | collective-permute-start | bytes 2359304 | tf_op jit(solution)/shard_map/ppermute | solution.py:375
  79.7 2.3 %copy-start.1 = (bf16[768,3072]{1,0:T(8,128)(2,1)S(1)}, bf16[768,3072]{1,0:T(8,128)(2,1)}, u32[]{:S(2)}) copy-start(bf16[768,3072]{1,0:T(8,128)(2,1)} %normalize.3.refs_0_) | copy-start | bytes 14155780
  85.3 9.3 %copy-start = (bf16[128,3072]{1,0:T(8,128)(2,1)S(1)}, bf16[128,3072]{1,0:T(8,128)(2,1)}, u32[]{:S(2)}) copy-start(bf16[128,3072]{1,0:T(8,128)(2,1)} %normalize.4.refs_0_) | copy-start | bytes 2359300
  85.4 9.3 %copy-start.2 = (bf16[64,3072]{1,0:T(8,128)(2,1)S(1)}, bf16[64,3072]{1,0:T(8,128)(2,1)}, u32[]{:S(2)}) copy-start(bf16[64,3072]{1,0:T(8,128)(2,1)} %normalize.5.refs_4_) | copy-start | bytes 1179652
  85.4 9.2 %collective-permute-start.15 = (bf16[128,3072]{1,0:T(8,128)(2,1)S(1)}, bf16[128,3072]{1,0:T(8,128)(2,1)S(1)}, u32[]{:S(2)}, u32[]{:S(2)}) collective-permute-start(bf16[128,3072]{1,0:T(8,128)(2,1)S(1)} %collective-permute-done.7.refs_2_), channel_id=1, source_target_pairs={{0,1},{1,0},{2,3},{3,2},{4,5},{5,4},{6,7},{7,6},{8,9},{9,8},{10,11... | collective-permute-start | bytes 2359304 | tf_op jit(solution)/shard_map/ppermute | solution.py:375
  87.7 6.9 %collective-permute-start.17 = (bf16[64,3072]{1,0:T(8,128)(2,1)S(1)}, bf16[64,3072]{1,0:T(8,128)(2,1)S(1)}, u32[]{:S(2)}, u32[]{:S(2)}) collective-permute-start(bf16[64,3072]{1,0:T(8,128)(2,1)S(1)} %collective-permute-done.6.refs_6_), channel_id=1, source_target_pairs={{0,1},{1,0},{2,3},{3,2},{4,5},{5,4},{6,7},{7,6},{8,9},{9,8},{10,11... | collective-permute-start | bytes 1179656 | tf_op jit(solution)/shard_map/ppermute | solution.py:375
  98.3 7.0 %copy-start.10 = (bf16[768,128]{1,0:T(8,128)(2,1)S(1)}, bf16[768,128]{1,0:T(8,128)(2,1)}, u32[]{:S(2)}) copy-start(bf16[768,128]{1,0:T(8,128)(2,1)} %copy-done.9) | copy-start | bytes 589828
  98.3 8.5 %copy-start.8 = (bf16[768,128]{1,0:T(8,128)(2,1)S(1)}, bf16[768,128]{1,0:T(8,128)(2,1)}, u32[]{:S(2)}) copy-start(bf16[768,128]{1,0:T(8,128)(2,1)} %copy-done.7) | copy-start | bytes 589828
  98.3 9.0 %copy-start.6 = (bf16[768,128]{1,0:T(8,128)(2,1)S(1)}, bf16[768,128]{1,0:T(8,128)(2,1)}, u32[]{:S(2)}) copy-start(bf16[768,128]{1,0:T(8,128)(2,1)} %copy-done.5) | copy-start | bytes 589828
  98.3 10.5 %slice-start = ((s8[4718592]{0:T(1024)(128)(4,1)}), s8[4194304]{0:T(1024)(128)(4,1)S(1)}, s32[]{:S(2)}) async-start(s8[4718592]{0:T(1024)(128)(4,1)} %bitcast.7), calls=%async_computation | async-start | bytes 8388608
  98.4 10.5 %slice-start.1 = ((s8[4718592]{0:T(1024)(128)(4,1)}), s8[524288]{0:T(1024)(128)(4,1)S(1)}, s32[]{:S(2)}) async-start(s8[4718592]{0:T(1024)(128)(4,1)} %bitcast.7), calls=%async_computation.1 | async-start | bytes 1048576
  98.4 26.2 %collective-permute-start.19 = (bf16[768,256]{1,0:T(8,128)(2,1)S(1)}, bf16[768,256]{1,0:T(8,128)(2,1)S(1)}, u32[]{:S(2)}, u32[]{:S(2)}) collective-permute-start(bf16[768,256]{1,0:T(8,128)(2,1)S(1)} %broadcast_select_fusion), channel_id=1, source_target_pairs={{0,8},{4,12},{8,0},{12,4},{1,9},{5,13},{9,1},{13,5},{2,10},{6,14},... | collective-permute-start | bytes 1179656 | tf_op jit(solution)/shard_map/ppermute | solution.py:375
  104.6 9.6 %copy-start.17 = (f32[2,128]{1,0:T(2,128)S(1)}, f32[2,128]{1,0:T(2,128)}, u32[]{:S(2)}) copy-start(f32[2,128]{1,0:T(2,128)} %see.1.limit0_ref) | copy-start | bytes 3076
  104.6 9.6 %copy-start.19 = (f32[2,128]{1,0:T(2,128)S(1)}, f32[2,128]{1,0:T(2,128)}, u32[]{:S(2)}) copy-start(f32[2,128]{1,0:T(2,128)} %copy-done.18) | copy-start | bytes 3076
  104.6 27.4 %collective-permute-start.18 = (bf16[768,256]{1,0:T(8,128)(2,1)S(1)}, bf16[768,256]{1,0:T(8,128)(2,1)S(1)}, u32[]{:S(2)}, u32[]{:S(2)}) collective-permute-start(bf16[768,256]{1,0:T(8,128)(2,1)S(1)} %broadcast_select_fusion.1), channel_id=1, source_target_pairs={{0,8},{4,12},{8,0},{12,4},{1,9},{5,13},{9,1},{13,5},{2,10},{6,14},... | collective-permute-start | bytes 1179656 | tf_op jit(solution)/shard_map/ppermute | solution.py:375
  105.3 14.0 %collective-permute-start.22 = (bf16[768,128]{1,0:T(8,128)(2,1)S(1)}, bf16[768,128]{1,0:T(8,128)(2,1)S(1)}, u32[]{:S(2)}, u32[]{:S(2)}) collective-permute-start(bf16[768,128]{1,0:T(8,128)(2,1)S(1)} %copy-done.10), channel_id=1, source_target_pairs={{0,16},{16,0},{1,17},{17,1},{2,18},{18,2},{3,19},{19,3},{4,20},{20... | collective-permute-start | bytes 589832 | tf_op jit(solution)/shard_map/ppermute | solution.py:375
  106.8 12.4 %collective-permute-start.21 = (bf16[768,128]{1,0:T(8,128)(2,1)S(1)}, bf16[768,128]{1,0:T(8,128)(2,1)S(1)}, u32[]{:S(2)}, u32[]{:S(2)}) collective-permute-start(bf16[768,128]{1,0:T(8,128)(2,1)S(1)} %copy-done.8), channel_id=1, source_target_pairs={{0,16},{16,0},{1,17},{17,1},{2,18},{18,2},{3,19},{19,3},{4,20},{20... | collective-permute-start | bytes 589832 | tf_op jit(solution)/shard_map/ppermute | solution.py:375
  107.3 11.9 %collective-permute-start.20 = (bf16[768,128]{1,0:T(8,128)(2,1)S(1)}, bf16[768,128]{1,0:T(8,128)(2,1)S(1)}, u32[]{:S(2)}, u32[]{:S(2)}) collective-permute-start(bf16[768,128]{1,0:T(8,128)(2,1)S(1)} %copy-done.6), channel_id=1, source_target_pairs={{0,16},{16,0},{1,17},{17,1},{2,18},{18,2},{3,19},{19,3},{4,20},{20... | collective-permute-start | bytes 589832 | tf_op jit(solution)/shard_map/ppermute | solution.py:375
  126.3 7.3 %copy-start.12 = (bf16[768,128]{1,0:T(8,128)(2,1)}, bf16[768,128]{1,0:T(8,128)(2,1)S(1)}, u32[]{:S(2)}) copy-start(bf16[768,128]{1,0:T(8,128)(2,1)S(1)} %get-tuple-element.711.refs_0_) | copy-start | bytes 589828
  134.3 7.8 %collective-permute-start.24 = (bf16[768,128]{1,0:T(8,128)(2,1)S(1)}, bf16[768,128]{1,0:T(8,128)(2,1)S(1)}, u32[]{:S(2)}, u32[]{:S(2)}) collective-permute-start(bf16[768,128]{1,0:T(8,128)(2,1)S(1)} %get-tuple-element.722), channel_id=1, source_target_pairs={{0,4},{4,0},{8,12},{12,8},{1,5},{5,1},{9,13},{13,9},{2,6},{6,2},{1... | collective-permute-start | bytes 589832 | tf_op jit(solution)/shard_map/ppermute | solution.py:375
  134.8 9.6 %collective-permute-start.23 = (bf16[768,128]{1,0:T(8,128)(2,1)S(1)}, bf16[768,128]{1,0:T(8,128)(2,1)S(1)}, u32[]{:S(2)}, u32[]{:S(2)}) collective-permute-start(bf16[768,128]{1,0:T(8,128)(2,1)S(1)} %get-tuple-element.721), channel_id=1, source_target_pairs={{0,4},{4,0},{8,12},{12,8},{1,5},{5,1},{9,13},{13,9},{2,6},{6,2},{1... | collective-permute-start | bytes 589832 | tf_op jit(solution)/shard_map/ppermute | solution.py:375
  142.1 2.2 %copy-start.23 = (bf16[768,128]{1,0:T(8,128)(2,1)}, bf16[768,128]{1,0:T(8,128)(2,1)S(1)}, u32[]{:S(2)}) copy-start(bf16[768,128]{1,0:T(8,128)(2,1)S(1)} %collective-permute-done.24.refs_3_) | copy-start | bytes 589828
  (4 other events, 2.8 us)

commit v5 on v4

--- a/solution.py
+++ b/solution.py
@@ -10,7 +10,9 @@
 EPS = 1e-06
 HIDDEN = -1e30
 COST = pl.CostEstimate(flops=1 << 20, bytes_accessed=1 << 10, transcendentals=0)
-MIDDLE = pl.CostEstimate(flops=1 << 33, bytes_accessed=1 << 10, transcendentals=0)
+SPACE = pl.CostEstimate(flops=1 << 34, bytes_accessed=1 << 10, transcendentals=0)
+SPACE1 = pl.CostEstimate(flops=1 << 32, bytes_accessed=1 << 10, transcendentals=0)
+SPACE2 = pl.CostEstimate(flops=1 << 32, bytes_accessed=1 << 10, transcendentals=0)
 LONG = pl.CostEstimate(flops=1 << 37, bytes_accessed=1 << 10, transcendentals=0)
 
 
@@ -178,67 +180,89 @@
     )(at, lists)
 
 
-def project(at, head_index, first, own_x, quarters, weights, bias, gain, norms, cost=COST):
-    rows, cols = weights[0].shape
+def project(at, part, source, pieces, weights, bias, gain, norms, cost=COST):
+    rows, cols = weights[0][0].shape
     head_dim = gain.shape[1]
-    sources = [own_x] if quarters is None else [part for _, _, part in quarters]
-    tokens = own_x.shape[0] if quarters is None else sum(part.shape[0] for part in sources)
+    sources = [source] if pieces is None else [piece for _, _, piece in pieces]
+    tokens = sum(piece.shape[0] for piece in sources)
     width = sources[0].shape[1]
+    count = len(sources)
     step = 256
+    join = cols < 256
 
     def kernel(at_ref, *refs):
-        x_refs, weight_refs = refs[: len(sources)], refs[len(sources) : len(sources) + 4]
-        b_ref, g_ref, out_ref = refs[len(sources) + 4 :]
+        x_refs, flat = refs[:count], refs[count : count + 8]
+        weight_refs = (flat[:4], flat[4:])
+        b_ref, g_ref, *out_refs = refs[count + 8 : count + 12]
         z, q = at_ref[0], at_ref[1]
-        here = pl.ds(pl.multiple_of(at_ref[head_index] * head_dim, 128), head_dim)
-
-        def piece(ref, to_row):
-            total = None
+
+        def block(ref, row, to_row):
+            totals = [None, None]
             for s in range(4):
                 cut = pl.multiple_of((z ^ s) * rows, 128)
-                part = jnp.dot(
-                    ref[:, pl.ds(cut, rows)],
-                    weight_refs[s][...],
-                    preferred_element_type=jnp.float32,
-                )
-                total = part if total is None else total + part
-            for i, row in enumerate(norms):
-                part = total[:, i * head_dim : (i + 1) * head_dim]
-                part = part + b_ref[first + i : first + i + 1, here]
-                if row is not None:
-                    mean = jnp.mean(part * part, axis=-1, keepdims=True)
-                    part = part * lax.rsqrt(mean + EPS) * g_ref[row : row + 1, :]
-                out_ref[pl.ds(to_row, ref.shape[0]), i * head_dim : (i + 1) * head_dim] = (
-                    part.astype(jnp.bfloat16)
-                )
-
-        if quarters is None:
-            piece(x_refs[0], 0)
+                x = ref[pl.ds(row, step), pl.ds(cut, rows)]
+                if join:
+                    w = jnp.concatenate([weight_refs[0][s][...], weight_refs[1][s][...]], axis=1)
+                    both = jnp.dot(x, w, preferred_element_type=jnp.float32)
+                    parts = [both[:, :cols], both[:, cols:]]
+                else:
+                    parts = [
+                        jnp.dot(x, w[s][...], preferred_element_type=jnp.float32)
+                        for w in weight_refs
+                    ]
+                totals = [p if t is None else t + p for t, p in zip(totals, parts)]
+            for h, (total, out_ref) in enumerate(zip(totals, out_refs)):
+                here = pl.ds(pl.multiple_of(at_ref[2 + h] * head_dim, 128), head_dim)
+                for i, norm in enumerate(norms):
+                    value = total[:, i * head_dim : (i + 1) * head_dim]
+                    value = value + b_ref[part[i] : part[i] + 1, here]
+                    if norm is not None:
+                        mean = jnp.mean(value * value, axis=-1, keepdims=True)
+                        value = value * lax.rsqrt(mean + EPS) * g_ref[norm : norm + 1, :]
+                    out_ref[to_row : to_row + step, i * head_dim : (i + 1) * head_dim] = (
+                        value.astype(jnp.bfloat16)
+                    )
+
+        if pieces is None:
+            block(x_refs[0], 0, 0)
         else:
-            for (i, start, _), ref in zip(quarters, x_refs):
-                piece(ref, pl.multiple_of((q ^ i) * (tokens // 4) + start, 64))
+            x_ref, sems = refs[-2:]
+            copies = []
+            for n, ((i, start, _), ref) in enumerate(zip(pieces, x_refs)):
+                row = pl.multiple_of((q ^ i) * (tokens // 4) + start, 32)
+                target = x_ref.at[pl.ds(row, ref.shape[0]), :]
+                copies.append(pltpu.make_async_copy(ref, target, sems.at[n]))
+                copies[-1].start()
+            for copy in copies:
+                copy.wait()
+            for r in range(0, tokens, step):
+                block(x_ref, r, r)
 
     smem = pl.BlockSpec(memory_space=pltpu.SMEM)
-    if quarters is None:
+    if pieces is None:
         grid = (tokens // step,)
         fixed = lambda shape: pl.BlockSpec(shape, lambda i: (0,) * len(shape))
         x_specs = [pl.BlockSpec((step, width), lambda i: (i, 0))]
         out_spec = pl.BlockSpec((step, cols), lambda i: (i, 0))
+        scratch = []
     else:
         grid = ()
         fixed = lambda shape: pl.BlockSpec()
-        x_specs = [pl.BlockSpec()] * len(sources)
+        x_specs = [pl.BlockSpec(memory_space=pl.ANY)] * count
         out_spec = pl.BlockSpec()
+        scratch = [pltpu.VMEM((tokens, width), jnp.bfloat16), pltpu.SemaphoreType.DMA((count,))]
+    flat = [*weights[0], *weights[1]]
     return pl.pallas_call(
         kernel,
         grid=grid,
-        in_specs=[smem, *x_specs, *(fixed(w.shape) for w in weights), fixed(bias.shape), fixed(gain.shape)],
-        out_specs=out_spec,
-        out_shape=jax.ShapeDtypeStruct((tokens, cols), jnp.bfloat16),
+        in_specs=[smem, *x_specs, *(fixed(w.shape) for w in flat), fixed(bias.shape), fixed(gain.shape)],
+        out_specs=[out_spec] * 2,
+        out_shape=[jax.ShapeDtypeStruct((tokens, cols), jnp.bfloat16)] * 2,
+        scratch_shapes=scratch,
         compiler_params=pltpu.CompilerParams(vmem_limit_bytes=40 << 20),
         cost_estimate=cost,
         name="project",
-    )(at, *sources, *weights, bias, gain)
+    )(at, *sources, *flat, bias, gain)
 
 
 def tile_step(query, rows_ref, at, tile, head_dim, limit, total, mixed):
@@ -385,27 +409,25 @@
     w = jnp.transpose(w_qkv, (1, 0, 2))
     line = Line()
 
-    cutting = (0, 2 * quarter // 3, quarter)
+    cutting = (0, quarter // 2, quarter)
     raws = [
         lax.dynamic_slice(frames, (at[1] * quarter + lo, 0), (hi - lo, frames.shape[1]))
         for lo, hi in zip(cutting, cutting[1:])
     ]
     raws_other = [to("seq", raw, 1) for raw in raws]
-    w, *_ = lax.optimization_barrier((w, *raws))
-    cuts = cut_heads(at, w, [(MINE, KV), (CROSS, KV), (MINE, Q), (CROSS, Q)], LONG)
+    frames, modulation, *_ = lax.optimization_barrier((frames, modulation, *raws))
+    own_x = line.reached(normalize(frames, modulation, 128, LONG))
+    (w,) = line.after(w)
+    cuts = cut_heads(at, w, [(MINE, KV), (CROSS, KV), (MINE, Q), (CROSS, Q)])
     cuts = line.reached(*cuts)
     own_w = {(MINE, KV): cuts[0], (MINE, Q): cuts[2]}
     got = {}
     for part, same, cross in ((KV, *cuts[:2]), (Q, *cuts[2:])):
         got[part] = [to("seq", same[0], 2), to("seq", cross[0], 3), to("seq", cross[0], 1)]
+    (block_lists,) = line.after(block_lists)
     own_limit = line.reached(see(at, block_lists, tile_dev))
     far_limit = to("seq", own_limit[0][0], 1)
-    frames, modulation = line.after(frames, modulation)
-    own_x = line.reached(normalize(frames, modulation, 128, MIDDLE))
     line.drop(cuts[1], cuts[3])
-    (w,) = line.after(w)
-    for key, box in zip(((TWIN, KV), (TWIN, Q)), line.reached(*cut_heads(at, w, [(TWIN, KV), (TWIN, Q)]))):
-        own_w[key] = box
 
     def arrive(value):
         box = line.reached(value)[0]
@@ -414,79 +436,82 @@
 
     def take(i):
         (raw,) = line.after(raws_other[i])
-        near = line.reached(normalize(raw, modulation, 64))[0]
+        near = line.reached(normalize(raw, modulation, 96))[0]
         return near, to("head", near[0], 1), to("fsdp", near[0], 1)
 
     def swap(part, which, kept, back):
         kept[which] = arrive(got[part][which])
         back[which] = to("groups", kept[which][0], 1)
 
-    def run(head, part, boxes, own, cost=COST):
-        (own_part,) = line.after(own_w[head, part][0])
-        own_w[head, part][0] = own_part
-        two, three, one = (box[0] for box in boxes)
+    def run(part, kept, back, own, cost=COST):
+        sets = []
+        for head, boxes in ((MINE, kept), (TWIN, back)):
+            box = own_w[head, part]
+            (box[0],) = line.after(box[0])
+            two, three, one = (b[0] for b in boxes)
+            sets.append([box[0], one, two, three])
         return line.reached(
-            project(
-                at, head, part[0], own_x[0][0] if own else None,
-                None if own else [(i, start, box[0]) for i, start, box in quarters],
-                [own_part, one, two, three], b_qkv, qk_gain, NORMS[part], cost,
+            *project(
+                at, part, own_x[0][0], None if own else [(i, start, box[0]) for i, start, box in pieces],
+                sets, b_qkv, qk_gain, NORMS[part], cost,
             )
         )
 
-    def send_edge(rows):
-        return to("seq", jnp.where(is_mid, rows[0][0], rows[1][0]), 2)
-
-    kv_boxes, kv_back, q_boxes, q_back = ([None] * 3 for _ in range(4))
+    def send_edge(own, far):
+        return to("seq", jnp.where(is_mid, own[0], far[0]), 2)
+
+    kv_kept, kv_back, q_kept, q_back = ([None] * 3 for _ in range(4))
     near0, near_c0, far0 = take(0)
-    swap(KV, 0, kv_boxes, kv_back)
+    swap(KV, 0, kv_kept, kv_back)
     near1, near_c1, far1 = take(1)
-    swap(KV, 1, kv_boxes, kv_back)
-    swap(KV, 2, kv_boxes, kv_back)
-    limits = own_limit + [arrive(far_limit)]
+    swap(KV, 1, kv_kept, kv_back)
+    kv_back[0] = arrive(kv_back[0])
+    swap(KV, 2, kv_kept, kv_back)
+    (w,) = line.after(w)
+    spaced = line.reached(*cut_heads(at, w, [(TWIN, KV), (TWIN, Q)], SPACE))
+    own_w[TWIN, KV], own_w[TWIN, Q] = spaced
     far0 = arrive(far0)
     far_c0 = to("head", far0[0], 1)
     far1 = arrive(far1)
     far_c1 = to("head", far1[0], 1)
+    limits = own_limit + [arrive(far_limit)]
     for which in range(3):
-        swap(Q, which, q_boxes, q_back)
-    rows_mine = run(MINE, KV, kv_boxes, True, LONG)
-    kv_twin = line.reached(*kv_back)
-    rows_twin = run(TWIN, KV, kv_twin, True, LONG)
+        swap(Q, which, q_kept, q_back)
+    kv_back[1:] = [arrive(value) for value in kv_back[1:]]
+    own_mine, own_twin = run(KV, kv_kept, kv_back, True, SPACE1)
     near_c0, far_c0, near_c1, far_c1 = line.reached(near_c0, far_c0, near_c1, far_c1)
-    quarters = [(0, 0, near0), (1, 0, near_c0), (2, 0, far0), (3, 0, far_c0)]
-    quarters += [(i, cutting[1], box) for i, box in enumerate((near1, near_c1, far1, far_c1))]
-    rows_mine += run(MINE, KV, kv_boxes, False)
-    halo_mine = send_edge(rows_mine)
-    rows_twin += run(TWIN, KV, kv_twin, False)
-    halo_twin = send_edge(rows_twin)
-    line.drop(*kv_boxes, *kv_twin)
-    q_mine = run(MINE, Q, q_boxes, True)
-    q_mine += run(MINE, Q, q_boxes, False)
-    line.drop(*q_boxes)
-
-    def pair(q, rows):
-        parts = attend_pair(at, [b[0] for b in limits], [b[0] for b in q], [b[0] for b in rows])
+    pieces = [(i, 0, box) for i, box in enumerate((near0, near_c0, far0, far_c0))]
+    pieces += [(i, cutting[1], box) for i, box in enumerate((near1, near_c1, far1, far_c1))]
+    far_mine, far_twin = run(KV, kv_kept, kv_back, False, SPACE2)
+    halo_mine = send_edge(own_mine, far_mine)
+    halo_twin = send_edge(own_twin, far_twin)
+    line.drop(*kv_kept, *kv_back)
+    q_back = line.reached(*q_back)
+    q_own = run(Q, q_kept, q_back, True)
+    q_far = run(Q, q_kept, q_back, False)
+    line.drop(*q_kept, *q_back, *own_x, *(box for *_, box in pieces))
+
+    def pair(h, rows):
+        parts = attend_pair(
+            at, [b[0] for b in limits], [q_own[h][0], q_far[h][0]], [b[0] for b in rows]
+        )
         return line.reached(*parts)
 
-    def finish(q, halo, parts):
+    def finish(h, halo, parts):
+        (halo,) = line.after(halo)
         keep, send = attend_halo(
-            at, [b[0] for b in limits], [b[0] for b in q], halo, *(b[0] for b in parts)
+            at, [b[0] for b in limits], [q_own[h][0], q_far[h][0]], halo, *(b[0] for b in parts)
         )
         return line.reached(keep)[0], to("seq", send, 1)
 
-    parts_mine = pair(q_mine, rows_mine)
-    q_twin_w = line.reached(*q_back)
-    q_twin = run(TWIN, Q, q_twin_w, True)
-    q_twin += run(TWIN, Q, q_twin_w, False)
-    line.drop(*q_twin_w, *own_x, *(box for *_, box in quarters), *rows_mine)
-    (halo_mine,) = line.after(halo_mine)
-    keep_mine, back_mine = finish(q_mine, halo_mine, parts_mine)
-    line.drop(*q_mine, *parts_mine)
-    q_twin[0][0], q_twin[1][0] = line.after(q_twin[0][0], q_twin[1][0])
-    parts_twin = pair(q_twin, rows_twin)
-    (halo_twin,) = line.after(halo_twin)
-    keep_twin, back_twin = finish(q_twin, halo_twin, parts_twin)
-    parts = [(MINE, keep_mine[0]), (TWIN, keep_twin[0]), (CROSS, back_mine), (CROSS_TWIN, back_twin)]
+    parts_mine = pair(0, (own_mine, far_mine))
+    keep_mine, back_mine = finish(0, halo_mine, parts_mine)
+    line.drop(*parts_mine)
+    q_own[1][0], q_far[1][0] = line.after(q_own[1][0], q_far[1][0])
+    parts_twin = pair(1, (own_twin, far_twin))
+    back_mine = arrive(back_mine)
+    keep_twin, back_twin = finish(1, halo_twin, parts_twin)
+    parts = [(MINE, keep_mine[0]), (TWIN, keep_twin[0]), (CROSS, back_mine[0]), (CROSS_TWIN, back_twin)]
     return assemble(at, parts)
 
 

time: 148 us -> 163 us (1.10)
  local copies, waits for them, and re-layouts: 10.8 us -> 19.7 us
  waiting for transfers between devices: 51.6 us -> 58.7 us
  Pallas kernels: 53.8 us -> 48.4 us
  starting transfers between devices: 30.6 us -> 34.5 us
    unnamed x54 -> x84, local copies, waits for them, and re-layouts: 6.86 us -> 17.3 us
    ppermute x25, waiting for transfers between devices: 51.6 us -> 58.7 us  [to(): lax.ppermute(value, axis, [(i, i ^ bit) for i in range(lax.axis_size(axis...]
    pallas_call x8 -> x4, Pallas kernels: 23.6 us -> 18.1 us  [project(): pl.pallas_call(kernel, grid=grid, in_specs=[smem, *x_specs, *(fixed(w.sha...]
    ppermute x25, starting transfers between devices: 30.6 us -> 34.5 us  [to(): lax.ppermute(value, axis, [(i, i ^ bit) for i in range(lax.axis_size(axis...]
    dynamic_slice x2 -> x1, local copies, waits for them, and re-layouts: 3.83 us -> 2.34 us  [per_device(): lax.dynamic_slice(frames, (at[1] * quarter + lo, 0), (hi - lo, frames.sha...]
  transfers between devices with their start and end apart: 25 -> 25, of which waited for: 9 -> 9; matrix products, arithmetic and copies ran while one was open for 1% -> 0% of each run, Pallas kernels for 31% -> 28%
where the time goes in v5:
time: 163 us; the launch traced here: 162 us
  waiting for transfers between devices  58.7 us (36%)
  Pallas kernels  48.4 us (30%)
  starting transfers between devices  34.5 us (21%)
  local copies, waits for them, and re-layouts  19.7 us (12%)
    ppermute x25, waiting for transfers between devices, to(): lax.ppermute(value, axis, [(i, i ^ bit) for i in range(lax.axis_size(axis...  58.7 us
    ppermute x25, starting transfers between devices, to(): lax.ppermute(value, axis, [(i, i ^ bit) for i in range(lax.axis_size(axis...  34.5 us
    pallas_call x4, Pallas kernels, project(): pl.pallas_call(kernel, grid=grid, in_specs=[smem, *x_specs, *(fixed(w.sha...  18.1 us
    unnamed x84, local copies, waits for them, and re-layouts  17.3 us
    pallas_call x3, Pallas kernels, normalize(): pl.pallas_call(norm_kernel, grid=(tokens // rows,), in_specs=[pl.BlockSpe...  12.2 us
    pallas_call x2, Pallas kernels, attend_pair(): pl.pallas_call(kernel, in_specs=[smem, smem, smem] + [vmem] * 4, out_spec...  9.93 us
  transfers between devices with their start and end apart: 25, of which 9 were waited for; matrix products, arithmetic and copies ran while one was open for 0% of the time, Pallas kernels for 28%

profile of v5, /device:TPU:0, one launch (start us, length us, event | category | flops | bytes accessed | tf_op | source)
XLA Modules:
  0.0 161.8 jit_solution(10829232110674915413)
XLA Ops:
  0.0 2.3 %constant_dynamic-slice_fusion = (bf16[96,3072]{1,0:T(8,128)(2,1)}, bf16[96,3072]{1,0:T(8,128)(2,1)}) fusion(bf16[768,3072]{1,0:T(8,128)(2,1)} %x_ref, s32[]{:T(128)S(6)} %select_n.28, s32[]{:T(128)S(6)} %select_n.27), kind=kLoop, calls=%fused_computation.2 | loop fusion | bytes 2359304 | tf_op jit(solution)/shard_map/dynamic_slice | solution.py:414
  2.3 3.0 %collective-permute-start.2 = (bf16[96,3072]{1,0:T(8,128)(2,1)}, bf16[96,3072]{1,0:T(8,128)(2,1)}, u32[]{:S(2)}, u32[]{:S(2)}) collective-permute-start(bf16[96,3072]{1,0:T(8,128)(2,1)} %get-tuple-element.878), channel_id=1, source_target_pairs={{0,4},{4,0},{8,12},{12,8},{1,5},{5,1},{9,13},{13,9},{2,6},{6,2},{1... | collective-permute-start | bytes 1769480 | tf_op jit(solution)/shard_map/ppermute | solution.py:399
  5.4 7.6 %normalize.3.refs_0_ = bf16[768,3072]{1,0:T(8,128)(2,1)} custom-call(bf16[768,3072]{1,0:T(8,128)(2,1)} %x_ref, f32[2,3072]{1,0:T(2,128)} %mod_ref.2), custom_call_target="tpu_custom_call" | custom-call | flops 137438953472 | bytes 1024 | tf_op jit(solution)/shard_map/normalize/pallas_call | solution.py:124
  13.0 0.8 cut_heads.2
  14.5 0.8 copy-done.33
  15.9 3.1 %collective-permute-start.1 = (bf16[768,256]{1,0:T(8,128)(2,1)S(1)}, bf16[768,256]{1,0:T(8,128)(2,1)}, u32[]{:S(2)}, u32[]{:S(2)}) collective-permute-start(bf16[768,256]{1,0:T(8,128)(2,1)S(1)} %get-tuple-element.687.refs_1_.refs_8_), channel_id=1, source_target_pairs={{0,8},{4,12},{8,0},{12,4},{1,9},{5,13},{9,1},{13,5},{2,10},{6,14},... | collective-permute-start | bytes 1179656 | tf_op jit(solution)/shard_map/ppermute | solution.py:399
  19.0 1.3 see.1.limit0_ref
  20.3 7.9 %collective-permute-done.2.x_ref = bf16[96,3072]{1,0:T(8,128)(2,1)} collective-permute-done((bf16[96,3072]{1,0:T(8,128)(2,1)}, bf16[96,3072]{1,0:T(8,128)(2,1)}, u32[]{:S(2)}, u32[]{:S(2)}) %collective-permute-start.2) | collective-permute-done | bytes 589856 | tf_op jit(solution)/shard_map/ppermute | solution.py:399
  28.3 2.3 %normalize.4.refs_0_ = bf16[96,3072]{1,0:T(8,128)(2,1)} custom-call(bf16[96,3072]{1,0:T(8,128)(2,1)} %collective-permute-done.2.x_ref, f32[2,3072]{1,0:T(2,128)} %mod_ref.2), custom_call_target="tpu_custom_call" | custom-call | flops 1048576 | bytes 1024 | tf_op jit(solution)/shard_map/normalize/pallas_call | solution.py:124
  30.6 2.0 %collective-permute-start.13 = (bf16[96,3072]{1,0:T(8,128)(2,1)}, bf16[96,3072]{1,0:T(8,128)(2,1)}, u32[]{:S(2)}, u32[]{:S(2)}) collective-permute-start(bf16[96,3072]{1,0:T(8,128)(2,1)} %normalize.4.refs_0_), channel_id=1, source_target_pairs={{0,2},{2,0},{1,3},{3,1},{4,6},{6,4},{5,7},{7,5},{8,10},{10,8},{9,1... | collective-permute-start | bytes 1769480 | tf_op jit(solution)/shard_map/ppermute | solution.py:399
  32.6 6.7 %collective-permute-done.1.refs_3_.refs_10_ = bf16[768,256]{1,0:T(8,128)(2,1)} collective-permute-done((bf16[768,256]{1,0:T(8,128)(2,1)S(1)}, bf16[768,256]{1,0:T(8,128)(2,1)}, u32[]{:S(2)}, u32[]{:S(2)}) %collective-permute-start.1) | collective-permute-done | bytes 393248 | tf_op jit(solution)/shard_map/ppermute | solution.py:399
  40.0 0.8 copy-done.37
  40.8 2.4 %normalize.5.refs_4_ = bf16[96,3072]{1,0:T(8,128)(2,1)} custom-call(bf16[96,3072]{1,0:T(8,128)(2,1)} %copy-done.37, f32[2,3072]{1,0:T(2,128)} %mod_ref.2), custom_call_target="tpu_custom_call" | custom-call | flops 1048576 | bytes 1024 | tf_op jit(solution)/shard_map/normalize/pallas_call | solution.py:124
  43.1 1.7 %collective-permute-start.12 = (bf16[96,3072]{1,0:T(8,128)(2,1)}, bf16[96,3072]{1,0:T(8,128)(2,1)}, u32[]{:S(2)}, u32[]{:S(2)}) collective-permute-start(bf16[96,3072]{1,0:T(8,128)(2,1)} %normalize.5.refs_4_), channel_id=1, source_target_pairs={{0,2},{2,0},{1,3},{3,1},{4,6},{6,4},{5,7},{7,5},{8,10},{10,8},{9,1... | collective-permute-start | bytes 1769480 | tf_op jit(solution)/shard_map/ppermute | solution.py:399
  44.8 3.6 %collective-permute-start.4 = (bf16[768,256]{1,0:T(8,128)(2,1)}, bf16[768,256]{1,0:T(8,128)(2,1)S(1)}, u32[]{:S(2)}, u32[]{:S(2)}) collective-permute-start(bf16[768,256]{1,0:T(8,128)(2,1)} %copy-done.33), channel_id=1, source_target_pairs={{0,12},{4,8},{8,4},{12,0},{1,13},{5,9},{9,5},{13,1},{2,14},{6,10},... | collective-permute-start | bytes 1179656 | tf_op jit(solution)/shard_map/ppermute | solution.py:399
  48.4 1.5 collective-permute-start.3
  49.9 9.0 %collective-permute-done.4.refs_4_.refs_11_ = bf16[768,256]{1,0:T(8,128)(2,1)S(1)} collective-permute-done((bf16[768,256]{1,0:T(8,128)(2,1)}, bf16[768,256]{1,0:T(8,128)(2,1)S(1)}, u32[]{:S(2)}, u32[]{:S(2)}) %collective-permute-start.4) | collective-permute-done | bytes 393248 | tf_op jit(solution)/shard_map/ppermute | solution.py:399
  58.9 6.8 %collective-permute-start.11 = (f32[2,128]{1,0:T(2,128)}, f32[2,128]{1,0:T(2,128)S(1)}, u32[]{:S(2)}, u32[]{:S(2)}) collective-permute-start(f32[2,128]{1,0:T(2,128)} %see.1.limit0_ref), channel_id=1, source_target_pairs={{0,4},{4,0},{8,12},{12,8},{1,5},{5,1},{9,13},{13,9},{2,6},{6,2},{1... | collective-permute-start | bytes 3080 | tf_op jit(solution)/shard_map/ppermute | solution.py:399
  65.7 0.8 copy-done.27
  66.5 2.3 %collective-permute-start.9 = (bf16[768,128]{1,0:T(8,128)(2,1)}, bf16[768,128]{1,0:T(8,128)(2,1)S(1)}, u32[]{:S(2)}, u32[]{:S(2)}) collective-permute-start(bf16[768,128]{1,0:T(8,128)(2,1)} %copy-done.34), channel_id=1, source_target_pairs={{0,12},{4,8},{8,4},{12,0},{1,13},{5,9},{9,5},{13,1},{2,14},{6,10},... | collective-permute-start | bytes 589832 | tf_op jit(solution)/shard_map/ppermute | solution.py:399
  68.8 1.1 collective-permute-start.8
  69.9 1.5 collective-permute-start.7
  74.0 0.8 copy-done.35
  74.7 7.8 %collective-permute-done.10.refs_3_.refs_10_ = bf16[768,128]{1,0:T(8,128)(2,1)S(1)} collective-permute-done((bf16[768,128]{1,0:T(8,128)(2,1)}, bf16[768,128]{1,0:T(8,128)(2,1)S(1)}, u32[]{:S(2)}, u32[]{:S(2)}) %collective-permute-start.10) | collective-permute-done | bytes 196640 | tf_op jit(solution)/shard_map/ppermute | solution.py:399
  84.4 0.8 copy-done.30
  85.2 3.3 %collective-permute-done.6.refs_6_.refs_13_ = bf16[768,256]{1,0:T(8,128)(2,1)} collective-permute-done((bf16[768,256]{1,0:T(8,128)(2,1)}, bf16[768,256]{1,0:T(8,128)(2,1)}, u32[]{:S(2)}, u32[]{:S(2)}) %collective-permute-start.6) | collective-permute-done | bytes 393248 | tf_op jit(solution)/shard_map/ppermute | solution.py:399
  88.5 1.5 collective-permute-start.22
  90.0 2.3 %copy-done = bf16[768,3072]{1,0:T(8,128)(2,1)S(1)} copy-done((bf16[768,3072]{1,0:T(8,128)(2,1)S(1)}, bf16[768,3072]{1,0:T(8,128)(2,1)}, u32[]{:S(2)}) %copy-start) | copy-done | bytes 4718616
  93.0 1.0 copy-done.22
  94.0 1.0 copy-done.25
  95.0 1.0 copy-done.28
  96.0 1.0 copy-done.31
  97.0 1.0 copy-done.36
  98.1 4.7 %project.4 = (bf16[768,256]{1,0:T(8,128)(2,1)S(1)}, bf16[768,256]{1,0:T(8,128)(2,1)S(1)}) custom-call(s32[6]{0:T(128)S(1)} %copy-done.16, bf16[768,3072]{1,0:T(8,128)(2,1)S(1)} %copy-done, bf16[768,256]{1,0:T(8,128)(2,1)S(1)} %copy-done.22, bf16[768,256]{1,0:T(8,128)(2,1)} %collective-permute-done.refs_2_.refs_9_, ...), custom_call_target="tpu_custom_call" | custom-call | flops 4294967296 | bytes 1024 | tf_op jit(solution)/shard_map/project/pallas_call | solution.py:255
  103.4 1.5 collective-permute-start.20
  105.0 5.9 %project.5 = (bf16[768,256]{1,0:T(8,128)(2,1)S(1)}, bf16[768,256]{1,0:T(8,128)(2,1)S(1)}) custom-call(s32[6]{0:T(128)S(1)} %copy-done.16, bf16[96,3072]{1,0:T(8,128)(2,1)S(1)} %copy-done.2, bf16[96,3072]{1,0:T(8,128)(2,1)S(1)} %collective-permute-done.14.refs_1_, bf16[96,3072]{1,0:T(8,128)(2,1)} %collective-permute-done.13.refs_2_, ...), custom_call_target="tpu_custom_call" | custom-call | flops 4294967296 | bytes 1024 | tf_op jit(solution)/shard_map/project/pallas_call | solution.py:255
  111.0 1.2 collective-permute-start.19
  112.3 1.8 %collective-permute-start.18 = (bf16[768,256]{1,0:T(8,128)(2,1)S(1)}, bf16[768,256]{1,0:T(8,128)(2,1)S(1)}, u32[]{:S(2)}, u32[]{:S(2)}) collective-permute-start(bf16[768,256]{1,0:T(8,128)(2,1)S(1)} %broadcast_select_fusion.1), channel_id=1, source_target_pairs={{0,8},{4,12},{8,0},{12,4},{1,9},{5,13},{9,1},{13,5},{2,10},{6,14},... | collective-permute-start | bytes 1179656 | tf_op jit(solution)/shard_map/ppermute | solution.py:399
  114.2 3.0 %project.6 = (bf16[768,128]{1,0:T(8,128)(2,1)S(1)}, bf16[768,128]{1,0:T(8,128)(2,1)S(1)}) custom-call(s32[6]{0:T(128)S(1)} %copy-done.16, bf16[768,3072]{1,0:T(8,128)(2,1)S(1)} %bitcast.8, bf16[768,128]{1,0:T(8,128)(2,1)S(1)} %copy-done.5, bf16[768,128]{1,0:T(8,128)(2,1)} %collective-permute-done.8.refs_2_.refs_9_, bf16[768,128]{1,0:T(8,128)(2,1)S(1)} %copy-done.7, ...), custom_call_target="tpu_custom_call" | custom-call | flops 1048576 | bytes 1024 | tf_op jit(solution)/shard_map/project/pallas_call | solution.py:255
  117.2 4.4 %project.7 = (bf16[768,128]{1,0:T(8,128)(2,1)S(1)}, bf16[768,128]{1,0:T(8,128)(2,1)S(1)}) custom-call(s32[6]{0:T(128)S(1)} %copy-done.16, bf16[96,3072]{1,0:T(8,128)(2,1)S(1)} %copy-done.2, bf16[96,3072]{1,0:T(8,128)(2,1)S(1)} %collective-permute-done.14.refs_1_, bf16[96,3072]{1,0:T(8,128)(2,1)} %collective-permute-done.13.refs_2_, ...), custom_call_target="tpu_custom_call" | custom-call | flops 1048576 | bytes 1024 | tf_op jit(solution)/shard_map/project/pallas_call | solution.py:255
  121.6 5.1 %attend_pair.2 = (bf16[768,128]{1,0:T(8,128)(2,1)S(1)}, f32[768,128]{1,0:T(8,128)S(1)}, f32[768,128]{1,0:T(8,128)S(1)}) custom-call(s32[6]{0:T(128)S(1)} %copy-done.16, f32[2,128]{1,0:T(2,128)S(1)} %copy-done.18, f32[2,128]{1,0:T(2,128)S(1)} %collective-permute-done.11.limit1_ref, bf16[768,128]{1,0:T(8,128)(2,1)S(1)} %get-tuple-element.834.q0_ref, ...), custom_call_target="tpu_custom_call" | custom-call | flops 1048576 | bytes 1024 | tf_op jit(solution)/shard_map/attend_pair/pallas_call | solution.py:318
  126.7 13.2 %collective-permute-done.19.halo_ref = bf16[768,256]{1,0:T(8,128)(2,1)S(1)} collective-permute-done((bf16[768,256]{1,0:T(8,128)(2,1)S(1)}, bf16[768,256]{1,0:T(8,128)(2,1)S(1)}, u32[]{:S(2)}, u32[]{:S(2)}) %collective-permute-start.19) | collective-permute-done | bytes 393248 | tf_op jit(solution)/shard_map/ppermute | solution.py:399
  139.8 1.6 %attend_halo.2 = (bf16[768,128]{1,0:T(8,128)(2,1)S(1)}, bf16[768,128]{1,0:T(8,128)(2,1)S(1)}) custom-call(s32[6]{0:T(128)S(1)} %copy-done.16, f32[2,128]{1,0:T(2,128)S(1)} %copy-done.18, f32[2,128]{1,0:T(2,128)S(1)} %collective-permute-done.11.limit1_ref, bf16[768,128]{1,0:T(8,128)(2,1)S(1)} %get-tuple-element.834.q0_ref, ...), custom_call_target="tpu_custom_call" | custom-call | flops 1048576 | bytes 1024 | tf_op jit(solution)/shard_map/attend_halo/pallas_call | solution.py:355
  141.5 4.9 %attend_pair.3 = (bf16[768,128]{1,0:T(8,128)(2,1)S(1)}, f32[768,128]{1,0:T(8,128)S(1)}, f32[768,128]{1,0:T(8,128)S(1)}) custom-call(s32[6]{0:T(128)S(1)} %copy-done.16, f32[2,128]{1,0:T(2,128)S(1)} %copy-done.18, f32[2,128]{1,0:T(2,128)S(1)} %collective-permute-done.11.limit1_ref, bf16[768,128]{1,0:T(8,128)(2,1)S(1)} %get-tuple-element.868.q0_ref, ...), custom_call_target="tpu_custom_call" | custom-call | flops 1048576 | bytes 1024 | tf_op jit(solution)/shard_map/attend_pair/pallas_call | solution.py:318
  146.4 3.3 %collective-permute-done.23.refs_2_ = bf16[768,128]{1,0:T(8,128)(2,1)S(1)} collective-permute-done((bf16[768,128]{1,0:T(8,128)(2,1)S(1)}, bf16[768,128]{1,0:T(8,128)(2,1)S(1)}, u32[]{:S(2)}, u32[]{:S(2)}) %collective-permute-start.23) | collective-permute-done | bytes 196640 | tf_op jit(solution)/shard_map/ppermute | solution.py:399
  149.7 1.6 %attend_halo.3 = (bf16[768,128]{1,0:T(8,128)(2,1)S(1)}, bf16[768,128]{1,0:T(8,128)(2,1)S(1)}) custom-call(s32[6]{0:T(128)S(1)} %copy-done.16, f32[2,128]{1,0:T(2,128)S(1)} %copy-done.18, f32[2,128]{1,0:T(2,128)S(1)} %collective-permute-done.11.limit1_ref, bf16[768,128]{1,0:T(8,128)(2,1)S(1)} %get-tuple-element.868.q0_ref, ...), custom_call_target="tpu_custom_call" | custom-call | flops 1048576 | bytes 1024 | tf_op jit(solution)/shard_map/attend_halo/pallas_call | solution.py:355
  152.0 6.8 %collective-permute-done.24.refs_3_ = bf16[768,128]{1,0:T(8,128)(2,1)S(1)} collective-permute-done((bf16[768,128]{1,0:T(8,128)(2,1)S(1)}, bf16[768,128]{1,0:T(8,128)(2,1)S(1)}, u32[]{:S(2)}, u32[]{:S(2)}) %collective-permute-start.24) | collective-permute-done | bytes 196640 | tf_op jit(solution)/shard_map/ppermute | solution.py:399
  159.6 2.2 %assemble.1 = bf16[768,512]{1,0:T(8,128)(2,1)} custom-call(s32[6]{0:T(128)} %copy-done.14, bf16[768,128]{1,0:T(8,128)(2,1)} %copy-done.12, bf16[768,128]{1,0:T(8,128)(2,1)} %copy-done.13, bf16[768,128]{1,0:T(8,128)(2,1)} %copy-done.38, bf16[768,128]{1,0:T(8,128)(2,1)} %copy-done.39), custom_call_target="tpu_custom_call" | custom-call | flops 1048576 | bytes 1024 | tf_op jit(solution)/shard_map/assemble/pallas_call | solution.py:375
  (106 shorter events, 9.6 us)
Async XLA Ops:
  2.3 25.9 %collective-permute-start.2 = (bf16[96,3072]{1,0:T(8,128)(2,1)}, bf16[96,3072]{1,0:T(8,128)(2,1)}, u32[]{:S(2)}, u32[]{:S(2)}) collective-permute-start(bf16[96,3072]{1,0:T(8,128)(2,1)} %get-tuple-element.878), channel_id=1, source_target_pairs={{0,4},{4,0},{8,12},{12,8},{1,5},{5,1},{9,13},{13,9},{2,6},{6,2},{1... | collective-permute-start | bytes 1769480 | tf_op jit(solution)/shard_map/ppermute | solution.py:399
  5.4 7.7 %copy-start.1 = (bf16[768,3,512]{2,0,1:T(8,128)(2,1)S(1)}, bf16[768,3,512]{2,0,1:T(8,128)(2,1)}, u32[]{:S(2)}) copy-start(bf16[768,3,512]{2,0,1:T(8,128)(2,1)} %param.8) | copy-start | bytes 7077892
  5.4 34.6 %collective-permute-start.5 = (bf16[96,3072]{1,0:T(8,128)(2,1)}, bf16[96,3072]{1,0:T(8,128)(2,1)S(1)}, u32[]{:S(2)}, u32[]{:S(2)}) collective-permute-start(bf16[96,3072]{1,0:T(8,128)(2,1)} %get-tuple-element.877), channel_id=1, source_target_pairs={{0,4},{4,0},{8,12},{12,8},{1,5},{5,1},{9,13},{13,9},{2,6},{6,2},{1... | collective-permute-start | bytes 1769480 | tf_op jit(solution)/shard_map/ppermute | solution.py:399
  13.0 6.0 %copy-start.14 = (s32[6]{0:T(128)}, s32[6]{0:T(128)S(1)}, u32[]{:S(2)}) copy-start(s32[6]{0:T(128)S(1)} %stack.27.at_ref.place_ref) | copy-start | bytes 76
  15.9 24.1 %copy-start.21 = (bf16[768,256]{1,0:T(8,128)(2,1)}, bf16[768,256]{1,0:T(8,128)(2,1)S(1)}, u32[]{:S(2)}) copy-start(bf16[768,256]{1,0:T(8,128)(2,1)S(1)} %get-tuple-element.687.refs_1_.refs_8_) | copy-start | bytes 1179652
  15.9 23.3 %collective-permute-start.1 = (bf16[768,256]{1,0:T(8,128)(2,1)S(1)}, bf16[768,256]{1,0:T(8,128)(2,1)}, u32[]{:S(2)}, u32[]{:S(2)}) collective-permute-start(bf16[768,256]{1,0:T(8,128)(2,1)S(1)} %get-tuple-element.687.refs_1_.refs_8_), channel_id=1, source_target_pairs={{0,8},{4,12},{8,0},{12,4},{1,9},{5,13},{9,1},{13,5},{2,10},{6,14},... | collective-permute-start | bytes 1179656 | tf_op jit(solution)/shard_map/ppermute | solution.py:399
  30.6 39.3 %collective-permute-start.13 = (bf16[96,3072]{1,0:T(8,128)(2,1)}, bf16[96,3072]{1,0:T(8,128)(2,1)}, u32[]{:S(2)}, u32[]{:S(2)}) collective-permute-start(bf16[96,3072]{1,0:T(8,128)(2,1)} %normalize.4.refs_0_), channel_id=1, source_target_pairs={{0,2},{2,0},{1,3},{3,1},{4,6},{6,4},{5,7},{7,5},{8,10},{10,8},{9,1... | collective-permute-start | bytes 1769480 | tf_op jit(solution)/shard_map/ppermute | solution.py:399
  40.8 49.2 %copy-start.16 = (s32[6]{0:T(128)S(1)}, s32[6]{0:T(128)}, u32[]{:S(2)}) copy-start(s32[6]{0:T(128)} %copy-done.14) | copy-start | bytes 76
  40.8 49.2 %copy-start.17 = (f32[3,512]{1,0:T(4,128)S(1)}, f32[3,512]{1,0:T(4,128)}, u32[]{:S(2)}) copy-start(f32[3,512]{1,0:T(4,128)} %refs_16_.3) | copy-start | bytes 18436
  43.1 39.4 %copy-start.3 = (bf16[96,3072]{1,0:T(8,128)(2,1)S(1)}, bf16[96,3072]{1,0:T(8,128)(2,1)}, u32[]{:S(2)}) copy-start(bf16[96,3072]{1,0:T(8,128)(2,1)} %normalize.5.refs_4_) | copy-start | bytes 1769476
  43.1 40.7 %copy-start.2 = (bf16[96,3072]{1,0:T(8,128)(2,1)S(1)}, bf16[96,3072]{1,0:T(8,128)(2,1)}, u32[]{:S(2)}) copy-start(bf16[96,3072]{1,0:T(8,128)(2,1)} %normalize.4.refs_0_) | copy-start | bytes 1769476
  43.1 28.3 %collective-permute-start.12 = (bf16[96,3072]{1,0:T(8,128)(2,1)}, bf16[96,3072]{1,0:T(8,128)(2,1)}, u32[]{:S(2)}, u32[]{:S(2)}) collective-permute-start(bf16[96,3072]{1,0:T(8,128)(2,1)} %normalize.5.refs_4_), channel_id=1, source_target_pairs={{0,2},{2,0},{1,3},{3,1},{4,6},{6,4},{5,7},{7,5},{8,10},{10,8},{9,1... | collective-permute-start | bytes 1769480 | tf_op jit(solution)/shard_map/ppermute | solution.py:399
  44.8 14.1 %collective-permute-start.4 = (bf16[768,256]{1,0:T(8,128)(2,1)}, bf16[768,256]{1,0:T(8,128)(2,1)S(1)}, u32[]{:S(2)}, u32[]{:S(2)}) collective-permute-start(bf16[768,256]{1,0:T(8,128)(2,1)} %copy-done.33), channel_id=1, source_target_pairs={{0,12},{4,8},{8,4},{12,0},{1,13},{5,9},{9,5},{13,1},{2,14},{6,10},... | collective-permute-start | bytes 1179656 | tf_op jit(solution)/shard_map/ppermute | solution.py:399
  48.4 17.3 %collective-permute-start.3 = (bf16[768,256]{1,0:T(8,128)(2,1)}, bf16[768,256]{1,0:T(8,128)(2,1)S(1)}, u32[]{:S(2)}, u32[]{:S(2)}) collective-permute-start(bf16[768,256]{1,0:T(8,128)(2,1)} %collective-permute-done.1.refs_3_.refs_10_), channel_id=1, source_target_pairs={{0,16},{16,0},{1,17},{17,1},{2,18},{18,2},{3,19},{19,3},{4,20},{20... | collective-permute-start | bytes 1179656 | tf_op jit(solution)/shard_map/ppermute | solution.py:399
  49.9 16.6 %collective-permute-start = (bf16[768,256]{1,0:T(8,128)(2,1)}, bf16[768,256]{1,0:T(8,128)(2,1)}, u32[]{:S(2)}, u32[]{:S(2)}) collective-permute-start(bf16[768,256]{1,0:T(8,128)(2,1)} %copy-done.33), channel_id=1, source_target_pairs={{0,4},{4,0},{8,12},{12,8},{1,5},{5,1},{9,13},{13,9},{2,6},{6,2},{1... | collective-permute-start | bytes 1179656 | tf_op jit(solution)/shard_map/ppermute | solution.py:399
  58.9 14.4 %copy-start.24 = (bf16[768,256]{1,0:T(8,128)(2,1)}, bf16[768,256]{1,0:T(8,128)(2,1)S(1)}, u32[]{:S(2)}) copy-start(bf16[768,256]{1,0:T(8,128)(2,1)S(1)} %collective-permute-done.4.refs_4_.refs_11_) | copy-start | bytes 1179652
  58.9 9.9 %collective-permute-start.11 = (f32[2,128]{1,0:T(2,128)}, f32[2,128]{1,0:T(2,128)S(1)}, u32[]{:S(2)}, u32[]{:S(2)}) collective-permute-start(f32[2,128]{1,0:T(2,128)} %see.1.limit0_ref), channel_id=1, source_target_pairs={{0,4},{4,0},{8,12},{12,8},{1,5},{5,1},{9,13},{13,9},{2,6},{6,2},{1... | collective-permute-start | bytes 3080 | tf_op jit(solution)/shard_map/ppermute | solution.py:399
  66.4 16.1 %collective-permute-start.10 = (bf16[768,128]{1,0:T(8,128)(2,1)}, bf16[768,128]{1,0:T(8,128)(2,1)S(1)}, u32[]{:S(2)}, u32[]{:S(2)}) collective-permute-start(bf16[768,128]{1,0:T(8,128)(2,1)} %copy-done.4), channel_id=1, source_target_pairs={{0,8},{4,12},{8,0},{12,4},{1,9},{5,13},{9,1},{13,5},{2,10},{6,14},... | collective-permute-start | bytes 589832 | tf_op jit(solution)/shard_map/ppermute | solution.py:399
  66.5 16.7 %collective-permute-start.9 = (bf16[768,128]{1,0:T(8,128)(2,1)}, bf16[768,128]{1,0:T(8,128)(2,1)S(1)}, u32[]{:S(2)}, u32[]{:S(2)}) collective-permute-start(bf16[768,128]{1,0:T(8,128)(2,1)} %copy-done.34), channel_id=1, source_target_pairs={{0,12},{4,8},{8,4},{12,0},{1,13},{5,9},{9,5},{13,1},{2,14},{6,10},... | collective-permute-start | bytes 589832 | tf_op jit(solution)/shard_map/ppermute | solution.py:399
  68.8 15.0 %collective-permute-start.8 = (bf16[768,128]{1,0:T(8,128)(2,1)}, bf16[768,128]{1,0:T(8,128)(2,1)}, u32[]{:S(2)}, u32[]{:S(2)}) collective-permute-start(bf16[768,128]{1,0:T(8,128)(2,1)} %copy-done.34), channel_id=1, source_target_pairs={{0,4},{4,0},{8,12},{12,8},{1,5},{5,1},{9,13},{13,9},{2,6},{6,2},{1... | collective-permute-start | bytes 589832 | tf_op jit(solution)/shard_map/ppermute | solution.py:399
  69.9 14.4 %collective-permute-start.7 = (bf16[768,256]{1,0:T(8,128)(2,1)S(1)}, bf16[768,256]{1,0:T(8,128)(2,1)S(1)}, u32[]{:S(2)}, u32[]{:S(2)}) collective-permute-start(bf16[768,256]{1,0:T(8,128)(2,1)S(1)} %collective-permute-done.4.refs_4_.refs_11_), channel_id=1, source_target_pairs={{0,16},{16,0},{1,17},{17,1},{2,18},{18,2},{3,19},{19,3},{4,20},{20... | collective-permute-start | bytes 1179656 | tf_op jit(solution)/shard_map/ppermute | solution.py:399
  71.5 17.0 %collective-permute-start.6 = (bf16[768,256]{1,0:T(8,128)(2,1)}, bf16[768,256]{1,0:T(8,128)(2,1)}, u32[]{:S(2)}, u32[]{:S(2)}) collective-permute-start(bf16[768,256]{1,0:T(8,128)(2,1)} %collective-permute-done.refs_2_.refs_9_), channel_id=1, source_target_pairs={{0,16},{16,0},{1,17},{17,1},{2,18},{18,2},{3,19},{19,3},{4,20},{20... | collective-permute-start | bytes 1179656 | tf_op jit(solution)/shard_map/ppermute | solution.py:399
  82.5 20.3 %collective-permute-start.16 = (bf16[96,3072]{1,0:T(8,128)(2,1)S(1)}, bf16[96,3072]{1,0:T(8,128)(2,1)S(1)}, u32[]{:S(2)}, u32[]{:S(2)}) collective-permute-start(bf16[96,3072]{1,0:T(8,128)(2,1)S(1)} %copy-done.3), channel_id=1, source_target_pairs={{0,1},{1,0},{2,3},{3,2},{4,5},{5,4},{6,7},{7,6},{8,9},{9,8},{10,11... | collective-permute-start | bytes 1769480 | tf_op jit(solution)/shard_map/ppermute | solution.py:399
  83.9 19.6 %collective-permute-start.14 = (bf16[96,3072]{1,0:T(8,128)(2,1)S(1)}, bf16[96,3072]{1,0:T(8,128)(2,1)S(1)}, u32[]{:S(2)}, u32[]{:S(2)}) collective-permute-start(bf16[96,3072]{1,0:T(8,128)(2,1)S(1)} %copy-done.2), channel_id=1, source_target_pairs={{0,1},{1,0},{2,3},{3,2},{4,5},{5,4},{6,7},{7,6},{8,9},{9,8},{10,11... | collective-permute-start | bytes 1769480 | tf_op jit(solution)/shard_map/ppermute | solution.py:399
  83.9 21.1 %collective-permute-start.17 = (bf16[96,3072]{1,0:T(8,128)(2,1)}, bf16[96,3072]{1,0:T(8,128)(2,1)S(1)}, u32[]{:S(2)}, u32[]{:S(2)}) collective-permute-start(bf16[96,3072]{1,0:T(8,128)(2,1)} %collective-permute-done.12.refs_6_), channel_id=1, source_target_pairs={{0,1},{1,0},{2,3},{3,2},{4,5},{5,4},{6,7},{7,6},{8,9},{9,8},{10,11... | collective-permute-start | bytes 1769480 | tf_op jit(solution)/shard_map/ppermute | solution.py:399
  85.1 19.8 %collective-permute-start.15 = (bf16[96,3072]{1,0:T(8,128)(2,1)}, bf16[96,3072]{1,0:T(8,128)(2,1)S(1)}, u32[]{:S(2)}, u32[]{:S(2)}) collective-permute-start(bf16[96,3072]{1,0:T(8,128)(2,1)} %collective-permute-done.13.refs_2_), channel_id=1, source_target_pairs={{0,1},{1,0},{2,3},{3,2},{4,5},{5,4},{6,7},{7,6},{8,9},{9,8},{10,11... | collective-permute-start | bytes 1769480 | tf_op jit(solution)/shard_map/ppermute | solution.py:399
  88.5 25.6 %collective-permute-start.22 = (bf16[768,128]{1,0:T(8,128)(2,1)}, bf16[768,128]{1,0:T(8,128)(2,1)S(1)}, u32[]{:S(2)}, u32[]{:S(2)}) collective-permute-start(bf16[768,128]{1,0:T(8,128)(2,1)} %collective-permute-done.8.refs_2_.refs_9_), channel_id=1, source_target_pairs={{0,16},{16,0},{1,17},{17,1},{2,18},{18,2},{3,19},{19,3},{4,20},{20... | collective-permute-start | bytes 589832 | tf_op jit(solution)/shard_map/ppermute | solution.py:399
  90.0 2.3 %copy-start = (bf16[768,3072]{1,0:T(8,128)(2,1)S(1)}, bf16[768,3072]{1,0:T(8,128)(2,1)}, u32[]{:S(2)}) copy-start(bf16[768,3072]{1,0:T(8,128)(2,1)} %normalize.3.refs_0_) | copy-start | bytes 14155780
  98.0 4.8 %copy-start.9 = (bf16[768,128]{1,0:T(8,128)(2,1)S(1)}, bf16[768,128]{1,0:T(8,128)(2,1)}, u32[]{:S(2)}) copy-start(bf16[768,128]{1,0:T(8,128)(2,1)} %copy-done.8) | copy-start | bytes 589828
  98.0 5.4 %copy-start.7 = (bf16[768,128]{1,0:T(8,128)(2,1)S(1)}, bf16[768,128]{1,0:T(8,128)(2,1)}, u32[]{:S(2)}) copy-start(bf16[768,128]{1,0:T(8,128)(2,1)} %copy-done.6) | copy-start | bytes 589828
  98.0 6.9 %copy-start.20 = (f32[2,128]{1,0:T(2,128)S(1)}, f32[2,128]{1,0:T(2,128)}, u32[]{:S(2)}) copy-start(f32[2,128]{1,0:T(2,128)} %refs_17_.3) | copy-start | bytes 3076
  98.0 6.9 %copy-start.23 = (bf16[768,256]{1,0:T(8,128)(2,1)S(1)}, bf16[768,256]{1,0:T(8,128)(2,1)}, u32[]{:S(2)}) copy-start(bf16[768,256]{1,0:T(8,128)(2,1)} %copy-done.21) | copy-start | bytes 1179652
  98.0 6.9 %copy-start.26 = (bf16[768,256]{1,0:T(8,128)(2,1)S(1)}, bf16[768,256]{1,0:T(8,128)(2,1)}, u32[]{:S(2)}) copy-start(bf16[768,256]{1,0:T(8,128)(2,1)} %copy-done.24) | copy-start | bytes 1179652
  98.0 6.9 %copy-start.29 = (bf16[768,256]{1,0:T(8,128)(2,1)S(1)}, bf16[768,256]{1,0:T(8,128)(2,1)}, u32[]{:S(2)}) copy-start(bf16[768,256]{1,0:T(8,128)(2,1)} %copy-done.27) | copy-start | bytes 1179652
  98.0 6.9 %copy-start.32 = (bf16[768,256]{1,0:T(8,128)(2,1)S(1)}, bf16[768,256]{1,0:T(8,128)(2,1)}, u32[]{:S(2)}) copy-start(bf16[768,256]{1,0:T(8,128)(2,1)} %copy-done.30) | copy-start | bytes 1179652
  98.1 16.1 %slice-start = ((s8[4718592]{0:T(1024)(128)(4,1)}), s8[4194304]{0:T(1024)(128)(4,1)S(1)}, s32[]{:S(2)}) async-start(s8[4718592]{0:T(1024)(128)(4,1)} %bitcast.7), calls=%async_computation | async-start | bytes 8388608
  102.8 11.3 %collective-permute-start.21 = (bf16[768,128]{1,0:T(8,128)(2,1)S(1)}, bf16[768,128]{1,0:T(8,128)(2,1)S(1)}, u32[]{:S(2)}, u32[]{:S(2)}) collective-permute-start(bf16[768,128]{1,0:T(8,128)(2,1)S(1)} %copy-done.9), channel_id=1, source_target_pairs={{0,16},{16,0},{1,17},{17,1},{2,18},{18,2},{3,19},{19,3},{4,20},{20... | collective-permute-start | bytes 589832 | tf_op jit(solution)/shard_map/ppermute | solution.py:399
  103.4 10.7 %collective-permute-start.20 = (bf16[768,128]{1,0:T(8,128)(2,1)S(1)}, bf16[768,128]{1,0:T(8,128)(2,1)S(1)}, u32[]{:S(2)}, u32[]{:S(2)}) collective-permute-start(bf16[768,128]{1,0:T(8,128)(2,1)S(1)} %copy-done.7), channel_id=1, source_target_pairs={{0,16},{16,0},{1,17},{17,1},{2,18},{18,2},{3,19},{19,3},{4,20},{20... | collective-permute-start | bytes 589832 | tf_op jit(solution)/shard_map/ppermute | solution.py:399
  105.0 9.2 %slice-start.1 = ((s8[4718592]{0:T(1024)(128)(4,1)}), s8[524288]{0:T(1024)(128)(4,1)S(1)}, s32[]{:S(2)}) async-start(s8[4718592]{0:T(1024)(128)(4,1)} %bitcast.7), calls=%async_computation.1 | async-start | bytes 1048576
  105.0 9.1 %copy-start.5 = (bf16[768,128]{1,0:T(8,128)(2,1)S(1)}, bf16[768,128]{1,0:T(8,128)(2,1)}, u32[]{:S(2)}) copy-start(bf16[768,128]{1,0:T(8,128)(2,1)} %copy-done.4) | copy-start | bytes 589828
  105.0 9.1 %copy-start.11 = (bf16[768,128]{1,0:T(8,128)(2,1)S(1)}, bf16[768,128]{1,0:T(8,128)(2,1)}, u32[]{:S(2)}) copy-start(bf16[768,128]{1,0:T(8,128)(2,1)} %copy-done.10) | copy-start | bytes 589828
  111.0 28.8 %collective-permute-start.19 = (bf16[768,256]{1,0:T(8,128)(2,1)S(1)}, bf16[768,256]{1,0:T(8,128)(2,1)S(1)}, u32[]{:S(2)}, u32[]{:S(2)}) collective-permute-start(bf16[768,256]{1,0:T(8,128)(2,1)S(1)} %broadcast_select_fusion), channel_id=1, source_target_pairs={{0,8},{4,12},{8,0},{12,4},{1,9},{5,13},{9,1},{13,5},{2,10},{6,14},... | collective-permute-start | bytes 1179656 | tf_op jit(solution)/shard_map/ppermute | solution.py:399
  112.3 37.4 %collective-permute-start.18 = (bf16[768,256]{1,0:T(8,128)(2,1)S(1)}, bf16[768,256]{1,0:T(8,128)(2,1)S(1)}, u32[]{:S(2)}, u32[]{:S(2)}) collective-permute-start(bf16[768,256]{1,0:T(8,128)(2,1)S(1)} %broadcast_select_fusion.1), channel_id=1, source_target_pairs={{0,8},{4,12},{8,0},{12,4},{1,9},{5,13},{9,1},{13,5},{2,10},{6,14},... | collective-permute-start | bytes 1179656 | tf_op jit(solution)/shard_map/ppermute | solution.py:399
  117.2 4.4 %copy-start.18 = (f32[2,128]{1,0:T(2,128)S(1)}, f32[2,128]{1,0:T(2,128)}, u32[]{:S(2)}) copy-start(f32[2,128]{1,0:T(2,128)} %see.1.limit0_ref) | copy-start | bytes 3076
  141.5 9.9 %copy-start.12 = (bf16[768,128]{1,0:T(8,128)(2,1)}, bf16[768,128]{1,0:T(8,128)(2,1)S(1)}, u32[]{:S(2)}) copy-start(bf16[768,128]{1,0:T(8,128)(2,1)S(1)} %get-tuple-element.865.refs_0_) | copy-start | bytes 589828
  141.5 8.3 %collective-permute-start.23 = (bf16[768,128]{1,0:T(8,128)(2,1)S(1)}, bf16[768,128]{1,0:T(8,128)(2,1)S(1)}, u32[]{:S(2)}, u32[]{:S(2)}) collective-permute-start(bf16[768,128]{1,0:T(8,128)(2,1)S(1)} %get-tuple-element.840), channel_id=1, source_target_pairs={{0,4},{4,0},{8,12},{12,8},{1,5},{5,1},{9,13},{13,9},{2,6},{6,2},{1... | collective-permute-start | bytes 589832 | tf_op jit(solution)/shard_map/ppermute | solution.py:399
  149.7 9.1 %copy-start.38 = (bf16[768,128]{1,0:T(8,128)(2,1)}, bf16[768,128]{1,0:T(8,128)(2,1)S(1)}, u32[]{:S(2)}) copy-start(bf16[768,128]{1,0:T(8,128)(2,1)S(1)} %collective-permute-done.23.refs_2_) | copy-start | bytes 589828
  152.0 6.8 %collective-permute-start.24 = (bf16[768,128]{1,0:T(8,128)(2,1)S(1)}, bf16[768,128]{1,0:T(8,128)(2,1)S(1)}, u32[]{:S(2)}, u32[]{:S(2)}) collective-permute-start(bf16[768,128]{1,0:T(8,128)(2,1)S(1)} %get-tuple-element.876), channel_id=1, source_target_pairs={{0,4},{4,0},{8,12},{12,8},{1,5},{5,1},{9,13},{13,9},{2,6},{6,2},{1... | collective-permute-start | bytes 589832 | tf_op jit(solution)/shard_map/ppermute | solution.py:399
  (19 other events, 14.9 us)

commit v6 on v5

--- a/solution.py
+++ b/solution.py
@@ -8,12 +8,9 @@
 from jax.sharding import PartitionSpec as P
 
 EPS = 1e-06
+VMEM = 60 << 20
 HIDDEN = -1e30
 COST = pl.CostEstimate(flops=1 << 20, bytes_accessed=1 << 10, transcendentals=0)
-SPACE = pl.CostEstimate(flops=1 << 34, bytes_accessed=1 << 10, transcendentals=0)
-SPACE1 = pl.CostEstimate(flops=1 << 32, bytes_accessed=1 << 10, transcendentals=0)
-SPACE2 = pl.CostEstimate(flops=1 << 32, bytes_accessed=1 << 10, transcendentals=0)
-LONG = pl.CostEstimate(flops=1 << 37, bytes_accessed=1 << 10, transcendentals=0)
 
 
 def with_halo(shard, sides, width):
@@ -119,7 +116,7 @@
     o_ref[...] = scaled.astype(jnp.bfloat16)
 
 
-def normalize(frames, modulation, rows, cost=COST):
+def normalize(frames, modulation, rows):
     tokens, width = frames.shape
     return pl.pallas_call(
         norm_kernel,
@@ -130,29 +127,28 @@
         ],
         out_specs=pl.BlockSpec((rows, width), lambda i: (i, 0)),
         out_shape=jax.ShapeDtypeStruct((tokens, width), jnp.bfloat16),
-        cost_estimate=cost,
+        cost_estimate=COST,
         name="normalize",
     )(frames, modulation)
 
 
-def cut_heads(at, w, groups, cost=COST):
+def cut_heads(at, w):
     rows = w.shape[1]
     head_dim = 128
-    widths = [head_dim * len(js) for _, js in groups]
 
     def kernel(at_ref, w_ref, *out_refs):
-        for (index, js), ref in zip(groups, out_refs):
-            cols = pl.ds(pl.multiple_of(at_ref[index] * head_dim, 128), head_dim)
-            for i, j in enumerate(js):
-                ref[:, i * head_dim : (i + 1) * head_dim] = w_ref[j, :, cols]
+        for j, ref in enumerate(out_refs):
+            for target in range(4):
+                cols = pl.ds(pl.multiple_of(at_ref[6 + target % 2] * head_dim, 128), head_dim)
+                ref[target] = w_ref[j, :, cols]
 
     return pl.pallas_call(
         kernel,
         in_specs=[pl.BlockSpec(memory_space=pltpu.SMEM), pl.BlockSpec()],
-        out_specs=[pl.BlockSpec()] * len(groups),
-        out_shape=[jax.ShapeDtypeStruct((rows, n), jnp.bfloat16) for n in widths],
-        compiler_params=pltpu.CompilerParams(vmem_limit_bytes=24 << 20),
-        cost_estimate=cost,
+        out_specs=[pl.BlockSpec()] * 3,
+        out_shape=[jax.ShapeDtypeStruct((4, rows, head_dim), jnp.bfloat16)] * 3,
+        compiler_params=pltpu.CompilerParams(vmem_limit_bytes=VMEM),
+        cost_estimate=COST,
         name="cut_heads",
     )(at, w)
 
@@ -180,63 +176,51 @@
     )(at, lists)
 
 
-def project(at, part, source, pieces, weights, bias, gain, norms, cost=COST):
-    rows, cols = weights[0][0].shape
-    head_dim = gain.shape[1]
+def project(at, head, part, source, pieces, weights, bias, gain):
+    shards, rows, head_dim = weights[0].shape
+    cols = head_dim * len(part)
     sources = [source] if pieces is None else [piece for _, _, piece in pieces]
     tokens = sum(piece.shape[0] for piece in sources)
     width = sources[0].shape[1]
     count = len(sources)
     step = 256
-    join = cols < 256
 
     def kernel(at_ref, *refs):
-        x_refs, flat = refs[:count], refs[count : count + 8]
-        weight_refs = (flat[:4], flat[4:])
-        b_ref, g_ref, *out_refs = refs[count + 8 : count + 12]
-        z, q = at_ref[0], at_ref[1]
-
-        def block(ref, row, to_row):
-            totals = [None, None]
-            for s in range(4):
-                cut = pl.multiple_of((z ^ s) * rows, 128)
-                x = ref[pl.ds(row, step), pl.ds(cut, rows)]
-                if join:
-                    w = jnp.concatenate([weight_refs[0][s][...], weight_refs[1][s][...]], axis=1)
-                    both = jnp.dot(x, w, preferred_element_type=jnp.float32)
-                    parts = [both[:, :cols], both[:, cols:]]
-                else:
-                    parts = [
-                        jnp.dot(x, w[s][...], preferred_element_type=jnp.float32)
-                        for w in weight_refs
-                    ]
-                totals = [p if t is None else t + p for t, p in zip(totals, parts)]
-            for h, (total, out_ref) in enumerate(zip(totals, out_refs)):
-                here = pl.ds(pl.multiple_of(at_ref[2 + h] * head_dim, 128), head_dim)
-                for i, norm in enumerate(norms):
-                    value = total[:, i * head_dim : (i + 1) * head_dim]
-                    value = value + b_ref[part[i] : part[i] + 1, here]
-                    if norm is not None:
-                        mean = jnp.mean(value * value, axis=-1, keepdims=True)
-                        value = value * lax.rsqrt(mean + EPS) * g_ref[norm : norm + 1, :]
-                    out_ref[to_row : to_row + step, i * head_dim : (i + 1) * head_dim] = (
-                        value.astype(jnp.bfloat16)
-                    )
+        x_refs, weight_refs = refs[:count], refs[count : count + len(part)]
+        b_ref, g_ref, out_ref = refs[count + len(part) : count + len(part) + 3]
+        here = pl.ds(pl.multiple_of(at_ref[head] * head_dim, 128), head_dim)
+
+        def block(ref, row):
+            total = None
+            for s in range(shards):
+                w = jnp.concatenate([ref[s] for ref in weight_refs], axis=1)
+                x = ref[row : row + step, s * rows : (s + 1) * rows]
+                product = jnp.dot(x, w, preferred_element_type=jnp.float32)
+                total = product if total is None else total + product
+            for i, j in enumerate(part):
+                value = total[:, i * head_dim : (i + 1) * head_dim] + b_ref[j : j + 1, here]
+                if j < 2:
+                    mean = jnp.mean(value * value, axis=-1, keepdims=True)
+                    value = value * lax.rsqrt(mean + EPS) * g_ref[j : j + 1, :]
+                out_ref[row : row + step, i * head_dim : (i + 1) * head_dim] = value.astype(
+                    jnp.bfloat16
+                )
 
         if pieces is None:
-            block(x_refs[0], 0, 0)
+            block(x_refs[0], 0)
         else:
             x_ref, sems = refs[-2:]
+            q = at_ref[1]
             copies = []
             for n, ((i, start, _), ref) in enumerate(zip(pieces, x_refs)):
-                row = pl.multiple_of((q ^ i) * (tokens // 4) + start, 32)
+                row = pl.multiple_of((q ^ i) * (tokens // 4) + start, 16)
                 target = x_ref.at[pl.ds(row, ref.shape[0]), :]
                 copies.append(pltpu.make_async_copy(ref, target, sems.at[n]))
                 copies[-1].start()
             for copy in copies:
                 copy.wait()
             for r in range(0, tokens, step):
-                block(x_ref, r, r)
+                block(x_ref, r)
 
     smem = pl.BlockSpec(memory_space=pltpu.SMEM)
     if pieces is None:
@@ -251,18 +235,17 @@
         x_specs = [pl.BlockSpec(memory_space=pl.ANY)] * count
         out_spec = pl.BlockSpec()
         scratch = [pltpu.VMEM((tokens, width), jnp.bfloat16), pltpu.SemaphoreType.DMA((count,))]
-    flat = [*weights[0], *weights[1]]
     return pl.pallas_call(
         kernel,
         grid=grid,
-        in_specs=[smem, *x_specs, *(fixed(w.shape) for w in flat), fixed(bias.shape), fixed(gain.shape)],
-        out_specs=[out_spec] * 2,
-        out_shape=[jax.ShapeDtypeStruct((tokens, cols), jnp.bfloat16)] * 2,
+        in_specs=[smem, *x_specs, *(fixed(w.shape) for w in weights), fixed(bias.shape), fixed(gain.shape)],
+        out_specs=out_spec,
+        out_shape=jax.ShapeDtypeStruct((tokens, cols), jnp.bfloat16),
         scratch_shapes=scratch,
-        compiler_params=pltpu.CompilerParams(vmem_limit_bytes=40 << 20),
-        cost_estimate=cost,
+        compiler_params=pltpu.CompilerParams(vmem_limit_bytes=VMEM),
+        cost_estimate=COST,
         name="project",
-    )(at, *sources, *flat, bias, gain)
+    )(at, *sources, *weights, bias, gain)
 
 
 def tile_step(query, rows_ref, at, tile, head_dim, limit, total, mixed):
@@ -324,7 +307,7 @@
             jax.ShapeDtypeStruct((tokens, head_dim), jnp.float32),
             jax.ShapeDtypeStruct((tokens, 128), jnp.float32),
         ],
-        compiler_params=pltpu.CompilerParams(vmem_limit_bytes=40 << 20),
+        compiler_params=pltpu.CompilerParams(vmem_limit_bytes=VMEM),
         cost_estimate=COST,
         name="attend_pair",
     )(place, *limits, *queries, *rows)
@@ -357,7 +340,7 @@
         in_specs=[smem, smem, smem] + [vmem] * 6,
         out_specs=[vmem, vmem],
         out_shape=[out, out],
-        compiler_params=pltpu.CompilerParams(vmem_limit_bytes=40 << 20),
+        compiler_params=pltpu.CompilerParams(vmem_limit_bytes=VMEM),
         cost_estimate=COST,
         name="attend_halo",
     )(place, *limits, *queries, halo, done, mixed, total)
@@ -401,33 +384,30 @@
     side = z % 2
     mine, twin = 2 * side + y, 2 * side + 1 - y
     across = 2 * (1 - side)
-    at = jnp.stack([z, 2 * x + core, mine, twin, across + y, across + 1 - y])
+    at = jnp.stack([z, 2 * x + core, mine, twin, across + y, across + 1 - y, y, 2 + y])
     MINE, TWIN, CROSS, CROSS_TWIN = 2, 3, 4, 5
-    KV, Q = (1, 2), (0,)
-    NORMS = {KV: (1, None), Q: (0,)}
     is_mid = (z == 1) | (z == 2)
     w = jnp.transpose(w_qkv, (1, 0, 2))
     line = Line()
 
-    cutting = (0, quarter // 2, quarter)
+    cutting = (0, quarter * 5 // 12, quarter)
     raws = [
         lax.dynamic_slice(frames, (at[1] * quarter + lo, 0), (hi - lo, frames.shape[1]))
         for lo, hi in zip(cutting, cutting[1:])
     ]
     raws_other = [to("seq", raw, 1) for raw in raws]
-    frames, modulation, *_ = lax.optimization_barrier((frames, modulation, *raws))
-    own_x = line.reached(normalize(frames, modulation, 128, LONG))
-    (w,) = line.after(w)
-    cuts = cut_heads(at, w, [(MINE, KV), (CROSS, KV), (MINE, Q), (CROSS, Q)])
-    cuts = line.reached(*cuts)
-    own_w = {(MINE, KV): cuts[0], (MINE, Q): cuts[2]}
-    got = {}
-    for part, same, cross in ((KV, *cuts[:2]), (Q, *cuts[2:])):
-        got[part] = [to("seq", same[0], 2), to("seq", cross[0], 3), to("seq", cross[0], 1)]
-    (block_lists,) = line.after(block_lists)
+    (w, *_) = lax.optimization_barrier((w, *raws))
+    cuts = line.reached(*cut_heads(at, w))
+
+    def exchange(value):
+        return lax.all_to_all(value, "seq", split_axis=0, concat_axis=0, tiled=True)
+
+    arrived_k = exchange(cuts[1][0])
     own_limit = line.reached(see(at, block_lists, tile_dev))
     far_limit = to("seq", own_limit[0][0], 1)
-    line.drop(cuts[1], cuts[3])
+    frames, modulation = line.after(frames, modulation)
+    own_x = line.reached(normalize(frames, modulation, 128))
+    line.drop(cuts[1])
 
     def arrive(value):
         box = line.reached(value)[0]
@@ -436,78 +416,76 @@
 
     def take(i):
         (raw,) = line.after(raws_other[i])
-        near = line.reached(normalize(raw, modulation, 96))[0]
+        near = line.reached(normalize(raw, modulation, raw.shape[0]))[0]
         return near, to("head", near[0], 1), to("fsdp", near[0], 1)
 
-    def swap(part, which, kept, back):
-        kept[which] = arrive(got[part][which])
-        back[which] = to("groups", kept[which][0], 1)
-
-    def run(part, kept, back, own, cost=COST):
-        sets = []
-        for head, boxes in ((MINE, kept), (TWIN, back)):
-            box = own_w[head, part]
-            (box[0],) = line.after(box[0])
-            two, three, one = (b[0] for b in boxes)
-            sets.append([box[0], one, two, three])
+    def run(head, part, weights, own):
         return line.reached(
-            *project(
-                at, part, own_x[0][0], None if own else [(i, start, box[0]) for i, start, box in pieces],
-                sets, b_qkv, qk_gain, NORMS[part], cost,
+            project(
+                at, head, part, own_x[0][0],
+                None if own else [(i, start, box[0]) for i, start, box in pieces],
+                [box[0] for box in weights], b_qkv, qk_gain,
             )
-        )
+        )[0]
 
     def send_edge(own, far):
         return to("seq", jnp.where(is_mid, own[0], far[0]), 2)
 
-    kv_kept, kv_back, q_kept, q_back = ([None] * 3 for _ in range(4))
     near0, near_c0, far0 = take(0)
-    swap(KV, 0, kv_kept, kv_back)
-    near1, near_c1, far1 = take(1)
-    swap(KV, 1, kv_kept, kv_back)
-    kv_back[0] = arrive(kv_back[0])
-    swap(KV, 2, kv_kept, kv_back)
-    (w,) = line.after(w)
-    spaced = line.reached(*cut_heads(at, w, [(TWIN, KV), (TWIN, Q)], SPACE))
-    own_w[TWIN, KV], own_w[TWIN, Q] = spaced
+    k_mine = arrive(arrived_k)
+    k_twin = to("groups", k_mine[0], 1)
     far0 = arrive(far0)
     far_c0 = to("head", far0[0], 1)
+    near1, near_c1, far1 = take(1)
+    (cuts[2][0],) = line.after(cuts[2][0])
+    arrived_v = exchange(cuts[2][0])
+    near_c0 = arrive(near_c0)
+    k_twin = arrive(k_twin)
+    v_mine = arrive(arrived_v)
+    v_twin = to("groups", v_mine[0], 1)
+    (cuts[0][0],) = line.after(cuts[0][0])
+    arrived_q = exchange(cuts[0][0])
+    line.drop(cuts[0], cuts[2])
+    own_mine = run(MINE, (1, 2), [k_mine, v_mine], True)
+    near_c1, far_c0 = arrive(near_c1), arrive(far_c0)
     far1 = arrive(far1)
     far_c1 = to("head", far1[0], 1)
     limits = own_limit + [arrive(far_limit)]
-    for which in range(3):
-        swap(Q, which, q_kept, q_back)
-    kv_back[1:] = [arrive(value) for value in kv_back[1:]]
-    own_mine, own_twin = run(KV, kv_kept, kv_back, True, SPACE1)
-    near_c0, far_c0, near_c1, far_c1 = line.reached(near_c0, far_c0, near_c1, far_c1)
+    far_c1 = arrive(far_c1)
     pieces = [(i, 0, box) for i, box in enumerate((near0, near_c0, far0, far_c0))]
     pieces += [(i, cutting[1], box) for i, box in enumerate((near1, near_c1, far1, far_c1))]
-    far_mine, far_twin = run(KV, kv_kept, kv_back, False, SPACE2)
+    far_mine = run(MINE, (1, 2), [k_mine, v_mine], False)
     halo_mine = send_edge(own_mine, far_mine)
+    v_twin = arrive(v_twin)
+    far_twin = run(TWIN, (1, 2), [k_twin, v_twin], False)
+    own_twin = run(TWIN, (1, 2), [k_twin, v_twin], True)
     halo_twin = send_edge(own_twin, far_twin)
-    line.drop(*kv_kept, *kv_back)
-    q_back = line.reached(*q_back)
-    q_own = run(Q, q_kept, q_back, True)
-    q_far = run(Q, q_kept, q_back, False)
-    line.drop(*q_kept, *q_back, *own_x, *(box for *_, box in pieces))
+    line.drop(k_mine, v_mine, k_twin, v_twin)
+    q_mine = arrive(arrived_q)
+    q_twin = to("groups", q_mine[0], 1)
+    queries = {0: [run(MINE, (0,), [q_mine], own) for own in (True, False)]}
+    line.drop(q_mine)
 
     def pair(h, rows):
+        (queries[h][0][0],) = line.after(queries[h][0][0])
         parts = attend_pair(
-            at, [b[0] for b in limits], [q_own[h][0], q_far[h][0]], [b[0] for b in rows]
+            at, [b[0] for b in limits], [b[0] for b in queries[h]], [b[0] for b in rows]
         )
         return line.reached(*parts)
 
     def finish(h, halo, parts):
         (halo,) = line.after(halo)
         keep, send = attend_halo(
-            at, [b[0] for b in limits], [q_own[h][0], q_far[h][0]], halo, *(b[0] for b in parts)
+            at, [b[0] for b in limits], [b[0] for b in queries[h]], halo, *(b[0] for b in parts)
         )
         return line.reached(keep)[0], to("seq", send, 1)
 
     parts_mine = pair(0, (own_mine, far_mine))
+    q_twin = arrive(q_twin)
+    queries[1] = [run(TWIN, (0,), [q_twin], own) for own in (True, False)]
+    line.drop(q_twin, *own_x, *(box for *_, box in pieces))
     keep_mine, back_mine = finish(0, halo_mine, parts_mine)
     line.drop(*parts_mine)
-    q_own[1][0], q_far[1][0] = line.after(q_own[1][0], q_far[1][0])
     parts_twin = pair(1, (own_twin, far_twin))
     back_mine = arrive(back_mine)
     keep_twin, back_twin = finish(1, halo_twin, parts_twin)

time: 163 us -> 177 us (1.086)
  Pallas kernels: 48.4 us -> 83.4 us
  local copies, waits for them, and re-layouts: 19.7 us -> 8.54 us
  waiting for transfers between devices: 58.7 us -> 48.7 us
    pallas_call x4 -> x8, Pallas kernels: 18.1 us -> 44.2 us  [project(): pl.pallas_call(kernel, grid=grid, in_specs=[smem, *x_specs, *(fixed(w.sha...]
    ppermute x25 -> x16, starting transfers between devices: 34.5 us -> 18.9 us  [to(): lax.ppermute(value, axis, [(i, i ^ bit) for i in range(lax.axis_size(axis...]
    all_to_all x0 -> x3, starting transfers between devices: none -> 14.8 us  [exchange(): return lax.all_to_all(value, 'seq', split_axis=0, concat_axis=0, tiled=True)]
    unnamed x84 -> x36, local copies, waits for them, and re-layouts: 17.3 us -> 5.64 us
    ppermute x25 -> x16, waiting for transfers between devices: 58.7 us -> 47.9 us  [to(): lax.ppermute(value, axis, [(i, i ^ bit) for i in range(lax.axis_size(axis...]
    pallas_call x2, Pallas kernels: 3.25 us -> 6.71 us  [attend_halo(): pl.pallas_call(kernel, in_specs=[smem, smem, smem] + [vmem] * 6, out_spec...]
    pallas_call x2, Pallas kernels: 9.93 us -> 13.4 us  [attend_pair(): pl.pallas_call(kernel, in_specs=[smem, smem, smem] + [vmem] * 4, out_spec...]
    pallas_call x2 -> x1, Pallas kernels: 1.4 us -> 3.49 us  [cut_heads(): pl.pallas_call(kernel, in_specs=[pl.BlockSpec(memory_space=pltpu.SMEM), p...]
  transfers between devices with their start and end apart: 25 -> 19, of which waited for: 9 -> 7; matrix products, arithmetic and copies ran while one was open for 0% -> 1% of each run, Pallas kernels for 28% -> 41%
where the time goes in v6:
time: 177 us; the launch traced here: 176 us
  Pallas kernels  83.4 us (47%)
  waiting for transfers between devices  48.7 us (28%)
  starting transfers between devices  33.8 us (19%)
  local copies, waits for them, and re-layouts  8.54 us (5%)
    ppermute x16, waiting for transfers between devices, to(): lax.ppermute(value, axis, [(i, i ^ bit) for i in range(lax.axis_size(axis...  47.9 us
    pallas_call x8, Pallas kernels, project(): pl.pallas_call(kernel, grid=grid, in_specs=[smem, *x_specs, *(fixed(w.sha...  44.2 us
    ppermute x16, starting transfers between devices, to(): lax.ppermute(value, axis, [(i, i ^ bit) for i in range(lax.axis_size(axis...  18.9 us
    all_to_all x3, starting transfers between devices, exchange(): return lax.all_to_all(value, 'seq', split_axis=0, concat_axis=0, tiled=True)  14.8 us
    pallas_call x2, Pallas kernels, attend_pair(): pl.pallas_call(kernel, in_specs=[smem, smem, smem] + [vmem] * 4, out_spec...  13.4 us
    pallas_call x3, Pallas kernels, normalize(): pl.pallas_call(norm_kernel, grid=(tokens // rows,), in_specs=[pl.BlockSpe...  12 us
    pallas_call x2, Pallas kernels, attend_halo(): pl.pallas_call(kernel, in_specs=[smem, smem, smem] + [vmem] * 6, out_spec...  6.71 us
    unnamed x36, local copies, waits for them, and re-layouts  5.64 us
  transfers between devices with their start and end apart: 19, of which 7 were waited for; matrix products, arithmetic and copies ran while one was open for 1% of the time, Pallas kernels for 41%

profile of v6, /device:TPU:0, one launch (start us, length us, event | category | flops | bytes accessed | tf_op | source)
XLA Modules:
  0.0 175.7 jit_solution(5714098049696506117)
XLA Ops:
  0.0 1.1 constant_dynamic-slice_fusion.1
  1.1 1.1 constant_dynamic-slice_fusion
  2.2 0.7 stack.35.at_ref.place_ref
  2.9 3.5 %cut_heads.1 = (bf16[4,768,128]{2,1,0:T(8,128)(2,1)}, bf16[4,768,128]{2,1,0:T(8,128)(2,1)}, bf16[4,768,128]{2,1,0:T(8,128)(2,1)}) custom-call(s32[8]{0:T(128)} %stack.35.at_ref.place_ref, bf16[3,768,512]{2,1,0:T(8,128)(2,1)} %bitcast.9), custom_call_target="tpu_custom_call" | custom-call | flops 1048576 | bytes 1024 | tf_op jit(solution)/shard_map/cut_heads/pallas_call | solution.py:145
  6.4 6.3 %all-to-all-start = ((bf16[4,768,128]{2,1,0:T(8,128)(2,1)}), bf16[4,768,128]{2,1,0:T(8,128)(2,1)}, u32[]{:S(2)}, u32[]{:S(2)}) async-start(bf16[4,768,128]{2,1,0:T(8,128)(2,1)} %get-tuple-element.267), calls=%async_computation | async-start | bytes 1572864 | tf_op jit(solution)/shard_map/all_to_all | solution.py:403
  12.7 2.0 %collective-permute-start.1 = (bf16[80,3072]{1,0:T(8,128)(2,1)S(1)}, bf16[80,3072]{1,0:T(8,128)(2,1)S(1)}, u32[]{:S(2)}, u32[]{:S(2)}) collective-permute-start(bf16[80,3072]{1,0:T(8,128)(2,1)S(1)} %constant_dynamic-slice_fusion), channel_id=1, source_target_pairs={{0,4},{4,0},{8,12},{12,8},{1,5},{5,1},{9,13},{13,9},{2,6},{6,2},{1... | collective-permute-start | bytes 1474568 | tf_op jit(solution)/shard_map/ppermute | solution.py:382
  14.8 1.4 see.1.limit0_ref
  16.1 7.3 %normalize.3.refs_0_ = bf16[768,3072]{1,0:T(8,128)(2,1)} custom-call(bf16[768,3072]{1,0:T(8,128)(2,1)} %x_ref, f32[2,3072]{1,0:T(2,128)} %mod_ref.2), custom_call_target="tpu_custom_call" | custom-call | flops 1048576 | bytes 1024 | tf_op jit(solution)/shard_map/normalize/pallas_call | solution.py:121
  23.5 16.2 %collective-permute-done.1.x_ref = bf16[80,3072]{1,0:T(8,128)(2,1)S(1)} collective-permute-done((bf16[80,3072]{1,0:T(8,128)(2,1)S(1)}, bf16[80,3072]{1,0:T(8,128)(2,1)S(1)}, u32[]{:S(2)}, u32[]{:S(2)}) %collective-permute-start.1) | collective-permute-done | bytes 491552 | tf_op jit(solution)/shard_map/ppermute | solution.py:382
  39.7 0.8 copy-done.11
  40.5 2.2 %normalize.4.refs_0_ = bf16[80,3072]{1,0:T(8,128)(2,1)} custom-call(bf16[80,3072]{1,0:T(8,128)(2,1)} %copy-done.11, f32[2,3072]{1,0:T(2,128)} %mod_ref.2), custom_call_target="tpu_custom_call" | custom-call | flops 1048576 | bytes 1024 | tf_op jit(solution)/shard_map/normalize/pallas_call | solution.py:121
  42.7 1.5 collective-permute-start.2
  44.2 9.0 %collective-permute-done.2.refs_2_ = bf16[80,3072]{1,0:T(8,128)(2,1)S(1)} collective-permute-done((bf16[80,3072]{1,0:T(8,128)(2,1)}, bf16[80,3072]{1,0:T(8,128)(2,1)S(1)}, u32[]{:S(2)}, u32[]{:S(2)}) %collective-permute-start.2) | collective-permute-done | bytes 491552 | tf_op jit(solution)/shard_map/ppermute | solution.py:382
  53.2 0.9 copy-done.10
  54.1 2.4 %normalize.5.refs_4_ = bf16[112,3072]{1,0:T(8,128)(2,1)} custom-call(bf16[112,3072]{1,0:T(8,128)(2,1)} %copy-done.10, f32[2,3072]{1,0:T(2,128)} %mod_ref.2), custom_call_target="tpu_custom_call" | custom-call | flops 1048576 | bytes 1024 | tf_op jit(solution)/shard_map/normalize/pallas_call | solution.py:121
  56.6 4.3 %all-to-all-start.1 = ((bf16[4,768,128]{2,1,0:T(8,128)(2,1)}), bf16[4,768,128]{2,1,0:T(8,128)(2,1)}, u32[]{:S(2)}, u32[]{:S(2)}) async-start(bf16[4,768,128]{2,1,0:T(8,128)(2,1)} %get-tuple-element.300), calls=%async_computation.1 | async-start | bytes 1572864 | tf_op jit(solution)/shard_map/all_to_all | solution.py:403
  60.9 1.6 collective-permute-start.3
  63.0 1.5 collective-permute-start.6
  64.6 14.5 %collective-permute-done.3.refs_1_.refs_8_ = bf16[4,768,128]{2,1,0:T(8,128)(2,1)} collective-permute-done((bf16[4,768,128]{2,1,0:T(8,128)(2,1)}, bf16[4,768,128]{2,1,0:T(8,128)(2,1)}, u32[]{:S(2)}, u32[]{:S(2)}) %collective-permute-start.3) | collective-permute-done | bytes 786464 | tf_op jit(solution)/shard_map/ppermute | solution.py:382
  79.1 0.8 all-to-all-done.1.refs_2_.refs_9_
  79.9 4.2 %all-to-all-start.2 = ((bf16[4,768,128]{2,1,0:T(8,128)(2,1)}), bf16[4,768,128]{2,1,0:T(8,128)(2,1)}, u32[]{:S(2)}, u32[]{:S(2)}) async-start(bf16[4,768,128]{2,1,0:T(8,128)(2,1)} %get-tuple-element.420), calls=%async_computation.2 | async-start | bytes 1572864 | tf_op jit(solution)/shard_map/all_to_all | solution.py:403
  84.1 1.6 collective-permute-start.5
  85.6 5.3 %project.8.rows0_ref = bf16[768,256]{1,0:T(8,128)(2,1)} custom-call(s32[8]{0:T(128)} %stack.35.at_ref.place_ref, bf16[768,3072]{1,0:T(8,128)(2,1)} %normalize.3.refs_0_, bf16[4,768,128]{2,1,0:T(8,128)(2,1)} %all-to-all-done.refs_1_.refs_8_, bf16[4,768,128]{2,1,0:T(8,128)(2,1)} %all-to-all-done.1.refs_2_.refs_9_, f32[3,512]{1,0:T(4,128)} %refs_9_.3, ...), custom_call_target="tpu_custom_call" | custom-call | flops 1048576 | bytes 1024 | tf_op jit(solution)/shard_map/project/pallas_call | solution.py:238
  91.1 2.0 %collective-permute-start.10 = (f32[2,128]{1,0:T(2,128)S(1)}, f32[2,128]{1,0:T(2,128)S(1)}, u32[]{:S(2)}, u32[]{:S(2)}) collective-permute-start(f32[2,128]{1,0:T(2,128)S(1)} %copy-done.16), channel_id=1, source_target_pairs={{0,4},{4,0},{8,12},{12,8},{1,5},{5,1},{9,13},{13,9},{2,6},{6,2},{1... | collective-permute-start | bytes 3080 | tf_op jit(solution)/shard_map/ppermute | solution.py:382
  93.1 3.4 %collective-permute-done.10.limit1_ref = f32[2,128]{1,0:T(2,128)S(1)} collective-permute-done((f32[2,128]{1,0:T(2,128)S(1)}, f32[2,128]{1,0:T(2,128)S(1)}, u32[]{:S(2)}, u32[]{:S(2)}) %collective-permute-start.10) | collective-permute-done | bytes 1056 | tf_op jit(solution)/shard_map/ppermute | solution.py:382
  96.5 0.8 copy-done.2
  97.4 6.0 %project.9.rows1_ref = bf16[768,256]{1,0:T(8,128)(2,1)} custom-call(s32[8]{0:T(128)} %stack.35.at_ref.place_ref, bf16[80,3072]{1,0:T(8,128)(2,1)} %normalize.4.refs_0_, bf16[80,3072]{1,0:T(8,128)(2,1)} %copy-done.4, bf16[80,3072]{1,0:T(8,128)(2,1)} %copy-done.3, bf16[80,3072]{1,0:T(8,128)(2,1)} %copy-done.5, bf16[112,3072]{1,0:T(8,128)(2,1)} %normalize.5.refs_4_, ...), custom_call_target="tpu_custom_call" | custom-call | flops 1048576 | bytes 1024 | tf_op jit(solution)/shard_map/project/pallas_call | solution.py:238
  103.4 5.3 %project.10.rows0_ref = bf16[768,256]{1,0:T(8,128)(2,1)} custom-call(s32[8]{0:T(128)} %stack.35.at_ref.place_ref, bf16[768,3072]{1,0:T(8,128)(2,1)} %normalize.3.refs_0_, bf16[4,768,128]{2,1,0:T(8,128)(2,1)} %collective-permute-done.3.refs_1_.refs_8_, bf16[4,768,128]{2,1,0:T(8,128)(2,1)} %collective-permute-done.5.refs_2_.refs_9_, f32[3,512]{1,0:T(4,128)} %refs_9_.3, ...), custom_call_target="tpu_custom_call" | custom-call | flops 1048576 | bytes 1024 | tf_op jit(solution)/shard_map/project/pallas_call | solution.py:238
  108.7 6.1 %project.11.rows1_ref = bf16[768,256]{1,0:T(8,128)(2,1)} custom-call(s32[8]{0:T(128)} %stack.35.at_ref.place_ref, bf16[80,3072]{1,0:T(8,128)(2,1)} %normalize.4.refs_0_, bf16[80,3072]{1,0:T(8,128)(2,1)} %copy-done.4, bf16[80,3072]{1,0:T(8,128)(2,1)} %copy-done.3, bf16[80,3072]{1,0:T(8,128)(2,1)} %copy-done.5, bf16[112,3072]{1,0:T(8,128)(2,1)} %normalize.5.refs_4_, ...), custom_call_target="tpu_custom_call" | custom-call | flops 1048576 | bytes 1024 | tf_op jit(solution)/shard_map/project/pallas_call | solution.py:238
  114.8 1.6 collective-permute-start.13
  116.5 4.5 %collective-permute-start.12 = (bf16[768,256]{1,0:T(8,128)(2,1)S(1)}, bf16[768,256]{1,0:T(8,128)(2,1)S(1)}, u32[]{:S(2)}, u32[]{:S(2)}) collective-permute-start(bf16[768,256]{1,0:T(8,128)(2,1)S(1)} %broadcast_select_fusion), channel_id=1, source_target_pairs={{0,8},{4,12},{8,0},{12,4},{1,9},{5,13},{9,1},{13,5},{2,10},{6,14},... | collective-permute-start | bytes 1179656 | tf_op jit(solution)/shard_map/ppermute | solution.py:382
  121.0 1.0 broadcast_select_fusion.1
  122.1 5.0 %project.12.q0_ref = bf16[768,128]{1,0:T(8,128)(2,1)} custom-call(s32[8]{0:T(128)} %stack.35.at_ref.place_ref, bf16[768,3072]{1,0:T(8,128)(2,1)} %normalize.3.refs_0_, bf16[4,768,128]{2,1,0:T(8,128)(2,1)} %all-to-all-done.2.refs_1_.refs_8_, f32[3,512]{1,0:T(4,128)} %refs_9_.3, f32[2,128]{1,0:T(2,128)} %refs_10_.7), custom_call_target="tpu_custom_call" | custom-call | flops 1048576 | bytes 1024 | tf_op jit(solution)/shard_map/project/pallas_call | solution.py:238
  127.1 5.7 %project.13.q1_ref = bf16[768,128]{1,0:T(8,128)(2,1)} custom-call(s32[8]{0:T(128)} %stack.35.at_ref.place_ref, bf16[80,3072]{1,0:T(8,128)(2,1)} %normalize.4.refs_0_, bf16[80,3072]{1,0:T(8,128)(2,1)} %copy-done.4, bf16[80,3072]{1,0:T(8,128)(2,1)} %copy-done.3, bf16[80,3072]{1,0:T(8,128)(2,1)} %copy-done.5, bf16[112,3072]{1,0:T(8,128)(2,1)} %normalize.5.refs_4_, ...), custom_call_target="tpu_custom_call" | custom-call | flops 1048576 | bytes 1024 | tf_op jit(solution)/shard_map/project/pallas_call | solution.py:238
  132.9 6.8 %attend_pair.2 = (bf16[768,128]{1,0:T(8,128)(2,1)}, f32[768,128]{1,0:T(8,128)}, f32[768,128]{1,0:T(8,128)}) custom-call(s32[8]{0:T(128)} %stack.35.at_ref.place_ref, f32[2,128]{1,0:T(2,128)} %see.1.limit0_ref, f32[2,128]{1,0:T(2,128)} %copy-done.17, bf16[768,128]{1,0:T(8,128)(2,1)} %project.12.q0_ref, bf16[768,128]{1,0:T(8,128)(2,1)} %project.13.q1_ref, ...), custom_call_target="tpu_custom_call" | custom-call | flops 1048576 | bytes 1024 | tf_op jit(solution)/shard_map/attend_pair/pallas_call | solution.py:301
  139.6 0.9 copy-done.9
  140.5 5.0 %project.14.q0_ref = bf16[768,128]{1,0:T(8,128)(2,1)} custom-call(s32[8]{0:T(128)} %stack.35.at_ref.place_ref, bf16[768,3072]{1,0:T(8,128)(2,1)} %normalize.3.refs_0_, bf16[4,768,128]{2,1,0:T(8,128)(2,1)} %copy-done.9, f32[3,512]{1,0:T(4,128)} %refs_9_.3, f32[2,128]{1,0:T(2,128)} %refs_10_.7), custom_call_target="tpu_custom_call" | custom-call | flops 1048576 | bytes 1024 | tf_op jit(solution)/shard_map/project/pallas_call | solution.py:238
  145.5 5.7 %project.15.q1_ref = bf16[768,128]{1,0:T(8,128)(2,1)} custom-call(s32[8]{0:T(128)} %stack.35.at_ref.place_ref, bf16[80,3072]{1,0:T(8,128)(2,1)} %normalize.4.refs_0_, bf16[80,3072]{1,0:T(8,128)(2,1)} %copy-done.4, bf16[80,3072]{1,0:T(8,128)(2,1)} %copy-done.3, bf16[80,3072]{1,0:T(8,128)(2,1)} %copy-done.5, bf16[112,3072]{1,0:T(8,128)(2,1)} %normalize.5.refs_4_, ...), custom_call_target="tpu_custom_call" | custom-call | flops 1048576 | bytes 1024 | tf_op jit(solution)/shard_map/project/pallas_call | solution.py:238
  151.3 0.7 copy-done.13
  152.0 3.4 %attend_halo.2 = (bf16[768,128]{1,0:T(8,128)(2,1)}, bf16[768,128]{1,0:T(8,128)(2,1)}) custom-call(s32[8]{0:T(128)} %stack.35.at_ref.place_ref, f32[2,128]{1,0:T(2,128)} %see.1.limit0_ref, f32[2,128]{1,0:T(2,128)} %copy-done.17, bf16[768,128]{1,0:T(8,128)(2,1)} %project.12.q0_ref, bf16[768,128]{1,0:T(8,128)(2,1)} %project.13.q1_ref, ...), custom_call_target="tpu_custom_call" | custom-call | flops 1048576 | bytes 1024 | tf_op jit(solution)/shard_map/attend_halo/pallas_call | solution.py:338
  155.3 0.8 collective-permute-start.14
  156.1 6.6 %attend_pair.3 = (bf16[768,128]{1,0:T(8,128)(2,1)}, f32[768,128]{1,0:T(8,128)}, f32[768,128]{1,0:T(8,128)}) custom-call(s32[8]{0:T(128)} %stack.35.at_ref.place_ref, f32[2,128]{1,0:T(2,128)} %see.1.limit0_ref, f32[2,128]{1,0:T(2,128)} %copy-done.17, bf16[768,128]{1,0:T(8,128)(2,1)} %project.14.q0_ref, bf16[768,128]{1,0:T(8,128)(2,1)} %project.15.q1_ref, ...), custom_call_target="tpu_custom_call" | custom-call | flops 1048576 | bytes 1024 | tf_op jit(solution)/shard_map/attend_pair/pallas_call | solution.py:301
  162.8 0.8 copy-done.12
  163.5 3.3 %attend_halo.3 = (bf16[768,128]{1,0:T(8,128)(2,1)}, bf16[768,128]{1,0:T(8,128)(2,1)}) custom-call(s32[8]{0:T(128)} %stack.35.at_ref.place_ref, f32[2,128]{1,0:T(2,128)} %see.1.limit0_ref, f32[2,128]{1,0:T(2,128)} %copy-done.17, bf16[768,128]{1,0:T(8,128)(2,1)} %project.14.q0_ref, bf16[768,128]{1,0:T(8,128)(2,1)} %project.15.q1_ref, ...), custom_call_target="tpu_custom_call" | custom-call | flops 1048576 | bytes 1024 | tf_op jit(solution)/shard_map/attend_halo/pallas_call | solution.py:338
  166.9 1.2 collective-permute-start.15
  168.1 4.7 %collective-permute-done.15.refs_3_ = bf16[768,128]{1,0:T(8,128)(2,1)S(1)} collective-permute-done((bf16[768,128]{1,0:T(8,128)(2,1)}, bf16[768,128]{1,0:T(8,128)(2,1)S(1)}, u32[]{:S(2)}, u32[]{:S(2)}) %collective-permute-start.15) | collective-permute-done | bytes 196640 | tf_op jit(solution)/shard_map/ppermute | solution.py:382
  172.8 0.7 copy-done.15
  173.5 2.2 %assemble.1 = bf16[768,512]{1,0:T(8,128)(2,1)} custom-call(s32[8]{0:T(128)} %stack.35.at_ref.place_ref, bf16[768,128]{1,0:T(8,128)(2,1)} %get-tuple-element.513.refs_0_, bf16[768,128]{1,0:T(8,128)(2,1)} %get-tuple-element.522.refs_1_, bf16[768,128]{1,0:T(8,128)(2,1)} %copy-done.14, bf16[768,128]{1,0:T(8,128)(2,1)} %copy-done.15), custom_call_target="tpu_custom_call" | custom-call | flops 1048576 | bytes 1024 | tf_op jit(solution)/shard_map/assemble/pallas_call | solution.py:358
  (49 shorter events, 0.9 us)
Async XLA Ops:
  6.4 37.8 %all-to-all-start = ((bf16[4,768,128]{2,1,0:T(8,128)(2,1)}), bf16[4,768,128]{2,1,0:T(8,128)(2,1)}, u32[]{:S(2)}, u32[]{:S(2)}) async-start(bf16[4,768,128]{2,1,0:T(8,128)(2,1)} %get-tuple-element.267), calls=%async_computation | async-start | bytes 1572864 | tf_op jit(solution)/shard_map/all_to_all | solution.py:403
  12.7 27.0 %collective-permute-start.1 = (bf16[80,3072]{1,0:T(8,128)(2,1)S(1)}, bf16[80,3072]{1,0:T(8,128)(2,1)S(1)}, u32[]{:S(2)}, u32[]{:S(2)}) collective-permute-start(bf16[80,3072]{1,0:T(8,128)(2,1)S(1)} %constant_dynamic-slice_fusion), channel_id=1, source_target_pairs={{0,4},{4,0},{8,12},{12,8},{1,5},{5,1},{9,13},{13,9},{2,6},{6,2},{1... | collective-permute-start | bytes 1474568 | tf_op jit(solution)/shard_map/ppermute | solution.py:382
  14.7 38.5 %collective-permute-start = (bf16[112,3072]{1,0:T(8,128)(2,1)S(1)}, bf16[112,3072]{1,0:T(8,128)(2,1)S(1)}, u32[]{:S(2)}, u32[]{:S(2)}) collective-permute-start(bf16[112,3072]{1,0:T(8,128)(2,1)S(1)} %constant_dynamic-slice_fusion.1), channel_id=1, source_target_pairs={{0,4},{4,0},{8,12},{12,8},{1,5},{5,1},{9,13},{13,9},{2,6},{6,2},{1... | collective-permute-start | bytes 2064392 | tf_op jit(solution)/shard_map/ppermute | solution.py:382
  39.7 0.8 copy-start.11
  42.7 10.5 %collective-permute-start.2 = (bf16[80,3072]{1,0:T(8,128)(2,1)}, bf16[80,3072]{1,0:T(8,128)(2,1)S(1)}, u32[]{:S(2)}, u32[]{:S(2)}) collective-permute-start(bf16[80,3072]{1,0:T(8,128)(2,1)} %normalize.4.refs_0_), channel_id=1, source_target_pairs={{0,2},{2,0},{1,3},{3,1},{4,6},{6,4},{5,7},{7,5},{8,10},{10,8},{9,1... | collective-permute-start | bytes 1474568 | tf_op jit(solution)/shard_map/ppermute | solution.py:382
  53.2 37.7 %copy-start.3 = (bf16[80,3072]{1,0:T(8,128)(2,1)}, bf16[80,3072]{1,0:T(8,128)(2,1)S(1)}, u32[]{:S(2)}) copy-start(bf16[80,3072]{1,0:T(8,128)(2,1)S(1)} %collective-permute-done.2.refs_2_) | copy-start | bytes 1474564
  53.2 0.9 copy-start.10
  56.6 34.5 %copy-start.16 = (f32[2,128]{1,0:T(2,128)S(1)}, f32[2,128]{1,0:T(2,128)}, u32[]{:S(2)}) copy-start(f32[2,128]{1,0:T(2,128)} %see.1.limit0_ref) | copy-start | bytes 3076
  56.6 23.3 %all-to-all-start.1 = ((bf16[4,768,128]{2,1,0:T(8,128)(2,1)}), bf16[4,768,128]{2,1,0:T(8,128)(2,1)}, u32[]{:S(2)}, u32[]{:S(2)}) async-start(bf16[4,768,128]{2,1,0:T(8,128)(2,1)} %get-tuple-element.300), calls=%async_computation.1 | async-start | bytes 1572864 | tf_op jit(solution)/shard_map/all_to_all | solution.py:403
  60.9 18.2 %collective-permute-start.3 = (bf16[4,768,128]{2,1,0:T(8,128)(2,1)}, bf16[4,768,128]{2,1,0:T(8,128)(2,1)}, u32[]{:S(2)}, u32[]{:S(2)}) collective-permute-start(bf16[4,768,128]{2,1,0:T(8,128)(2,1)} %all-to-all-done.refs_1_.refs_8_), channel_id=1, source_target_pairs={{0,16},{16,0},{1,17},{17,1},{2,18},{18,2},{3,19},{19,3},{4,20},{20... | collective-permute-start | bytes 2359304 | tf_op jit(solution)/shard_map/ppermute | solution.py:382
  62.5 2.1 %collective-permute-start.4 = (bf16[80,3072]{1,0:T(8,128)(2,1)}, bf16[80,3072]{1,0:T(8,128)(2,1)S(1)}, u32[]{:S(2)}, u32[]{:S(2)}) collective-permute-start(bf16[80,3072]{1,0:T(8,128)(2,1)} %normalize.4.refs_0_), channel_id=1, source_target_pairs={{0,1},{1,0},{2,3},{3,2},{4,5},{5,4},{6,7},{7,6},{8,9},{9,8},{10,11... | collective-permute-start | bytes 1474568 | tf_op jit(solution)/shard_map/ppermute | solution.py:382
  62.5 28.5 %collective-permute-start.8 = (bf16[112,3072]{1,0:T(8,128)(2,1)}, bf16[112,3072]{1,0:T(8,128)(2,1)S(1)}, u32[]{:S(2)}, u32[]{:S(2)}) collective-permute-start(bf16[112,3072]{1,0:T(8,128)(2,1)} %normalize.5.refs_4_), channel_id=1, source_target_pairs={{0,1},{1,0},{2,3},{3,2},{4,5},{5,4},{6,7},{7,6},{8,9},{9,8},{10,11... | collective-permute-start | bytes 2064392 | tf_op jit(solution)/shard_map/ppermute | solution.py:382
  63.0 28.0 %collective-permute-start.6 = (bf16[112,3072]{1,0:T(8,128)(2,1)}, bf16[112,3072]{1,0:T(8,128)(2,1)S(1)}, u32[]{:S(2)}, u32[]{:S(2)}) collective-permute-start(bf16[112,3072]{1,0:T(8,128)(2,1)} %normalize.5.refs_4_), channel_id=1, source_target_pairs={{0,2},{2,0},{1,3},{3,1},{4,6},{6,4},{5,7},{7,5},{8,10},{10,8},{9,1... | collective-permute-start | bytes 2064392 | tf_op jit(solution)/shard_map/ppermute | solution.py:382
  64.5 26.5 %collective-permute-start.7 = (bf16[80,3072]{1,0:T(8,128)(2,1)S(1)}, bf16[80,3072]{1,0:T(8,128)(2,1)S(1)}, u32[]{:S(2)}, u32[]{:S(2)}) collective-permute-start(bf16[80,3072]{1,0:T(8,128)(2,1)S(1)} %collective-permute-done.2.refs_2_), channel_id=1, source_target_pairs={{0,1},{1,0},{2,3},{3,2},{4,5},{5,4},{6,7},{7,6},{8,9},{9,8},{10,11... | collective-permute-start | bytes 1474568 | tf_op jit(solution)/shard_map/ppermute | solution.py:382
  64.6 31.9 %copy-start.4 = (bf16[80,3072]{1,0:T(8,128)(2,1)}, bf16[80,3072]{1,0:T(8,128)(2,1)S(1)}, u32[]{:S(2)}) copy-start(bf16[80,3072]{1,0:T(8,128)(2,1)S(1)} %collective-permute-done.4.refs_1_) | copy-start | bytes 1474564
  79.9 35.0 %all-to-all-start.2 = ((bf16[4,768,128]{2,1,0:T(8,128)(2,1)}), bf16[4,768,128]{2,1,0:T(8,128)(2,1)}, u32[]{:S(2)}, u32[]{:S(2)}) async-start(bf16[4,768,128]{2,1,0:T(8,128)(2,1)} %get-tuple-element.420), calls=%async_computation.2 | async-start | bytes 1572864 | tf_op jit(solution)/shard_map/all_to_all | solution.py:403
  84.1 19.3 %collective-permute-start.5 = (bf16[4,768,128]{2,1,0:T(8,128)(2,1)}, bf16[4,768,128]{2,1,0:T(8,128)(2,1)}, u32[]{:S(2)}, u32[]{:S(2)}) collective-permute-start(bf16[4,768,128]{2,1,0:T(8,128)(2,1)} %all-to-all-done.1.refs_2_.refs_9_), channel_id=1, source_target_pairs={{0,16},{16,0},{1,17},{17,1},{2,18},{18,2},{3,19},{19,3},{4,20},{20... | collective-permute-start | bytes 2359304 | tf_op jit(solution)/shard_map/ppermute | solution.py:382
  91.0 5.5 %copy-start = (bf16[112,3072]{1,0:T(8,128)(2,1)}, bf16[112,3072]{1,0:T(8,128)(2,1)S(1)}, u32[]{:S(2)}) copy-start(bf16[112,3072]{1,0:T(8,128)(2,1)S(1)} %collective-permute-done.8.refs_5_) | copy-start | bytes 2064388
  91.0 5.5 %copy-start.5 = (bf16[80,3072]{1,0:T(8,128)(2,1)}, bf16[80,3072]{1,0:T(8,128)(2,1)S(1)}, u32[]{:S(2)}) copy-start(bf16[80,3072]{1,0:T(8,128)(2,1)S(1)} %collective-permute-done.7.refs_3_) | copy-start | bytes 1474564
  91.0 5.5 %copy-start.1 = (bf16[112,3072]{1,0:T(8,128)(2,1)}, bf16[112,3072]{1,0:T(8,128)(2,1)S(1)}, u32[]{:S(2)}) copy-start(bf16[112,3072]{1,0:T(8,128)(2,1)S(1)} %collective-permute-done.6.refs_6_) | copy-start | bytes 2064388
  91.0 5.5 %collective-permute-start.9 = (bf16[112,3072]{1,0:T(8,128)(2,1)S(1)}, bf16[112,3072]{1,0:T(8,128)(2,1)S(1)}, u32[]{:S(2)}, u32[]{:S(2)}) collective-permute-start(bf16[112,3072]{1,0:T(8,128)(2,1)S(1)} %collective-permute-done.6.refs_6_), channel_id=1, source_target_pairs={{0,1},{1,0},{2,3},{3,2},{4,5},{5,4},{6,7},{7,6},{8,9},{9,8},{10,11... | collective-permute-start | bytes 2064392 | tf_op jit(solution)/shard_map/ppermute | solution.py:382
  91.1 5.4 %collective-permute-start.10 = (f32[2,128]{1,0:T(2,128)S(1)}, f32[2,128]{1,0:T(2,128)S(1)}, u32[]{:S(2)}, u32[]{:S(2)}) collective-permute-start(f32[2,128]{1,0:T(2,128)S(1)} %copy-done.16), channel_id=1, source_target_pairs={{0,4},{4,0},{8,12},{12,8},{1,5},{5,1},{9,13},{13,9},{2,6},{6,2},{1... | collective-permute-start | bytes 3080 | tf_op jit(solution)/shard_map/ppermute | solution.py:382
  96.5 36.4 %copy-start.17 = (f32[2,128]{1,0:T(2,128)}, f32[2,128]{1,0:T(2,128)S(1)}, u32[]{:S(2)}) copy-start(f32[2,128]{1,0:T(2,128)S(1)} %collective-permute-done.10.limit1_ref) | copy-start | bytes 3076
  96.5 0.8 copy-start.2
  108.7 7.7 %copy-start.7 = (bf16[768,256]{1,0:T(8,128)(2,1)S(1)}, bf16[768,256]{1,0:T(8,128)(2,1)}, u32[]{:S(2)}) copy-start(bf16[768,256]{1,0:T(8,128)(2,1)} %project.8.rows0_ref) | copy-start | bytes 1179652
  108.7 7.7 %copy-start.8 = (bf16[768,256]{1,0:T(8,128)(2,1)S(1)}, bf16[768,256]{1,0:T(8,128)(2,1)}, u32[]{:S(2)}) copy-start(bf16[768,256]{1,0:T(8,128)(2,1)} %project.9.rows1_ref) | copy-start | bytes 1179652
  108.7 12.3 %copy-start.6 = (bf16[768,256]{1,0:T(8,128)(2,1)S(1)}, bf16[768,256]{1,0:T(8,128)(2,1)}, u32[]{:S(2)}) copy-start(bf16[768,256]{1,0:T(8,128)(2,1)} %project.10.rows0_ref) | copy-start | bytes 1179652
  114.8 24.8 %collective-permute-start.13 = (bf16[4,768,128]{2,1,0:T(8,128)(2,1)}, bf16[4,768,128]{2,1,0:T(8,128)(2,1)S(1)}, u32[]{:S(2)}, u32[]{:S(2)}) collective-permute-start(bf16[4,768,128]{2,1,0:T(8,128)(2,1)} %all-to-all-done.2.refs_1_.refs_8_), channel_id=1, source_target_pairs={{0,16},{16,0},{1,17},{17,1},{2,18},{18,2},{3,19},{19,3},{4,20},{20... | collective-permute-start | bytes 2359304 | tf_op jit(solution)/shard_map/ppermute | solution.py:382
  116.5 34.8 %collective-permute-start.12 = (bf16[768,256]{1,0:T(8,128)(2,1)S(1)}, bf16[768,256]{1,0:T(8,128)(2,1)S(1)}, u32[]{:S(2)}, u32[]{:S(2)}) collective-permute-start(bf16[768,256]{1,0:T(8,128)(2,1)S(1)} %broadcast_select_fusion), channel_id=1, source_target_pairs={{0,8},{4,12},{8,0},{12,4},{1,9},{5,13},{9,1},{13,5},{2,10},{6,14},... | collective-permute-start | bytes 1179656 | tf_op jit(solution)/shard_map/ppermute | solution.py:382
  122.0 40.7 %collective-permute-start.11 = (bf16[768,256]{1,0:T(8,128)(2,1)S(1)}, bf16[768,256]{1,0:T(8,128)(2,1)S(1)}, u32[]{:S(2)}, u32[]{:S(2)}) collective-permute-start(bf16[768,256]{1,0:T(8,128)(2,1)S(1)} %broadcast_select_fusion.1), channel_id=1, source_target_pairs={{0,8},{4,12},{8,0},{12,4},{1,9},{5,13},{9,1},{13,5},{2,10},{6,14},... | collective-permute-start | bytes 1179656 | tf_op jit(solution)/shard_map/ppermute | solution.py:382
  139.6 0.9 copy-start.9
  151.2 0.7 copy-start.13
  155.3 7.4 %collective-permute-start.14 = (bf16[768,128]{1,0:T(8,128)(2,1)}, bf16[768,128]{1,0:T(8,128)(2,1)S(1)}, u32[]{:S(2)}, u32[]{:S(2)}) collective-permute-start(bf16[768,128]{1,0:T(8,128)(2,1)} %get-tuple-element.488), channel_id=1, source_target_pairs={{0,4},{4,0},{8,12},{12,8},{1,5},{5,1},{9,13},{13,9},{2,6},{6,2},{1... | collective-permute-start | bytes 589832 | tf_op jit(solution)/shard_map/ppermute | solution.py:382
  162.7 10.0 %copy-start.14 = (bf16[768,128]{1,0:T(8,128)(2,1)}, bf16[768,128]{1,0:T(8,128)(2,1)S(1)}, u32[]{:S(2)}) copy-start(bf16[768,128]{1,0:T(8,128)(2,1)S(1)} %collective-permute-done.14.refs_2_) | copy-start | bytes 589828
  162.8 0.8 copy-start.12
  166.9 5.9 %collective-permute-start.15 = (bf16[768,128]{1,0:T(8,128)(2,1)}, bf16[768,128]{1,0:T(8,128)(2,1)S(1)}, u32[]{:S(2)}, u32[]{:S(2)}) collective-permute-start(bf16[768,128]{1,0:T(8,128)(2,1)} %get-tuple-element.524), channel_id=1, source_target_pairs={{0,4},{4,0},{8,12},{12,8},{1,5},{5,1},{9,13},{13,9},{2,6},{6,2},{1... | collective-permute-start | bytes 589832 | tf_op jit(solution)/shard_map/ppermute | solution.py:382
  172.8 0.7 copy-start.15

commit v7 on v6

--- a/solution.py
+++ b/solution.py
@@ -8,8 +8,10 @@
 from jax.sharding import PartitionSpec as P
 
 EPS = 1e-06
-VMEM = 60 << 20
+VMEM = 28 << 20
+FIRST = 8
 HIDDEN = -1e30
+SPACE = pl.CostEstimate(flops=1 << 36, bytes_accessed=1 << 10, transcendentals=0)
 COST = pl.CostEstimate(flops=1 << 20, bytes_accessed=1 << 10, transcendentals=0)
 
 
@@ -132,23 +134,25 @@
     )(frames, modulation)
 
 
-def cut_heads(at, w):
+def cut_heads(at, w, groups, cost=None):
     rows = w.shape[1]
     head_dim = 128
+    shapes = [(len(indices), rows, head_dim * len(js)) for indices, js in groups]
 
     def kernel(at_ref, w_ref, *out_refs):
-        for j, ref in enumerate(out_refs):
-            for target in range(4):
-                cols = pl.ds(pl.multiple_of(at_ref[6 + target % 2] * head_dim, 128), head_dim)
-                ref[target] = w_ref[j, :, cols]
+        for (indices, js), ref in zip(groups, out_refs):
+            for n, index in enumerate(indices):
+                cols = pl.ds(pl.multiple_of(at_ref[index] * head_dim, 128), head_dim)
+                for i, j in enumerate(js):
+                    ref[n, :, i * head_dim : (i + 1) * head_dim] = w_ref[j, :, cols]
 
     return pl.pallas_call(
         kernel,
         in_specs=[pl.BlockSpec(memory_space=pltpu.SMEM), pl.BlockSpec()],
-        out_specs=[pl.BlockSpec()] * 3,
-        out_shape=[jax.ShapeDtypeStruct((4, rows, head_dim), jnp.bfloat16)] * 3,
+        out_specs=[pl.BlockSpec()] * len(groups),
+        out_shape=[jax.ShapeDtypeStruct(shape, jnp.bfloat16) for shape in shapes],
         compiler_params=pltpu.CompilerParams(vmem_limit_bytes=VMEM),
-        cost_estimate=COST,
+        cost_estimate=cost or COST,
         name="cut_heads",
     )(at, w)
 
@@ -176,47 +180,63 @@
     )(at, lists)
 
 
-def project(at, head, part, source, pieces, weights, bias, gain):
-    shards, rows, head_dim = weights[0].shape
-    cols = head_dim * len(part)
-    sources = [source] if pieces is None else [piece for _, _, piece in pieces]
+def project(at, part, source, pieces, weights, bias, gain, cost=None):
+    *_, rows, cols = weights[0][0].shape
+    head_dim = gain.shape[1]
+    sources = [source] if pieces is None else [array for array, _ in pieces]
     tokens = sum(piece.shape[0] for piece in sources)
     width = sources[0].shape[1]
     count = len(sources)
+    each = len(weights[0])
     step = 256
 
     def kernel(at_ref, *refs):
-        x_refs, weight_refs = refs[:count], refs[count : count + len(part)]
-        b_ref, g_ref, out_ref = refs[count + len(part) : count + len(part) + 3]
-        here = pl.ds(pl.multiple_of(at_ref[head] * head_dim, 128), head_dim)
+        x_refs, flat = refs[:count], refs[count : count + 2 * each]
+        weight_refs = (flat[:each], flat[each:])
+        b_ref, g_ref, *out_refs = refs[count + 2 * each : count + 2 * each + 4]
+        z, q = at_ref[0], at_ref[1]
 
         def block(ref, row):
             total = None
-            for s in range(shards):
-                w = jnp.concatenate([ref[s] for ref in weight_refs], axis=1)
-                x = ref[row : row + step, s * rows : (s + 1) * rows]
-                product = jnp.dot(x, w, preferred_element_type=jnp.float32)
+            for s in range(4):
+                if each == 1:
+                    w = [refs[0][s] for refs in weight_refs]
+                    x = ref[pl.ds(row, step), s * rows : (s + 1) * rows]
+                else:
+                    w = [refs[s][0] for refs in weight_refs]
+                    x = ref[pl.ds(row, step), pl.ds(pl.multiple_of((z ^ s) * rows, 128), rows)]
+                product = jnp.dot(
+                    x, jnp.concatenate(w, axis=1), preferred_element_type=jnp.float32
+                )
                 total = product if total is None else total + product
-            for i, j in enumerate(part):
-                value = total[:, i * head_dim : (i + 1) * head_dim] + b_ref[j : j + 1, here]
-                if j < 2:
-                    mean = jnp.mean(value * value, axis=-1, keepdims=True)
-                    value = value * lax.rsqrt(mean + EPS) * g_ref[j : j + 1, :]
-                out_ref[row : row + step, i * head_dim : (i + 1) * head_dim] = value.astype(
-                    jnp.bfloat16
-                )
+            for h, out_ref in enumerate(out_refs):
+                here = pl.ds(pl.multiple_of(at_ref[2 + h] * head_dim, 128), head_dim)
+                for i, j in enumerate(part):
+                    first = h * cols + i * head_dim
+                    value = total[:, first : first + head_dim] + b_ref[j : j + 1, here]
+                    if j < 2:
+                        mean = jnp.mean(value * value, axis=-1, keepdims=True)
+                        value = value * lax.rsqrt(mean + EPS) * g_ref[j : j + 1, :]
+                    out_ref[pl.ds(row, step), i * head_dim : (i + 1) * head_dim] = value.astype(
+                        jnp.bfloat16
+                    )
 
         if pieces is None:
             block(x_refs[0], 0)
         else:
             x_ref, sems = refs[-2:]
-            q = at_ref[1]
             copies = []
-            for n, ((i, start, _), ref) in enumerate(zip(pieces, x_refs)):
-                row = pl.multiple_of((q ^ i) * (tokens // 4) + start, 16)
-                target = x_ref.at[pl.ds(row, ref.shape[0]), :]
-                copies.append(pltpu.make_async_copy(ref, target, sems.at[n]))
-                copies[-1].start()
+            for (_, parts), ref in zip(pieces, x_refs):
+                for i, start, first, size in parts:
+                    row = pl.multiple_of((q ^ i) * (tokens // 4) + start, 16)
+                    copies.append(
+                        pltpu.make_async_copy(
+                            ref.at[pl.ds(first, size), :],
+                            x_ref.at[pl.ds(row, size), :],
+                            sems.at[len(copies)],
+                        )
+                    )
+                    copies[-1].start()
             for copy in copies:
                 copy.wait()
             for r in range(0, tokens, step):
@@ -234,18 +254,20 @@
         fixed = lambda shape: pl.BlockSpec()
         x_specs = [pl.BlockSpec(memory_space=pl.ANY)] * count
         out_spec = pl.BlockSpec()
-        scratch = [pltpu.VMEM((tokens, width), jnp.bfloat16), pltpu.SemaphoreType.DMA((count,))]
+        copies = sum(len(parts) for _, parts in pieces)
+        scratch = [pltpu.VMEM((tokens, width), jnp.bfloat16), pltpu.SemaphoreType.DMA((copies,))]
+    flat = [*weights[0], *weights[1]]
     return pl.pallas_call(
         kernel,
         grid=grid,
-        in_specs=[smem, *x_specs, *(fixed(w.shape) for w in weights), fixed(bias.shape), fixed(gain.shape)],
-        out_specs=out_spec,
-        out_shape=jax.ShapeDtypeStruct((tokens, cols), jnp.bfloat16),
+        in_specs=[smem, *x_specs, *(fixed(w.shape) for w in flat), fixed(bias.shape), fixed(gain.shape)],
+        out_specs=[out_spec] * 2,
+        out_shape=[jax.ShapeDtypeStruct((tokens, cols), jnp.bfloat16)] * 2,
         scratch_shapes=scratch,
         compiler_params=pltpu.CompilerParams(vmem_limit_bytes=VMEM),
-        cost_estimate=COST,
+        cost_estimate=cost or COST,
         name="project",
-    )(at, *sources, *weights, bias, gain)
+    )(at, *sources, *flat, bias, gain)
 
 
 def tile_step(query, rows_ref, at, tile, head_dim, limit, total, mixed):
@@ -390,106 +412,114 @@
     w = jnp.transpose(w_qkv, (1, 0, 2))
     line = Line()
 
-    cutting = (0, quarter * 5 // 12, quarter)
+    def arrive(value):
+        box = line.reached(value)[0]
+        (box[0],) = line.after(box[0])
+        return box
+
+    cutting = (0, quarter * FIRST // 12, quarter)
     raws = [
         lax.dynamic_slice(frames, (at[1] * quarter + lo, 0), (hi - lo, frames.shape[1]))
         for lo, hi in zip(cutting, cutting[1:])
     ]
     raws_other = [to("seq", raw, 1) for raw in raws]
     (w, *_) = lax.optimization_barrier((w, *raws))
-    cuts = line.reached(*cut_heads(at, w))
-
-    def exchange(value):
-        return lax.all_to_all(value, "seq", split_axis=0, concat_axis=0, tiled=True)
-
-    arrived_k = exchange(cuts[1][0])
+    same, cross, q_sent = line.reached(
+        *cut_heads(at, w, [((MINE,), (1, 2)), ((CROSS,), (1, 2)), ((6, 7, 6, 7), (0,))])
+    )
+    got = [to("seq", same[0], 2), to("seq", cross[0], 3), to("seq", cross[0], 1)]
     own_limit = line.reached(see(at, block_lists, tile_dev))
     far_limit = to("seq", own_limit[0][0], 1)
     frames, modulation = line.after(frames, modulation)
     own_x = line.reached(normalize(frames, modulation, 128))
-    line.drop(cuts[1])
-
-    def arrive(value):
-        box = line.reached(value)[0]
-        (box[0],) = line.after(box[0])
-        return box
+    line.drop(cross)
 
     def take(i):
         (raw,) = line.after(raws_other[i])
         near = line.reached(normalize(raw, modulation, raw.shape[0]))[0]
-        return near, to("head", near[0], 1), to("fsdp", near[0], 1)
-
-    def run(head, part, weights, own):
+        return near, to("fsdp", near[0], 1)
+
+    def spread(near, far):
+        far = arrive(far)
+        both = jnp.concatenate([near[0], far[0]], axis=0)
+        return far, to("head", both, 1)
+
+    def swap(which):
+        kept = arrive(got[which])
+        return kept, to("groups", kept[0], 1)
+
+    def run(part, weights, own, cost=None):
+        sets = [[box[0] for box in boxes] for boxes in weights]
         return line.reached(
-            project(
-                at, head, part, own_x[0][0],
-                None if own else [(i, start, box[0]) for i, start, box in pieces],
-                [box[0] for box in weights], b_qkv, qk_gain,
+            *project(
+                at, part, own_x[0][0], None if own else [(box[0], parts) for box, parts in pieces],
+                sets, b_qkv, qk_gain, cost,
             )
-        )[0]
+        )
 
     def send_edge(own, far):
         return to("seq", jnp.where(is_mid, own[0], far[0]), 2)
 
-    near0, near_c0, far0 = take(0)
-    k_mine = arrive(arrived_k)
-    k_twin = to("groups", k_mine[0], 1)
-    far0 = arrive(far0)
-    far_c0 = to("head", far0[0], 1)
-    near1, near_c1, far1 = take(1)
-    (cuts[2][0],) = line.after(cuts[2][0])
-    arrived_v = exchange(cuts[2][0])
-    near_c0 = arrive(near_c0)
-    k_twin = arrive(k_twin)
-    v_mine = arrive(arrived_v)
-    v_twin = to("groups", v_mine[0], 1)
-    (cuts[0][0],) = line.after(cuts[0][0])
-    arrived_q = exchange(cuts[0][0])
-    line.drop(cuts[0], cuts[2])
-    own_mine = run(MINE, (1, 2), [k_mine, v_mine], True)
-    near_c1, far_c0 = arrive(near_c1), arrive(far_c0)
-    far1 = arrive(far1)
-    far_c1 = to("head", far1[0], 1)
+    near0, far0 = take(0)
+    two_mine, two_twin = swap(0)
+    near1, far1 = take(1)
+    three_mine, three_twin = swap(1)
+    (q_sent[0],) = line.after(q_sent[0])
+    q_got = lax.all_to_all(q_sent[0], "seq", split_axis=0, concat_axis=0, tiled=True)
+    line.drop(q_sent)
+    one_mine, one_twin = swap(2)
+    (w,) = line.after(w)
+    own_kv = [same, line.reached(*cut_heads(at, w, [((TWIN,), (1, 2))], SPACE))[0]]
+    far0, core0 = spread(near0, far0)
+    two_twin = arrive(two_twin)
+    far1, core1 = spread(near1, far1)
+    three_twin = arrive(three_twin)
+    one_twin = arrive(one_twin)
+    kv_w = [[own_kv[0], one_mine, two_mine, three_mine], [own_kv[1], one_twin, two_twin, three_twin]]
+    own_mine, own_twin = run((1, 2), kv_w, True, SPACE)
     limits = own_limit + [arrive(far_limit)]
-    far_c1 = arrive(far_c1)
-    pieces = [(i, 0, box) for i, box in enumerate((near0, near_c0, far0, far_c0))]
-    pieces += [(i, cutting[1], box) for i, box in enumerate((near1, near_c1, far1, far_c1))]
-    far_mine = run(MINE, (1, 2), [k_mine, v_mine], False)
+    core0 = arrive(core0)
+    q_mine = arrive(q_got)
+    q_twin = to("groups", q_mine[0], 1)
+    core1 = arrive(core1)
+    n0, n1 = cutting[1], quarter - cutting[1]
+    pieces = [
+        (near0, [(0, 0, 0, n0)]),
+        (far0, [(2, 0, 0, n0)]),
+        (core0, [(1, 0, 0, n0), (3, 0, n0, n0)]),
+        (near1, [(0, n0, 0, n1)]),
+        (far1, [(2, n0, 0, n1)]),
+        (core1, [(1, n0, 0, n1), (3, n0, n1, n1)]),
+    ]
+    far_mine, far_twin = run((1, 2), kv_w, False)
     halo_mine = send_edge(own_mine, far_mine)
-    v_twin = arrive(v_twin)
-    far_twin = run(TWIN, (1, 2), [k_twin, v_twin], False)
-    own_twin = run(TWIN, (1, 2), [k_twin, v_twin], True)
     halo_twin = send_edge(own_twin, far_twin)
-    line.drop(k_mine, v_mine, k_twin, v_twin)
-    q_mine = arrive(arrived_q)
-    q_twin = to("groups", q_mine[0], 1)
-    queries = {0: [run(MINE, (0,), [q_mine], own) for own in (True, False)]}
-    line.drop(q_mine)
+    line.drop(*kv_w[0], *kv_w[1])
+    q_twin = arrive(q_twin)
+    q_own = run((0,), [[q_mine], [q_twin]], True)
+    q_far = run((0,), [[q_mine], [q_twin]], False)
+    line.drop(q_mine, q_twin, *own_x, *(box for box, _ in pieces))
 
     def pair(h, rows):
-        (queries[h][0][0],) = line.after(queries[h][0][0])
+        (q_own[h][0],) = line.after(q_own[h][0])
         parts = attend_pair(
-            at, [b[0] for b in limits], [b[0] for b in queries[h]], [b[0] for b in rows]
+            at, [b[0] for b in limits], [q_own[h][0], q_far[h][0]], [b[0] for b in rows]
         )
         return line.reached(*parts)
 
     def finish(h, halo, parts):
         (halo,) = line.after(halo)
         keep, send = attend_halo(
-            at, [b[0] for b in limits], [b[0] for b in queries[h]], halo, *(b[0] for b in parts)
+            at, [b[0] for b in limits], [q_own[h][0], q_far[h][0]], halo, *(b[0] for b in parts)
         )
         return line.reached(keep)[0], to("seq", send, 1)
 
     parts_mine = pair(0, (own_mine, far_mine))
-    q_twin = arrive(q_twin)
-    queries[1] = [run(TWIN, (0,), [q_twin], own) for own in (True, False)]
-    line.drop(q_twin, *own_x, *(box for *_, box in pieces))
+    parts_twin = pair(1, (own_twin, far_twin))
     keep_mine, back_mine = finish(0, halo_mine, parts_mine)
     line.drop(*parts_mine)
-    parts_twin = pair(1, (own_twin, far_twin))
-    back_mine = arrive(back_mine)
     keep_twin, back_twin = finish(1, halo_twin, parts_twin)
-    parts = [(MINE, keep_mine[0]), (TWIN, keep_twin[0]), (CROSS, back_mine[0]), (CROSS_TWIN, back_twin)]
+    parts = [(MINE, keep_mine[0]), (TWIN, keep_twin[0]), (CROSS, back_mine), (CROSS_TWIN, back_twin)]
     return assemble(at, parts)
 
 

time: 177 us -> 149 us (0.84)
  Pallas kernels: 83.4 us -> 48.1 us
  local copies, waits for them, and re-layouts: 8.54 us -> 22.2 us
  starting transfers between devices: 33.8 us -> 27 us
    pallas_call x8 -> x4, Pallas kernels: 44.2 us -> 17.2 us  [project(): pl.pallas_call(kernel, grid=grid, in_specs=[smem, *x_specs, *(fixed(w.sha...]
    unnamed x36 -> x70, local copies, waits for them, and re-layouts: 5.64 us -> 18.1 us
    all_to_all x3 -> x1, starting transfers between devices: 14.8 us -> 5 us  [per_device(): lax.all_to_all(q_sent[0], 'seq', split_axis=0, concat_axis=0, tiled=True)]
    pallas_call x2, Pallas kernels: 13.4 us -> 10.2 us  [attend_pair(): pl.pallas_call(kernel, in_specs=[smem, smem, smem] + [vmem] * 4, out_spec...]
    pallas_call x2, Pallas kernels: 6.71 us -> 3.58 us  [attend_halo(): pl.pallas_call(kernel, in_specs=[smem, smem, smem] + [vmem] * 6, out_spec...]
    ppermute x16 -> x18, starting transfers between devices: 18.9 us -> 22 us  [to(): lax.ppermute(value, axis, [(i, i ^ bit) for i in range(lax.axis_size(axis...]
    pallas_call x1 -> x2, Pallas kernels: 3.49 us -> 1.43 us  [cut_heads(): pl.pallas_call(kernel, in_specs=[pl.BlockSpec(memory_space=pltpu.SMEM), p...]
    dynamic_slice x2, local copies, waits for them, and re-layouts: 2.21 us -> 4 us  [per_device(): lax.dynamic_slice(frames, (at[1] * quarter + lo, 0), (hi - lo, frames.sha...]
  transfers between devices with their start and end apart: 19 -> 19, of which waited for: 7 -> 11; matrix products, arithmetic and copies ran while one was open for 1% -> 2% of each run, Pallas kernels for 41% -> 31%
where the time goes in v7:
time: 149 us; the launch traced here: 148 us
  waiting for transfers between devices  49 us (33%)
  Pallas kernels  48.1 us (32%)
  starting transfers between devices  27 us (18%)
  local copies, waits for them, and re-layouts  22.2 us (15%)
    ppermute x18, waiting for transfers between devices, to(): lax.ppermute(value, axis, [(i, i ^ bit) for i in range(lax.axis_size(axis...  49 us
    ppermute x18, starting transfers between devices, to(): lax.ppermute(value, axis, [(i, i ^ bit) for i in range(lax.axis_size(axis...  22 us
    unnamed x70, local copies, waits for them, and re-layouts  18.1 us
    pallas_call x4, Pallas kernels, project(): pl.pallas_call(kernel, grid=grid, in_specs=[smem, *x_specs, *(fixed(w.sha...  17.2 us
    pallas_call x3, Pallas kernels, normalize(): pl.pallas_call(norm_kernel, grid=(tokens // rows,), in_specs=[pl.BlockSpe...  12.1 us
    pallas_call x2, Pallas kernels, attend_pair(): pl.pallas_call(kernel, in_specs=[smem, smem, smem] + [vmem] * 4, out_spec...  10.2 us
    all_to_all x1, starting transfers between devices, per_device(): lax.all_to_all(q_sent[0], 'seq', split_axis=0, concat_axis=0, tiled=True)  5 us
    dynamic_slice x2, local copies, waits for them, and re-layouts, per_device(): lax.dynamic_slice(frames, (at[1] * quarter + lo, 0), (hi - lo, frames.sha...  4 us
  transfers between devices with their start and end apart: 19, of which 11 were waited for; matrix products, arithmetic and copies ran while one was open for 2% of the time, Pallas kernels for 31%

profile of v7, /device:TPU:0, one launch (start us, length us, event | category | flops | bytes accessed | tf_op | source)
XLA Modules:
  0.0 147.9 jit_solution(2069102005152883001)
XLA Ops:
  0.0 2.2 %constant_dynamic-slice_fusion = bf16[128,3072]{1,0:T(8,128)(2,1)} fusion(bf16[768,3072]{1,0:T(8,128)(2,1)} %x_ref, s32[]{:T(128)S(6)} %select_n.28), kind=kLoop, calls=%fused_computation.4 | loop fusion | bytes 1572868 | tf_op jit(solution)/shard_map/dynamic_slice | solution.py:422
  2.2 3.0 %collective-permute-start.2 = (bf16[128,3072]{1,0:T(8,128)(2,1)}, bf16[128,3072]{1,0:T(8,128)(2,1)}, u32[]{:S(2)}, u32[]{:S(2)}) collective-permute-start(bf16[128,3072]{1,0:T(8,128)(2,1)} %constant_dynamic-slice_fusion), channel_id=1, source_target_pairs={{0,4},{4,0},{8,12},{12,8},{1,5},{5,1},{9,13},{13,9},{2,6},{6,2},{1... | collective-permute-start | bytes 2359304 | tf_op jit(solution)/shard_map/ppermute | solution.py:404
  5.3 1.8 %constant_dynamic-slice_fusion.1 = bf16[64,3072]{1,0:T(8,128)(2,1)} fusion(bf16[768,3072]{1,0:T(8,128)(2,1)} %x_ref, s32[]{:T(128)S(6)} %select_n.27), kind=kLoop, calls=%fused_computation.5 | loop fusion | bytes 786436 | tf_op jit(solution)/shard_map/dynamic_slice | solution.py:422
  7.1 0.8 cut_heads.2
  8.0 0.9 copy-done.11
  8.8 2.6 %collective-permute-start.1 = (bf16[1,768,256]{2,1,0:T(8,128)(2,1)S(1)}, bf16[1,768,256]{2,1,0:T(8,128)(2,1)S(1)}, u32[]{:S(2)}, u32[]{:S(2)}) collective-permute-start(bf16[1,768,256]{2,1,0:T(8,128)(2,1)S(1)} %get-tuple-element.458.refs_1_.refs_6_), channel_id=1, source_target_pairs={{0,8},{4,12},{8,0},{12,4},{1,9},{5,13},{9,1},{13,5},{2,10},{6,14},... | collective-permute-start | bytes 1179656 | tf_op jit(solution)/shard_map/ppermute | solution.py:404
  11.9 1.3 collective-permute-start.7
  13.4 1.4 see.1.limit0_ref
  14.8 7.4 %normalize.3.refs_0_ = bf16[768,3072]{1,0:T(8,128)(2,1)} custom-call(bf16[768,3072]{1,0:T(8,128)(2,1)} %x_ref, f32[2,3072]{1,0:T(2,128)} %mod_ref.2), custom_call_target="tpu_custom_call" | custom-call | flops 1048576 | bytes 1024 | tf_op jit(solution)/shard_map/normalize/pallas_call | solution.py:123
  22.2 10.2 %collective-permute-done.2.x_ref = bf16[128,3072]{1,0:T(8,128)(2,1)} collective-permute-done((bf16[128,3072]{1,0:T(8,128)(2,1)}, bf16[128,3072]{1,0:T(8,128)(2,1)}, u32[]{:S(2)}, u32[]{:S(2)}) %collective-permute-start.2) | collective-permute-done | bytes 786464 | tf_op jit(solution)/shard_map/ppermute | solution.py:404
  32.4 2.6 %normalize.4.refs_0_ = bf16[128,3072]{1,0:T(8,128)(2,1)} custom-call(bf16[128,3072]{1,0:T(8,128)(2,1)} %collective-permute-done.2.x_ref, f32[2,3072]{1,0:T(2,128)} %mod_ref.2), custom_call_target="tpu_custom_call" | custom-call | flops 1048576 | bytes 1024 | tf_op jit(solution)/shard_map/normalize/pallas_call | solution.py:123
  35.0 2.0 %collective-permute-start.5 = (bf16[128,3072]{1,0:T(8,128)(2,1)}, bf16[128,3072]{1,0:T(8,128)(2,1)S(1)}, u32[]{:S(2)}, u32[]{:S(2)}) collective-permute-start(bf16[128,3072]{1,0:T(8,128)(2,1)} %normalize.4.refs_0_), channel_id=1, source_target_pairs={{0,2},{2,0},{1,3},{3,1},{4,6},{6,4},{5,7},{7,5},{8,10},{10,8},{9,1... | collective-permute-start | bytes 2359304 | tf_op jit(solution)/shard_map/ppermute | solution.py:404
  37.0 3.7 %collective-permute-done.x_ref = bf16[64,3072]{1,0:T(8,128)(2,1)S(1)} collective-permute-done((bf16[64,3072]{1,0:T(8,128)(2,1)}, bf16[64,3072]{1,0:T(8,128)(2,1)S(1)}, u32[]{:S(2)}, u32[]{:S(2)}) %collective-permute-start) | collective-permute-done | bytes 393248 | tf_op jit(solution)/shard_map/ppermute | solution.py:404
  40.7 2.2 %collective-permute-start.4 = (bf16[1,768,256]{2,1,0:T(8,128)(2,1)S(1)}, bf16[1,768,256]{2,1,0:T(8,128)(2,1)}, u32[]{:S(2)}, u32[]{:S(2)}) collective-permute-start(bf16[1,768,256]{2,1,0:T(8,128)(2,1)S(1)} %collective-permute-done.1.refs_3_.refs_8_), channel_id=1, source_target_pairs={{0,16},{16,0},{1,17},{17,1},{2,18},{18,2},{3,19},{19,3},{4,20},{20... | collective-permute-start | bytes 1179656 | tf_op jit(solution)/shard_map/ppermute | solution.py:404
  42.9 2.1 %normalize.5.refs_3_ = bf16[64,3072]{1,0:T(8,128)(2,1)} custom-call(bf16[64,3072]{1,0:T(8,128)(2,1)} %copy-done.32, f32[2,3072]{1,0:T(2,128)} %mod_ref.2), custom_call_target="tpu_custom_call" | custom-call | flops 1048576 | bytes 1024 | tf_op jit(solution)/shard_map/normalize/pallas_call | solution.py:123
  45.0 6.8 %collective-permute-done.7.refs_4_.refs_9_ = bf16[1,768,256]{2,1,0:T(8,128)(2,1)} collective-permute-done((bf16[1,768,256]{2,1,0:T(8,128)(2,1)S(1)}, bf16[1,768,256]{2,1,0:T(8,128)(2,1)}, u32[]{:S(2)}, u32[]{:S(2)}) %collective-permute-start.7) | collective-permute-done | bytes 393248 | tf_op jit(solution)/shard_map/ppermute | solution.py:404
  51.8 1.5 %collective-permute-start.3 = (bf16[64,3072]{1,0:T(8,128)(2,1)}, bf16[64,3072]{1,0:T(8,128)(2,1)S(1)}, u32[]{:S(2)}, u32[]{:S(2)}) collective-permute-start(bf16[64,3072]{1,0:T(8,128)(2,1)} %normalize.5.refs_3_), channel_id=1, source_target_pairs={{0,2},{2,0},{1,3},{3,1},{4,6},{6,4},{5,7},{7,5},{8,10},{10,8},{9,1... | collective-permute-start | bytes 1179656 | tf_op jit(solution)/shard_map/ppermute | solution.py:404
  53.3 3.6 %collective-permute-done.6.refs_2_.refs_7_ = bf16[1,768,256]{2,1,0:T(8,128)(2,1)} collective-permute-done((bf16[1,768,256]{2,1,0:T(8,128)(2,1)S(1)}, bf16[1,768,256]{2,1,0:T(8,128)(2,1)}, u32[]{:S(2)}, u32[]{:S(2)}) %collective-permute-start.6) | collective-permute-done | bytes 393248 | tf_op jit(solution)/shard_map/ppermute | solution.py:404
  56.8 1.7 %collective-permute-start.11 = (bf16[1,768,256]{2,1,0:T(8,128)(2,1)}, bf16[1,768,256]{2,1,0:T(8,128)(2,1)}, u32[]{:S(2)}, u32[]{:S(2)}) collective-permute-start(bf16[1,768,256]{2,1,0:T(8,128)(2,1)} %collective-permute-done.6.refs_2_.refs_7_), channel_id=1, source_target_pairs={{0,16},{16,0},{1,17},{17,1},{2,18},{18,2},{3,19},{19,3},{4,20},{20... | collective-permute-start | bytes 1179656 | tf_op jit(solution)/shard_map/ppermute | solution.py:404
  58.5 1.7 %copy-done.8 = bf16[768,3,512]{2,0,1:T(8,128)(2,1)S(1)} copy-done((bf16[768,3,512]{2,0,1:T(8,128)(2,1)S(1)}, bf16[768,3,512]{2,0,1:T(8,128)(2,1)}, u32[]{:S(2)}) %copy-start.8) | copy-done | bytes 2359320
  61.6 5.0 %all-to-all-start = ((bf16[4,768,128]{2,1,0:T(8,128)(2,1)}), bf16[4,768,128]{2,1,0:T(8,128)(2,1)S(1)}, u32[]{:S(2)}, u32[]{:S(2)}) async-start(bf16[4,768,128]{2,1,0:T(8,128)(2,1)} %copy-done.11), calls=%async_computation | async-start | bytes 1572864 | tf_op jit(solution)/shard_map/all_to_all | solution.py:468
  67.2 1.0 pad_maximum_fusion.1
  68.9 7.4 %collective-permute-done.12.refs_8_.refs_13_ = bf16[1,768,256]{2,1,0:T(8,128)(2,1)S(1)} collective-permute-done((bf16[1,768,256]{2,1,0:T(8,128)(2,1)}, bf16[1,768,256]{2,1,0:T(8,128)(2,1)S(1)}, u32[]{:S(2)}, u32[]{:S(2)}) %collective-permute-start.12) | collective-permute-done | bytes 393248 | tf_op jit(solution)/shard_map/ppermute | solution.py:404
  76.4 2.4 %copy-done = bf16[768,3072]{1,0:T(8,128)(2,1)S(1)} copy-done((bf16[768,3072]{1,0:T(8,128)(2,1)S(1)}, bf16[768,3072]{1,0:T(8,128)(2,1)}, u32[]{:S(2)}) %copy-start) | copy-done | bytes 4718616
  78.8 4.7 %project.4 = (bf16[768,256]{1,0:T(8,128)(2,1)S(1)}, bf16[768,256]{1,0:T(8,128)(2,1)S(1)}) custom-call(s32[8]{0:T(128)S(1)} %copy-done.27, bf16[768,3072]{1,0:T(8,128)(2,1)S(1)} %copy-done, bf16[1,768,256]{2,1,0:T(8,128)(2,1)S(1)} %copy-done.13, bf16[1,768,256]{2,1,0:T(8,128)(2,1)} %collective-permute-done.6.refs_2_.refs_7_, ...), custom_call_target="tpu_custom_call" | custom-call | flops 68719476736 | bytes 1024 | tf_op jit(solution)/shard_map/project/pallas_call | solution.py:260
  84.3 1.2 copy-done.3
  85.5 0.7 collective-permute-start.15
  86.3 1.4 copy-done.4
  87.7 1.0 copy-done.14
  88.7 1.0 copy-done.17
  89.7 1.0 copy-done.20
  90.7 1.0 copy-done.22
  92.4 6.0 %project.5 = (bf16[768,256]{1,0:T(8,128)(2,1)S(1)}, bf16[768,256]{1,0:T(8,128)(2,1)S(1)}) custom-call(s32[8]{0:T(128)S(1)} %copy-done.27, bf16[128,3072]{1,0:T(8,128)(2,1)S(1)} %copy-done.2, bf16[128,3072]{1,0:T(8,128)(2,1)S(1)} %collective-permute-done.5.refs_1_, bf16[256,3072]{1,0:T(8,128)(2,1)S(1)} %copy-done.4, bf16[64,3072]{1,0:T(8,128)(2,1)S(1)} %copy-done.6, ...), custom_call_target="tpu_custom_call" | custom-call | flops 1048576 | bytes 1024 | tf_op jit(solution)/shard_map/project/pallas_call | solution.py:260
  98.4 2.7 %collective-permute-start.14 = (bf16[768,256]{1,0:T(8,128)(2,1)S(1)}, bf16[768,256]{1,0:T(8,128)(2,1)S(1)}, u32[]{:S(2)}, u32[]{:S(2)}) collective-permute-start(bf16[768,256]{1,0:T(8,128)(2,1)S(1)} %broadcast_select_fusion), channel_id=1, source_target_pairs={{0,8},{4,12},{8,0},{12,4},{1,9},{5,13},{9,1},{13,5},{2,10},{6,14},... | collective-permute-start | bytes 1179656 | tf_op jit(solution)/shard_map/ppermute | solution.py:404
  101.5 2.5 %collective-permute-done.15.refs_2_.refs_7_ = bf16[4,768,128]{2,1,0:T(8,128)(2,1)S(1)} collective-permute-done((bf16[4,768,128]{2,1,0:T(8,128)(2,1)S(1)}, bf16[4,768,128]{2,1,0:T(8,128)(2,1)S(1)}, u32[]{:S(2)}, u32[]{:S(2)}) %collective-permute-start.15) | collective-permute-done | bytes 786464 | tf_op jit(solution)/shard_map/ppermute | solution.py:404
  104.0 2.3 %copy-done.1 = bf16[768,3072]{1,0:T(8,128)(2,1)S(1)} copy-done((bf16[768,3072]{1,0:T(8,128)(2,1)S(1)}, bf16[768,3072]{1,0:T(8,128)(2,1)}, u32[]{:S(2)}) %copy-start.1) | copy-done | bytes 4718616
  106.4 2.6 %project.6 = (bf16[768,128]{1,0:T(8,128)(2,1)S(1)}, bf16[768,128]{1,0:T(8,128)(2,1)S(1)}) custom-call(s32[8]{0:T(128)S(1)} %copy-done.27, bf16[768,3072]{1,0:T(8,128)(2,1)S(1)} %copy-done.1, bf16[4,768,128]{2,1,0:T(8,128)(2,1)S(1)} %all-to-all-done.refs_1_.refs_6_, bf16[4,768,128]{2,1,0:T(8,128)(2,1)S(1)} %collective-permute-done.15.refs_2_.refs_7_, ...), custom_call_target="tpu_custom_call" | custom-call | flops 1048576 | bytes 1024 | tf_op jit(solution)/shard_map/project/pallas_call | solution.py:260
  109.0 3.9 %project.7 = (bf16[768,128]{1,0:T(8,128)(2,1)S(1)}, bf16[768,128]{1,0:T(8,128)(2,1)S(1)}) custom-call(s32[8]{0:T(128)S(1)} %copy-done.27, bf16[128,3072]{1,0:T(8,128)(2,1)S(1)} %copy-done.2, bf16[128,3072]{1,0:T(8,128)(2,1)S(1)} %collective-permute-done.5.refs_1_, bf16[256,3072]{1,0:T(8,128)(2,1)S(1)} %copy-done.5, bf16[64,3072]{1,0:T(8,128)(2,1)S(1)} %copy-done.6, ...), custom_call_target="tpu_custom_call" | custom-call | flops 1048576 | bytes 1024 | tf_op jit(solution)/shard_map/project/pallas_call | solution.py:260
  112.9 5.2 %attend_pair.2 = (bf16[768,128]{1,0:T(8,128)(2,1)S(1)}, f32[768,128]{1,0:T(8,128)S(1)}, f32[768,128]{1,0:T(8,128)S(1)}) custom-call(s32[8]{0:T(128)S(1)} %copy-done.27, f32[2,128]{1,0:T(2,128)S(1)} %copy-done.28, f32[2,128]{1,0:T(2,128)} %collective-permute-done.10.limit1_ref, bf16[768,128]{1,0:T(8,128)(2,1)S(1)} %get-tuple-element.521.q0_ref, ...), custom_call_target="tpu_custom_call" | custom-call | flops 1048576 | bytes 1024 | tf_op jit(solution)/shard_map/attend_pair/pallas_call | solution.py:323
  118.1 5.0 %attend_pair.3 = (bf16[768,128]{1,0:T(8,128)(2,1)S(1)}, f32[768,128]{1,0:T(8,128)S(1)}, f32[768,128]{1,0:T(8,128)S(1)}) custom-call(s32[8]{0:T(128)S(1)} %copy-done.27, f32[2,128]{1,0:T(2,128)S(1)} %copy-done.28, f32[2,128]{1,0:T(2,128)} %collective-permute-done.10.limit1_ref, bf16[768,128]{1,0:T(8,128)(2,1)S(1)} %get-tuple-element.536.q0_ref, ...), custom_call_target="tpu_custom_call" | custom-call | flops 1048576 | bytes 1024 | tf_op jit(solution)/shard_map/attend_pair/pallas_call | solution.py:323
  123.2 2.4 %collective-permute-done.14.halo_ref = bf16[768,256]{1,0:T(8,128)(2,1)S(1)} collective-permute-done((bf16[768,256]{1,0:T(8,128)(2,1)S(1)}, bf16[768,256]{1,0:T(8,128)(2,1)S(1)}, u32[]{:S(2)}, u32[]{:S(2)}) %collective-permute-start.14) | collective-permute-done | bytes 393248 | tf_op jit(solution)/shard_map/ppermute | solution.py:404
  125.6 1.8 %attend_halo.2 = (bf16[768,128]{1,0:T(8,128)(2,1)S(1)}, bf16[768,128]{1,0:T(8,128)(2,1)S(1)}) custom-call(s32[8]{0:T(128)S(1)} %copy-done.27, f32[2,128]{1,0:T(2,128)S(1)} %copy-done.28, f32[2,128]{1,0:T(2,128)} %collective-permute-done.10.limit1_ref, bf16[768,128]{1,0:T(8,128)(2,1)S(1)} %get-tuple-element.521.q0_ref, ...), custom_call_target="tpu_custom_call" | custom-call | flops 1048576 | bytes 1024 | tf_op jit(solution)/shard_map/attend_halo/pallas_call | solution.py:360
  128.1 5.9 %collective-permute-done.13.halo_ref = bf16[768,256]{1,0:T(8,128)(2,1)S(1)} collective-permute-done((bf16[768,256]{1,0:T(8,128)(2,1)S(1)}, bf16[768,256]{1,0:T(8,128)(2,1)S(1)}, u32[]{:S(2)}, u32[]{:S(2)}) %collective-permute-start.13) | collective-permute-done | bytes 393248 | tf_op jit(solution)/shard_map/ppermute | solution.py:404
  133.9 1.8 %attend_halo.3 = (bf16[768,128]{1,0:T(8,128)(2,1)S(1)}, bf16[768,128]{1,0:T(8,128)(2,1)S(1)}) custom-call(s32[8]{0:T(128)S(1)} %copy-done.27, f32[2,128]{1,0:T(2,128)S(1)} %copy-done.28, f32[2,128]{1,0:T(2,128)} %collective-permute-done.10.limit1_ref, bf16[768,128]{1,0:T(8,128)(2,1)S(1)} %get-tuple-element.536.q0_ref, ...), custom_call_target="tpu_custom_call" | custom-call | flops 1048576 | bytes 1024 | tf_op jit(solution)/shard_map/attend_halo/pallas_call | solution.py:360
  136.4 2.0 %collective-permute-start.17 = (bf16[768,128]{1,0:T(8,128)(2,1)S(1)}, bf16[768,128]{1,0:T(8,128)(2,1)S(1)}, u32[]{:S(2)}, u32[]{:S(2)}) collective-permute-start(bf16[768,128]{1,0:T(8,128)(2,1)S(1)} %get-tuple-element.544), channel_id=1, source_target_pairs={{0,4},{4,0},{8,12},{12,8},{1,5},{5,1},{9,13},{13,9},{2,6},{6,2},{1... | collective-permute-start | bytes 589832 | tf_op jit(solution)/shard_map/ppermute | solution.py:404
  138.4 3.3 %collective-permute-done.16.refs_2_ = bf16[768,128]{1,0:T(8,128)(2,1)S(1)} collective-permute-done((bf16[768,128]{1,0:T(8,128)(2,1)S(1)}, bf16[768,128]{1,0:T(8,128)(2,1)S(1)}, u32[]{:S(2)}, u32[]{:S(2)}) %collective-permute-start.16) | collective-permute-done | bytes 196640 | tf_op jit(solution)/shard_map/ppermute | solution.py:404
  141.7 3.3 %collective-permute-done.17.refs_3_ = bf16[768,128]{1,0:T(8,128)(2,1)S(1)} collective-permute-done((bf16[768,128]{1,0:T(8,128)(2,1)S(1)}, bf16[768,128]{1,0:T(8,128)(2,1)S(1)}, u32[]{:S(2)}, u32[]{:S(2)}) %collective-permute-start.17) | collective-permute-done | bytes 196640 | tf_op jit(solution)/shard_map/ppermute | solution.py:404
  145.6 2.2 %assemble.1 = bf16[768,512]{1,0:T(8,128)(2,1)} custom-call(s32[8]{0:T(128)} %copy-done.26, bf16[768,128]{1,0:T(8,128)(2,1)} %copy-done.23, bf16[768,128]{1,0:T(8,128)(2,1)} %copy-done.24, bf16[768,128]{1,0:T(8,128)(2,1)} %copy-done.33, bf16[768,128]{1,0:T(8,128)(2,1)} %copy-done.34), custom_call_target="tpu_custom_call" | custom-call | flops 1048576 | bytes 1024 | tf_op jit(solution)/shard_map/assemble/pallas_call | solution.py:380
  (82 shorter events, 7.4 us)
Async XLA Ops:
  0.0 7.1 %copy-start.7 = (bf16[768,3,512]{2,0,1:T(8,128)(2,1)S(1)}, bf16[768,3,512]{2,0,1:T(8,128)(2,1)}, u32[]{:S(2)}) copy-start(bf16[768,3,512]{2,0,1:T(8,128)(2,1)} %param.8) | copy-start | bytes 7077892
  2.2 30.1 %collective-permute-start.2 = (bf16[128,3072]{1,0:T(8,128)(2,1)}, bf16[128,3072]{1,0:T(8,128)(2,1)}, u32[]{:S(2)}, u32[]{:S(2)}) collective-permute-start(bf16[128,3072]{1,0:T(8,128)(2,1)} %constant_dynamic-slice_fusion), channel_id=1, source_target_pairs={{0,4},{4,0},{8,12},{12,8},{1,5},{5,1},{9,13},{13,9},{2,6},{6,2},{1... | collective-permute-start | bytes 2359304 | tf_op jit(solution)/shard_map/ppermute | solution.py:404
  7.1 6.3 %copy-start.26 = (s32[8]{0:T(128)}, s32[8]{0:T(128)S(1)}, u32[]{:S(2)}) copy-start(s32[8]{0:T(128)S(1)} %stack.35.at_ref.place_ref) | copy-start | bytes 100
  7.9 0.9 copy-start.11
  8.8 13.4 %copy-start.12 = (bf16[1,768,256]{2,1,0:T(8,128)(2,1)}, bf16[1,768,256]{2,1,0:T(8,128)(2,1)S(1)}, u32[]{:S(2)}) copy-start(bf16[1,768,256]{2,1,0:T(8,128)(2,1)S(1)} %get-tuple-element.458.refs_1_.refs_6_) | copy-start | bytes 1179652
  8.8 26.2 %collective-permute-start.1 = (bf16[1,768,256]{2,1,0:T(8,128)(2,1)S(1)}, bf16[1,768,256]{2,1,0:T(8,128)(2,1)S(1)}, u32[]{:S(2)}, u32[]{:S(2)}) collective-permute-start(bf16[1,768,256]{2,1,0:T(8,128)(2,1)S(1)} %get-tuple-element.458.refs_1_.refs_6_), channel_id=1, source_target_pairs={{0,8},{4,12},{8,0},{12,4},{1,9},{5,13},{9,1},{13,5},{2,10},{6,14},... | collective-permute-start | bytes 1179656 | tf_op jit(solution)/shard_map/ppermute | solution.py:404
  11.4 29.3 %collective-permute-start = (bf16[64,3072]{1,0:T(8,128)(2,1)}, bf16[64,3072]{1,0:T(8,128)(2,1)S(1)}, u32[]{:S(2)}, u32[]{:S(2)}) collective-permute-start(bf16[64,3072]{1,0:T(8,128)(2,1)} %constant_dynamic-slice_fusion.1), channel_id=1, source_target_pairs={{0,4},{4,0},{8,12},{12,8},{1,5},{5,1},{9,13},{13,9},{2,6},{6,2},{1... | collective-permute-start | bytes 1179656 | tf_op jit(solution)/shard_map/ppermute | solution.py:404
  11.9 39.9 %collective-permute-start.7 = (bf16[1,768,256]{2,1,0:T(8,128)(2,1)S(1)}, bf16[1,768,256]{2,1,0:T(8,128)(2,1)}, u32[]{:S(2)}, u32[]{:S(2)}) collective-permute-start(bf16[1,768,256]{2,1,0:T(8,128)(2,1)S(1)} %get-tuple-element.277), channel_id=1, source_target_pairs={{0,12},{4,8},{8,4},{12,0},{1,13},{5,9},{9,5},{13,1},{2,14},{6,10},... | collective-permute-start | bytes 1179656 | tf_op jit(solution)/shard_map/ppermute | solution.py:404
  13.2 43.6 %collective-permute-start.6 = (bf16[1,768,256]{2,1,0:T(8,128)(2,1)S(1)}, bf16[1,768,256]{2,1,0:T(8,128)(2,1)}, u32[]{:S(2)}, u32[]{:S(2)}) collective-permute-start(bf16[1,768,256]{2,1,0:T(8,128)(2,1)S(1)} %get-tuple-element.277), channel_id=1, source_target_pairs={{0,4},{4,0},{8,12},{12,8},{1,5},{5,1},{9,13},{13,9},{2,6},{6,2},{1... | collective-permute-start | bytes 1179656 | tf_op jit(solution)/shard_map/ppermute | solution.py:404
  14.8 17.6 %copy-start.28 = (f32[2,128]{1,0:T(2,128)S(1)}, f32[2,128]{1,0:T(2,128)}, u32[]{:S(2)}) copy-start(f32[2,128]{1,0:T(2,128)} %see.1.limit0_ref) | copy-start | bytes 3076
  22.2 36.3 %copy-start.27 = (s32[8]{0:T(128)S(1)}, s32[8]{0:T(128)}, u32[]{:S(2)}) copy-start(s32[8]{0:T(128)} %copy-done.26) | copy-start | bytes 100
  32.4 51.9 %collective-permute-start.10 = (f32[2,128]{1,0:T(2,128)S(1)}, f32[2,128]{1,0:T(2,128)}, u32[]{:S(2)}, u32[]{:S(2)}) collective-permute-start(f32[2,128]{1,0:T(2,128)S(1)} %copy-done.28), channel_id=1, source_target_pairs={{0,4},{4,0},{8,12},{12,8},{1,5},{5,1},{9,13},{13,9},{2,6},{6,2},{1... | collective-permute-start | bytes 3080 | tf_op jit(solution)/shard_map/ppermute | solution.py:404
  35.0 25.8 %copy-start.15 = (bf16[1,768,256]{2,1,0:T(8,128)(2,1)}, bf16[1,768,256]{2,1,0:T(8,128)(2,1)S(1)}, u32[]{:S(2)}) copy-start(bf16[1,768,256]{2,1,0:T(8,128)(2,1)S(1)} %collective-permute-done.1.refs_3_.refs_8_) | copy-start | bytes 1179652
  35.0 31.6 %collective-permute-start.5 = (bf16[128,3072]{1,0:T(8,128)(2,1)}, bf16[128,3072]{1,0:T(8,128)(2,1)S(1)}, u32[]{:S(2)}, u32[]{:S(2)}) collective-permute-start(bf16[128,3072]{1,0:T(8,128)(2,1)} %normalize.4.refs_0_), channel_id=1, source_target_pairs={{0,2},{2,0},{1,3},{3,1},{4,6},{6,4},{5,7},{7,5},{8,10},{10,8},{9,1... | collective-permute-start | bytes 2359304 | tf_op jit(solution)/shard_map/ppermute | solution.py:404
  40.7 2.2 %copy-start.32 = (bf16[64,3072]{1,0:T(8,128)(2,1)}, bf16[64,3072]{1,0:T(8,128)(2,1)S(1)}, u32[]{:S(2)}) copy-start(bf16[64,3072]{1,0:T(8,128)(2,1)S(1)} %collective-permute-done.x_ref) | copy-start | bytes 1179652
  40.7 26.5 %collective-permute-start.4 = (bf16[1,768,256]{2,1,0:T(8,128)(2,1)S(1)}, bf16[1,768,256]{2,1,0:T(8,128)(2,1)}, u32[]{:S(2)}, u32[]{:S(2)}) collective-permute-start(bf16[1,768,256]{2,1,0:T(8,128)(2,1)S(1)} %collective-permute-done.1.refs_3_.refs_8_), channel_id=1, source_target_pairs={{0,16},{16,0},{1,17},{17,1},{2,18},{18,2},{3,19},{19,3},{4,20},{20... | collective-permute-start | bytes 1179656 | tf_op jit(solution)/shard_map/ppermute | solution.py:404
  45.0 22.2 %copy-start.6 = (bf16[64,3072]{1,0:T(8,128)(2,1)S(1)}, bf16[64,3072]{1,0:T(8,128)(2,1)}, u32[]{:S(2)}) copy-start(bf16[64,3072]{1,0:T(8,128)(2,1)} %normalize.5.refs_3_) | copy-start | bytes 1179652
  51.8 15.4 %collective-permute-start.3 = (bf16[64,3072]{1,0:T(8,128)(2,1)}, bf16[64,3072]{1,0:T(8,128)(2,1)S(1)}, u32[]{:S(2)}, u32[]{:S(2)}) collective-permute-start(bf16[64,3072]{1,0:T(8,128)(2,1)} %normalize.5.refs_3_), channel_id=1, source_target_pairs={{0,2},{2,0},{1,3},{3,1},{4,6},{6,4},{5,7},{7,5},{8,10},{10,8},{9,1... | collective-permute-start | bytes 1179656 | tf_op jit(solution)/shard_map/ppermute | solution.py:404
  56.8 19.5 %collective-permute-start.11 = (bf16[1,768,256]{2,1,0:T(8,128)(2,1)}, bf16[1,768,256]{2,1,0:T(8,128)(2,1)}, u32[]{:S(2)}, u32[]{:S(2)}) collective-permute-start(bf16[1,768,256]{2,1,0:T(8,128)(2,1)} %collective-permute-done.6.refs_2_.refs_7_), channel_id=1, source_target_pairs={{0,16},{16,0},{1,17},{17,1},{2,18},{18,2},{3,19},{19,3},{4,20},{20... | collective-permute-start | bytes 1179656 | tf_op jit(solution)/shard_map/ppermute | solution.py:404
  58.5 1.7 %copy-start.8 = (bf16[768,3,512]{2,0,1:T(8,128)(2,1)S(1)}, bf16[768,3,512]{2,0,1:T(8,128)(2,1)}, u32[]{:S(2)}) copy-start(bf16[768,3,512]{2,0,1:T(8,128)(2,1)} %param.8) | copy-start | bytes 7077892
  61.6 6.6 %copy-start.2 = (bf16[128,3072]{1,0:T(8,128)(2,1)S(1)}, bf16[128,3072]{1,0:T(8,128)(2,1)}, u32[]{:S(2)}) copy-start(bf16[128,3072]{1,0:T(8,128)(2,1)} %normalize.4.refs_0_) | copy-start | bytes 2359300
  61.6 23.9 %all-to-all-start = ((bf16[4,768,128]{2,1,0:T(8,128)(2,1)}), bf16[4,768,128]{2,1,0:T(8,128)(2,1)S(1)}, u32[]{:S(2)}, u32[]{:S(2)}) async-start(bf16[4,768,128]{2,1,0:T(8,128)(2,1)} %copy-done.11), calls=%async_computation | async-start | bytes 1572864 | tf_op jit(solution)/shard_map/all_to_all | solution.py:468
  66.6 9.7 %copy-start.13 = (bf16[1,768,256]{2,1,0:T(8,128)(2,1)S(1)}, bf16[1,768,256]{2,1,0:T(8,128)(2,1)}, u32[]{:S(2)}) copy-start(bf16[1,768,256]{2,1,0:T(8,128)(2,1)} %copy-done.12) | copy-start | bytes 1179652
  66.6 9.7 %copy-start.16 = (bf16[1,768,256]{2,1,0:T(8,128)(2,1)S(1)}, bf16[1,768,256]{2,1,0:T(8,128)(2,1)}, u32[]{:S(2)}) copy-start(bf16[1,768,256]{2,1,0:T(8,128)(2,1)} %copy-done.15) | copy-start | bytes 1179652
  66.6 9.8 %copy-start.19 = (bf16[1,768,256]{2,1,0:T(8,128)(2,1)S(1)}, bf16[1,768,256]{2,1,0:T(8,128)(2,1)}, u32[]{:S(2)}) copy-start(bf16[1,768,256]{2,1,0:T(8,128)(2,1)} %copy-done.18) | copy-start | bytes 1179652
  66.6 9.8 %copy-start.25 = (f32[3,512]{1,0:T(4,128)S(1)}, f32[3,512]{1,0:T(4,128)}, u32[]{:S(2)}) copy-start(f32[3,512]{1,0:T(4,128)} %refs_8_.1) | copy-start | bytes 18436
  66.6 9.8 %copy-start.29 = (f32[2,128]{1,0:T(2,128)S(1)}, f32[2,128]{1,0:T(2,128)}, u32[]{:S(2)}) copy-start(f32[2,128]{1,0:T(2,128)} %refs_9_.3) | copy-start | bytes 3076
  66.6 9.7 %collective-permute-start.12 = (bf16[1,768,256]{2,1,0:T(8,128)(2,1)}, bf16[1,768,256]{2,1,0:T(8,128)(2,1)S(1)}, u32[]{:S(2)}, u32[]{:S(2)}) collective-permute-start(bf16[1,768,256]{2,1,0:T(8,128)(2,1)} %collective-permute-done.7.refs_4_.refs_9_), channel_id=1, source_target_pairs={{0,16},{16,0},{1,17},{17,1},{2,18},{18,2},{3,19},{19,3},{4,20},{20... | collective-permute-start | bytes 1179656 | tf_op jit(solution)/shard_map/ppermute | solution.py:404
  68.2 18.1 %collective-permute-start.8 = (bf16[128,3072]{1,0:T(8,128)(2,1)}, bf16[128,3072]{1,0:T(8,128)(2,1)}, u32[]{:S(2)}, u32[]{:S(2)}) collective-permute-start(bf16[128,3072]{1,0:T(8,128)(2,1)} %pad_maximum_fusion.1), channel_id=1, source_target_pairs={{0,1},{1,0},{2,3},{3,2},{4,5},{5,4},{6,7},{7,6},{8,9},{9,8},{10,11... | collective-permute-start | bytes 2359304 | tf_op jit(solution)/shard_map/ppermute | solution.py:404
  68.3 15.9 %collective-permute-start.9 = (bf16[256,3072]{1,0:T(8,128)(2,1)S(1)}, bf16[256,3072]{1,0:T(8,128)(2,1)S(1)}, u32[]{:S(2)}, u32[]{:S(2)}) collective-permute-start(bf16[256,3072]{1,0:T(8,128)(2,1)S(1)} %pad_maximum_fusion), channel_id=1, source_target_pairs={{0,1},{1,0},{2,3},{3,2},{4,5},{5,4},{6,7},{7,6},{8,9},{9,8},{10,11... | collective-permute-start | bytes 4718600 | tf_op jit(solution)/shard_map/ppermute | solution.py:404
  76.3 7.2 %copy-start.21 = (bf16[1,768,256]{2,1,0:T(8,128)(2,1)}, bf16[1,768,256]{2,1,0:T(8,128)(2,1)S(1)}, u32[]{:S(2)}) copy-start(bf16[1,768,256]{2,1,0:T(8,128)(2,1)S(1)} %collective-permute-done.12.refs_8_.refs_13_) | copy-start | bytes 1179652
  76.4 2.4 %copy-start = (bf16[768,3072]{1,0:T(8,128)(2,1)S(1)}, bf16[768,3072]{1,0:T(8,128)(2,1)}, u32[]{:S(2)}) copy-start(bf16[768,3072]{1,0:T(8,128)(2,1)} %normalize.3.refs_0_) | copy-start | bytes 14155780
  84.2 1.2 copy-start.3
  85.5 18.5 %collective-permute-start.15 = (bf16[4,768,128]{2,1,0:T(8,128)(2,1)S(1)}, bf16[4,768,128]{2,1,0:T(8,128)(2,1)S(1)}, u32[]{:S(2)}, u32[]{:S(2)}) collective-permute-start(bf16[4,768,128]{2,1,0:T(8,128)(2,1)S(1)} %all-to-all-done.refs_1_.refs_6_), channel_id=1, source_target_pairs={{0,16},{16,0},{1,17},{17,1},{2,18},{18,2},{3,19},{19,3},{4,20},{20... | collective-permute-start | bytes 2359304 | tf_op jit(solution)/shard_map/ppermute | solution.py:404
  86.3 1.4 copy-start.4
  87.7 1.0 copy-start.14
  88.7 1.0 copy-start.17
  89.7 1.0 copy-start.20
  90.7 1.0 copy-start.22
  92.3 6.0 %copy-start.10 = (bf16[768,256]{1,0:T(8,128)(2,1)S(1)}, bf16[768,256]{1,0:T(8,128)(2,1)}, u32[]{:S(2)}) copy-start(bf16[768,256]{1,0:T(8,128)(2,1)} %copy-done.9) | copy-start | bytes 1179652
  98.3 5.7 %copy-start.31 = (f32[2,128]{1,0:T(2,128)S(1)}, f32[2,128]{1,0:T(2,128)}, u32[]{:S(2)}) copy-start(f32[2,128]{1,0:T(2,128)} %refs_9_.3) | copy-start | bytes 3076
  98.4 27.2 %collective-permute-start.14 = (bf16[768,256]{1,0:T(8,128)(2,1)S(1)}, bf16[768,256]{1,0:T(8,128)(2,1)S(1)}, u32[]{:S(2)}, u32[]{:S(2)}) collective-permute-start(bf16[768,256]{1,0:T(8,128)(2,1)S(1)} %broadcast_select_fusion), channel_id=1, source_target_pairs={{0,8},{4,12},{8,0},{12,4},{1,9},{5,13},{9,1},{13,5},{2,10},{6,14},... | collective-permute-start | bytes 1179656 | tf_op jit(solution)/shard_map/ppermute | solution.py:404
  101.2 32.8 %collective-permute-start.13 = (bf16[768,256]{1,0:T(8,128)(2,1)S(1)}, bf16[768,256]{1,0:T(8,128)(2,1)S(1)}, u32[]{:S(2)}, u32[]{:S(2)}) collective-permute-start(bf16[768,256]{1,0:T(8,128)(2,1)S(1)} %broadcast_select_fusion.1), channel_id=1, source_target_pairs={{0,8},{4,12},{8,0},{12,4},{1,9},{5,13},{9,1},{13,5},{2,10},{6,14},... | collective-permute-start | bytes 1179656 | tf_op jit(solution)/shard_map/ppermute | solution.py:404
  104.0 2.3 %copy-start.1 = (bf16[768,3072]{1,0:T(8,128)(2,1)S(1)}, bf16[768,3072]{1,0:T(8,128)(2,1)}, u32[]{:S(2)}) copy-start(bf16[768,3072]{1,0:T(8,128)(2,1)} %normalize.3.refs_0_) | copy-start | bytes 14155780
  106.4 2.6 %copy-start.5 = (bf16[256,3072]{1,0:T(8,128)(2,1)S(1)}, bf16[256,3072]{1,0:T(8,128)(2,1)}, u32[]{:S(2)}) copy-start(bf16[256,3072]{1,0:T(8,128)(2,1)} %copy-done.3) | copy-start | bytes 4718596
  133.9 7.8 %collective-permute-start.16 = (bf16[768,128]{1,0:T(8,128)(2,1)S(1)}, bf16[768,128]{1,0:T(8,128)(2,1)S(1)}, u32[]{:S(2)}, u32[]{:S(2)}) collective-permute-start(bf16[768,128]{1,0:T(8,128)(2,1)S(1)} %get-tuple-element.543), channel_id=1, source_target_pairs={{0,4},{4,0},{8,12},{12,8},{1,5},{5,1},{9,13},{13,9},{2,6},{6,2},{1... | collective-permute-start | bytes 589832 | tf_op jit(solution)/shard_map/ppermute | solution.py:404
  136.4 8.6 %collective-permute-start.17 = (bf16[768,128]{1,0:T(8,128)(2,1)S(1)}, bf16[768,128]{1,0:T(8,128)(2,1)S(1)}, u32[]{:S(2)}, u32[]{:S(2)}) collective-permute-start(bf16[768,128]{1,0:T(8,128)(2,1)S(1)} %get-tuple-element.544), channel_id=1, source_target_pairs={{0,4},{4,0},{8,12},{12,8},{1,5},{5,1},{9,13},{13,9},{2,6},{6,2},{1... | collective-permute-start | bytes 589832 | tf_op jit(solution)/shard_map/ppermute | solution.py:404
  141.7 3.3 %copy-start.33 = (bf16[768,128]{1,0:T(8,128)(2,1)}, bf16[768,128]{1,0:T(8,128)(2,1)S(1)}, u32[]{:S(2)}) copy-start(bf16[768,128]{1,0:T(8,128)(2,1)S(1)} %collective-permute-done.16.refs_2_) | copy-start | bytes 589828
  (6 other events, 4.2 us)

commit v8 on v7

--- a/solution.py
+++ b/solution.py
@@ -9,6 +9,7 @@
 
 EPS = 1e-06
 VMEM = 28 << 20
+WHOLE = 60 << 20
 FIRST = 8
 HIDDEN = -1e30
 SPACE = pl.CostEstimate(flops=1 << 36, bytes_accessed=1 << 10, transcendentals=0)
@@ -180,94 +181,117 @@
     )(at, lists)
 
 
-def project(at, part, source, pieces, weights, bias, gain, cost=None):
+def project(at, heads, part, own, pieces, weights, bias, gain, cost=None):
     *_, rows, cols = weights[0][0].shape
     head_dim = gain.shape[1]
-    sources = [source] if pieces is None else [array for array, _ in pieces]
+    sources = [own] if pieces is None else [array for array, _ in pieces]
     tokens = sum(piece.shape[0] for piece in sources)
     width = sources[0].shape[1]
     count = len(sources)
     each = len(weights[0])
     step = 256
+    flat = [array for arrays in weights for array in arrays]
+    moves = tokens // step if pieces is None else sum(len(parts) for _, parts in pieces)
 
     def kernel(at_ref, *refs):
-        x_refs, flat = refs[:count], refs[count : count + 2 * each]
-        weight_refs = (flat[:each], flat[each:])
-        b_ref, g_ref, *out_refs = refs[count + 2 * each : count + 2 * each + 4]
+        x_refs, flat_refs = refs[:count], refs[count : count + len(flat)]
+        b_ref, g_ref, *out_refs = refs[count + len(flat) : count + len(flat) + 2 + len(heads)]
+        x_ref, w_ref, x_sems, w_sems = refs[-4:]
         z, q = at_ref[0], at_ref[1]
-
-        def block(ref, row):
-            total = None
-            for s in range(4):
-                if each == 1:
-                    w = [refs[0][s] for refs in weight_refs]
-                    x = ref[pl.ds(row, step), s * rows : (s + 1) * rows]
-                else:
-                    w = [refs[s][0] for refs in weight_refs]
-                    x = ref[pl.ds(row, step), pl.ds(pl.multiple_of((z ^ s) * rows, 128), rows)]
-                product = jnp.dot(
-                    x, jnp.concatenate(w, axis=1), preferred_element_type=jnp.float32
+        loads = []
+        for n, ref in enumerate(flat_refs):
+            target = w_ref.at[n // each] if each == 1 else w_ref.at[n // each, pl.ds(n % each, 1)]
+            loads.append(pltpu.make_async_copy(ref, target, w_sems.at[n]))
+        copies = []
+        if pieces is None:
+            for r in range(tokens // step):
+                at_rows = pl.ds(r * step, step)
+                copies.append(
+                    pltpu.make_async_copy(x_refs[0].at[at_rows], x_ref.at[at_rows], x_sems.at[r])
                 )
-                total = product if total is None else total + product
-            for h, out_ref in enumerate(out_refs):
-                here = pl.ds(pl.multiple_of(at_ref[2 + h] * head_dim, 128), head_dim)
-                for i, j in enumerate(part):
-                    first = h * cols + i * head_dim
-                    value = total[:, first : first + head_dim] + b_ref[j : j + 1, here]
-                    if j < 2:
-                        mean = jnp.mean(value * value, axis=-1, keepdims=True)
-                        value = value * lax.rsqrt(mean + EPS) * g_ref[j : j + 1, :]
-                    out_ref[pl.ds(row, step), i * head_dim : (i + 1) * head_dim] = value.astype(
-                        jnp.bfloat16
-                    )
-
-        if pieces is None:
-            block(x_refs[0], 0)
         else:
-            x_ref, sems = refs[-2:]
-            copies = []
             for (_, parts), ref in zip(pieces, x_refs):
                 for i, start, first, size in parts:
                     row = pl.multiple_of((q ^ i) * (tokens // 4) + start, 16)
                     copies.append(
                         pltpu.make_async_copy(
-                            ref.at[pl.ds(first, size), :],
-                            x_ref.at[pl.ds(row, size), :],
-                            sems.at[len(copies)],
+                            ref.at[pl.ds(first, size)],
+                            x_ref.at[pl.ds(row, size)],
+                            x_sems.at[len(copies)],
                         )
                     )
-                    copies[-1].start()
+        for copy in loads + copies:
+            copy.start()
+        for copy in loads:
+            copy.wait()
+        if pieces is not None:
             for copy in copies:
                 copy.wait()
-            for r in range(0, tokens, step):
-                block(x_ref, r)
-
-    smem = pl.BlockSpec(memory_space=pltpu.SMEM)
-    if pieces is None:
-        grid = (tokens // step,)
-        fixed = lambda shape: pl.BlockSpec(shape, lambda i: (0,) * len(shape))
-        x_specs = [pl.BlockSpec((step, width), lambda i: (i, 0))]
-        out_spec = pl.BlockSpec((step, cols), lambda i: (i, 0))
-        scratch = []
-    else:
-        grid = ()
-        fixed = lambda shape: pl.BlockSpec()
-        x_specs = [pl.BlockSpec(memory_space=pl.ANY)] * count
-        out_spec = pl.BlockSpec()
-        copies = sum(len(parts) for _, parts in pieces)
-        scratch = [pltpu.VMEM((tokens, width), jnp.bfloat16), pltpu.SemaphoreType.DMA((copies,))]
-    flat = [*weights[0], *weights[1]]
-    return pl.pallas_call(
-        kernel,
-        grid=grid,
-        in_specs=[smem, *x_specs, *(fixed(w.shape) for w in flat), fixed(bias.shape), fixed(gain.shape)],
-        out_specs=[out_spec] * 2,
-        out_shape=[jax.ShapeDtypeStruct((tokens, cols), jnp.bfloat16)] * 2,
-        scratch_shapes=scratch,
-        compiler_params=pltpu.CompilerParams(vmem_limit_bytes=VMEM),
+        for r in range(tokens // step):
+            if pieces is None:
+                copies[r].wait()
+            here = slice(r * step, (r + 1) * step)
+            total = None
+            for s in range(4):
+                first = s * rows if each == 1 else pl.multiple_of((z ^ s) * rows, 128)
+                product = jnp.dot(
+                    x_ref[here, pl.ds(first, rows)],
+                    jnp.concatenate([w_ref[h, s] for h in range(len(heads))], axis=1),
+                    preferred_element_type=jnp.float32,
+                )
+                total = product if total is None else total + product
+            for h, (head, out_ref) in enumerate(zip(heads, out_refs)):
+                lanes = pl.ds(pl.multiple_of(at_ref[head] * head_dim, 128), head_dim)
+                for i, j in enumerate(part):
+                    first = h * cols + i * head_dim
+                    value = total[:, first : first + head_dim] + b_ref[j : j + 1, lanes]
+                    if j < 2:
+                        mean = jnp.mean(value * value, axis=-1, keepdims=True)
+                        value = value * lax.rsqrt(mean + EPS) * g_ref[j : j + 1, :]
+                    out_ref[here, i * head_dim : (i + 1) * head_dim] = value.astype(jnp.bfloat16)
+
+    hbm = pl.BlockSpec(memory_space=pltpu.HBM)
+    return pl.pallas_call(
+        kernel,
+        in_specs=[pl.BlockSpec(memory_space=pltpu.SMEM)]
+        + [hbm] * (count + len(flat))
+        + [pl.BlockSpec()] * 2,
+        out_specs=[pl.BlockSpec()] * len(heads),
+        out_shape=[jax.ShapeDtypeStruct((tokens, cols), jnp.bfloat16)] * len(heads),
+        scratch_shapes=[
+            pltpu.VMEM((tokens, width), jnp.bfloat16),
+            pltpu.VMEM((len(heads), 4, rows, cols), jnp.bfloat16),
+            pltpu.SemaphoreType.DMA((moves,)),
+            pltpu.SemaphoreType.DMA((len(flat),)),
+        ],
+        compiler_params=pltpu.CompilerParams(vmem_limit_bytes=WHOLE),
         cost_estimate=cost or COST,
         name="project",
     )(at, *sources, *flat, bias, gain)
+
+
+def take_rows(at, frames, sizes):
+    width = frames.shape[1]
+    quarter = sum(sizes)
+
+    def kernel(at_ref, x_ref, *out_refs):
+        first = 0
+        for ref in out_refs:
+            ref[...] = x_ref[first : first + ref.shape[0], :]
+            first += ref.shape[0]
+
+    return pl.pallas_call(
+        kernel,
+        grid_spec=pltpu.PrefetchScalarGridSpec(
+            num_scalar_prefetch=1,
+            grid=(1,),
+            in_specs=[pl.BlockSpec((quarter, width), lambda i, at: (at[1], 0))],
+            out_specs=[pl.BlockSpec((size, width), lambda i, at: (0, 0)) for size in sizes],
+        ),
+        out_shape=[jax.ShapeDtypeStruct((size, width), jnp.bfloat16) for size in sizes],
+        cost_estimate=COST,
+        name="take_rows",
+    )(at, frames)
 
 
 def tile_step(query, rows_ref, at, tile, head_dim, limit, total, mixed):
@@ -418,10 +442,7 @@
         return box
 
     cutting = (0, quarter * FIRST // 12, quarter)
-    raws = [
-        lax.dynamic_slice(frames, (at[1] * quarter + lo, 0), (hi - lo, frames.shape[1]))
-        for lo, hi in zip(cutting, cutting[1:])
-    ]
+    raws = take_rows(at, frames, [hi - lo for lo, hi in zip(cutting, cutting[1:])])
     raws_other = [to("seq", raw, 1) for raw in raws]
     (w, *_) = lax.optimization_barrier((w, *raws))
     same, cross, q_sent = line.reached(
@@ -448,11 +469,11 @@
         kept = arrive(got[which])
         return kept, to("groups", kept[0], 1)
 
-    def run(part, weights, own, cost=None):
+    def run(heads, part, weights, own, cost=None):
         sets = [[box[0] for box in boxes] for boxes in weights]
         return line.reached(
             *project(
-                at, part, own_x[0][0], None if own else [(box[0], parts) for box, parts in pieces],
+                at, heads, part, own_x[0][0], None if own else [(box[0], parts) for box, parts in pieces],
                 sets, b_qkv, qk_gain, cost,
             )
         )
@@ -463,24 +484,23 @@
     near0, far0 = take(0)
     two_mine, two_twin = swap(0)
     near1, far1 = take(1)
-    three_mine, three_twin = swap(1)
     (q_sent[0],) = line.after(q_sent[0])
     q_got = lax.all_to_all(q_sent[0], "seq", split_axis=0, concat_axis=0, tiled=True)
     line.drop(q_sent)
+    limits = own_limit + [arrive(far_limit)]
+    three_mine, three_twin = swap(1)
     one_mine, one_twin = swap(2)
     (w,) = line.after(w)
     own_kv = [same, line.reached(*cut_heads(at, w, [((TWIN,), (1, 2))], SPACE))[0]]
     far0, core0 = spread(near0, far0)
     two_twin = arrive(two_twin)
+    three_twin = arrive(three_twin)
     far1, core1 = spread(near1, far1)
-    three_twin = arrive(three_twin)
-    one_twin = arrive(one_twin)
-    kv_w = [[own_kv[0], one_mine, two_mine, three_mine], [own_kv[1], one_twin, two_twin, three_twin]]
-    own_mine, own_twin = run((1, 2), kv_w, True, SPACE)
-    limits = own_limit + [arrive(far_limit)]
-    core0 = arrive(core0)
+    w_mine = [own_kv[0], one_mine, two_mine, three_mine]
+    (own_mine,) = run((MINE,), (1, 2), [w_mine], True, SPACE)
     q_mine = arrive(q_got)
     q_twin = to("groups", q_mine[0], 1)
+    core0 = arrive(core0)
     core1 = arrive(core1)
     n0, n1 = cutting[1], quarter - cutting[1]
     pieces = [
@@ -491,13 +511,17 @@
         (far1, [(2, n0, 0, n1)]),
         (core1, [(1, n0, 0, n1), (3, n0, n1, n1)]),
     ]
-    far_mine, far_twin = run((1, 2), kv_w, False)
+    (far_mine,) = run((MINE,), (1, 2), [w_mine], False)
     halo_mine = send_edge(own_mine, far_mine)
+    one_twin = arrive(one_twin)
+    w_twin = [own_kv[1], one_twin, two_twin, three_twin]
+    (far_twin,) = run((TWIN,), (1, 2), [w_twin], False)
+    (own_twin,) = run((TWIN,), (1, 2), [w_twin], True)
     halo_twin = send_edge(own_twin, far_twin)
-    line.drop(*kv_w[0], *kv_w[1])
+    line.drop(*w_mine, *w_twin)
     q_twin = arrive(q_twin)
-    q_own = run((0,), [[q_mine], [q_twin]], True)
-    q_far = run((0,), [[q_mine], [q_twin]], False)
+    q_own = run((MINE, TWIN), (0,), [[q_mine], [q_twin]], True)
+    q_far = run((MINE, TWIN), (0,), [[q_mine], [q_twin]], False)
     line.drop(q_mine, q_twin, *own_x, *(box for box, _ in pieces))
 
     def pair(h, rows):
@@ -515,9 +539,9 @@
         return line.reached(keep)[0], to("seq", send, 1)
 
     parts_mine = pair(0, (own_mine, far_mine))
-    parts_twin = pair(1, (own_twin, far_twin))
     keep_mine, back_mine = finish(0, halo_mine, parts_mine)
     line.drop(*parts_mine)
+    parts_twin = pair(1, (own_twin, far_twin))
     keep_twin, back_twin = finish(1, halo_twin, parts_twin)
     parts = [(MINE, keep_mine[0]), (TWIN, keep_twin[0]), (CROSS, back_mine), (CROSS_TWIN, back_twin)]
     return assemble(at, parts)

time: 149 us -> 155 us (1.040)
  Pallas kernels: 48.1 us -> 72 us
  local copies, waits for them, and re-layouts: 22.2 us -> 6.76 us
  waiting for transfers between devices: 49 us -> 41.6 us
  other arithmetic: 1.21 us -> 6.62 us
    pallas_call x4 -> x7, Pallas kernels: 17.2 us -> 40.8 us  [the longest x6 37.6 us: project(): pl.pallas_call(kernel, in_specs=[pl.BlockSpec(memory_space=pltpu.SMEM)] +...]
    unnamed x70 -> x54, local copies, waits for them, and re-layouts: 18.1 us -> 6.13 us
    ppermute x18, waiting for transfers between devices: 49 us -> 38.6 us  [to(): lax.ppermute(value, axis, [(i, i ^ bit) for i in range(lax.axis_size(axis...]
    dynamic_slice x2 -> x0, local copies, waits for them, and re-layouts: 4 us -> none  [per_device(): lax.dynamic_slice(frames, (at[1] * quarter + lo, 0), (hi - lo, frames.sha...]
    concatenate x2, other arithmetic: 1.11 us -> 4.5 us  [spread(): both = jnp.concatenate([near[0], far[0]], axis=0)]
    all_to_all x1, waiting for transfers between devices: 0.08 us -> 2.95 us  [per_device(): lax.all_to_all(q_sent[0], 'seq', split_axis=0, concat_axis=0, tiled=True)]
    select_n x2, other arithmetic: 0.1 us -> 2.12 us  [send_edge(): return to('seq', jnp.where(is_mid, own[0], far[0]), 2)]
  transfers between devices with their start and end apart: 19 -> 19, of which waited for: 11 -> 7; matrix products, arithmetic and copies ran while one was open for 2% -> 4% of each run, Pallas kernels for 31% -> 42%
where the time goes in v8:
time: 155 us; the launch traced here: 154 us
  Pallas kernels  72 us (46%)
  waiting for transfers between devices  41.6 us (27%)
  starting transfers between devices  26.7 us (17%)
  local copies, waits for them, and re-layouts  6.76 us (4%)
  other arithmetic  6.62 us (4%)
    ppermute x18, waiting for transfers between devices, to(): lax.ppermute(value, axis, [(i, i ^ bit) for i in range(lax.axis_size(axis...  38.6 us
    pallas_call x6, Pallas kernels, project(): pl.pallas_call(kernel, in_specs=[pl.BlockSpec(memory_space=pltpu.SMEM)] +...  37.6 us
    ppermute x18, starting transfers between devices, to(): lax.ppermute(value, axis, [(i, i ^ bit) for i in range(lax.axis_size(axis...  21.7 us
    pallas_call x3, Pallas kernels, normalize(): pl.pallas_call(norm_kernel, grid=(tokens // rows,), in_specs=[pl.BlockSpe...  12.1 us
    pallas_call x2, Pallas kernels, attend_pair(): pl.pallas_call(kernel, in_specs=[smem, smem, smem] + [vmem] * 4, out_spec...  10 us
    unnamed x54, local copies, waits for them, and re-layouts  6.13 us
    all_to_all x1, starting transfers between devices, per_device(): lax.all_to_all(q_sent[0], 'seq', split_axis=0, concat_axis=0, tiled=True)  5 us
    concatenate x2, other arithmetic, spread(): both = jnp.concatenate([near[0], far[0]], axis=0)  4.5 us
  transfers between devices with their start and end apart: 19, of which 7 were waited for; matrix products, arithmetic and copies ran while one was open for 4% of the time, Pallas kernels for 42%

profile of v8, /device:TPU:0, one launch (start us, length us, event | category | flops | bytes accessed | tf_op | source)
XLA Modules:
  0.0 154.0 jit_solution(10356194299069647800)
XLA Ops:
  0.0 0.6 stack.35.at_ref.place_ref
  0.6 3.2 %take_rows.1 = (bf16[128,3072]{1,0:T(8,128)(2,1)}, bf16[64,3072]{1,0:T(8,128)(2,1)}) custom-call(s32[8]{0:T(128)} %stack.35.at_ref.place_ref, bf16[768,3072]{1,0:T(8,128)(2,1)} %x_ref.2), custom_call_target="tpu_custom_call" | custom-call | flops 1048576 | bytes 1024 | tf_op jit(solution)/shard_map/take_rows/pallas_call | solution.py:283
  3.8 3.0 %collective-permute-start.5 = (bf16[128,3072]{1,0:T(8,128)(2,1)}, bf16[128,3072]{1,0:T(8,128)(2,1)}, u32[]{:S(2)}, u32[]{:S(2)}) collective-permute-start(bf16[128,3072]{1,0:T(8,128)(2,1)} %get-tuple-element.259), channel_id=1, source_target_pairs={{0,4},{4,0},{8,12},{12,8},{1,5},{5,1},{9,13},{13,9},{2,6},{6,2},{1... | collective-permute-start | bytes 2359304 | tf_op jit(solution)/shard_map/ppermute | solution.py:428
  6.8 1.7 %cut_heads.2 = (bf16[1,768,256]{2,1,0:T(8,128)(2,1)S(1)}, bf16[1,768,256]{2,1,0:T(8,128)(2,1)S(1)}, bf16[4,768,128]{2,1,0:T(8,128)(2,1)}) custom-call(s32[8]{0:T(128)S(1)} %copy-done.14, bf16[3,768,512]{2,1,0:T(8,128)(2,1)S(1)} %bitcast.9), custom_call_target="tpu_custom_call" | custom-call | flops 1048576 | bytes 1024 | tf_op jit(solution)/shard_map/cut_heads/pallas_call | solution.py:150
  8.5 2.6 %collective-permute-start.4 = (bf16[1,768,256]{2,1,0:T(8,128)(2,1)S(1)}, bf16[1,768,256]{2,1,0:T(8,128)(2,1)}, u32[]{:S(2)}, u32[]{:S(2)}) collective-permute-start(bf16[1,768,256]{2,1,0:T(8,128)(2,1)S(1)} %get-tuple-element.412.refs_1_.refs_6_), channel_id=1, source_target_pairs={{0,8},{4,12},{8,0},{12,4},{1,9},{5,13},{9,1},{13,5},{2,10},{6,14},... | collective-permute-start | bytes 1179656 | tf_op jit(solution)/shard_map/ppermute | solution.py:428
  11.6 1.3 collective-permute-start.1
  13.2 1.4 see.1.limit0_ref
  14.5 7.4 %normalize.3.refs_0_ = bf16[768,3072]{1,0:T(8,128)(2,1)} custom-call(bf16[768,3072]{1,0:T(8,128)(2,1)} %x_ref.2, f32[2,3072]{1,0:T(2,128)} %mod_ref.2), custom_call_target="tpu_custom_call" | custom-call | flops 1048576 | bytes 1024 | tf_op jit(solution)/shard_map/normalize/pallas_call | solution.py:124
  21.9 12.1 %collective-permute-done.5.x_ref = bf16[128,3072]{1,0:T(8,128)(2,1)} collective-permute-done((bf16[128,3072]{1,0:T(8,128)(2,1)}, bf16[128,3072]{1,0:T(8,128)(2,1)}, u32[]{:S(2)}, u32[]{:S(2)}) %collective-permute-start.5) | collective-permute-done | bytes 786464 | tf_op jit(solution)/shard_map/ppermute | solution.py:428
  33.9 2.6 %normalize.4.refs_0_ = bf16[128,3072]{1,0:T(8,128)(2,1)} custom-call(bf16[128,3072]{1,0:T(8,128)(2,1)} %collective-permute-done.5.x_ref, f32[2,3072]{1,0:T(2,128)} %mod_ref.2), custom_call_target="tpu_custom_call" | custom-call | flops 1048576 | bytes 1024 | tf_op jit(solution)/shard_map/normalize/pallas_call | solution.py:124
  36.5 2.0 %collective-permute-start.10 = (bf16[128,3072]{1,0:T(8,128)(2,1)}, bf16[128,3072]{1,0:T(8,128)(2,1)}, u32[]{:S(2)}, u32[]{:S(2)}) collective-permute-start(bf16[128,3072]{1,0:T(8,128)(2,1)} %normalize.4.refs_0_), channel_id=1, source_target_pairs={{0,2},{2,0},{1,3},{3,1},{4,6},{6,4},{5,7},{7,5},{8,10},{10,8},{9,1... | collective-permute-start | bytes 2359304 | tf_op jit(solution)/shard_map/ppermute | solution.py:428
  38.5 3.7 %collective-permute-done.3.x_ref = bf16[64,3072]{1,0:T(8,128)(2,1)S(1)} collective-permute-done((bf16[64,3072]{1,0:T(8,128)(2,1)}, bf16[64,3072]{1,0:T(8,128)(2,1)S(1)}, u32[]{:S(2)}, u32[]{:S(2)}) %collective-permute-start.3) | collective-permute-done | bytes 393248 | tf_op jit(solution)/shard_map/ppermute | solution.py:428
  42.3 2.2 %collective-permute-start.9 = (bf16[1,768,256]{2,1,0:T(8,128)(2,1)}, bf16[1,768,256]{2,1,0:T(8,128)(2,1)S(1)}, u32[]{:S(2)}, u32[]{:S(2)}) collective-permute-start(bf16[1,768,256]{2,1,0:T(8,128)(2,1)} %collective-permute-done.4.refs_3_.refs_8_), channel_id=1, source_target_pairs={{0,16},{16,0},{1,17},{17,1},{2,18},{18,2},{3,19},{19,3},{4,20},{20... | collective-permute-start | bytes 1179656 | tf_op jit(solution)/shard_map/ppermute | solution.py:428
  44.5 2.1 %normalize.5.refs_3_ = bf16[64,3072]{1,0:T(8,128)(2,1)} custom-call(bf16[64,3072]{1,0:T(8,128)(2,1)} %copy-done.24, f32[2,3072]{1,0:T(2,128)} %mod_ref.2), custom_call_target="tpu_custom_call" | custom-call | flops 1048576 | bytes 1024 | tf_op jit(solution)/shard_map/normalize/pallas_call | solution.py:124
  46.6 11.8 %collective-permute-done.2.limit1_ref = f32[2,128]{1,0:T(2,128)S(1)} collective-permute-done((f32[2,128]{1,0:T(2,128)S(1)}, f32[2,128]{1,0:T(2,128)S(1)}, u32[]{:S(2)}, u32[]{:S(2)}) %collective-permute-start.2) | collective-permute-done | bytes 1056 | tf_op jit(solution)/shard_map/ppermute | solution.py:428
  58.4 1.7 %collective-permute-start.7 = (bf16[64,3072]{1,0:T(8,128)(2,1)}, bf16[64,3072]{1,0:T(8,128)(2,1)}, u32[]{:S(2)}, u32[]{:S(2)}) collective-permute-start(bf16[64,3072]{1,0:T(8,128)(2,1)} %normalize.5.refs_3_), channel_id=1, source_target_pairs={{0,2},{2,0},{1,3},{3,1},{4,6},{6,4},{5,7},{7,5},{8,10},{10,8},{9,1... | collective-permute-start | bytes 1179656 | tf_op jit(solution)/shard_map/ppermute | solution.py:428
  60.1 1.5 collective-permute-start.8
  62.1 0.6 cut_heads.3.refs_1_.refs_6_
  62.7 0.8 copy-done.4
  63.5 5.0 %all-to-all-start = ((bf16[4,768,128]{2,1,0:T(8,128)(2,1)}), bf16[4,768,128]{2,1,0:T(8,128)(2,1)}, u32[]{:S(2)}, u32[]{:S(2)}) async-start(bf16[4,768,128]{2,1,0:T(8,128)(2,1)} %get-tuple-element.366), calls=%async_computation | async-start | bytes 1572864 | tf_op jit(solution)/shard_map/all_to_all | solution.py:488
  68.5 3.8 %collective-permute-done.8.refs_4_.refs_9_ = bf16[1,768,256]{2,1,0:T(8,128)(2,1)S(1)} collective-permute-done((bf16[1,768,256]{2,1,0:T(8,128)(2,1)}, bf16[1,768,256]{2,1,0:T(8,128)(2,1)S(1)}, u32[]{:S(2)}, u32[]{:S(2)}) %collective-permute-start.8) | collective-permute-done | bytes 393248 | tf_op jit(solution)/shard_map/ppermute | solution.py:428
  72.3 2.5 %pad_maximum_fusion = bf16[256,3072]{1,0:T(8,128)(2,1)} fusion(bf16[128,3072]{1,0:T(8,128)(2,1)} %collective-permute-done.10.refs_1_, bf16[128,3072]{1,0:T(8,128)(2,1)S(1)} %copy-done.18), kind=kLoop, calls=%fused_computation | loop fusion | flops 3145728 | bytes 3145728 | tf_op jit(solution)/shard_map/concatenate | solution.py:465
  75.0 2.0 %pad_maximum_fusion.1 = bf16[128,3072]{1,0:T(8,128)(2,1)} fusion(bf16[64,3072]{1,0:T(8,128)(2,1)} %collective-permute-done.7.refs_4_, bf16[64,3072]{1,0:T(8,128)(2,1)S(1)} %copy-done.20), kind=kLoop, calls=%fused_computation.1 | loop fusion | flops 1572864 | bytes 1572864 | tf_op jit(solution)/shard_map/concatenate | solution.py:465
  77.4 6.6 %project.6.rows0_ref = bf16[768,256]{1,0:T(8,128)(2,1)} custom-call(s32[8]{0:T(128)} %stack.35.at_ref.place_ref, bf16[768,3072]{1,0:T(8,128)(2,1)} %normalize.3.refs_0_, bf16[1,768,256]{2,1,0:T(8,128)(2,1)} %copy-done.11, bf16[1,768,256]{2,1,0:T(8,128)(2,1)} %collective-permute-done.refs_2_.refs_7_, ...), custom_call_target="tpu_custom_call" | custom-call | flops 68719476736 | bytes 1024 | tf_op jit(solution)/shard_map/project/pallas_call | solution.py:254
  84.0 2.9 %all-to-all-done.refs_1_.refs_6_ = bf16[4,768,128]{2,1,0:T(8,128)(2,1)} async-done(((bf16[4,768,128]{2,1,0:T(8,128)(2,1)}), bf16[4,768,128]{2,1,0:T(8,128)(2,1)}, u32[]{:S(2)}, u32[]{:S(2)}) %all-to-all-start) | async-done | bytes 786464 | tf_op jit(solution)/shard_map/all_to_all | solution.py:488
  87.0 1.5 collective-permute-start.15
  88.5 1.2 copy-done.19
  89.7 0.9 copy-done.21
  90.6 5.8 %project.7.rows1_ref = bf16[768,256]{1,0:T(8,128)(2,1)} custom-call(s32[8]{0:T(128)} %stack.35.at_ref.place_ref, bf16[128,3072]{1,0:T(8,128)(2,1)} %normalize.4.refs_0_, bf16[128,3072]{1,0:T(8,128)(2,1)} %collective-permute-done.10.refs_1_, bf16[256,3072]{1,0:T(8,128)(2,1)} %copy-done.19, bf16[64,3072]{1,0:T(8,128)(2,1)} %normalize.5.refs_3_, ...), custom_call_target="tpu_custom_call" | custom-call | flops 1048576 | bytes 1024 | tf_op jit(solution)/shard_map/project/pallas_call | solution.py:254
  96.4 1.1 broadcast_select_fusion
  97.6 6.6 %project.8.rows0_ref = bf16[768,256]{1,0:T(8,128)(2,1)} custom-call(s32[8]{0:T(128)} %stack.35.at_ref.place_ref, bf16[768,3072]{1,0:T(8,128)(2,1)} %normalize.3.refs_0_, bf16[1,768,256]{2,1,0:T(8,128)(2,1)} %copy-done.4, bf16[1,768,256]{2,1,0:T(8,128)(2,1)} %collective-permute-done.6.refs_2_.refs_7_, bf16[1,768,256]{2,1,0:T(8,128)(2,1)} %copy-done.22, ...), custom_call_target="tpu_custom_call" | custom-call | flops 1048576 | bytes 1024 | tf_op jit(solution)/shard_map/project/pallas_call | solution.py:254
  104.2 6.0 %project.9.rows1_ref = bf16[768,256]{1,0:T(8,128)(2,1)} custom-call(s32[8]{0:T(128)} %stack.35.at_ref.place_ref, bf16[128,3072]{1,0:T(8,128)(2,1)} %normalize.4.refs_0_, bf16[128,3072]{1,0:T(8,128)(2,1)} %collective-permute-done.10.refs_1_, bf16[256,3072]{1,0:T(8,128)(2,1)} %copy-done.19, bf16[64,3072]{1,0:T(8,128)(2,1)} %normalize.5.refs_3_, ...), custom_call_target="tpu_custom_call" | custom-call | flops 1048576 | bytes 1024 | tf_op jit(solution)/shard_map/project/pallas_call | solution.py:254
  110.2 1.1 broadcast_select_fusion.1
  111.3 2.0 %collective-permute-start.13 = (bf16[768,256]{1,0:T(8,128)(2,1)S(1)}, bf16[768,256]{1,0:T(8,128)(2,1)S(1)}, u32[]{:S(2)}, u32[]{:S(2)}) collective-permute-start(bf16[768,256]{1,0:T(8,128)(2,1)S(1)} %broadcast_select_fusion.1), channel_id=1, source_target_pairs={{0,8},{4,12},{8,0},{12,4},{1,9},{5,13},{9,1},{13,5},{2,10},{6,14},... | collective-permute-start | bytes 1179656 | tf_op jit(solution)/shard_map/ppermute | solution.py:428
  113.2 6.6 %project.10 = (bf16[768,128]{1,0:T(8,128)(2,1)}, bf16[768,128]{1,0:T(8,128)(2,1)}) custom-call(s32[8]{0:T(128)} %stack.35.at_ref.place_ref, bf16[768,3072]{1,0:T(8,128)(2,1)} %normalize.3.refs_0_, bf16[4,768,128]{2,1,0:T(8,128)(2,1)} %all-to-all-done.refs_1_.refs_6_, bf16[4,768,128]{2,1,0:T(8,128)(2,1)} %collective-permute-done.15.refs_2_.refs_7_, ...), custom_call_target="tpu_custom_call" | custom-call | flops 1048576 | bytes 1024 | tf_op jit(solution)/shard_map/project/pallas_call | solution.py:254
  119.9 5.9 %project.11 = (bf16[768,128]{1,0:T(8,128)(2,1)}, bf16[768,128]{1,0:T(8,128)(2,1)}) custom-call(s32[8]{0:T(128)} %stack.35.at_ref.place_ref, bf16[128,3072]{1,0:T(8,128)(2,1)} %normalize.4.refs_0_, bf16[128,3072]{1,0:T(8,128)(2,1)} %collective-permute-done.10.refs_1_, bf16[256,3072]{1,0:T(8,128)(2,1)} %copy-done.19, bf16[64,3072]{1,0:T(8,128)(2,1)} %normalize.5.refs_3_, ...), custom_call_target="tpu_custom_call" | custom-call | flops 1048576 | bytes 1024 | tf_op jit(solution)/shard_map/project/pallas_call | solution.py:254
  125.9 1.0 copy-done.9
  126.9 5.1 %attend_pair.2 = (bf16[768,128]{1,0:T(8,128)(2,1)S(1)}, f32[768,128]{1,0:T(8,128)S(1)}, f32[768,128]{1,0:T(8,128)S(1)}) custom-call(s32[8]{0:T(128)S(1)} %copy-done.16, f32[2,128]{1,0:T(2,128)S(1)} %copy-done.17, f32[2,128]{1,0:T(2,128)S(1)} %collective-permute-done.2.limit1_ref, bf16[768,128]{1,0:T(8,128)(2,1)S(1)} %copy-done.8, ...), custom_call_target="tpu_custom_call" | custom-call | flops 1048576 | bytes 1024 | tf_op jit(solution)/shard_map/attend_pair/pallas_call | solution.py:347
  132.0 0.9 copy-done.10
  132.9 1.6 %attend_halo.2 = (bf16[768,128]{1,0:T(8,128)(2,1)S(1)}, bf16[768,128]{1,0:T(8,128)(2,1)S(1)}) custom-call(s32[8]{0:T(128)S(1)} %copy-done.16, f32[2,128]{1,0:T(2,128)S(1)} %copy-done.17, f32[2,128]{1,0:T(2,128)S(1)} %collective-permute-done.2.limit1_ref, bf16[768,128]{1,0:T(8,128)(2,1)S(1)} %copy-done.8, bf16[768,128]{1,0:T(8,128)(2,1)S(1)} %copy-done.10, ...), custom_call_target="tpu_custom_call" | custom-call | flops 1048576 | bytes 1024 | tf_op jit(solution)/shard_map/attend_halo/pallas_call | solution.py:384
  134.6 4.9 %attend_pair.3 = (bf16[768,128]{1,0:T(8,128)(2,1)S(1)}, f32[768,128]{1,0:T(8,128)S(1)}, f32[768,128]{1,0:T(8,128)S(1)}) custom-call(s32[8]{0:T(128)S(1)} %copy-done.16, f32[2,128]{1,0:T(2,128)S(1)} %copy-done.17, f32[2,128]{1,0:T(2,128)S(1)} %collective-permute-done.2.limit1_ref, bf16[768,128]{1,0:T(8,128)(2,1)S(1)} %copy-done.6, ...), custom_call_target="tpu_custom_call" | custom-call | flops 1048576 | bytes 1024 | tf_op jit(solution)/shard_map/attend_pair/pallas_call | solution.py:347
  139.5 1.6 %attend_halo.3 = (bf16[768,128]{1,0:T(8,128)(2,1)S(1)}, bf16[768,128]{1,0:T(8,128)(2,1)S(1)}) custom-call(s32[8]{0:T(128)S(1)} %copy-done.16, f32[2,128]{1,0:T(2,128)S(1)} %copy-done.17, f32[2,128]{1,0:T(2,128)S(1)} %collective-permute-done.2.limit1_ref, bf16[768,128]{1,0:T(8,128)(2,1)S(1)} %copy-done.6, bf16[768,128]{1,0:T(8,128)(2,1)S(1)} %copy-done.7, ...), custom_call_target="tpu_custom_call" | custom-call | flops 1048576 | bytes 1024 | tf_op jit(solution)/shard_map/attend_halo/pallas_call | solution.py:384
  141.2 0.7 copy-done.13
  141.9 2.0 %collective-permute-start.16 = (bf16[768,128]{1,0:T(8,128)(2,1)S(1)}, bf16[768,128]{1,0:T(8,128)(2,1)S(1)}, u32[]{:S(2)}, u32[]{:S(2)}) collective-permute-start(bf16[768,128]{1,0:T(8,128)(2,1)S(1)} %get-tuple-element.511), channel_id=1, source_target_pairs={{0,4},{4,0},{8,12},{12,8},{1,5},{5,1},{9,13},{13,9},{2,6},{6,2},{1... | collective-permute-start | bytes 589832 | tf_op jit(solution)/shard_map/ppermute | solution.py:428
  143.9 5.1 %collective-permute-done.17.refs_3_ = bf16[768,128]{1,0:T(8,128)(2,1)S(1)} collective-permute-done((bf16[768,128]{1,0:T(8,128)(2,1)S(1)}, bf16[768,128]{1,0:T(8,128)(2,1)S(1)}, u32[]{:S(2)}, u32[]{:S(2)}) %collective-permute-start.17) | collective-permute-done | bytes 196640 | tf_op jit(solution)/shard_map/ppermute | solution.py:428
  148.9 2.1 %collective-permute-done.16.refs_2_ = bf16[768,128]{1,0:T(8,128)(2,1)S(1)} collective-permute-done((bf16[768,128]{1,0:T(8,128)(2,1)S(1)}, bf16[768,128]{1,0:T(8,128)(2,1)S(1)}, u32[]{:S(2)}, u32[]{:S(2)}) %collective-permute-start.16) | collective-permute-done | bytes 196640 | tf_op jit(solution)/shard_map/ppermute | solution.py:428
  151.0 0.7 copy-done.26
  151.7 2.2 %assemble.1 = bf16[768,512]{1,0:T(8,128)(2,1)} custom-call(s32[8]{0:T(128)} %stack.35.at_ref.place_ref, bf16[768,128]{1,0:T(8,128)(2,1)} %copy-done.12, bf16[768,128]{1,0:T(8,128)(2,1)} %copy-done.13, bf16[768,128]{1,0:T(8,128)(2,1)} %copy-done.26, bf16[768,128]{1,0:T(8,128)(2,1)} %copy-done.25), custom_call_target="tpu_custom_call" | custom-call | flops 1048576 | bytes 1024 | tf_op jit(solution)/shard_map/assemble/pallas_call | solution.py:404
  (67 shorter events, 2.0 us)
Async XLA Ops:
  0.6 6.2 %copy-start.3 = (bf16[768,3,512]{2,0,1:T(8,128)(2,1)S(1)}, bf16[768,3,512]{2,0,1:T(8,128)(2,1)}, u32[]{:S(2)}) copy-start(bf16[768,3,512]{2,0,1:T(8,128)(2,1)} %param.8) | copy-start | bytes 7077892
  0.6 6.2 %copy-start.14 = (s32[8]{0:T(128)S(1)}, s32[8]{0:T(128)}, u32[]{:S(2)}) copy-start(s32[8]{0:T(128)} %stack.35.at_ref.place_ref) | copy-start | bytes 100
  3.8 30.1 %collective-permute-start.5 = (bf16[128,3072]{1,0:T(8,128)(2,1)}, bf16[128,3072]{1,0:T(8,128)(2,1)}, u32[]{:S(2)}, u32[]{:S(2)}) collective-permute-start(bf16[128,3072]{1,0:T(8,128)(2,1)} %get-tuple-element.259), channel_id=1, source_target_pairs={{0,4},{4,0},{8,12},{12,8},{1,5},{5,1},{9,13},{13,9},{2,6},{6,2},{1... | collective-permute-start | bytes 2359304 | tf_op jit(solution)/shard_map/ppermute | solution.py:428
  8.5 13.3 %copy-start.11 = (bf16[1,768,256]{2,1,0:T(8,128)(2,1)}, bf16[1,768,256]{2,1,0:T(8,128)(2,1)S(1)}, u32[]{:S(2)}) copy-start(bf16[1,768,256]{2,1,0:T(8,128)(2,1)S(1)} %get-tuple-element.412.refs_1_.refs_6_) | copy-start | bytes 1179652
  8.5 28.0 %collective-permute-start.4 = (bf16[1,768,256]{2,1,0:T(8,128)(2,1)S(1)}, bf16[1,768,256]{2,1,0:T(8,128)(2,1)}, u32[]{:S(2)}, u32[]{:S(2)}) collective-permute-start(bf16[1,768,256]{2,1,0:T(8,128)(2,1)S(1)} %get-tuple-element.412.refs_1_.refs_6_), channel_id=1, source_target_pairs={{0,8},{4,12},{8,0},{12,4},{1,9},{5,13},{9,1},{13,5},{2,10},{6,14},... | collective-permute-start | bytes 1179656 | tf_op jit(solution)/shard_map/ppermute | solution.py:428
  11.1 31.1 %collective-permute-start.3 = (bf16[64,3072]{1,0:T(8,128)(2,1)}, bf16[64,3072]{1,0:T(8,128)(2,1)S(1)}, u32[]{:S(2)}, u32[]{:S(2)}) collective-permute-start(bf16[64,3072]{1,0:T(8,128)(2,1)} %get-tuple-element.260), channel_id=1, source_target_pairs={{0,4},{4,0},{8,12},{12,8},{1,5},{5,1},{9,13},{13,9},{2,6},{6,2},{1... | collective-permute-start | bytes 1179656 | tf_op jit(solution)/shard_map/ppermute | solution.py:428
  11.6 48.5 %collective-permute-start.1 = (bf16[1,768,256]{2,1,0:T(8,128)(2,1)S(1)}, bf16[1,768,256]{2,1,0:T(8,128)(2,1)}, u32[]{:S(2)}, u32[]{:S(2)}) collective-permute-start(bf16[1,768,256]{2,1,0:T(8,128)(2,1)S(1)} %get-tuple-element.262), channel_id=1, source_target_pairs={{0,12},{4,8},{8,4},{12,0},{1,13},{5,9},{9,5},{13,1},{2,14},{6,10},... | collective-permute-start | bytes 1179656 | tf_op jit(solution)/shard_map/ppermute | solution.py:428
  12.9 48.7 %collective-permute-start = (bf16[1,768,256]{2,1,0:T(8,128)(2,1)S(1)}, bf16[1,768,256]{2,1,0:T(8,128)(2,1)}, u32[]{:S(2)}, u32[]{:S(2)}) collective-permute-start(bf16[1,768,256]{2,1,0:T(8,128)(2,1)S(1)} %get-tuple-element.262), channel_id=1, source_target_pairs={{0,4},{4,0},{8,12},{12,8},{1,5},{5,1},{9,13},{13,9},{2,6},{6,2},{1... | collective-permute-start | bytes 1179656 | tf_op jit(solution)/shard_map/ppermute | solution.py:428
  14.5 19.4 %copy-start.17 = (f32[2,128]{1,0:T(2,128)S(1)}, f32[2,128]{1,0:T(2,128)}, u32[]{:S(2)}) copy-start(f32[2,128]{1,0:T(2,128)} %see.1.limit0_ref) | copy-start | bytes 3076
  21.9 40.2 %copy-start.15 = (s32[8]{0:T(128)S(1)}, s32[8]{0:T(128)}, u32[]{:S(2)}) copy-start(s32[8]{0:T(128)} %stack.35.at_ref.place_ref) | copy-start | bytes 100
  33.9 24.5 %collective-permute-start.2 = (f32[2,128]{1,0:T(2,128)S(1)}, f32[2,128]{1,0:T(2,128)S(1)}, u32[]{:S(2)}, u32[]{:S(2)}) collective-permute-start(f32[2,128]{1,0:T(2,128)S(1)} %copy-done.17), channel_id=1, source_target_pairs={{0,4},{4,0},{8,12},{12,8},{1,5},{5,1},{9,13},{13,9},{2,6},{6,2},{1... | collective-permute-start | bytes 3080 | tf_op jit(solution)/shard_map/ppermute | solution.py:428
  36.5 31.9 %collective-permute-start.10 = (bf16[128,3072]{1,0:T(8,128)(2,1)}, bf16[128,3072]{1,0:T(8,128)(2,1)}, u32[]{:S(2)}, u32[]{:S(2)}) collective-permute-start(bf16[128,3072]{1,0:T(8,128)(2,1)} %normalize.4.refs_0_), channel_id=1, source_target_pairs={{0,2},{2,0},{1,3},{3,1},{4,6},{6,4},{5,7},{7,5},{8,10},{10,8},{9,1... | collective-permute-start | bytes 2359304 | tf_op jit(solution)/shard_map/ppermute | solution.py:428
  42.3 2.2 %copy-start.24 = (bf16[64,3072]{1,0:T(8,128)(2,1)}, bf16[64,3072]{1,0:T(8,128)(2,1)S(1)}, u32[]{:S(2)}) copy-start(bf16[64,3072]{1,0:T(8,128)(2,1)S(1)} %collective-permute-done.3.x_ref) | copy-start | bytes 1179652
  42.3 26.2 %collective-permute-start.9 = (bf16[1,768,256]{2,1,0:T(8,128)(2,1)}, bf16[1,768,256]{2,1,0:T(8,128)(2,1)S(1)}, u32[]{:S(2)}, u32[]{:S(2)}) collective-permute-start(bf16[1,768,256]{2,1,0:T(8,128)(2,1)} %collective-permute-done.4.refs_3_.refs_8_), channel_id=1, source_target_pairs={{0,16},{16,0},{1,17},{17,1},{2,18},{18,2},{3,19},{19,3},{4,20},{20... | collective-permute-start | bytes 1179656 | tf_op jit(solution)/shard_map/ppermute | solution.py:428
  58.4 16.5 %collective-permute-start.7 = (bf16[64,3072]{1,0:T(8,128)(2,1)}, bf16[64,3072]{1,0:T(8,128)(2,1)}, u32[]{:S(2)}, u32[]{:S(2)}) collective-permute-start(bf16[64,3072]{1,0:T(8,128)(2,1)} %normalize.5.refs_3_), channel_id=1, source_target_pairs={{0,2},{2,0},{1,3},{3,1},{4,6},{6,4},{5,7},{7,5},{8,10},{10,8},{9,1... | collective-permute-start | bytes 1179656 | tf_op jit(solution)/shard_map/ppermute | solution.py:428
  60.1 12.3 %collective-permute-start.8 = (bf16[1,768,256]{2,1,0:T(8,128)(2,1)}, bf16[1,768,256]{2,1,0:T(8,128)(2,1)S(1)}, u32[]{:S(2)}, u32[]{:S(2)}) collective-permute-start(bf16[1,768,256]{2,1,0:T(8,128)(2,1)} %collective-permute-done.1.refs_4_.refs_9_), channel_id=1, source_target_pairs={{0,16},{16,0},{1,17},{17,1},{2,18},{18,2},{3,19},{19,3},{4,20},{20... | collective-permute-start | bytes 1179656 | tf_op jit(solution)/shard_map/ppermute | solution.py:428
  61.6 34.8 %collective-permute-start.6 = (bf16[1,768,256]{2,1,0:T(8,128)(2,1)}, bf16[1,768,256]{2,1,0:T(8,128)(2,1)}, u32[]{:S(2)}, u32[]{:S(2)}) collective-permute-start(bf16[1,768,256]{2,1,0:T(8,128)(2,1)} %collective-permute-done.refs_2_.refs_7_), channel_id=1, source_target_pairs={{0,16},{16,0},{1,17},{17,1},{2,18},{18,2},{3,19},{19,3},{4,20},{20... | collective-permute-start | bytes 1179656 | tf_op jit(solution)/shard_map/ppermute | solution.py:428
  62.7 0.8 copy-start.4
  63.5 8.8 %copy-start.18 = (bf16[128,3072]{1,0:T(8,128)(2,1)S(1)}, bf16[128,3072]{1,0:T(8,128)(2,1)}, u32[]{:S(2)}) copy-start(bf16[128,3072]{1,0:T(8,128)(2,1)} %normalize.4.refs_0_) | copy-start | bytes 2359300
  63.5 23.5 %all-to-all-start = ((bf16[4,768,128]{2,1,0:T(8,128)(2,1)}), bf16[4,768,128]{2,1,0:T(8,128)(2,1)}, u32[]{:S(2)}, u32[]{:S(2)}) async-start(bf16[4,768,128]{2,1,0:T(8,128)(2,1)} %get-tuple-element.366), calls=%async_computation | async-start | bytes 1572864 | tf_op jit(solution)/shard_map/all_to_all | solution.py:488
  68.5 6.5 %copy-start.20 = (bf16[64,3072]{1,0:T(8,128)(2,1)S(1)}, bf16[64,3072]{1,0:T(8,128)(2,1)}, u32[]{:S(2)}) copy-start(bf16[64,3072]{1,0:T(8,128)(2,1)} %normalize.5.refs_3_) | copy-start | bytes 1179652
  68.5 6.4 %copy-start.22 = (bf16[1,768,256]{2,1,0:T(8,128)(2,1)}, bf16[1,768,256]{2,1,0:T(8,128)(2,1)S(1)}, u32[]{:S(2)}) copy-start(bf16[1,768,256]{2,1,0:T(8,128)(2,1)S(1)} %collective-permute-done.9.refs_3_.refs_8_) | copy-start | bytes 1179652
  72.3 2.5 %copy-start.23 = (bf16[1,768,256]{2,1,0:T(8,128)(2,1)}, bf16[1,768,256]{2,1,0:T(8,128)(2,1)S(1)}, u32[]{:S(2)}) copy-start(bf16[1,768,256]{2,1,0:T(8,128)(2,1)S(1)} %collective-permute-done.8.refs_4_.refs_9_) | copy-start | bytes 1179652
  74.9 13.6 %collective-permute-start.12 = (bf16[256,3072]{1,0:T(8,128)(2,1)}, bf16[256,3072]{1,0:T(8,128)(2,1)S(1)}, u32[]{:S(2)}, u32[]{:S(2)}) collective-permute-start(bf16[256,3072]{1,0:T(8,128)(2,1)} %pad_maximum_fusion), channel_id=1, source_target_pairs={{0,1},{1,0},{2,3},{3,2},{4,5},{5,4},{6,7},{7,6},{8,9},{9,8},{10,11... | collective-permute-start | bytes 4718600 | tf_op jit(solution)/shard_map/ppermute | solution.py:428
  76.9 11.6 %collective-permute-start.11 = (bf16[128,3072]{1,0:T(8,128)(2,1)}, bf16[128,3072]{1,0:T(8,128)(2,1)S(1)}, u32[]{:S(2)}, u32[]{:S(2)}) collective-permute-start(bf16[128,3072]{1,0:T(8,128)(2,1)} %pad_maximum_fusion.1), channel_id=1, source_target_pairs={{0,1},{1,0},{2,3},{3,2},{4,5},{5,4},{6,7},{7,6},{8,9},{9,8},{10,11... | collective-permute-start | bytes 2359304 | tf_op jit(solution)/shard_map/ppermute | solution.py:428
  84.0 12.4 %copy-start.5 = (bf16[768,256]{1,0:T(8,128)(2,1)S(1)}, bf16[768,256]{1,0:T(8,128)(2,1)}, u32[]{:S(2)}) copy-start(bf16[768,256]{1,0:T(8,128)(2,1)} %project.6.rows0_ref) | copy-start | bytes 1179652
  87.0 26.2 %collective-permute-start.15 = (bf16[4,768,128]{2,1,0:T(8,128)(2,1)}, bf16[4,768,128]{2,1,0:T(8,128)(2,1)}, u32[]{:S(2)}, u32[]{:S(2)}) collective-permute-start(bf16[4,768,128]{2,1,0:T(8,128)(2,1)} %all-to-all-done.refs_1_.refs_6_), channel_id=1, source_target_pairs={{0,16},{16,0},{1,17},{17,1},{2,18},{18,2},{3,19},{19,3},{4,20},{20... | collective-permute-start | bytes 2359304 | tf_op jit(solution)/shard_map/ppermute | solution.py:428
  88.5 1.2 copy-start.19
  89.7 0.9 copy-start.21
  97.5 34.5 %collective-permute-start.14 = (bf16[768,256]{1,0:T(8,128)(2,1)S(1)}, bf16[768,256]{1,0:T(8,128)(2,1)S(1)}, u32[]{:S(2)}, u32[]{:S(2)}) collective-permute-start(bf16[768,256]{1,0:T(8,128)(2,1)S(1)} %broadcast_select_fusion), channel_id=1, source_target_pairs={{0,8},{4,12},{8,0},{12,4},{1,9},{5,13},{9,1},{13,5},{2,10},{6,14},... | collective-permute-start | bytes 1179656 | tf_op jit(solution)/shard_map/ppermute | solution.py:428
  104.2 6.0 %copy-start = (bf16[768,256]{1,0:T(8,128)(2,1)S(1)}, bf16[768,256]{1,0:T(8,128)(2,1)}, u32[]{:S(2)}) copy-start(bf16[768,256]{1,0:T(8,128)(2,1)} %project.8.rows0_ref) | copy-start | bytes 1179652
  111.3 28.2 %collective-permute-start.13 = (bf16[768,256]{1,0:T(8,128)(2,1)S(1)}, bf16[768,256]{1,0:T(8,128)(2,1)S(1)}, u32[]{:S(2)}, u32[]{:S(2)}) collective-permute-start(bf16[768,256]{1,0:T(8,128)(2,1)S(1)} %broadcast_select_fusion.1), channel_id=1, source_target_pairs={{0,8},{4,12},{8,0},{12,4},{1,9},{5,13},{9,1},{13,5},{2,10},{6,14},... | collective-permute-start | bytes 1179656 | tf_op jit(solution)/shard_map/ppermute | solution.py:428
  119.8 6.0 %copy-start.2 = (bf16[768,256]{1,0:T(8,128)(2,1)S(1)}, bf16[768,256]{1,0:T(8,128)(2,1)}, u32[]{:S(2)}) copy-start(bf16[768,256]{1,0:T(8,128)(2,1)} %project.7.rows1_ref) | copy-start | bytes 1179652
  119.8 6.0 %copy-start.8 = (bf16[768,128]{1,0:T(8,128)(2,1)S(1)}, bf16[768,128]{1,0:T(8,128)(2,1)}, u32[]{:S(2)}) copy-start(bf16[768,128]{1,0:T(8,128)(2,1)} %get-tuple-element.483.q0_ref) | copy-start | bytes 589828
  119.9 6.0 %copy-start.16 = (s32[8]{0:T(128)S(1)}, s32[8]{0:T(128)}, u32[]{:S(2)}) copy-start(s32[8]{0:T(128)} %stack.35.at_ref.place_ref) | copy-start | bytes 100
  125.8 8.8 %copy-start.1 = (bf16[768,256]{1,0:T(8,128)(2,1)S(1)}, bf16[768,256]{1,0:T(8,128)(2,1)}, u32[]{:S(2)}) copy-start(bf16[768,256]{1,0:T(8,128)(2,1)} %project.9.rows1_ref) | copy-start | bytes 1179652
  125.8 8.8 %copy-start.6 = (bf16[768,128]{1,0:T(8,128)(2,1)S(1)}, bf16[768,128]{1,0:T(8,128)(2,1)}, u32[]{:S(2)}) copy-start(bf16[768,128]{1,0:T(8,128)(2,1)} %get-tuple-element.504.q0_ref) | copy-start | bytes 589828
  125.8 8.8 %copy-start.7 = (bf16[768,128]{1,0:T(8,128)(2,1)S(1)}, bf16[768,128]{1,0:T(8,128)(2,1)}, u32[]{:S(2)}) copy-start(bf16[768,128]{1,0:T(8,128)(2,1)} %get-tuple-element.505.q1_ref) | copy-start | bytes 589828
  125.9 1.0 copy-start.9
  132.0 0.9 copy-start.10
  134.6 6.6 %copy-start.12 = (bf16[768,128]{1,0:T(8,128)(2,1)}, bf16[768,128]{1,0:T(8,128)(2,1)S(1)}, u32[]{:S(2)}) copy-start(bf16[768,128]{1,0:T(8,128)(2,1)S(1)} %get-tuple-element.501.refs_0_) | copy-start | bytes 589828
  141.1 0.7 copy-start.13
  141.8 7.1 %collective-permute-start.17 = (bf16[768,128]{1,0:T(8,128)(2,1)S(1)}, bf16[768,128]{1,0:T(8,128)(2,1)S(1)}, u32[]{:S(2)}, u32[]{:S(2)}) collective-permute-start(bf16[768,128]{1,0:T(8,128)(2,1)S(1)} %get-tuple-element.512), channel_id=1, source_target_pairs={{0,4},{4,0},{8,12},{12,8},{1,5},{5,1},{9,13},{13,9},{2,6},{6,2},{1... | collective-permute-start | bytes 589832 | tf_op jit(solution)/shard_map/ppermute | solution.py:428
  141.9 9.1 %collective-permute-start.16 = (bf16[768,128]{1,0:T(8,128)(2,1)S(1)}, bf16[768,128]{1,0:T(8,128)(2,1)S(1)}, u32[]{:S(2)}, u32[]{:S(2)}) collective-permute-start(bf16[768,128]{1,0:T(8,128)(2,1)S(1)} %get-tuple-element.511), channel_id=1, source_target_pairs={{0,4},{4,0},{8,12},{12,8},{1,5},{5,1},{9,13},{13,9},{2,6},{6,2},{1... | collective-permute-start | bytes 589832 | tf_op jit(solution)/shard_map/ppermute | solution.py:428
  148.9 2.1 %copy-start.25 = (bf16[768,128]{1,0:T(8,128)(2,1)}, bf16[768,128]{1,0:T(8,128)(2,1)S(1)}, u32[]{:S(2)}) copy-start(bf16[768,128]{1,0:T(8,128)(2,1)S(1)} %collective-permute-done.17.refs_3_) | copy-start | bytes 589828
  151.0 0.7 copy-start.26

commit v9 on v8

v9 whole, which is shorter than its diff:
```python
import math

import jax
import jax.numpy as jnp
from jax import lax
from jax.experimental import pallas as pl
from jax.experimental.pallas import tpu as pltpu
from jax.sharding import PartitionSpec as P

EPS = 1e-06
VMEM = 28 << 20
WHOLE = 60 << 20
FIRST = 8
HIDDEN = -1e30
SPACE = pl.CostEstimate(flops=1 << 36, bytes_accessed=1 << 10, transcendentals=0)
COST = pl.CostEstimate(flops=1 << 20, bytes_accessed=1 << 10, transcendentals=0)


def with_halo(shard, sides, width):
    for axis, dim in sides:
        devices, length = (lax.axis_size(axis), shard.shape[dim])
        up = [(i, (i + 1) % devices) for i in range(devices - 1)]
        down = [(j, i) for i, j in up]
        last = lax.slice_in_dim(shard, length - width, length, axis=dim)
        first = lax.slice_in_dim(shard, 0, width, axis=dim)
        before = lax.ppermute(last, axis, up)
        after = lax.ppermute(first, axis, down)
        shard = jnp.concatenate([before, shard, after], axis=dim)
    return shard


def normed_heads(tensor, gain_row, head_dim):
    shaped = tensor.reshape(tensor.shape[0], tensor.shape[1] // head_dim, head_dim)
    scaled = (
        shaped * lax.rsqrt(jnp.mean(shaped * shaped, axis=-1, keepdims=True) + EPS) * gain_row
    )
    return scaled.astype(jnp.bfloat16)


def visible_tiles(block_lists):
    position = lax.axis_index("seq")
    tile_dev = block_lists.shape[0]
    candidates = (position - 1) * tile_dev + jnp.arange(3 * tile_dev, dtype=jnp.int32)
    matches = (block_lists[:, :, None] == candidates[None, None, :]) & (
        block_lists[:, :, None] >= 0
    )
    return jnp.any(matches, axis=1)


def general(frames, modulation, w_qkv, b_qkv, qk_gain, block_lists):
    inputs = frames.astype(jnp.float32)
    average = jnp.mean(inputs, axis=-1, keepdims=True)
    centred = inputs - average
    variance = jnp.mean(centred * centred, axis=-1, keepdims=True)
    normed = centred * lax.rsqrt(variance + EPS) * (1.0 + modulation[0]) + modulation[1]
    normed = normed.astype(jnp.bfloat16)
    tokens = normed.shape[0]
    width_cols = w_qkv.shape[2]
    head_dim = qk_gain.shape[1]
    heads = width_cols // head_dim
    projected = jnp.einsum(
        "td,djc->tjc",
        normed,
        lax.all_gather(w_qkv, "seq", axis=0, tiled=True),
        preferred_element_type=jnp.float32,
    )
    projected = projected + b_qkv
    queries = normed_heads(projected[:, 0], qk_gain[0], head_dim)
    key_rows = normed_heads(projected[:, 1], qk_gain[1], head_dim)
    values = projected[:, 2].astype(jnp.bfloat16).reshape(tokens, heads, head_dim)
    stacked = jnp.stack([key_rows, values], axis=0)
    neighbourhood = with_halo(stacked, (("seq", 1),), tokens)
    tile_len = tokens // block_lists.shape[0]
    allowed_keys = jnp.repeat(
        jnp.repeat(visible_tiles(block_lists), tile_len, axis=0), tile_len, axis=1
    )
    factor = 1.0 / math.sqrt(head_dim)
    scores = (
        jnp.einsum("qhd,khd->hqk", queries, neighbourhood[0], preferred_element_type=jnp.float32)
        * factor
    )
    weights = jnp.where(allowed_keys[None, :, :], jnp.exp(scores), 0.0)
    totals = jnp.sum(weights, axis=-1)
    mixture = jnp.einsum(
        "hqk,khd->qhd",
        weights.astype(jnp.bfloat16),
        neighbourhood[1],
        preferred_element_type=jnp.float32,
    )
    result = (mixture / jnp.transpose(totals)[:, :, None]).astype(jnp.bfloat16)
    return result.reshape(tokens, width_cols)


class Line:
    def __init__(self):
        self.held = []

    def reached(self, *values):
        boxes = [[v] for v in values]
        self.held += boxes
        return boxes

    def after(self, *values):
        out = lax.optimization_barrier((*values, *(box[0] for box in self.held)))
        for box, value in zip(self.held, out[len(values) :]):
            box[0] = value
        return out[: len(values)]

    def drop(self, *boxes):
        self.held = [box for box in self.held if all(box is not b for b in boxes)]
        return [box[0] for box in boxes]


def norm_kernel(x_ref, mod_ref, o_ref):
    x = x_ref[...].astype(jnp.float32)
    centred = x - jnp.mean(x, axis=-1, keepdims=True)
    variance = jnp.mean(centred * centred, axis=-1, keepdims=True)
    scaled = centred * lax.rsqrt(variance + EPS) * (1.0 + mod_ref[0:1, :]) + mod_ref[1:2, :]
    o_ref[...] = scaled.astype(jnp.bfloat16)


def normalize(frames, modulation, rows):
    tokens, width = frames.shape
    return pl.pallas_call(
        norm_kernel,
        grid=(tokens // rows,),
        in_specs=[
            pl.BlockSpec((rows, width), lambda i: (i, 0)),
            pl.BlockSpec((2, width), lambda i: (0, 0)),
        ],
        out_specs=pl.BlockSpec((rows, width), lambda i: (i, 0)),
        out_shape=jax.ShapeDtypeStruct((tokens, width), jnp.bfloat16),
        cost_estimate=COST,
        name="normalize",
    )(frames, modulation)


def cut_heads(at, w, groups, cost=None):
    rows = w.shape[1]
    head_dim = 128
    shapes = [(len(indices), rows, head_dim * len(js)) for indices, js in groups]

    def kernel(at_ref, w_ref, *out_refs):
        for (indices, js), ref in zip(groups, out_refs):
            for n, index in enumerate(indices):
                cols = pl.ds(pl.multiple_of(at_ref[index] * head_dim, 128), head_dim)
                for i, j in enumerate(js):
                    ref[n, :, i * head_dim : (i + 1) * head_dim] = w_ref[j, :, cols]

    return pl.pallas_call(
        kernel,
        in_specs=[pl.BlockSpec(memory_space=pltpu.SMEM), pl.BlockSpec()],
        out_specs=[pl.BlockSpec()] * len(groups),
        out_shape=[jax.ShapeDtypeStruct(shape, jnp.bfloat16) for shape in shapes],
        compiler_params=pltpu.CompilerParams(vmem_limit_bytes=VMEM),
        cost_estimate=cost or COST,
        name="cut_heads",
    )(at, w)


def see(at, lists, tile_dev):
    def kernel(at_ref, lists_ref, o_ref):
        lists = lists_ref[...]
        z = at_ref[0]
        lane = lax.broadcasted_iota(jnp.int32, o_ref.shape, 1)
        out = jnp.full(o_ref.shape, HIDDEN, jnp.float32)
        for c, column in enumerate((z, z ^ 1, jnp.where(z < 2, 2, 1))):
            for t in range(tile_dev):
                hit = (lists == column * tile_dev + t).astype(jnp.float32)
                listed = jnp.max(hit, axis=1, keepdims=True) > 0.0
                out = jnp.where((lane == c * tile_dev + t) & listed, 0.0, out)
        o_ref[...] = out

    return pl.pallas_call(
        kernel,
        in_specs=[pl.BlockSpec(memory_space=pltpu.SMEM), pl.BlockSpec()],
        out_specs=pl.BlockSpec(),
        out_shape=jax.ShapeDtypeStruct((lists.shape[0], 128), jnp.float32),
        cost_estimate=COST,
        name="see",
    )(at, lists)


def load_columns(at, own, pieces, x_ref, sems, step):
    count, tokens, _ = x_ref.shape
    copies = ([], [])
    for r in range(0, tokens if own is not None else 0, step):
        copies[0].append((own.at[pl.ds(r, step)], x_ref.at[0, pl.ds(r, step)]))
    for ref, parts in pieces:
        for i, start, first, size in parts:
            row = pl.multiple_of((at[1] ^ i) * (tokens // 4) + start, 16)
            copies[1].append((ref.at[pl.ds(first, size)], x_ref.at[count - 1, pl.ds(row, size)]))
    made, n = ([], []), 0
    for group, out in zip(copies, made):
        for source, target in group:
            out.append(pltpu.make_async_copy(source, target, sems.at[n]))
            n += 1
    return made


def normed(value, gain):
    mean = jnp.mean(value * value, axis=-1, keepdims=True)
    return value * lax.rsqrt(mean + EPS) * gain


def keys_values(at, head, own, pieces, weights, bias, gain, own_rows=None):
    _, rows, cols = weights[0].shape
    head_dim = gain.shape[1]
    arrays, parts = zip(*pieces) if pieces else ((), ())
    width = (arrays or (own,))[0].shape[1]
    tokens = own.shape[0] if own is not None else own_rows.shape[0]
    columns = [0] * (own is not None) + [1] * bool(pieces)
    step = 256
    moves = tokens // step + sum(map(len, parts))
    sources = [own] * (own is not None) + list(arrays)
    known = [] if own_rows is None else [own_rows]
    n_out = (own is not None) + 2 * bool(pieces)

    def kernel(at_ref, *refs):
        x_sources, weight_refs = refs[: len(sources)], refs[len(sources) : len(sources) + 4]
        b_ref, g_ref, *rest = refs[len(sources) + 4 :]
        own_in, out_refs = rest[: len(known)], rest[len(known) : len(known) + n_out]
        x_ref, w_ref, x_sems, w_sems = rest[-4:]
        z = at_ref[0]
        is_mid = (z == 1) | (z == 2)
        lanes = pl.ds(pl.multiple_of(at_ref[head] * head_dim, 128), head_dim)
        loads = [
            pltpu.make_async_copy(ref, w_ref.at[pl.ds(s, 1)], w_sems.at[s])
            for s, ref in enumerate(weight_refs)
        ]
        piece_refs = x_sources[len(sources) - len(arrays) :]
        own_moves, far_moves = load_columns(
            at_ref, x_sources[0] if 0 in columns else None, list(zip(piece_refs, parts)), x_ref, x_sems, step
        )
        for copy in [*loads, *own_moves, *far_moves]:
            copy.start()
        for copy in loads:
            copy.wait()
        for column in columns:
            if column:
                for copy in far_moves:
                    copy.wait()
            out_ref = out_refs[0 if column == 0 else -2]
            for r in range(tokens // step):
                if not column:
                    own_moves[r].wait()
                here = slice(r * step, (r + 1) * step)
                total = None
                for s in range(4):
                    first = pl.multiple_of((z ^ s) * rows, 128)
                    product = jnp.dot(
                        x_ref[columns.index(column), here, pl.ds(first, rows)], w_ref[s],
                        preferred_element_type=jnp.float32,
                    )
                    total = product if total is None else total + product
                key = normed(total[:, :head_dim] + b_ref[1:2, lanes], g_ref[1:2, :])
                out_ref[here, :head_dim] = key.astype(jnp.bfloat16)
                value = total[:, head_dim:] + b_ref[2:3, lanes]
                out_ref[here, head_dim:] = value.astype(jnp.bfloat16)
                if column:
                    own_ref = own_in[0] if known else out_refs[0]
                    out_refs[-1][here, :] = jnp.where(is_mid, own_ref[here, :], out_ref[here, :])

    hbm = pl.BlockSpec(memory_space=pltpu.HBM)
    out = jax.ShapeDtypeStruct((tokens, cols), jnp.bfloat16)
    return pl.pallas_call(
        kernel,
        in_specs=[pl.BlockSpec(memory_space=pltpu.SMEM)]
        + [hbm] * (len(sources) + 4)
        + [pl.BlockSpec()] * (2 + len(known)),
        out_specs=[pl.BlockSpec()] * n_out,
        out_shape=[out] * n_out,
        scratch_shapes=[
            pltpu.VMEM((len(columns), tokens, width), jnp.bfloat16),
            pltpu.VMEM((4, rows, cols), jnp.bfloat16),
            pltpu.SemaphoreType.DMA((moves,)),
            pltpu.SemaphoreType.DMA((4,)),
        ],
        compiler_params=pltpu.CompilerParams(vmem_limit_bytes=WHOLE),
        cost_estimate=SPACE,
        name="keys_values",
    )(at, *sources, *weights, bias, gain, *known)


def take_rows(at, frames, sizes):
    width = frames.shape[1]
    quarter = sum(sizes)

    def kernel(at_ref, x_ref, *out_refs):
        first = 0
        for ref in out_refs:
            ref[...] = x_ref[first : first + ref.shape[0], :]
            first += ref.shape[0]

    return pl.pallas_call(
        kernel,
        grid_spec=pltpu.PrefetchScalarGridSpec(
            num_scalar_prefetch=1,
            grid=(1,),
            in_specs=[pl.BlockSpec((quarter, width), lambda i, at: (at[1], 0))],
            out_specs=[pl.BlockSpec((size, width), lambda i, at: (0, 0)) for size in sizes],
        ),
        out_shape=[jax.ShapeDtypeStruct((size, width), jnp.bfloat16) for size in sizes],
        cost_estimate=COST,
        name="take_rows",
    )(at, frames)


def attend_pair(at, limits, own, pieces, weights, bias, gain, rows):
    tokens, width = own.shape
    head_dim = gain.shape[1]
    tiles = limits[0].shape[0]
    tile = tokens // tiles
    arrays, parts = zip(*pieces)
    step = 256
    moves = tokens // step + sum(map(len, parts))
    shard = weights[0].shape[1]

    def kernel(at_ref, limit0_ref, limit1_ref, own_ref, *refs):
        piece_refs, weight_refs = refs[: len(arrays)], refs[len(arrays) : len(arrays) + 2]
        row_refs = refs[len(arrays) + 2 : len(arrays) + 6]
        (b_ref, g_ref, edge_ref, done_ref, mixed_ref, total_ref,
         x_ref, w_ref, q_ref, kv_ref, x_sems, w_sems) = refs[len(arrays) + 6 :]
        z = at_ref[0]
        is_mid = (z == 1) | (z == 2)
        loads = [
            pltpu.make_async_copy(ref, w_ref.at[h], w_sems.at[h])
            for h, ref in enumerate(weight_refs)
        ]
        own_moves, far_moves = load_columns(at_ref, own_ref, list(zip(piece_refs, parts)), x_ref, x_sems, step)
        late = [
            pltpu.make_async_copy(ref, kv_ref.at[n // 2, n % 2], w_sems.at[2 + n])
            for n, ref in enumerate(row_refs)
        ]
        for copy in [*loads, *own_moves, *far_moves, *late]:
            copy.start()
        for copy in loads:
            copy.wait()
        for column in range(2):
            if column:
                for copy in far_moves:
                    copy.wait()
            for r in range(tokens // step):
                if not column:
                    own_moves[r].wait()
                here = slice(r * step, (r + 1) * step)
                total = None
                for s in range(4):
                    product = jnp.dot(
                        x_ref[column, here, s * shard : (s + 1) * shard],
                        jnp.concatenate([w_ref[0, s], w_ref[1, s]], axis=1),
                        preferred_element_type=jnp.float32,
                    )
                    total = product if total is None else total + product
                for h in range(2):
                    lanes = pl.ds(pl.multiple_of(at_ref[2 + h] * head_dim, 128), head_dim)
                    value = total[:, h * head_dim : (h + 1) * head_dim] + b_ref[0:1, lanes]
                    q_ref[h, column, here, :] = normed(value, g_ref[0:1, :]).astype(jnp.bfloat16)
        for copy in late:
            copy.wait()

        @pl.loop(0, 2)
        def _(h):
            for column in range(2):
                is_edge = is_mid if column == 0 else jnp.logical_not(is_mid)
                for i in range(tiles):
                    here = slice(i * tile, (i + 1) * tile)
                    query = q_ref[h, column, here, :]
                    total = jnp.zeros((tile, 128), jnp.float32)
                    mixed = jnp.zeros((tile, head_dim), jnp.float32)
                    for other in range(2):
                        for t in range(tiles):
                            limit = (limit0_ref, limit1_ref)[column][i, (other ^ column) * tiles + t]
                            total, mixed = tile_step(
                                query, kv_ref.at[h, other], t * tile, tile, head_dim, limit, total, mixed
                            )

                    @pl.when(is_edge)
                    def _():
                        edge_ref[h, here, :] = query
                        mixed_ref[h, here, :] = mixed
                        total_ref[h, here, :] = total

                    @pl.when(jnp.logical_not(is_edge))
                    def _():
                        rows = mixed / jnp.sum(total, axis=-1, keepdims=True)
                        done_ref[h, here, :] = rows.astype(jnp.bfloat16)

    smem = pl.BlockSpec(memory_space=pltpu.SMEM)
    hbm = pl.BlockSpec(memory_space=pltpu.HBM)
    shape = (2, tokens, head_dim)
    return pl.pallas_call(
        kernel,
        in_specs=[smem] * 3 + [hbm] * (1 + len(arrays) + 6) + [pl.BlockSpec()] * 2,
        out_specs=[pl.BlockSpec()] * 4,
        out_shape=[
            jax.ShapeDtypeStruct(shape, jnp.bfloat16),
            jax.ShapeDtypeStruct(shape, jnp.bfloat16),
            jax.ShapeDtypeStruct(shape, jnp.float32),
            jax.ShapeDtypeStruct((2, tokens, 128), jnp.float32),
        ],
        scratch_shapes=[
            pltpu.VMEM((2, tokens, width), jnp.bfloat16),
            pltpu.VMEM((2, 4, shard, head_dim), jnp.bfloat16),
            pltpu.VMEM((2, 2, tokens, head_dim), jnp.bfloat16),
            pltpu.VMEM((2, 2, tokens, 2 * head_dim), jnp.bfloat16),
            pltpu.SemaphoreType.DMA((moves,)),
            pltpu.SemaphoreType.DMA((6,)),
        ],
        compiler_params=pltpu.CompilerParams(vmem_limit_bytes=WHOLE),
        cost_estimate=COST,
        name="attend_pair",
    )(at, *limits, own, *arrays, *weights, *rows, bias, gain)


def attend_halo(at, h, limits, query, halo, done, mixed, total):
    _, tokens, head_dim = query.shape
    tiles = limits[0].shape[0]
    tile = tokens // tiles

    def kernel(at_ref, limit0_ref, limit1_ref, q_ref, halo_ref, done_ref, mixed_ref, total_ref, keep_ref, send_ref):
        is_mid = (at_ref[0] == 1) | (at_ref[0] == 2)
        for i in range(tiles):
            here = slice(i * tile, (i + 1) * tile)
            sums, rows = total_ref[0, here, :], mixed_ref[0, here, :]
            for t in range(tiles):
                limit = jnp.where(is_mid, limit0_ref[i, 2 * tiles + t], limit1_ref[i, 2 * tiles + t])
                sums, rows = tile_step(
                    q_ref[0, here, :], halo_ref, t * tile, tile, head_dim, limit, sums, rows
                )
            edge = (rows / jnp.sum(sums, axis=-1, keepdims=True)).astype(jnp.bfloat16)
            outer = done_ref[0, here, :]
            keep_ref[here, :] = jnp.where(is_mid, edge, outer)
            send_ref[here, :] = jnp.where(is_mid, outer, edge)

    smem = pl.BlockSpec(memory_space=pltpu.SMEM)
    one = pl.BlockSpec((1, tokens, head_dim), lambda i: (h, 0, 0))
    fixed = lambda shape: pl.BlockSpec(shape, lambda i: (0,) * len(shape))
    out = jax.ShapeDtypeStruct((tokens, head_dim), jnp.bfloat16)
    return pl.pallas_call(
        kernel,
        grid=(1,),
        in_specs=[smem] * 3 + [one, fixed(halo.shape), one, one, one],
        out_specs=[fixed(out.shape)] * 2,
        out_shape=[out] * 2,
        compiler_params=pltpu.CompilerParams(vmem_limit_bytes=VMEM),
        cost_estimate=SPACE,
        name="attend_halo",
    )(at, *limits, query, halo, done, mixed, total)


def assemble(at, parts, carried=None, cost=None, heads=4):
    (first, one), (second, two) = parts
    tokens, head_dim = one.shape
    carried = () if carried is None else (carried,)

    def kernel(at_ref, one_ref, two_ref, *rest):
        @pl.when(pl.program_id(0) == 0)
        def _():
            rest[-1][...] = one_ref[...]

        @pl.when(pl.program_id(0) == 1)
        def _():
            rest[-1][...] = two_ref[...]

    whole = pl.BlockSpec((tokens, head_dim), lambda i, at: (0, 0))
    return pl.pallas_call(
        kernel,
        grid_spec=pltpu.PrefetchScalarGridSpec(
            num_scalar_prefetch=1,
            grid=(2,),
            in_specs=[whole, whole] + [pl.BlockSpec(memory_space=pl.ANY)] * len(carried),
            out_specs=pl.BlockSpec(
                (tokens, head_dim), lambda i, at: (0, jnp.where(i == 0, at[first], at[second]))
            ),
        ),
        out_shape=jax.ShapeDtypeStruct((tokens, head_dim * heads), jnp.bfloat16),
        input_output_aliases={3: 0} if carried else {},
        cost_estimate=cost or COST,
        name="assemble",
    )(at, one, two, *carried)


def tile_step(query, rows_ref, at, tile, head_dim, limit, total, mixed):
    scale = math.log2(math.e) / math.sqrt(head_dim)
    keys = rows_ref[at : at + tile, :head_dim]
    values = rows_ref[at : at + tile, head_dim:]
    scores = lax.dot_general(
        query, keys, (((1,), (1,)), ((), ())), preferred_element_type=jnp.float32
    )
    weights = jnp.exp2(scores * scale + limit)
    for c in range(tile // 128):
        total = total + weights[:, c * 128 : (c + 1) * 128]
    mixed = mixed + jnp.dot(
        weights.astype(jnp.bfloat16), values, preferred_element_type=jnp.float32
    )
    return total, mixed


def per_device(frames, modulation, w_qkv, b_qkv, qk_gain, block_lists):
    sizes = tuple(lax.axis_size(a) for a in ("groups", "seq", "fsdp", "head"))
    head_dim = qk_gain.shape[1]
    width_cols = w_qkv.shape[2]
    tokens = frames.shape[0]
    if sizes != (2, 4, 2, 2) or width_cols != 4 * head_dim:
        return general(frames, modulation, w_qkv, b_qkv, qk_gain, block_lists)

    y, z, x, core = (lax.axis_index(a).astype(jnp.int32) for a in ("groups", "seq", "fsdp", "head"))
    rows = w_qkv.shape[0]
    quarter = tokens // 4
    tile_dev = block_lists.shape[0]

    def to(axis, value, bit):
        return lax.ppermute(value, axis, [(i, i ^ bit) for i in range(lax.axis_size(axis))])

    side = z % 2
    mine, twin = 2 * side + y, 2 * side + 1 - y
    across = 2 * (1 - side)
    at = jnp.stack([z, 2 * x + core, mine, twin, across + y, across + 1 - y, y, 2 + y])
    MINE, TWIN, CROSS, CROSS_TWIN = 2, 3, 4, 5
    is_mid = (z == 1) | (z == 2)
    w = jnp.transpose(w_qkv, (1, 0, 2))
    line = Line()

    def arrive(value):
        box = line.reached(value)[0]
        (box[0],) = line.after(box[0])
        return box

    cutting = (0, quarter * FIRST // 12, quarter)
    raws = take_rows(at, frames, [hi - lo for lo, hi in zip(cutting, cutting[1:])])
    raws_other = [to("seq", raw, 1) for raw in raws]
    (w, *_) = lax.optimization_barrier((w, *raws))
    same, cross, q_sent = line.reached(
        *cut_heads(at, w, [((MINE,), (1, 2)), ((CROSS,), (1, 2)), ((6, 7, 6, 7), (0,))])
    )
    got = [to("seq", same[0], 2), to("seq", cross[0], 3), to("seq", cross[0], 1)]
    own_limit = line.reached(see(at, block_lists, tile_dev))
    frames, modulation = line.after(frames, modulation)
    own_x = line.reached(normalize(frames, modulation, 128))
    line.drop(cross)

    def take(i):
        (raw,) = line.after(raws_other[i])
        near = line.reached(normalize(raw, modulation, raw.shape[0]))[0]
        return near, to("fsdp", near[0], 1)

    def spread(near, far):
        far = arrive(far)
        both = jnp.concatenate([near[0], far[0]], axis=0)
        return far, to("head", both, 1)

    def swap(which):
        kept = arrive(got[which])
        return kept, to("groups", kept[0], 1)

    near0, far0 = take(0)
    two_mine, two_twin = swap(0)
    near1, far1 = take(1)
    (q_sent[0],) = line.after(q_sent[0])
    q_got = lax.all_to_all(q_sent[0], "seq", split_axis=0, concat_axis=0, tiled=True)
    line.drop(q_sent)
    three_mine, three_twin = swap(1)
    one_mine, one_twin = swap(2)
    (w,) = line.after(w)
    own_kv = [same, line.reached(*cut_heads(at, w, [((TWIN,), (1, 2))], SPACE))[0]]
    far0, core0 = spread(near0, far0)
    two_twin = arrive(two_twin)
    three_twin = arrive(three_twin)
    far1, core1 = spread(near1, far1)
    w_mine = [own_kv[0], one_mine, two_mine, three_mine]

    def kv(head, boxes, own, pieces, own_rows=None):
        (boxes[0][0],) = line.after(boxes[0][0])
        weights = [box[0] for box in boxes]
        return keys_values(at, head, own, pieces, weights, b_qkv, qk_gain, own_rows)

    own_mine = line.reached(*kv(MINE, w_mine, own_x[0][0], None))[0]
    (own_limit[0][0],) = line.after(own_limit[0][0])
    far_limit = to("seq", own_limit[0][0], 1)
    q_mine = arrive(q_got)
    q_twin = to("groups", q_mine[0], 1)
    core0 = arrive(core0)
    core1 = arrive(core1)
    n0, n1 = cutting[1], quarter - cutting[1]
    pieces = [
        (near0, [(0, 0, 0, n0)]),
        (far0, [(2, 0, 0, n0)]),
        (core0, [(1, 0, 0, n0), (3, 0, n0, n0)]),
        (near1, [(0, n0, 0, n1)]),
        (far1, [(2, n0, 0, n1)]),
        (core1, [(1, n0, 0, n1), (3, n0, n1, n1)]),
    ]

    def column_arrays():
        return own_x[0][0], [(box[0], parts) for box, parts in pieces]

    far, edge = kv(MINE, w_mine, None, column_arrays()[1], own_mine[0])
    rows_mine, halo_mine = [own_mine, *line.reached(far)], to("seq", edge, 2)
    one_twin = arrive(one_twin)
    w_twin = [own_kv[1], one_twin, two_twin, three_twin]
    own, far, edge = kv(TWIN, w_twin, *column_arrays())
    rows_twin, halo_twin = line.reached(own, far), to("seq", edge, 2)
    line.drop(*w_mine, *w_twin)
    limits = own_limit + [arrive(far_limit)]
    q_twin = arrive(q_twin)
    parts = line.reached(
        *attend_pair(
            at, [b[0] for b in limits], *column_arrays(), [q_mine[0], q_twin[0]], b_qkv, qk_gain,
            [b[0] for b in (*rows_mine, *rows_twin)],
        )
    )
    line.drop(q_mine, q_twin, *own_x, *(box for box, _ in pieces), *rows_mine, *rows_twin)

    def finish(h, halo):
        (halo,) = line.after(halo)
        query, *rest = [b[0] for b in parts]
        keep, send = attend_halo(at, h, [b[0] for b in limits], query, halo, *rest)
        return line.reached(keep)[0], to("seq", send, 1)

    keep_mine, back_mine = finish(0, halo_mine)
    keep_twin, back_twin = finish(1, halo_twin)
    half_done = assemble(at, [(MINE, keep_mine[0]), (CROSS, back_mine)], None, SPACE)
    return assemble(at, [(TWIN, keep_twin[0]), (CROSS_TWIN, back_twin)], half_done)


def solution(mesh):
    placed = (
        P(("groups", "seq"), None),
        P("groups", None),
        P("seq", None, ("fsdp", "head")),
        P(None, ("fsdp", "head")),
        P(),
        P(("groups", "seq"), None),
    )
    return jax.shard_map(
        per_device,
        mesh=mesh,
        in_specs=placed,
        out_specs=P(("groups", "seq"), ("fsdp", "head")),
        check_vma=False,
    )
```

time: 155 us -> 149 us (0.961)
  waiting for transfers between devices: 41.6 us -> 32.9 us
  local copies, waits for them, and re-layouts: 6.76 us -> 11.4 us
  starting transfers between devices: 26.7 us -> 29.7 us
  other arithmetic: 6.62 us -> 3.64 us
    ppermute x18, waiting for transfers between devices: 38.6 us -> 26.9 us  [to(): lax.ppermute(value, axis, [(i, i ^ bit) for i in range(lax.axis_size(axis...]
    unnamed x54 -> x52, local copies, waits for them, and re-layouts: 6.13 us -> 10.8 us
    ppermute x18, starting transfers between devices: 21.7 us -> 24.7 us  [to(): lax.ppermute(value, axis, [(i, i ^ bit) for i in range(lax.axis_size(axis...]
    all_to_all x1, waiting for transfers between devices: 2.95 us -> 6 us  [per_device(): lax.all_to_all(q_sent[0], 'seq', split_axis=0, concat_axis=0, tiled=True)]
    select_n x2 -> x0, other arithmetic: 2.12 us -> none  [send_edge(): return to('seq', jnp.where(is_mid, own[0], far[0]), 2)]
    pallas_call x11 -> x8, Pallas kernels: 53.1 us -> 51.7 us  [the longest x3 24 us: keys_values(): pl.pallas_call(kernel, in_specs=[pl.BlockSpec(memory_space=pltpu.SMEM)] +...]
  transfers between devices with their start and end apart: 19 -> 19, of which waited for: 7 -> 6; matrix products, arithmetic and copies ran while one was open for 4% -> 2% of each run, Pallas kernels for 42% -> 44%
where the time goes in v9:
time: 149 us
  Pallas kernels  70.5 us (47%)
  waiting for transfers between devices  32.9 us (22%)
  starting transfers between devices  29.7 us (20%)
  local copies, waits for them, and re-layouts  11.4 us (8%)
  other arithmetic  3.64 us (2%)
    ppermute x18, waiting for transfers between devices, to(): lax.ppermute(value, axis, [(i, i ^ bit) for i in range(lax.axis_size(axis...  26.9 us
    ppermute x18, starting transfers between devices, to(): lax.ppermute(value, axis, [(i, i ^ bit) for i in range(lax.axis_size(axis...  24.7 us
    pallas_call x3, Pallas kernels, keys_values(): pl.pallas_call(kernel, in_specs=[pl.BlockSpec(memory_space=pltpu.SMEM)] +...  24 us
    pallas_call x1, Pallas kernels, attend_pair(): pl.pallas_call(kernel, in_specs=[smem] * 3 + [hbm] * (1 + len(arrays) + 6...  19.4 us
    pallas_call x3, Pallas kernels, normalize(): pl.pallas_call(norm_kernel, grid=(tokens // rows,), in_specs=[pl.BlockSpe...  12 us
    unnamed x52, local copies, waits for them, and re-layouts  10.8 us
    all_to_all x1, waiting for transfers between devices, per_device(): lax.all_to_all(q_sent[0], 'seq', split_axis=0, concat_axis=0, tiled=True)  6 us
    all_to_all x1, starting transfers between devices, per_device(): lax.all_to_all(q_sent[0], 'seq', split_axis=0, concat_axis=0, tiled=True)  5 us
  transfers between devices with their start and end apart: 19, of which 6 were waited for; matrix products, arithmetic and copies ran while one was open for 2% of the time, Pallas kernels for 44%

profile of v9, /device:TPU:0, one launch (start us, length us, event | category | flops | bytes accessed | tf_op | source)
XLA Modules:
  0.0 148.5 jit_solution(18004965646559385530)
XLA Ops:
  0.0 0.7 stack.35.at_ref
  0.7 3.1 %take_rows.1 = (bf16[128,3072]{1,0:T(8,128)(2,1)}, bf16[64,3072]{1,0:T(8,128)(2,1)}) custom-call(s32[8]{0:T(128)} %stack.35.at_ref, bf16[768,3072]{1,0:T(8,128)(2,1)} %x_ref.2), custom_call_target="tpu_custom_call" | custom-call | flops 1048576 | bytes 1024 | tf_op jit(solution)/shard_map/take_rows/pallas_call | solution.py:295
  3.8 3.0 %collective-permute-start.4 = (bf16[128,3072]{1,0:T(8,128)(2,1)}, bf16[128,3072]{1,0:T(8,128)(2,1)}, u32[]{:S(2)}, u32[]{:S(2)}) collective-permute-start(bf16[128,3072]{1,0:T(8,128)(2,1)} %get-tuple-element.290), channel_id=1, source_target_pairs={{0,4},{4,0},{8,12},{12,8},{1,5},{5,1},{9,13},{13,9},{2,6},{6,2},{1... | collective-permute-start | bytes 2359304 | tf_op jit(solution)/shard_map/ppermute | solution.py:514
  6.8 1.7 %cut_heads.2 = (bf16[1,768,256]{2,1,0:T(8,128)(2,1)S(1)}, bf16[1,768,256]{2,1,0:T(8,128)(2,1)S(1)}, bf16[4,768,128]{2,1,0:T(8,128)(2,1)}) custom-call(s32[8]{0:T(128)S(1)} %copy-done.2, bf16[3,768,512]{2,1,0:T(8,128)(2,1)S(1)} %bitcast.9), custom_call_target="tpu_custom_call" | custom-call | flops 1048576 | bytes 1024 | tf_op jit(solution)/shard_map/cut_heads/pallas_call | solution.py:150
  8.5 2.6 %collective-permute-start.3 = (bf16[1,768,256]{2,1,0:T(8,128)(2,1)S(1)}, bf16[1,768,256]{2,1,0:T(8,128)(2,1)}, u32[]{:S(2)}, u32[]{:S(2)}) collective-permute-start(bf16[1,768,256]{2,1,0:T(8,128)(2,1)S(1)} %get-tuple-element.471.refs_1_.refs_6_), channel_id=1, source_target_pairs={{0,8},{4,12},{8,0},{12,4},{1,9},{5,13},{9,1},{13,5},{2,10},{6,14},... | collective-permute-start | bytes 1179656 | tf_op jit(solution)/shard_map/ppermute | solution.py:514
  11.6 1.3 collective-permute-start.1
  13.1 1.4 see.1.limit0_ref
  14.5 7.4 %normalize.3.refs_0_.own_ref = bf16[768,3072]{1,0:T(8,128)(2,1)} custom-call(bf16[768,3072]{1,0:T(8,128)(2,1)} %x_ref.2, f32[2,3072]{1,0:T(2,128)} %mod_ref.2), custom_call_target="tpu_custom_call" | custom-call | flops 1048576 | bytes 1024 | tf_op jit(solution)/shard_map/normalize/pallas_call | solution.py:124
  21.9 12.1 %collective-permute-done.4.x_ref = bf16[128,3072]{1,0:T(8,128)(2,1)} collective-permute-done((bf16[128,3072]{1,0:T(8,128)(2,1)}, bf16[128,3072]{1,0:T(8,128)(2,1)}, u32[]{:S(2)}, u32[]{:S(2)}) %collective-permute-start.4) | collective-permute-done | bytes 786464 | tf_op jit(solution)/shard_map/ppermute | solution.py:514
  33.9 2.6 %normalize.4.refs_0_.refs_1_ = bf16[128,3072]{1,0:T(8,128)(2,1)} custom-call(bf16[128,3072]{1,0:T(8,128)(2,1)} %collective-permute-done.4.x_ref, f32[2,3072]{1,0:T(2,128)} %mod_ref.2), custom_call_target="tpu_custom_call" | custom-call | flops 1048576 | bytes 1024 | tf_op jit(solution)/shard_map/normalize/pallas_call | solution.py:124
  36.5 2.0 %collective-permute-start.9 = (bf16[128,3072]{1,0:T(8,128)(2,1)}, bf16[128,3072]{1,0:T(8,128)(2,1)}, u32[]{:S(2)}, u32[]{:S(2)}) collective-permute-start(bf16[128,3072]{1,0:T(8,128)(2,1)} %normalize.4.refs_0_.refs_1_), channel_id=1, source_target_pairs={{0,2},{2,0},{1,3},{3,1},{4,6},{6,4},{5,7},{7,5},{8,10},{10,8},{9,1... | collective-permute-start | bytes 2359304 | tf_op jit(solution)/shard_map/ppermute | solution.py:514
  38.5 1.5 %collective-permute-start.8 = (bf16[1,768,256]{2,1,0:T(8,128)(2,1)}, bf16[1,768,256]{2,1,0:T(8,128)(2,1)}, u32[]{:S(2)}, u32[]{:S(2)}) collective-permute-start(bf16[1,768,256]{2,1,0:T(8,128)(2,1)} %collective-permute-done.3.refs_3_.refs_8_), channel_id=1, source_target_pairs={{0,16},{16,0},{1,17},{17,1},{2,18},{18,2},{3,19},{19,3},{4,20},{20... | collective-permute-start | bytes 1179656 | tf_op jit(solution)/shard_map/ppermute | solution.py:514
  40.0 2.2 %collective-permute-done.2.x_ref = bf16[64,3072]{1,0:T(8,128)(2,1)S(1)} collective-permute-done((bf16[64,3072]{1,0:T(8,128)(2,1)}, bf16[64,3072]{1,0:T(8,128)(2,1)S(1)}, u32[]{:S(2)}, u32[]{:S(2)}) %collective-permute-start.2) | collective-permute-done | bytes 393248 | tf_op jit(solution)/shard_map/ppermute | solution.py:514
  42.3 0.8 copy-done.22
  43.0 2.1 %normalize.5.refs_3_.refs_4_ = bf16[64,3072]{1,0:T(8,128)(2,1)} custom-call(bf16[64,3072]{1,0:T(8,128)(2,1)} %copy-done.22, f32[2,3072]{1,0:T(2,128)} %mod_ref.2), custom_call_target="tpu_custom_call" | custom-call | flops 1048576 | bytes 1024 | tf_op jit(solution)/shard_map/normalize/pallas_call | solution.py:124
  45.1 2.2 %collective-permute-start.6 = (bf16[64,3072]{1,0:T(8,128)(2,1)}, bf16[64,3072]{1,0:T(8,128)(2,1)S(1)}, u32[]{:S(2)}, u32[]{:S(2)}) collective-permute-start(bf16[64,3072]{1,0:T(8,128)(2,1)} %normalize.5.refs_3_.refs_4_), channel_id=1, source_target_pairs={{0,2},{2,0},{1,3},{3,1},{4,6},{6,4},{5,7},{7,5},{8,10},{10,8},{9,1... | collective-permute-start | bytes 1179656 | tf_op jit(solution)/shard_map/ppermute | solution.py:514
  47.3 6.0 %collective-permute-done.1.refs_4_.refs_9_ = bf16[1,768,256]{2,1,0:T(8,128)(2,1)} collective-permute-done((bf16[1,768,256]{2,1,0:T(8,128)(2,1)S(1)}, bf16[1,768,256]{2,1,0:T(8,128)(2,1)}, u32[]{:S(2)}, u32[]{:S(2)}) %collective-permute-start.1) | collective-permute-done | bytes 393248 | tf_op jit(solution)/shard_map/ppermute | solution.py:514
  53.3 1.5 %collective-permute-start.7 = (bf16[1,768,256]{2,1,0:T(8,128)(2,1)}, bf16[1,768,256]{2,1,0:T(8,128)(2,1)S(1)}, u32[]{:S(2)}, u32[]{:S(2)}) collective-permute-start(bf16[1,768,256]{2,1,0:T(8,128)(2,1)} %collective-permute-done.1.refs_4_.refs_9_), channel_id=1, source_target_pairs={{0,16},{16,0},{1,17},{17,1},{2,18},{18,2},{3,19},{19,3},{4,20},{20... | collective-permute-start | bytes 1179656 | tf_op jit(solution)/shard_map/ppermute | solution.py:514
  54.9 3.5 %collective-permute-done.refs_2_.refs_7_ = bf16[1,768,256]{2,1,0:T(8,128)(2,1)} collective-permute-done((bf16[1,768,256]{2,1,0:T(8,128)(2,1)S(1)}, bf16[1,768,256]{2,1,0:T(8,128)(2,1)}, u32[]{:S(2)}, u32[]{:S(2)}) %collective-permute-start) | collective-permute-done | bytes 393248 | tf_op jit(solution)/shard_map/ppermute | solution.py:514
  58.4 1.7 %collective-permute-start.5 = (bf16[1,768,256]{2,1,0:T(8,128)(2,1)}, bf16[1,768,256]{2,1,0:T(8,128)(2,1)}, u32[]{:S(2)}, u32[]{:S(2)}) collective-permute-start(bf16[1,768,256]{2,1,0:T(8,128)(2,1)} %collective-permute-done.refs_2_.refs_7_), channel_id=1, source_target_pairs={{0,16},{16,0},{1,17},{17,1},{2,18},{18,2},{3,19},{19,3},{4,20},{20... | collective-permute-start | bytes 1179656 | tf_op jit(solution)/shard_map/ppermute | solution.py:514
  60.1 0.6 cut_heads.3.refs_7_
  60.7 0.8 copy-done.14
  61.5 5.0 %all-to-all-start = ((bf16[4,768,128]{2,1,0:T(8,128)(2,1)}), bf16[4,768,128]{2,1,0:T(8,128)(2,1)S(1)}, u32[]{:S(2)}, u32[]{:S(2)}) async-start(bf16[4,768,128]{2,1,0:T(8,128)(2,1)} %get-tuple-element.384), calls=%async_computation | async-start | bytes 1572864 | tf_op jit(solution)/shard_map/all_to_all | solution.py:561
  66.5 2.6 %pad_maximum_fusion = bf16[256,3072]{1,0:T(8,128)(2,1)} fusion(bf16[128,3072]{1,0:T(8,128)(2,1)} %collective-permute-done.9.refs_1_.refs_2_, bf16[128,3072]{1,0:T(8,128)(2,1)S(1)} %copy-done.16), kind=kLoop, calls=%fused_computation | loop fusion | flops 3145728 | bytes 3145728 | tf_op jit(solution)/shard_map/concatenate | solution.py:550
  69.1 1.0 pad_maximum_fusion.1
  70.7 6.6 %keys_values.3.refs_12_.refs_8_ = bf16[768,256]{1,0:T(8,128)(2,1)} custom-call(s32[8]{0:T(128)} %stack.35.at_ref, bf16[768,3072]{1,0:T(8,128)(2,1)} %normalize.3.refs_0_.own_ref, bf16[1,768,256]{2,1,0:T(8,128)(2,1)} %copy-done.11, bf16[1,768,256]{2,1,0:T(8,128)(2,1)} %collective-permute-done.refs_2_.refs_7_, ...), custom_call_target="tpu_custom_call" | custom-call | flops 68719476736 | bytes 1024 | tf_op jit(solution)/shard_map/keys_values/pallas_call | solution.py:266
  77.3 2.1 %collective-permute-start.15 = (f32[2,128]{1,0:T(2,128)S(1)}, f32[2,128]{1,0:T(2,128)S(1)}, u32[]{:S(2)}, u32[]{:S(2)}) collective-permute-start(f32[2,128]{1,0:T(2,128)S(1)} %copy-done.5), channel_id=1, source_target_pairs={{0,4},{4,0},{8,12},{12,8},{1,5},{5,1},{9,13},{13,9},{2,6},{6,2},{1... | collective-permute-start | bytes 3080 | tf_op jit(solution)/shard_map/ppermute | solution.py:514
  79.4 6.0 %all-to-all-done.refs_6_ = bf16[4,768,128]{2,1,0:T(8,128)(2,1)S(1)} async-done(((bf16[4,768,128]{2,1,0:T(8,128)(2,1)}), bf16[4,768,128]{2,1,0:T(8,128)(2,1)S(1)}, u32[]{:S(2)}, u32[]{:S(2)}) %all-to-all-start) | async-done | bytes 786464 | tf_op jit(solution)/shard_map/all_to_all | solution.py:561
  85.9 0.9 copy-done.20
  86.9 6.4 %keys_values.4 = (bf16[768,256]{1,0:T(8,128)(2,1)}, bf16[768,256]{1,0:T(8,128)(2,1)}) custom-call(s32[8]{0:T(128)} %stack.35.at_ref, bf16[128,3072]{1,0:T(8,128)(2,1)} %normalize.4.refs_0_.refs_1_, bf16[128,3072]{1,0:T(8,128)(2,1)} %collective-permute-done.9.refs_1_.refs_2_, bf16[256,3072]{1,0:T(8,128)(2,1)} %collective-permute-done.11.refs_2_.refs_3_, ...), custom_call_target="tpu_custom_call" | custom-call | flops 68719476736 | bytes 1024 | tf_op jit(solution)/shard_map/keys_values/pallas_call | solution.py:266
  93.4 11.0 %keys_values.5 = (bf16[768,256]{1,0:T(8,128)(2,1)}, bf16[768,256]{1,0:T(8,128)(2,1)}, bf16[768,256]{1,0:T(8,128)(2,1)}) custom-call(s32[8]{0:T(128)} %stack.35.at_ref, bf16[768,3072]{1,0:T(8,128)(2,1)} %normalize.3.refs_0_.own_ref, bf16[128,3072]{1,0:T(8,128)(2,1)} %normalize.4.refs_0_.refs_1_, bf16[128,3072]{1,0:T(8,128)(2,1)} %collective-permute-done.9.refs_1_.refs_2_, ...), custom_call_target="tpu_custom_call" | custom-call | flops 68719476736 | bytes 1024 | tf_op jit(solution)/shard_map/keys_values/pallas_call | solution.py:266
  104.4 3.0 %collective-permute-start.12 = (bf16[768,256]{1,0:T(8,128)(2,1)}, bf16[768,256]{1,0:T(8,128)(2,1)S(1)}, u32[]{:S(2)}, u32[]{:S(2)}) collective-permute-start(bf16[768,256]{1,0:T(8,128)(2,1)} %get-tuple-element.508), channel_id=1, source_target_pairs={{0,8},{4,12},{8,0},{12,4},{1,9},{5,13},{9,1},{13,5},{2,10},{6,14},... | collective-permute-start | bytes 1179656 | tf_op jit(solution)/shard_map/ppermute | solution.py:514
  107.9 0.9 copy-done.21
  108.8 19.4 %attend_pair.1 = (bf16[2,768,128]{2,1,0:T(8,128)(2,1)}, bf16[2,768,128]{2,1,0:T(8,128)(2,1)}, f32[2,768,128]{2,1,0:T(8,128)}, f32[2,768,128]{2,1,0:T(8,128)}) custom-call(s32[8]{0:T(128)} %stack.35.at_ref, f32[2,128]{1,0:T(2,128)} %see.1.limit0_ref, f32[2,128]{1,0:T(2,128)} %copy-done.7, bf16[768,3072]{1,0:T(8,128)(2,1)} %normalize.3.refs_0_.own_ref, ...), custom_call_target="tpu_custom_call" | custom-call | flops 1048576 | bytes 1024 | tf_op jit(solution)/shard_map/attend_pair/pallas_call | solution.py:392
  128.2 0.6 copy-done.8
  128.8 1.1 copy-done.9
  130.0 1.1 copy-done.10
  131.1 1.0 copy-done.12
  132.1 1.0 copy-done.13
  133.1 1.6 %attend_halo.2 = (bf16[768,128]{1,0:T(8,128)(2,1)S(1)}, bf16[768,128]{1,0:T(8,128)(2,1)S(1)}) custom-call(s32[8]{0:T(128)S(1)} %copy-done.4, f32[2,128]{1,0:T(2,128)S(1)} %copy-done.6, f32[2,128]{1,0:T(2,128)S(1)} %copy-done.8, bf16[2,768,128]{2,1,0:T(8,128)(2,1)S(1)} %copy-done.12, bf16[768,256]{1,0:T(8,128)(2,1)S(1)} %collective-permute-done.13.halo_ref, ...), custom_call_target="tpu_custom_call" | custom-call | flops 68719476736 | bytes 1024 | tf_op jit(solution)/shard_map/attend_halo/pallas_call | solution.py:440
  134.8 1.6 %attend_halo.3 = (bf16[768,128]{1,0:T(8,128)(2,1)S(1)}, bf16[768,128]{1,0:T(8,128)(2,1)S(1)}) custom-call(s32[8]{0:T(128)S(1)} %copy-done.4, f32[2,128]{1,0:T(2,128)S(1)} %copy-done.6, f32[2,128]{1,0:T(2,128)S(1)} %copy-done.8, bf16[2,768,128]{2,1,0:T(8,128)(2,1)S(1)} %copy-done.12, bf16[768,256]{1,0:T(8,128)(2,1)S(1)} %collective-permute-done.12.halo_ref, ...), custom_call_target="tpu_custom_call" | custom-call | flops 68719476736 | bytes 1024 | tf_op jit(solution)/shard_map/attend_halo/pallas_call | solution.py:440
  136.5 0.7 copy-done.1
  137.2 2.0 %collective-permute-start.16 = (bf16[768,128]{1,0:T(8,128)(2,1)S(1)}, bf16[768,128]{1,0:T(8,128)(2,1)S(1)}, u32[]{:S(2)}, u32[]{:S(2)}) collective-permute-start(bf16[768,128]{1,0:T(8,128)(2,1)S(1)} %get-tuple-element.572), channel_id=1, source_target_pairs={{0,4},{4,0},{8,12},{12,8},{1,5},{5,1},{9,13},{13,9},{2,6},{6,2},{1... | collective-permute-start | bytes 589832 | tf_op jit(solution)/shard_map/ppermute | solution.py:514
  139.2 3.0 %collective-permute-done.17.two_ref = bf16[768,128]{1,0:T(8,128)(2,1)S(1)} collective-permute-done((bf16[768,128]{1,0:T(8,128)(2,1)S(1)}, bf16[768,128]{1,0:T(8,128)(2,1)S(1)}, u32[]{:S(2)}, u32[]{:S(2)}) %collective-permute-start.17) | collective-permute-done | bytes 196640 | tf_op jit(solution)/shard_map/ppermute | solution.py:514
  142.2 0.7 copy-done.25
  142.9 2.5 %assemble.2.rest_0_ = bf16[768,512]{1,0:T(8,128)(2,1)} custom-call(s32[8]{0:T(128)} %stack.35.at_ref, bf16[768,128]{1,0:T(8,128)(2,1)} %copy-done.15, bf16[768,128]{1,0:T(8,128)(2,1)} %copy-done.25), custom_call_target="tpu_custom_call" | custom-call | flops 68719476736 | bytes 1024 | tf_op jit(solution)/shard_map/assemble/pallas_call | solution.py:467
  145.4 0.7 copy-done.23
  146.0 2.5 %assemble.3 = bf16[768,512]{1,0:T(8,128)(2,1)} custom-call(s32[8]{0:T(128)} %stack.35.at_ref, bf16[768,128]{1,0:T(8,128)(2,1)} %copy-done.1, bf16[768,128]{1,0:T(8,128)(2,1)} %copy-done.23, bf16[768,512]{1,0:T(8,128)(2,1)} %assemble.2.rest_0_), custom_call_target="tpu_custom_call", output_to_operand_aliasing={{}: (3, {})} | custom-call | flops 1048576 | bytes 1024 | tf_op jit(solution)/shard_map/assemble/pallas_call | solution.py:467
  (60 shorter events, 2.4 us)
Async XLA Ops:
  0.7 6.2 %copy-start = (bf16[768,3,512]{2,0,1:T(8,128)(2,1)S(1)}, bf16[768,3,512]{2,0,1:T(8,128)(2,1)}, u32[]{:S(2)}) copy-start(bf16[768,3,512]{2,0,1:T(8,128)(2,1)} %param.8) | copy-start | bytes 7077892
  0.7 6.2 %copy-start.2 = (s32[8]{0:T(128)S(1)}, s32[8]{0:T(128)}, u32[]{:S(2)}) copy-start(s32[8]{0:T(128)} %stack.35.at_ref) | copy-start | bytes 100
  3.8 30.1 %collective-permute-start.4 = (bf16[128,3072]{1,0:T(8,128)(2,1)}, bf16[128,3072]{1,0:T(8,128)(2,1)}, u32[]{:S(2)}, u32[]{:S(2)}) collective-permute-start(bf16[128,3072]{1,0:T(8,128)(2,1)} %get-tuple-element.290), channel_id=1, source_target_pairs={{0,4},{4,0},{8,12},{12,8},{1,5},{5,1},{9,13},{13,9},{2,6},{6,2},{1... | collective-permute-start | bytes 2359304 | tf_op jit(solution)/shard_map/ppermute | solution.py:514
  8.5 13.3 %copy-start.11 = (bf16[1,768,256]{2,1,0:T(8,128)(2,1)}, bf16[1,768,256]{2,1,0:T(8,128)(2,1)S(1)}, u32[]{:S(2)}) copy-start(bf16[1,768,256]{2,1,0:T(8,128)(2,1)S(1)} %get-tuple-element.471.refs_1_.refs_6_) | copy-start | bytes 1179652
  8.5 30.0 %collective-permute-start.3 = (bf16[1,768,256]{2,1,0:T(8,128)(2,1)S(1)}, bf16[1,768,256]{2,1,0:T(8,128)(2,1)}, u32[]{:S(2)}, u32[]{:S(2)}) collective-permute-start(bf16[1,768,256]{2,1,0:T(8,128)(2,1)S(1)} %get-tuple-element.471.refs_1_.refs_6_), channel_id=1, source_target_pairs={{0,8},{4,12},{8,0},{12,4},{1,9},{5,13},{9,1},{13,5},{2,10},{6,14},... | collective-permute-start | bytes 1179656 | tf_op jit(solution)/shard_map/ppermute | solution.py:514
  11.1 31.1 %collective-permute-start.2 = (bf16[64,3072]{1,0:T(8,128)(2,1)}, bf16[64,3072]{1,0:T(8,128)(2,1)S(1)}, u32[]{:S(2)}, u32[]{:S(2)}) collective-permute-start(bf16[64,3072]{1,0:T(8,128)(2,1)} %get-tuple-element.291), channel_id=1, source_target_pairs={{0,4},{4,0},{8,12},{12,8},{1,5},{5,1},{9,13},{13,9},{2,6},{6,2},{1... | collective-permute-start | bytes 1179656 | tf_op jit(solution)/shard_map/ppermute | solution.py:514
  11.6 41.8 %collective-permute-start.1 = (bf16[1,768,256]{2,1,0:T(8,128)(2,1)S(1)}, bf16[1,768,256]{2,1,0:T(8,128)(2,1)}, u32[]{:S(2)}, u32[]{:S(2)}) collective-permute-start(bf16[1,768,256]{2,1,0:T(8,128)(2,1)S(1)} %get-tuple-element.293), channel_id=1, source_target_pairs={{0,12},{4,8},{8,4},{12,0},{1,13},{5,9},{9,5},{13,1},{2,14},{6,10},... | collective-permute-start | bytes 1179656 | tf_op jit(solution)/shard_map/ppermute | solution.py:514
  12.9 45.5 %collective-permute-start = (bf16[1,768,256]{2,1,0:T(8,128)(2,1)S(1)}, bf16[1,768,256]{2,1,0:T(8,128)(2,1)}, u32[]{:S(2)}, u32[]{:S(2)}) collective-permute-start(bf16[1,768,256]{2,1,0:T(8,128)(2,1)S(1)} %get-tuple-element.293), channel_id=1, source_target_pairs={{0,4},{4,0},{8,12},{12,8},{1,5},{5,1},{9,13},{13,9},{2,6},{6,2},{1... | collective-permute-start | bytes 1179656 | tf_op jit(solution)/shard_map/ppermute | solution.py:514
  21.9 38.2 %copy-start.3 = (s32[8]{0:T(128)S(1)}, s32[8]{0:T(128)}, u32[]{:S(2)}) copy-start(s32[8]{0:T(128)} %stack.35.at_ref) | copy-start | bytes 100
  36.5 29.9 %collective-permute-start.9 = (bf16[128,3072]{1,0:T(8,128)(2,1)}, bf16[128,3072]{1,0:T(8,128)(2,1)}, u32[]{:S(2)}, u32[]{:S(2)}) collective-permute-start(bf16[128,3072]{1,0:T(8,128)(2,1)} %normalize.4.refs_0_.refs_1_), channel_id=1, source_target_pairs={{0,2},{2,0},{1,3},{3,1},{4,6},{6,4},{5,7},{7,5},{8,10},{10,8},{9,1... | collective-permute-start | bytes 2359304 | tf_op jit(solution)/shard_map/ppermute | solution.py:514
  38.5 28.0 %collective-permute-start.8 = (bf16[1,768,256]{2,1,0:T(8,128)(2,1)}, bf16[1,768,256]{2,1,0:T(8,128)(2,1)}, u32[]{:S(2)}, u32[]{:S(2)}) collective-permute-start(bf16[1,768,256]{2,1,0:T(8,128)(2,1)} %collective-permute-done.3.refs_3_.refs_8_), channel_id=1, source_target_pairs={{0,16},{16,0},{1,17},{17,1},{2,18},{18,2},{3,19},{19,3},{4,20},{20... | collective-permute-start | bytes 1179656 | tf_op jit(solution)/shard_map/ppermute | solution.py:514
  42.3 0.8 copy-start.22
  45.1 24.0 %collective-permute-start.6 = (bf16[64,3072]{1,0:T(8,128)(2,1)}, bf16[64,3072]{1,0:T(8,128)(2,1)S(1)}, u32[]{:S(2)}, u32[]{:S(2)}) collective-permute-start(bf16[64,3072]{1,0:T(8,128)(2,1)} %normalize.5.refs_3_.refs_4_), channel_id=1, source_target_pairs={{0,2},{2,0},{1,3},{3,1},{4,6},{6,4},{5,7},{7,5},{8,10},{10,8},{9,1... | collective-permute-start | bytes 1179656 | tf_op jit(solution)/shard_map/ppermute | solution.py:514
  53.3 13.1 %collective-permute-start.7 = (bf16[1,768,256]{2,1,0:T(8,128)(2,1)}, bf16[1,768,256]{2,1,0:T(8,128)(2,1)S(1)}, u32[]{:S(2)}, u32[]{:S(2)}) collective-permute-start(bf16[1,768,256]{2,1,0:T(8,128)(2,1)} %collective-permute-done.1.refs_4_.refs_9_), channel_id=1, source_target_pairs={{0,16},{16,0},{1,17},{17,1},{2,18},{18,2},{3,19},{19,3},{4,20},{20... | collective-permute-start | bytes 1179656 | tf_op jit(solution)/shard_map/ppermute | solution.py:514
  58.4 34.9 %collective-permute-start.5 = (bf16[1,768,256]{2,1,0:T(8,128)(2,1)}, bf16[1,768,256]{2,1,0:T(8,128)(2,1)}, u32[]{:S(2)}, u32[]{:S(2)}) collective-permute-start(bf16[1,768,256]{2,1,0:T(8,128)(2,1)} %collective-permute-done.refs_2_.refs_7_), channel_id=1, source_target_pairs={{0,16},{16,0},{1,17},{17,1},{2,18},{18,2},{3,19},{19,3},{4,20},{20... | collective-permute-start | bytes 1179656 | tf_op jit(solution)/shard_map/ppermute | solution.py:514
  60.7 0.8 copy-start.14
  61.5 5.0 %copy-start.16 = (bf16[128,3072]{1,0:T(8,128)(2,1)S(1)}, bf16[128,3072]{1,0:T(8,128)(2,1)}, u32[]{:S(2)}) copy-start(bf16[128,3072]{1,0:T(8,128)(2,1)} %normalize.4.refs_0_.refs_1_) | copy-start | bytes 2359300
  61.5 24.0 %all-to-all-start = ((bf16[4,768,128]{2,1,0:T(8,128)(2,1)}), bf16[4,768,128]{2,1,0:T(8,128)(2,1)S(1)}, u32[]{:S(2)}, u32[]{:S(2)}) async-start(bf16[4,768,128]{2,1,0:T(8,128)(2,1)} %get-tuple-element.384), calls=%async_computation | async-start | bytes 1572864 | tf_op jit(solution)/shard_map/all_to_all | solution.py:561
  66.5 2.6 %copy-start.17 = (bf16[64,3072]{1,0:T(8,128)(2,1)S(1)}, bf16[64,3072]{1,0:T(8,128)(2,1)}, u32[]{:S(2)}) copy-start(bf16[64,3072]{1,0:T(8,128)(2,1)} %normalize.5.refs_3_.refs_4_) | copy-start | bytes 1179652
  66.5 2.6 %copy-start.24 = (bf16[1,768,256]{2,1,0:T(8,128)(2,1)}, bf16[1,768,256]{2,1,0:T(8,128)(2,1)S(1)}, u32[]{:S(2)}) copy-start(bf16[1,768,256]{2,1,0:T(8,128)(2,1)S(1)} %collective-permute-done.7.refs_10_) | copy-start | bytes 1179652
  69.1 8.2 %copy-start.19 = (bf16[64,3072]{1,0:T(8,128)(2,1)}, bf16[64,3072]{1,0:T(8,128)(2,1)S(1)}, u32[]{:S(2)}) copy-start(bf16[64,3072]{1,0:T(8,128)(2,1)S(1)} %collective-permute-done.6.refs_4_.refs_5_) | copy-start | bytes 1179652
  70.2 7.2 %copy-start.5 = (f32[2,128]{1,0:T(2,128)S(1)}, f32[2,128]{1,0:T(2,128)}, u32[]{:S(2)}) copy-start(f32[2,128]{1,0:T(2,128)} %see.1.limit0_ref) | copy-start | bytes 3076
  70.2 15.8 %collective-permute-start.10 = (bf16[128,3072]{1,0:T(8,128)(2,1)}, bf16[128,3072]{1,0:T(8,128)(2,1)S(1)}, u32[]{:S(2)}, u32[]{:S(2)}) collective-permute-start(bf16[128,3072]{1,0:T(8,128)(2,1)} %pad_maximum_fusion.1), channel_id=1, source_target_pairs={{0,1},{1,0},{2,3},{3,2},{4,5},{5,4},{6,7},{7,6},{8,9},{9,8},{10,11... | collective-permute-start | bytes 2359304 | tf_op jit(solution)/shard_map/ppermute | solution.py:514
  70.2 15.8 %collective-permute-start.11 = (bf16[256,3072]{1,0:T(8,128)(2,1)}, bf16[256,3072]{1,0:T(8,128)(2,1)}, u32[]{:S(2)}, u32[]{:S(2)}) collective-permute-start(bf16[256,3072]{1,0:T(8,128)(2,1)} %pad_maximum_fusion), channel_id=1, source_target_pairs={{0,1},{1,0},{2,3},{3,2},{4,5},{5,4},{6,7},{7,6},{8,9},{9,8},{10,11... | collective-permute-start | bytes 4718600 | tf_op jit(solution)/shard_map/ppermute | solution.py:514
  77.3 30.0 %collective-permute-start.15 = (f32[2,128]{1,0:T(2,128)S(1)}, f32[2,128]{1,0:T(2,128)S(1)}, u32[]{:S(2)}, u32[]{:S(2)}) collective-permute-start(f32[2,128]{1,0:T(2,128)S(1)} %copy-done.5), channel_id=1, source_target_pairs={{0,4},{4,0},{8,12},{12,8},{1,5},{5,1},{9,13},{13,9},{2,6},{6,2},{1... | collective-permute-start | bytes 3080 | tf_op jit(solution)/shard_map/ppermute | solution.py:514
  85.4 7.9 %copy-start.18 = (bf16[4,768,128]{2,1,0:T(8,128)(2,1)}, bf16[4,768,128]{2,1,0:T(8,128)(2,1)S(1)}, u32[]{:S(2)}) copy-start(bf16[4,768,128]{2,1,0:T(8,128)(2,1)S(1)} %all-to-all-done.refs_6_) | copy-start | bytes 2359300
  85.4 21.9 %collective-permute-start.14 = (bf16[4,768,128]{2,1,0:T(8,128)(2,1)S(1)}, bf16[4,768,128]{2,1,0:T(8,128)(2,1)S(1)}, u32[]{:S(2)}, u32[]{:S(2)}) collective-permute-start(bf16[4,768,128]{2,1,0:T(8,128)(2,1)S(1)} %all-to-all-done.refs_6_), channel_id=1, source_target_pairs={{0,16},{16,0},{1,17},{17,1},{2,18},{18,2},{3,19},{19,3},{4,20},{20... | collective-permute-start | bytes 2359304 | tf_op jit(solution)/shard_map/ppermute | solution.py:514
  85.9 0.9 copy-start.20
  93.3 34.9 %collective-permute-start.13 = (bf16[768,256]{1,0:T(8,128)(2,1)}, bf16[768,256]{1,0:T(8,128)(2,1)S(1)}, u32[]{:S(2)}, u32[]{:S(2)}) collective-permute-start(bf16[768,256]{1,0:T(8,128)(2,1)} %get-tuple-element.509), channel_id=1, source_target_pairs={{0,8},{4,12},{8,0},{12,4},{1,9},{5,13},{9,1},{13,5},{2,10},{6,14},... | collective-permute-start | bytes 1179656 | tf_op jit(solution)/shard_map/ppermute | solution.py:514
  104.4 30.4 %collective-permute-start.12 = (bf16[768,256]{1,0:T(8,128)(2,1)}, bf16[768,256]{1,0:T(8,128)(2,1)S(1)}, u32[]{:S(2)}, u32[]{:S(2)}) collective-permute-start(bf16[768,256]{1,0:T(8,128)(2,1)} %get-tuple-element.508), channel_id=1, source_target_pairs={{0,8},{4,12},{8,0},{12,4},{1,9},{5,13},{9,1},{13,5},{2,10},{6,14},... | collective-permute-start | bytes 1179656 | tf_op jit(solution)/shard_map/ppermute | solution.py:514
  107.3 0.5 copy-start.7
  107.3 20.9 %copy-start.4 = (s32[8]{0:T(128)S(1)}, s32[8]{0:T(128)}, u32[]{:S(2)}) copy-start(s32[8]{0:T(128)} %stack.35.at_ref) | copy-start | bytes 100
  107.3 20.9 %copy-start.6 = (f32[2,128]{1,0:T(2,128)S(1)}, f32[2,128]{1,0:T(2,128)}, u32[]{:S(2)}) copy-start(f32[2,128]{1,0:T(2,128)} %see.1.limit0_ref) | copy-start | bytes 3076
  107.9 0.9 copy-start.21
  128.2 0.6 copy-start.8
  128.8 1.1 copy-start.9
  130.0 1.1 copy-start.10
  131.1 1.0 copy-start.12
  132.1 1.0 copy-start.13
  134.7 1.7 %copy-start.15 = (bf16[768,128]{1,0:T(8,128)(2,1)}, bf16[768,128]{1,0:T(8,128)(2,1)S(1)}, u32[]{:S(2)}) copy-start(bf16[768,128]{1,0:T(8,128)(2,1)S(1)} %get-tuple-element.573.one_ref) | copy-start | bytes 589828
  134.8 7.4 %collective-permute-start.17 = (bf16[768,128]{1,0:T(8,128)(2,1)S(1)}, bf16[768,128]{1,0:T(8,128)(2,1)S(1)}, u32[]{:S(2)}, u32[]{:S(2)}) collective-permute-start(bf16[768,128]{1,0:T(8,128)(2,1)S(1)} %get-tuple-element.574), channel_id=1, source_target_pairs={{0,4},{4,0},{8,12},{12,8},{1,5},{5,1},{9,13},{13,9},{2,6},{6,2},{1... | collective-permute-start | bytes 589832 | tf_op jit(solution)/shard_map/ppermute | solution.py:514
  136.5 0.7 copy-start.1
  137.2 8.2 %collective-permute-start.16 = (bf16[768,128]{1,0:T(8,128)(2,1)S(1)}, bf16[768,128]{1,0:T(8,128)(2,1)S(1)}, u32[]{:S(2)}, u32[]{:S(2)}) collective-permute-start(bf16[768,128]{1,0:T(8,128)(2,1)S(1)} %get-tuple-element.572), channel_id=1, source_target_pairs={{0,4},{4,0},{8,12},{12,8},{1,5},{5,1},{9,13},{13,9},{2,6},{6,2},{1... | collective-permute-start | bytes 589832 | tf_op jit(solution)/shard_map/ppermute | solution.py:514
  142.2 0.7 copy-start.25
  145.4 0.7 copy-start.23

commit v10 on v9

--- a/solution.py
+++ b/solution.py
@@ -198,6 +198,18 @@
     return made
 
 
+def start(copies):
+    for copy in copies:
+        copy.start()
+
+
+def start_next(waves, n):
+    if n + 1 < len(waves):
+        start(waves[n + 1])
+    for copy in waves[n]:
+        copy.wait()
+
+
 def normed(value, gain):
     mean = jnp.mean(value * value, axis=-1, keepdims=True)
     return value * lax.rsqrt(mean + EPS) * gain
@@ -232,18 +244,17 @@
         own_moves, far_moves = load_columns(
             at_ref, x_sources[0] if 0 in columns else None, list(zip(piece_refs, parts)), x_ref, x_sems, step
         )
-        for copy in [*loads, *own_moves, *far_moves]:
-            copy.start()
+        waves = [[move] for move in own_moves] + [far_moves] * bool(far_moves)
+        start([*loads, *waves[0]])
         for copy in loads:
             copy.wait()
         for column in columns:
             if column:
-                for copy in far_moves:
-                    copy.wait()
+                start_next(waves, len(own_moves))
             out_ref = out_refs[0 if column == 0 else -2]
             for r in range(tokens // step):
                 if not column:
-                    own_moves[r].wait()
+                    start_next(waves, r)
                 here = slice(r * step, (r + 1) * step)
                 total = None
                 for s in range(4):
@@ -332,17 +343,16 @@
             pltpu.make_async_copy(ref, kv_ref.at[n // 2, n % 2], w_sems.at[2 + n])
             for n, ref in enumerate(row_refs)
         ]
-        for copy in [*loads, *own_moves, *far_moves, *late]:
-            copy.start()
+        waves = [[move] for move in own_moves] + [far_moves, late]
+        start([*loads, *waves[0]])
         for copy in loads:
             copy.wait()
         for column in range(2):
             if column:
-                for copy in far_moves:
-                    copy.wait()
+                start_next(waves, len(own_moves))
             for r in range(tokens // step):
                 if not column:
-                    own_moves[r].wait()
+                    start_next(waves, r)
                 here = slice(r * step, (r + 1) * step)
                 total = None
                 for s in range(4):
@@ -443,42 +453,33 @@
         in_specs=[smem] * 3 + [one, fixed(halo.shape), one, one, one],
         out_specs=[fixed(out.shape)] * 2,
         out_shape=[out] * 2,
-        compiler_params=pltpu.CompilerParams(vmem_limit_bytes=VMEM),
+        compiler_params=pltpu.CompilerParams(vmem_limit_bytes=WHOLE),
         cost_estimate=SPACE,
         name="attend_halo",
     )(at, *limits, query, halo, done, mixed, total)
 
 
-def assemble(at, parts, carried=None, cost=None, heads=4):
-    (first, one), (second, two) = parts
-    tokens, head_dim = one.shape
-    carried = () if carried is None else (carried,)
-
-    def kernel(at_ref, one_ref, two_ref, *rest):
-        @pl.when(pl.program_id(0) == 0)
-        def _():
-            rest[-1][...] = one_ref[...]
-
-        @pl.when(pl.program_id(0) == 1)
-        def _():
-            rest[-1][...] = two_ref[...]
-
-    whole = pl.BlockSpec((tokens, head_dim), lambda i, at: (0, 0))
+def assemble(at, parts):
+    indices, arrays = zip(*parts)
+    tokens, head_dim = arrays[0].shape
+    rows = tokens // 3
+
+    def kernel(at_ref, *refs):
+        for index, ref in zip(indices, refs):
+            lanes = pl.ds(pl.multiple_of(at_ref[index] * head_dim, 128), head_dim)
+            refs[-1][:, lanes] = ref[...]
+
     return pl.pallas_call(
         kernel,
-        grid_spec=pltpu.PrefetchScalarGridSpec(
-            num_scalar_prefetch=1,
-            grid=(2,),
-            in_specs=[whole, whole] + [pl.BlockSpec(memory_space=pl.ANY)] * len(carried),
-            out_specs=pl.BlockSpec(
-                (tokens, head_dim), lambda i, at: (0, jnp.where(i == 0, at[first], at[second]))
-            ),
-        ),
-        out_shape=jax.ShapeDtypeStruct((tokens, head_dim * heads), jnp.bfloat16),
-        input_output_aliases={3: 0} if carried else {},
-        cost_estimate=cost or COST,
+        grid=(tokens // rows,),
+        in_specs=[pl.BlockSpec(memory_space=pltpu.SMEM)]
+        + [pl.BlockSpec((rows, head_dim), lambda i: (i, 0))] * len(arrays),
+        out_specs=pl.BlockSpec((rows, head_dim * len(arrays)), lambda i: (i, 0)),
+        out_shape=jax.ShapeDtypeStruct((tokens, head_dim * len(arrays)), jnp.bfloat16),
+        compiler_params=pltpu.CompilerParams(vmem_limit_bytes=WHOLE),
+        cost_estimate=COST,
         name="assemble",
-    )(at, one, two, *carried)
+    )(at, *arrays)
 
 
 def tile_step(query, rows_ref, at, tile, head_dim, limit, total, mixed):
@@ -578,8 +579,6 @@
     own_mine = line.reached(*kv(MINE, w_mine, own_x[0][0], None))[0]
     (own_limit[0][0],) = line.after(own_limit[0][0])
     far_limit = to("seq", own_limit[0][0], 1)
-    q_mine = arrive(q_got)
-    q_twin = to("groups", q_mine[0], 1)
     core0 = arrive(core0)
     core1 = arrive(core1)
     n0, n1 = cutting[1], quarter - cutting[1]
@@ -597,6 +596,8 @@
 
     far, edge = kv(MINE, w_mine, None, column_arrays()[1], own_mine[0])
     rows_mine, halo_mine = [own_mine, *line.reached(far)], to("seq", edge, 2)
+    q_mine = arrive(q_got)
+    q_twin = to("groups", q_mine[0], 1)
     one_twin = arrive(one_twin)
     w_twin = [own_kv[1], one_twin, two_twin, three_twin]
     own, far, edge = kv(TWIN, w_twin, *column_arrays())
@@ -620,8 +621,8 @@
 
     keep_mine, back_mine = finish(0, halo_mine)
     keep_twin, back_twin = finish(1, halo_twin)
-    half_done = assemble(at, [(MINE, keep_mine[0]), (CROSS, back_mine)], None, SPACE)
-    return assemble(at, [(TWIN, keep_twin[0]), (CROSS_TWIN, back_twin)], half_done)
+    parts = [(MINE, keep_mine[0]), (TWIN, keep_twin[0]), (CROSS, back_mine), (CROSS_TWIN, back_twin)]
+    return assemble(at, parts)
 
 
 def solution(mesh):

time: 149 us -> 146 us (0.980)
  local copies, waits for them, and re-layouts: 11.4 us -> 6.78 us
    ppermute x18, waiting for transfers between devices: 26.9 us -> 33.8 us  [to(): lax.ppermute(value, axis, [(i, i ^ bit) for i in range(lax.axis_size(axis...]
    all_to_all x1, waiting for transfers between devices: 6 us -> 0.01 us  [per_device(): lax.all_to_all(q_sent[0], 'seq', split_axis=0, concat_axis=0, tiled=True)]
    unnamed x52 -> x38, local copies, waits for them, and re-layouts: 10.8 us -> 6.11 us
    pallas_call x2, Pallas kernels: 3.26 us -> 6.37 us  [attend_halo(): pl.pallas_call(kernel, grid=(1,), in_specs=[smem] * 3 + [one, fixed(halo....]
    pallas_call x2 -> x1, Pallas kernels: 4.94 us -> 2.9 us  [assemble(): pl.pallas_call(kernel, grid=(tokens // rows,), in_specs=[pl.BlockSpec(mem...]
  transfers between devices with their start and end apart: 19 -> 19, of which waited for: 6 -> 7; matrix products, arithmetic and copies ran while one was open for 2% -> 2% of each run, Pallas kernels for 44% -> 44%
where the time goes in v10:
time: 146 us; the launch traced here: 145 us
  Pallas kernels  70.4 us (48%)
  waiting for transfers between devices  33.8 us (23%)
  starting transfers between devices  30.1 us (21%)
  local copies, waits for them, and re-layouts  6.78 us (5%)
  other arithmetic  3.57 us (2%)
    ppermute x18, waiting for transfers between devices, to(): lax.ppermute(value, axis, [(i, i ^ bit) for i in range(lax.axis_size(axis...  33.8 us
    ppermute x18, starting transfers between devices, to(): lax.ppermute(value, axis, [(i, i ^ bit) for i in range(lax.axis_size(axis...  25.2 us
    pallas_call x3, Pallas kernels, keys_values(): pl.pallas_call(kernel, in_specs=[pl.BlockSpec(memory_space=pltpu.SMEM)] +...  22.8 us
    pallas_call x1, Pallas kernels, attend_pair(): pl.pallas_call(kernel, in_specs=[smem] * 3 + [hbm] * (1 + len(arrays) + 6...  19.4 us
    pallas_call x3, Pallas kernels, normalize(): pl.pallas_call(norm_kernel, grid=(tokens // rows,), in_specs=[pl.BlockSpe...  12.1 us
    pallas_call x2, Pallas kernels, attend_halo(): pl.pallas_call(kernel, grid=(1,), in_specs=[smem] * 3 + [one, fixed(halo....  6.37 us
    unnamed x38, local copies, waits for them, and re-layouts  6.11 us
    all_to_all x1, starting transfers between devices, per_device(): lax.all_to_all(q_sent[0], 'seq', split_axis=0, concat_axis=0, tiled=True)  4.87 us
  transfers between devices with their start and end apart: 19, of which 7 were waited for; matrix products, arithmetic and copies ran while one was open for 2% of the time, Pallas kernels for 44%

profile of v10, /device:TPU:0, one launch (start us, length us, event | category | flops | bytes accessed | tf_op | source)
XLA Modules:
  0.0 144.8 jit_solution(9325043028293954587)
XLA Ops:
  0.0 0.7 stack.35.at_ref
  0.7 3.1 %take_rows.1 = (bf16[128,3072]{1,0:T(8,128)(2,1)}, bf16[64,3072]{1,0:T(8,128)(2,1)}) custom-call(s32[8]{0:T(128)} %stack.35.at_ref, bf16[768,3072]{1,0:T(8,128)(2,1)} %x_ref.2), custom_call_target="tpu_custom_call" | custom-call | flops 1048576 | bytes 1024 | tf_op jit(solution)/shard_map/take_rows/pallas_call | solution.py:306
  3.8 3.0 %collective-permute-start.4 = (bf16[128,3072]{1,0:T(8,128)(2,1)}, bf16[128,3072]{1,0:T(8,128)(2,1)}, u32[]{:S(2)}, u32[]{:S(2)}) collective-permute-start(bf16[128,3072]{1,0:T(8,128)(2,1)} %get-tuple-element.286), channel_id=1, source_target_pairs={{0,4},{4,0},{8,12},{12,8},{1,5},{5,1},{9,13},{13,9},{2,6},{6,2},{1... | collective-permute-start | bytes 2359304 | tf_op jit(solution)/shard_map/ppermute | solution.py:515
  6.8 1.7 %cut_heads.2 = (bf16[1,768,256]{2,1,0:T(8,128)(2,1)S(1)}, bf16[1,768,256]{2,1,0:T(8,128)(2,1)S(1)}, bf16[4,768,128]{2,1,0:T(8,128)(2,1)}) custom-call(s32[8]{0:T(128)S(1)} %copy-done.1, bf16[3,768,512]{2,1,0:T(8,128)(2,1)S(1)} %bitcast.9), custom_call_target="tpu_custom_call" | custom-call | flops 1048576 | bytes 1024 | tf_op jit(solution)/shard_map/cut_heads/pallas_call | solution.py:150
  8.5 2.6 %collective-permute-start.3 = (bf16[1,768,256]{2,1,0:T(8,128)(2,1)S(1)}, bf16[1,768,256]{2,1,0:T(8,128)(2,1)}, u32[]{:S(2)}, u32[]{:S(2)}) collective-permute-start(bf16[1,768,256]{2,1,0:T(8,128)(2,1)S(1)} %get-tuple-element.450.refs_1_.refs_6_), channel_id=1, source_target_pairs={{0,8},{4,12},{8,0},{12,4},{1,9},{5,13},{9,1},{13,5},{2,10},{6,14},... | collective-permute-start | bytes 1179656 | tf_op jit(solution)/shard_map/ppermute | solution.py:515
  11.1 0.4 collective-permute-start.2
  11.6 1.3 collective-permute-start.1
  13.2 1.4 see.1.limit0_ref
  14.5 7.4 %normalize.3.refs_0_.own_ref = bf16[768,3072]{1,0:T(8,128)(2,1)} custom-call(bf16[768,3072]{1,0:T(8,128)(2,1)} %x_ref.2, f32[2,3072]{1,0:T(2,128)} %mod_ref.2), custom_call_target="tpu_custom_call" | custom-call | flops 1048576 | bytes 1024 | tf_op jit(solution)/shard_map/normalize/pallas_call | solution.py:124
  21.9 12.1 %collective-permute-done.4.x_ref = bf16[128,3072]{1,0:T(8,128)(2,1)} collective-permute-done((bf16[128,3072]{1,0:T(8,128)(2,1)}, bf16[128,3072]{1,0:T(8,128)(2,1)}, u32[]{:S(2)}, u32[]{:S(2)}) %collective-permute-start.4) | collective-permute-done | bytes 786464 | tf_op jit(solution)/shard_map/ppermute | solution.py:515
  33.9 2.6 %normalize.4.refs_0_.refs_1_ = bf16[128,3072]{1,0:T(8,128)(2,1)} custom-call(bf16[128,3072]{1,0:T(8,128)(2,1)} %collective-permute-done.4.x_ref, f32[2,3072]{1,0:T(2,128)} %mod_ref.2), custom_call_target="tpu_custom_call" | custom-call | flops 1048576 | bytes 1024 | tf_op jit(solution)/shard_map/normalize/pallas_call | solution.py:124
  36.5 2.0 %collective-permute-start.9 = (bf16[128,3072]{1,0:T(8,128)(2,1)}, bf16[128,3072]{1,0:T(8,128)(2,1)}, u32[]{:S(2)}, u32[]{:S(2)}) collective-permute-start(bf16[128,3072]{1,0:T(8,128)(2,1)} %normalize.4.refs_0_.refs_1_), channel_id=1, source_target_pairs={{0,2},{2,0},{1,3},{3,1},{4,6},{6,4},{5,7},{7,5},{8,10},{10,8},{9,1... | collective-permute-start | bytes 2359304 | tf_op jit(solution)/shard_map/ppermute | solution.py:515
  38.5 1.5 %collective-permute-start.8 = (bf16[1,768,256]{2,1,0:T(8,128)(2,1)}, bf16[1,768,256]{2,1,0:T(8,128)(2,1)}, u32[]{:S(2)}, u32[]{:S(2)}) collective-permute-start(bf16[1,768,256]{2,1,0:T(8,128)(2,1)} %collective-permute-done.3.refs_3_.refs_8_), channel_id=1, source_target_pairs={{0,16},{16,0},{1,17},{17,1},{2,18},{18,2},{3,19},{19,3},{4,20},{20... | collective-permute-start | bytes 1179656 | tf_op jit(solution)/shard_map/ppermute | solution.py:515
  40.0 2.2 %collective-permute-done.2.x_ref = bf16[64,3072]{1,0:T(8,128)(2,1)S(1)} collective-permute-done((bf16[64,3072]{1,0:T(8,128)(2,1)}, bf16[64,3072]{1,0:T(8,128)(2,1)S(1)}, u32[]{:S(2)}, u32[]{:S(2)}) %collective-permute-start.2) | collective-permute-done | bytes 393248 | tf_op jit(solution)/shard_map/ppermute | solution.py:515
  42.3 0.8 copy-done.11
  43.0 2.1 %normalize.5.refs_3_.refs_4_ = bf16[64,3072]{1,0:T(8,128)(2,1)} custom-call(bf16[64,3072]{1,0:T(8,128)(2,1)} %copy-done.11, f32[2,3072]{1,0:T(2,128)} %mod_ref.2), custom_call_target="tpu_custom_call" | custom-call | flops 1048576 | bytes 1024 | tf_op jit(solution)/shard_map/normalize/pallas_call | solution.py:124
  45.1 2.2 %collective-permute-start.6 = (bf16[64,3072]{1,0:T(8,128)(2,1)}, bf16[64,3072]{1,0:T(8,128)(2,1)S(1)}, u32[]{:S(2)}, u32[]{:S(2)}) collective-permute-start(bf16[64,3072]{1,0:T(8,128)(2,1)} %normalize.5.refs_3_.refs_4_), channel_id=1, source_target_pairs={{0,2},{2,0},{1,3},{3,1},{4,6},{6,4},{5,7},{7,5},{8,10},{10,8},{9,1... | collective-permute-start | bytes 1179656 | tf_op jit(solution)/shard_map/ppermute | solution.py:515
  47.3 6.0 %collective-permute-done.1.refs_4_.refs_9_ = bf16[1,768,256]{2,1,0:T(8,128)(2,1)} collective-permute-done((bf16[1,768,256]{2,1,0:T(8,128)(2,1)S(1)}, bf16[1,768,256]{2,1,0:T(8,128)(2,1)}, u32[]{:S(2)}, u32[]{:S(2)}) %collective-permute-start.1) | collective-permute-done | bytes 393248 | tf_op jit(solution)/shard_map/ppermute | solution.py:515
  53.4 1.5 %collective-permute-start.7 = (bf16[1,768,256]{2,1,0:T(8,128)(2,1)}, bf16[1,768,256]{2,1,0:T(8,128)(2,1)S(1)}, u32[]{:S(2)}, u32[]{:S(2)}) collective-permute-start(bf16[1,768,256]{2,1,0:T(8,128)(2,1)} %collective-permute-done.1.refs_4_.refs_9_), channel_id=1, source_target_pairs={{0,16},{16,0},{1,17},{17,1},{2,18},{18,2},{3,19},{19,3},{4,20},{20... | collective-permute-start | bytes 1179656 | tf_op jit(solution)/shard_map/ppermute | solution.py:515
  54.9 3.5 %collective-permute-done.refs_2_.refs_7_ = bf16[1,768,256]{2,1,0:T(8,128)(2,1)} collective-permute-done((bf16[1,768,256]{2,1,0:T(8,128)(2,1)S(1)}, bf16[1,768,256]{2,1,0:T(8,128)(2,1)}, u32[]{:S(2)}, u32[]{:S(2)}) %collective-permute-start) | collective-permute-done | bytes 393248 | tf_op jit(solution)/shard_map/ppermute | solution.py:515
  58.4 1.7 %collective-permute-start.5 = (bf16[1,768,256]{2,1,0:T(8,128)(2,1)}, bf16[1,768,256]{2,1,0:T(8,128)(2,1)}, u32[]{:S(2)}, u32[]{:S(2)}) collective-permute-start(bf16[1,768,256]{2,1,0:T(8,128)(2,1)} %collective-permute-done.refs_2_.refs_7_), channel_id=1, source_target_pairs={{0,16},{16,0},{1,17},{17,1},{2,18},{18,2},{3,19},{19,3},{4,20},{20... | collective-permute-start | bytes 1179656 | tf_op jit(solution)/shard_map/ppermute | solution.py:515
  60.1 4.9 %all-to-all-start = ((bf16[4,768,128]{2,1,0:T(8,128)(2,1)}), bf16[4,768,128]{2,1,0:T(8,128)(2,1)}, u32[]{:S(2)}, u32[]{:S(2)}) async-start(bf16[4,768,128]{2,1,0:T(8,128)(2,1)} %get-tuple-element.329), calls=%async_computation | async-start | bytes 1572864 | tf_op jit(solution)/shard_map/all_to_all | solution.py:562
  65.0 0.6 cut_heads.3.refs_7_
  65.6 0.5 copy-done.5
  66.1 2.5 %pad_maximum_fusion = bf16[256,3072]{1,0:T(8,128)(2,1)} fusion(bf16[128,3072]{1,0:T(8,128)(2,1)} %collective-permute-done.9.refs_1_.refs_2_, bf16[128,3072]{1,0:T(8,128)(2,1)S(1)} %copy-done.5), kind=kLoop, calls=%fused_computation | loop fusion | flops 3145728 | bytes 3145728 | tf_op jit(solution)/shard_map/concatenate | solution.py:551
  68.7 1.0 pad_maximum_fusion.1
  69.7 0.5 collective-permute-start.11
  70.2 6.5 %keys_values.3.refs_12_.refs_8_ = bf16[768,256]{1,0:T(8,128)(2,1)} custom-call(s32[8]{0:T(128)} %stack.35.at_ref, bf16[768,3072]{1,0:T(8,128)(2,1)} %normalize.3.refs_0_.own_ref, bf16[1,768,256]{2,1,0:T(8,128)(2,1)} %copy-done.3, bf16[1,768,256]{2,1,0:T(8,128)(2,1)} %collective-permute-done.refs_2_.refs_7_, ...), custom_call_target="tpu_custom_call" | custom-call | flops 68719476736 | bytes 1024 | tf_op jit(solution)/shard_map/keys_values/pallas_call | solution.py:277
  76.8 2.1 %collective-permute-start.15 = (f32[2,128]{1,0:T(2,128)S(1)}, f32[2,128]{1,0:T(2,128)S(1)}, u32[]{:S(2)}, u32[]{:S(2)}) collective-permute-start(f32[2,128]{1,0:T(2,128)S(1)} %copy-done.14), channel_id=1, source_target_pairs={{0,4},{4,0},{8,12},{12,8},{1,5},{5,1},{9,13},{13,9},{2,6},{6,2},{1... | collective-permute-start | bytes 3080 | tf_op jit(solution)/shard_map/ppermute | solution.py:515
  78.9 1.2 copy-done.8
  80.0 0.9 copy-done.9
  80.9 6.5 %keys_values.4 = (bf16[768,256]{1,0:T(8,128)(2,1)}, bf16[768,256]{1,0:T(8,128)(2,1)}) custom-call(s32[8]{0:T(128)} %stack.35.at_ref, bf16[128,3072]{1,0:T(8,128)(2,1)} %normalize.4.refs_0_.refs_1_, bf16[128,3072]{1,0:T(8,128)(2,1)} %collective-permute-done.9.refs_1_.refs_2_, bf16[256,3072]{1,0:T(8,128)(2,1)} %copy-done.8, ...), custom_call_target="tpu_custom_call" | custom-call | flops 68719476736 | bytes 1024 | tf_op jit(solution)/shard_map/keys_values/pallas_call | solution.py:277
  87.4 0.6 collective-permute-start.14
  88.0 3.8 %collective-permute-start.13 = (bf16[768,256]{1,0:T(8,128)(2,1)}, bf16[768,256]{1,0:T(8,128)(2,1)S(1)}, u32[]{:S(2)}, u32[]{:S(2)}) collective-permute-start(bf16[768,256]{1,0:T(8,128)(2,1)} %get-tuple-element.501), channel_id=1, source_target_pairs={{0,8},{4,12},{8,0},{12,4},{1,9},{5,13},{9,1},{13,5},{2,10},{6,14},... | collective-permute-start | bytes 1179656 | tf_op jit(solution)/shard_map/ppermute | solution.py:515
  91.8 9.9 %keys_values.5 = (bf16[768,256]{1,0:T(8,128)(2,1)}, bf16[768,256]{1,0:T(8,128)(2,1)}, bf16[768,256]{1,0:T(8,128)(2,1)}) custom-call(s32[8]{0:T(128)} %stack.35.at_ref, bf16[768,3072]{1,0:T(8,128)(2,1)} %normalize.3.refs_0_.own_ref, bf16[128,3072]{1,0:T(8,128)(2,1)} %normalize.4.refs_0_.refs_1_, bf16[128,3072]{1,0:T(8,128)(2,1)} %collective-permute-done.9.refs_1_.refs_2_, ...), custom_call_target="tpu_custom_call" | custom-call | flops 68719476736 | bytes 1024 | tf_op jit(solution)/shard_map/keys_values/pallas_call | solution.py:277
  101.8 5.1 %collective-permute-done.14.refs_7_ = bf16[4,768,128]{2,1,0:T(8,128)(2,1)S(1)} collective-permute-done((bf16[4,768,128]{2,1,0:T(8,128)(2,1)}, bf16[4,768,128]{2,1,0:T(8,128)(2,1)S(1)}, u32[]{:S(2)}, u32[]{:S(2)}) %collective-permute-start.14) | collective-permute-done | bytes 786464 | tf_op jit(solution)/shard_map/ppermute | solution.py:515
  106.8 0.9 copy-done.10
  107.7 19.4 %attend_pair.1 = (bf16[2,768,128]{2,1,0:T(8,128)(2,1)}, bf16[2,768,128]{2,1,0:T(8,128)(2,1)}, f32[2,768,128]{2,1,0:T(8,128)}, f32[2,768,128]{2,1,0:T(8,128)}) custom-call(s32[8]{0:T(128)} %stack.35.at_ref, f32[2,128]{1,0:T(2,128)} %see.1.limit0_ref, f32[2,128]{1,0:T(2,128)} %copy-done.15, bf16[768,3072]{1,0:T(8,128)(2,1)} %normalize.3.refs_0_.own_ref, ...), custom_call_target="tpu_custom_call" | custom-call | flops 1048576 | bytes 1024 | tf_op jit(solution)/shard_map/attend_pair/pallas_call | solution.py:402
  127.1 0.7 copy-done.17
  127.9 3.2 %attend_halo.2 = (bf16[768,128]{1,0:T(8,128)(2,1)}, bf16[768,128]{1,0:T(8,128)(2,1)}) custom-call(s32[8]{0:T(128)} %stack.35.at_ref, f32[2,128]{1,0:T(2,128)} %see.1.limit0_ref, f32[2,128]{1,0:T(2,128)} %copy-done.15, bf16[2,768,128]{2,1,0:T(8,128)(2,1)} %get-tuple-element.559.q_ref, bf16[768,256]{1,0:T(8,128)(2,1)} %copy-done.17, ...), custom_call_target="tpu_custom_call" | custom-call | flops 68719476736 | bytes 1024 | tf_op jit(solution)/shard_map/attend_halo/pallas_call | solution.py:450
  131.1 0.3 collective-permute-start.16
  131.4 0.4 copy-done.18
  131.8 3.2 %attend_halo.3 = (bf16[768,128]{1,0:T(8,128)(2,1)}, bf16[768,128]{1,0:T(8,128)(2,1)}) custom-call(s32[8]{0:T(128)} %stack.35.at_ref, f32[2,128]{1,0:T(2,128)} %see.1.limit0_ref, f32[2,128]{1,0:T(2,128)} %copy-done.15, bf16[2,768,128]{2,1,0:T(8,128)(2,1)} %get-tuple-element.559.q_ref, bf16[768,256]{1,0:T(8,128)(2,1)} %copy-done.18, ...), custom_call_target="tpu_custom_call" | custom-call | flops 68719476736 | bytes 1024 | tf_op jit(solution)/shard_map/attend_halo/pallas_call | solution.py:450
  135.0 1.4 collective-permute-start.17
  136.4 1.0 collective-permute-done.16.refs_2_
  137.3 3.9 %collective-permute-done.17.refs_3_ = bf16[768,128]{1,0:T(8,128)(2,1)S(1)} collective-permute-done((bf16[768,128]{1,0:T(8,128)(2,1)}, bf16[768,128]{1,0:T(8,128)(2,1)S(1)}, u32[]{:S(2)}, u32[]{:S(2)}) %collective-permute-start.17) | collective-permute-done | bytes 196640 | tf_op jit(solution)/shard_map/ppermute | solution.py:515
  141.2 0.7 copy-done.13
  141.9 2.9 %assemble.1 = bf16[768,512]{1,0:T(8,128)(2,1)} custom-call(s32[8]{0:T(128)} %stack.35.at_ref, bf16[768,128]{1,0:T(8,128)(2,1)} %get-tuple-element.556.refs_0_, bf16[768,128]{1,0:T(8,128)(2,1)} %get-tuple-element.564.refs_1_, bf16[768,128]{1,0:T(8,128)(2,1)} %copy-done.12, bf16[768,128]{1,0:T(8,128)(2,1)} %copy-done.13), custom_call_target="tpu_custom_call" | custom-call | flops 1048576 | bytes 1024 | tf_op jit(solution)/shard_map/assemble/pallas_call | solution.py:472
  (45 shorter events, 0.4 us)
Async XLA Ops:
  0.7 6.2 %copy-start = (bf16[768,3,512]{2,0,1:T(8,128)(2,1)S(1)}, bf16[768,3,512]{2,0,1:T(8,128)(2,1)}, u32[]{:S(2)}) copy-start(bf16[768,3,512]{2,0,1:T(8,128)(2,1)} %param.8) | copy-start | bytes 7077892
  0.7 6.2 %copy-start.1 = (s32[8]{0:T(128)S(1)}, s32[8]{0:T(128)}, u32[]{:S(2)}) copy-start(s32[8]{0:T(128)} %stack.35.at_ref) | copy-start | bytes 100
  3.8 30.1 %collective-permute-start.4 = (bf16[128,3072]{1,0:T(8,128)(2,1)}, bf16[128,3072]{1,0:T(8,128)(2,1)}, u32[]{:S(2)}, u32[]{:S(2)}) collective-permute-start(bf16[128,3072]{1,0:T(8,128)(2,1)} %get-tuple-element.286), channel_id=1, source_target_pairs={{0,4},{4,0},{8,12},{12,8},{1,5},{5,1},{9,13},{13,9},{2,6},{6,2},{1... | collective-permute-start | bytes 2359304 | tf_op jit(solution)/shard_map/ppermute | solution.py:515
  8.5 13.3 %copy-start.3 = (bf16[1,768,256]{2,1,0:T(8,128)(2,1)}, bf16[1,768,256]{2,1,0:T(8,128)(2,1)S(1)}, u32[]{:S(2)}) copy-start(bf16[1,768,256]{2,1,0:T(8,128)(2,1)S(1)} %get-tuple-element.450.refs_1_.refs_6_) | copy-start | bytes 1179652
  8.5 30.0 %collective-permute-start.3 = (bf16[1,768,256]{2,1,0:T(8,128)(2,1)S(1)}, bf16[1,768,256]{2,1,0:T(8,128)(2,1)}, u32[]{:S(2)}, u32[]{:S(2)}) collective-permute-start(bf16[1,768,256]{2,1,0:T(8,128)(2,1)S(1)} %get-tuple-element.450.refs_1_.refs_6_), channel_id=1, source_target_pairs={{0,8},{4,12},{8,0},{12,4},{1,9},{5,13},{9,1},{13,5},{2,10},{6,14},... | collective-permute-start | bytes 1179656 | tf_op jit(solution)/shard_map/ppermute | solution.py:515
  11.1 31.1 %collective-permute-start.2 = (bf16[64,3072]{1,0:T(8,128)(2,1)}, bf16[64,3072]{1,0:T(8,128)(2,1)S(1)}, u32[]{:S(2)}, u32[]{:S(2)}) collective-permute-start(bf16[64,3072]{1,0:T(8,128)(2,1)} %get-tuple-element.287), channel_id=1, source_target_pairs={{0,4},{4,0},{8,12},{12,8},{1,5},{5,1},{9,13},{13,9},{2,6},{6,2},{1... | collective-permute-start | bytes 1179656 | tf_op jit(solution)/shard_map/ppermute | solution.py:515
  11.6 41.8 %collective-permute-start.1 = (bf16[1,768,256]{2,1,0:T(8,128)(2,1)S(1)}, bf16[1,768,256]{2,1,0:T(8,128)(2,1)}, u32[]{:S(2)}, u32[]{:S(2)}) collective-permute-start(bf16[1,768,256]{2,1,0:T(8,128)(2,1)S(1)} %get-tuple-element.289), channel_id=1, source_target_pairs={{0,12},{4,8},{8,4},{12,0},{1,13},{5,9},{9,5},{13,1},{2,14},{6,10},... | collective-permute-start | bytes 1179656 | tf_op jit(solution)/shard_map/ppermute | solution.py:515
  12.9 45.5 %collective-permute-start = (bf16[1,768,256]{2,1,0:T(8,128)(2,1)S(1)}, bf16[1,768,256]{2,1,0:T(8,128)(2,1)}, u32[]{:S(2)}, u32[]{:S(2)}) collective-permute-start(bf16[1,768,256]{2,1,0:T(8,128)(2,1)S(1)} %get-tuple-element.289), channel_id=1, source_target_pairs={{0,4},{4,0},{8,12},{12,8},{1,5},{5,1},{9,13},{13,9},{2,6},{6,2},{1... | collective-permute-start | bytes 1179656 | tf_op jit(solution)/shard_map/ppermute | solution.py:515
  36.5 28.4 %copy-start.2 = (s32[8]{0:T(128)S(1)}, s32[8]{0:T(128)}, u32[]{:S(2)}) copy-start(s32[8]{0:T(128)} %stack.35.at_ref) | copy-start | bytes 100
  36.5 29.1 %collective-permute-start.9 = (bf16[128,3072]{1,0:T(8,128)(2,1)}, bf16[128,3072]{1,0:T(8,128)(2,1)}, u32[]{:S(2)}, u32[]{:S(2)}) collective-permute-start(bf16[128,3072]{1,0:T(8,128)(2,1)} %normalize.4.refs_0_.refs_1_), channel_id=1, source_target_pairs={{0,2},{2,0},{1,3},{3,1},{4,6},{6,4},{5,7},{7,5},{8,10},{10,8},{9,1... | collective-permute-start | bytes 2359304 | tf_op jit(solution)/shard_map/ppermute | solution.py:515
  38.5 27.1 %collective-permute-start.8 = (bf16[1,768,256]{2,1,0:T(8,128)(2,1)}, bf16[1,768,256]{2,1,0:T(8,128)(2,1)}, u32[]{:S(2)}, u32[]{:S(2)}) collective-permute-start(bf16[1,768,256]{2,1,0:T(8,128)(2,1)} %collective-permute-done.3.refs_3_.refs_8_), channel_id=1, source_target_pairs={{0,16},{16,0},{1,17},{17,1},{2,18},{18,2},{3,19},{19,3},{4,20},{20... | collective-permute-start | bytes 1179656 | tf_op jit(solution)/shard_map/ppermute | solution.py:515
  42.3 0.8 copy-start.11
  45.1 23.5 %collective-permute-start.6 = (bf16[64,3072]{1,0:T(8,128)(2,1)}, bf16[64,3072]{1,0:T(8,128)(2,1)S(1)}, u32[]{:S(2)}, u32[]{:S(2)}) collective-permute-start(bf16[64,3072]{1,0:T(8,128)(2,1)} %normalize.5.refs_3_.refs_4_), channel_id=1, source_target_pairs={{0,2},{2,0},{1,3},{3,1},{4,6},{6,4},{5,7},{7,5},{8,10},{10,8},{9,1... | collective-permute-start | bytes 1179656 | tf_op jit(solution)/shard_map/ppermute | solution.py:515
  53.4 12.3 %collective-permute-start.7 = (bf16[1,768,256]{2,1,0:T(8,128)(2,1)}, bf16[1,768,256]{2,1,0:T(8,128)(2,1)S(1)}, u32[]{:S(2)}, u32[]{:S(2)}) collective-permute-start(bf16[1,768,256]{2,1,0:T(8,128)(2,1)} %collective-permute-done.1.refs_4_.refs_9_), channel_id=1, source_target_pairs={{0,16},{16,0},{1,17},{17,1},{2,18},{18,2},{3,19},{19,3},{4,20},{20... | collective-permute-start | bytes 1179656 | tf_op jit(solution)/shard_map/ppermute | solution.py:515
  58.4 29.6 %collective-permute-start.5 = (bf16[1,768,256]{2,1,0:T(8,128)(2,1)}, bf16[1,768,256]{2,1,0:T(8,128)(2,1)}, u32[]{:S(2)}, u32[]{:S(2)}) collective-permute-start(bf16[1,768,256]{2,1,0:T(8,128)(2,1)} %collective-permute-done.refs_2_.refs_7_), channel_id=1, source_target_pairs={{0,16},{16,0},{1,17},{17,1},{2,18},{18,2},{3,19},{19,3},{4,20},{20... | collective-permute-start | bytes 1179656 | tf_op jit(solution)/shard_map/ppermute | solution.py:515
  60.1 27.3 %all-to-all-start = ((bf16[4,768,128]{2,1,0:T(8,128)(2,1)}), bf16[4,768,128]{2,1,0:T(8,128)(2,1)}, u32[]{:S(2)}, u32[]{:S(2)}) async-start(bf16[4,768,128]{2,1,0:T(8,128)(2,1)} %get-tuple-element.329), calls=%async_computation | async-start | bytes 1572864 | tf_op jit(solution)/shard_map/all_to_all | solution.py:562
  65.0 1.1 copy-start.5
  65.6 3.1 %copy-start.4 = (bf16[1,768,256]{2,1,0:T(8,128)(2,1)}, bf16[1,768,256]{2,1,0:T(8,128)(2,1)S(1)}, u32[]{:S(2)}) copy-start(bf16[1,768,256]{2,1,0:T(8,128)(2,1)S(1)} %cut_heads.3.refs_7_) | copy-start | bytes 1179652
  65.6 3.1 %copy-start.6 = (bf16[64,3072]{1,0:T(8,128)(2,1)S(1)}, bf16[64,3072]{1,0:T(8,128)(2,1)}, u32[]{:S(2)}) copy-start(bf16[64,3072]{1,0:T(8,128)(2,1)} %normalize.5.refs_3_.refs_4_) | copy-start | bytes 1179652
  66.1 2.6 %copy-start.16 = (bf16[1,768,256]{2,1,0:T(8,128)(2,1)}, bf16[1,768,256]{2,1,0:T(8,128)(2,1)S(1)}, u32[]{:S(2)}) copy-start(bf16[1,768,256]{2,1,0:T(8,128)(2,1)S(1)} %collective-permute-done.7.refs_10_) | copy-start | bytes 1179652
  68.7 8.1 %copy-start.7 = (bf16[64,3072]{1,0:T(8,128)(2,1)}, bf16[64,3072]{1,0:T(8,128)(2,1)S(1)}, u32[]{:S(2)}) copy-start(bf16[64,3072]{1,0:T(8,128)(2,1)S(1)} %collective-permute-done.6.refs_4_.refs_5_) | copy-start | bytes 1179652
  69.7 7.1 %copy-start.14 = (f32[2,128]{1,0:T(2,128)S(1)}, f32[2,128]{1,0:T(2,128)}, u32[]{:S(2)}) copy-start(f32[2,128]{1,0:T(2,128)} %see.1.limit0_ref) | copy-start | bytes 3076
  69.7 9.2 %collective-permute-start.10 = (bf16[128,3072]{1,0:T(8,128)(2,1)}, bf16[128,3072]{1,0:T(8,128)(2,1)S(1)}, u32[]{:S(2)}, u32[]{:S(2)}) collective-permute-start(bf16[128,3072]{1,0:T(8,128)(2,1)} %pad_maximum_fusion.1), channel_id=1, source_target_pairs={{0,1},{1,0},{2,3},{3,2},{4,5},{5,4},{6,7},{7,6},{8,9},{9,8},{10,11... | collective-permute-start | bytes 2359304 | tf_op jit(solution)/shard_map/ppermute | solution.py:515
  69.7 9.2 %collective-permute-start.11 = (bf16[256,3072]{1,0:T(8,128)(2,1)}, bf16[256,3072]{1,0:T(8,128)(2,1)S(1)}, u32[]{:S(2)}, u32[]{:S(2)}) collective-permute-start(bf16[256,3072]{1,0:T(8,128)(2,1)} %pad_maximum_fusion), channel_id=1, source_target_pairs={{0,1},{1,0},{2,3},{3,2},{4,5},{5,4},{6,7},{7,6},{8,9},{9,8},{10,11... | collective-permute-start | bytes 4718600 | tf_op jit(solution)/shard_map/ppermute | solution.py:515
  76.8 24.9 %collective-permute-start.15 = (f32[2,128]{1,0:T(2,128)S(1)}, f32[2,128]{1,0:T(2,128)S(1)}, u32[]{:S(2)}, u32[]{:S(2)}) collective-permute-start(f32[2,128]{1,0:T(2,128)S(1)} %copy-done.14), channel_id=1, source_target_pairs={{0,4},{4,0},{8,12},{12,8},{1,5},{5,1},{9,13},{13,9},{2,6},{6,2},{1... | collective-permute-start | bytes 3080 | tf_op jit(solution)/shard_map/ppermute | solution.py:515
  78.8 1.2 copy-start.8
  80.0 0.9 copy-start.9
  87.4 19.4 %collective-permute-start.14 = (bf16[4,768,128]{2,1,0:T(8,128)(2,1)}, bf16[4,768,128]{2,1,0:T(8,128)(2,1)S(1)}, u32[]{:S(2)}, u32[]{:S(2)}) collective-permute-start(bf16[4,768,128]{2,1,0:T(8,128)(2,1)} %all-to-all-done.refs_6_), channel_id=1, source_target_pairs={{0,16},{16,0},{1,17},{17,1},{2,18},{18,2},{3,19},{19,3},{4,20},{20... | collective-permute-start | bytes 2359304 | tf_op jit(solution)/shard_map/ppermute | solution.py:515
  88.0 39.2 %collective-permute-start.13 = (bf16[768,256]{1,0:T(8,128)(2,1)}, bf16[768,256]{1,0:T(8,128)(2,1)S(1)}, u32[]{:S(2)}, u32[]{:S(2)}) collective-permute-start(bf16[768,256]{1,0:T(8,128)(2,1)} %get-tuple-element.501), channel_id=1, source_target_pairs={{0,8},{4,12},{8,0},{12,4},{1,9},{5,13},{9,1},{13,5},{2,10},{6,14},... | collective-permute-start | bytes 1179656 | tf_op jit(solution)/shard_map/ppermute | solution.py:515
  101.7 5.2 %copy-start.15 = (f32[2,128]{1,0:T(2,128)}, f32[2,128]{1,0:T(2,128)S(1)}, u32[]{:S(2)}) copy-start(f32[2,128]{1,0:T(2,128)S(1)} %collective-permute-done.15.limit1_ref) | copy-start | bytes 3076
  101.7 29.4 %collective-permute-start.12 = (bf16[768,256]{1,0:T(8,128)(2,1)}, bf16[768,256]{1,0:T(8,128)(2,1)S(1)}, u32[]{:S(2)}, u32[]{:S(2)}) collective-permute-start(bf16[768,256]{1,0:T(8,128)(2,1)} %get-tuple-element.500), channel_id=1, source_target_pairs={{0,8},{4,12},{8,0},{12,4},{1,9},{5,13},{9,1},{13,5},{2,10},{6,14},... | collective-permute-start | bytes 1179656 | tf_op jit(solution)/shard_map/ppermute | solution.py:515
  106.8 0.9 copy-start.10
  127.1 0.7 copy-start.17
  131.1 0.7 copy-start.18
  131.1 6.2 %collective-permute-start.16 = (bf16[768,128]{1,0:T(8,128)(2,1)}, bf16[768,128]{1,0:T(8,128)(2,1)S(1)}, u32[]{:S(2)}, u32[]{:S(2)}) collective-permute-start(bf16[768,128]{1,0:T(8,128)(2,1)} %get-tuple-element.565), channel_id=1, source_target_pairs={{0,4},{4,0},{8,12},{12,8},{1,5},{5,1},{9,13},{13,9},{2,6},{6,2},{1... | collective-permute-start | bytes 589832 | tf_op jit(solution)/shard_map/ppermute | solution.py:515
  135.0 6.2 %collective-permute-start.17 = (bf16[768,128]{1,0:T(8,128)(2,1)}, bf16[768,128]{1,0:T(8,128)(2,1)S(1)}, u32[]{:S(2)}, u32[]{:S(2)}) collective-permute-start(bf16[768,128]{1,0:T(8,128)(2,1)} %get-tuple-element.566), channel_id=1, source_target_pairs={{0,4},{4,0},{8,12},{12,8},{1,5},{5,1},{9,13},{13,9},{2,6},{6,2},{1... | collective-permute-start | bytes 589832 | tf_op jit(solution)/shard_map/ppermute | solution.py:515
  137.3 3.9 %copy-start.12 = (bf16[768,128]{1,0:T(8,128)(2,1)}, bf16[768,128]{1,0:T(8,128)(2,1)S(1)}, u32[]{:S(2)}) copy-start(bf16[768,128]{1,0:T(8,128)(2,1)S(1)} %collective-permute-done.16.refs_2_) | copy-start | bytes 589828
  141.2 0.7 copy-start.13

commit v11 on v10

--- a/solution.py
+++ b/solution.py
@@ -379,11 +379,11 @@
                     total = jnp.zeros((tile, 128), jnp.float32)
                     mixed = jnp.zeros((tile, head_dim), jnp.float32)
                     for other in range(2):
-                        for t in range(tiles):
-                            limit = (limit0_ref, limit1_ref)[column][i, (other ^ column) * tiles + t]
-                            total, mixed = tile_step(
-                                query, kv_ref.at[h, other], t * tile, tile, head_dim, limit, total, mixed
-                            )
+                        limits_ref = (limit0_ref, limit1_ref)[column]
+                        seen = [limits_ref[i, (other ^ column) * tiles + t] for t in range(tiles)]
+                        total, mixed = column_step(
+                            query, kv_ref.at[h, other], tile, head_dim, seen, total, mixed
+                        )
 
                     @pl.when(is_edge)
                     def _():
@@ -433,11 +433,11 @@
         for i in range(tiles):
             here = slice(i * tile, (i + 1) * tile)
             sums, rows = total_ref[0, here, :], mixed_ref[0, here, :]
-            for t in range(tiles):
-                limit = jnp.where(is_mid, limit0_ref[i, 2 * tiles + t], limit1_ref[i, 2 * tiles + t])
-                sums, rows = tile_step(
-                    q_ref[0, here, :], halo_ref, t * tile, tile, head_dim, limit, sums, rows
-                )
+            seen = [
+                jnp.where(is_mid, limit0_ref[i, 2 * tiles + t], limit1_ref[i, 2 * tiles + t])
+                for t in range(tiles)
+            ]
+            sums, rows = column_step(q_ref[0, here, :], halo_ref, tile, head_dim, seen, sums, rows)
             edge = (rows / jnp.sum(sums, axis=-1, keepdims=True)).astype(jnp.bfloat16)
             outer = done_ref[0, here, :]
             keep_ref[here, :] = jnp.where(is_mid, edge, outer)
@@ -482,18 +482,19 @@
     )(at, *arrays)
 
 
-def tile_step(query, rows_ref, at, tile, head_dim, limit, total, mixed):
+def column_step(query, rows_ref, tile, head_dim, limits, total, mixed):
     scale = math.log2(math.e) / math.sqrt(head_dim)
-    keys = rows_ref[at : at + tile, :head_dim]
-    values = rows_ref[at : at + tile, head_dim:]
     scores = lax.dot_general(
-        query, keys, (((1,), (1,)), ((), ())), preferred_element_type=jnp.float32
-    )
-    weights = jnp.exp2(scores * scale + limit)
-    for c in range(tile // 128):
-        total = total + weights[:, c * 128 : (c + 1) * 128]
+        query, rows_ref[:, :head_dim], (((1,), (1,)), ((), ())), preferred_element_type=jnp.float32
+    )
+    rounded = []
+    for t, limit in enumerate(limits):
+        weights = jnp.exp2(scores[:, t * tile : (t + 1) * tile] * scale + limit)
+        for c in range(tile // 128):
+            total = total + weights[:, c * 128 : (c + 1) * 128]
+        rounded.append(weights.astype(jnp.bfloat16))
     mixed = mixed + jnp.dot(
-        weights.astype(jnp.bfloat16), values, preferred_element_type=jnp.float32
+        jnp.concatenate(rounded, axis=1), rows_ref[:, head_dim:], preferred_element_type=jnp.float32
     )
     return total, mixed
 
@@ -555,12 +556,12 @@
         kept = arrive(got[which])
         return kept, to("groups", kept[0], 1)
 
+    (q_sent[0],) = line.after(q_sent[0])
+    q_got = lax.all_to_all(q_sent[0], "seq", split_axis=0, concat_axis=0, tiled=True)
+    line.drop(q_sent)
     near0, far0 = take(0)
     two_mine, two_twin = swap(0)
     near1, far1 = take(1)
-    (q_sent[0],) = line.after(q_sent[0])
-    q_got = lax.all_to_all(q_sent[0], "seq", split_axis=0, concat_axis=0, tiled=True)
-    line.drop(q_sent)
     three_mine, three_twin = swap(1)
     one_mine, one_twin = swap(2)
     (w,) = line.after(w)
@@ -569,6 +570,8 @@
     two_twin = arrive(two_twin)
     three_twin = arrive(three_twin)
     far1, core1 = spread(near1, far1)
+    q_mine = arrive(q_got)
+    q_twin = to("groups", q_mine[0], 1)
     w_mine = [own_kv[0], one_mine, two_mine, three_mine]
 
     def kv(head, boxes, own, pieces, own_rows=None):
@@ -596,8 +599,6 @@
 
     far, edge = kv(MINE, w_mine, None, column_arrays()[1], own_mine[0])
     rows_mine, halo_mine = [own_mine, *line.reached(far)], to("seq", edge, 2)
-    q_mine = arrive(q_got)
-    q_twin = to("groups", q_mine[0], 1)
     one_twin = arrive(one_twin)
     w_twin = [own_kv[1], one_twin, two_twin, three_twin]
     own, far, edge = kv(TWIN, w_twin, *column_arrays())

time: 146 us -> 147 us (level)
    unnamed x38 -> x36, local copies, waits for them, and re-layouts: 6.11 us -> 6.13 us
  transfers between devices with their start and end apart: 19 -> 19, of which waited for: 7 -> 5; matrix products, arithmetic and copies ran while one was open for 2% -> 2% of each run, Pallas kernels for 44% -> 45%
where the time goes in v11:
time: 147 us; the launch traced here: 146 us
  Pallas kernels  71.2 us (48%)
  waiting for transfers between devices  34.6 us (24%)
  starting transfers between devices  29.8 us (20%)
  local copies, waits for them, and re-layouts  6.74 us (5%)
  other arithmetic  3.35 us (2%)
    ppermute x18, waiting for transfers between devices, to(): lax.ppermute(value, axis, [(i, i ^ bit) for i in range(lax.axis_size(axis...  34.6 us
    ppermute x18, starting transfers between devices, to(): lax.ppermute(value, axis, [(i, i ^ bit) for i in range(lax.axis_size(axis...  25.6 us
    pallas_call x3, Pallas kernels, keys_values(): pl.pallas_call(kernel, in_specs=[pl.BlockSpec(memory_space=pltpu.SMEM)] +...  22.8 us
    pallas_call x1, Pallas kernels, attend_pair(): pl.pallas_call(kernel, in_specs=[smem] * 3 + [hbm] * (1 + len(arrays) + 6...  20.7 us
    pallas_call x3, Pallas kernels, normalize(): pl.pallas_call(norm_kernel, grid=(tokens // rows,), in_specs=[pl.BlockSpe...  12 us
    unnamed x36, local copies, waits for them, and re-layouts  6.13 us
    pallas_call x2, Pallas kernels, attend_halo(): pl.pallas_call(kernel, grid=(1,), in_specs=[smem] * 3 + [one, fixed(halo....  5.88 us
    all_to_all x1, starting transfers between devices, per_device(): lax.all_to_all(q_sent[0], 'seq', split_axis=0, concat_axis=0, tiled=True)  4.21 us
  transfers between devices with their start and end apart: 19, of which 5 were waited for; matrix products, arithmetic and copies ran while one was open for 2% of the time, Pallas kernels for 45%

profile of v11, /device:TPU:0, one launch (start us, length us, event | category | flops | bytes accessed | tf_op | source)
XLA Modules:
  0.0 146.0 jit_solution(1878024900120847631)
XLA Ops:
  0.0 0.6 stack.35.at_ref
  0.6 3.1 %take_rows.1 = (bf16[128,3072]{1,0:T(8,128)(2,1)}, bf16[64,3072]{1,0:T(8,128)(2,1)}) custom-call(s32[8]{0:T(128)} %stack.35.at_ref, bf16[768,3072]{1,0:T(8,128)(2,1)} %x_ref.2), custom_call_target="tpu_custom_call" | custom-call | flops 1048576 | bytes 1024 | tf_op jit(solution)/shard_map/take_rows/pallas_call | solution.py:306
  3.7 3.0 %collective-permute-start.4 = (bf16[128,3072]{1,0:T(8,128)(2,1)}, bf16[128,3072]{1,0:T(8,128)(2,1)}, u32[]{:S(2)}, u32[]{:S(2)}) collective-permute-start(bf16[128,3072]{1,0:T(8,128)(2,1)} %get-tuple-element.285), channel_id=1, source_target_pairs={{0,4},{4,0},{8,12},{12,8},{1,5},{5,1},{9,13},{13,9},{2,6},{6,2},{1... | collective-permute-start | bytes 2359304 | tf_op jit(solution)/shard_map/ppermute | solution.py:516
  6.8 1.7 %cut_heads.2 = (bf16[1,768,256]{2,1,0:T(8,128)(2,1)S(1)}, bf16[1,768,256]{2,1,0:T(8,128)(2,1)S(1)}, bf16[4,768,128]{2,1,0:T(8,128)(2,1)}) custom-call(s32[8]{0:T(128)S(1)} %copy-done.1, bf16[3,768,512]{2,1,0:T(8,128)(2,1)S(1)} %bitcast.9), custom_call_target="tpu_custom_call" | custom-call | flops 1048576 | bytes 1024 | tf_op jit(solution)/shard_map/cut_heads/pallas_call | solution.py:150
  8.5 2.6 %collective-permute-start.3 = (bf16[1,768,256]{2,1,0:T(8,128)(2,1)S(1)}, bf16[1,768,256]{2,1,0:T(8,128)(2,1)}, u32[]{:S(2)}, u32[]{:S(2)}) collective-permute-start(bf16[1,768,256]{2,1,0:T(8,128)(2,1)S(1)} %get-tuple-element.461.refs_1_.refs_6_), channel_id=1, source_target_pairs={{0,8},{4,12},{8,0},{12,4},{1,9},{5,13},{9,1},{13,5},{2,10},{6,14},... | collective-permute-start | bytes 1179656 | tf_op jit(solution)/shard_map/ppermute | solution.py:516
  11.1 0.4 collective-permute-start.2
  11.6 1.3 collective-permute-start.1
  12.9 0.2 collective-permute-start
  13.1 1.3 see.1.limit0_ref
  14.5 7.3 %normalize.3.refs_0_.own_ref = bf16[768,3072]{1,0:T(8,128)(2,1)} custom-call(bf16[768,3072]{1,0:T(8,128)(2,1)} %x_ref.2, f32[2,3072]{1,0:T(2,128)} %mod_ref.2), custom_call_target="tpu_custom_call" | custom-call | flops 1048576 | bytes 1024 | tf_op jit(solution)/shard_map/normalize/pallas_call | solution.py:124
  21.8 4.2 %all-to-all-start = ((bf16[4,768,128]{2,1,0:T(8,128)(2,1)}), bf16[4,768,128]{2,1,0:T(8,128)(2,1)}, u32[]{:S(2)}, u32[]{:S(2)}) async-start(bf16[4,768,128]{2,1,0:T(8,128)(2,1)} %get-tuple-element.373), calls=%async_computation | async-start | bytes 1572864 | tf_op jit(solution)/shard_map/all_to_all | solution.py:560
  26.1 7.8 %collective-permute-done.4.x_ref = bf16[128,3072]{1,0:T(8,128)(2,1)} collective-permute-done((bf16[128,3072]{1,0:T(8,128)(2,1)}, bf16[128,3072]{1,0:T(8,128)(2,1)}, u32[]{:S(2)}, u32[]{:S(2)}) %collective-permute-start.4) | collective-permute-done | bytes 786464 | tf_op jit(solution)/shard_map/ppermute | solution.py:516
  33.9 2.6 %normalize.4.refs_0_.refs_1_ = bf16[128,3072]{1,0:T(8,128)(2,1)} custom-call(bf16[128,3072]{1,0:T(8,128)(2,1)} %collective-permute-done.4.x_ref, f32[2,3072]{1,0:T(2,128)} %mod_ref.2), custom_call_target="tpu_custom_call" | custom-call | flops 1048576 | bytes 1024 | tf_op jit(solution)/shard_map/normalize/pallas_call | solution.py:124
  36.5 2.0 %collective-permute-start.9 = (bf16[128,3072]{1,0:T(8,128)(2,1)}, bf16[128,3072]{1,0:T(8,128)(2,1)}, u32[]{:S(2)}, u32[]{:S(2)}) collective-permute-start(bf16[128,3072]{1,0:T(8,128)(2,1)} %normalize.4.refs_0_.refs_1_), channel_id=1, source_target_pairs={{0,2},{2,0},{1,3},{3,1},{4,6},{6,4},{5,7},{7,5},{8,10},{10,8},{9,1... | collective-permute-start | bytes 2359304 | tf_op jit(solution)/shard_map/ppermute | solution.py:516
  38.5 1.5 %collective-permute-start.8 = (bf16[1,768,256]{2,1,0:T(8,128)(2,1)}, bf16[1,768,256]{2,1,0:T(8,128)(2,1)}, u32[]{:S(2)}, u32[]{:S(2)}) collective-permute-start(bf16[1,768,256]{2,1,0:T(8,128)(2,1)} %collective-permute-done.3.refs_3_.refs_8_), channel_id=1, source_target_pairs={{0,16},{16,0},{1,17},{17,1},{2,18},{18,2},{3,19},{19,3},{4,20},{20... | collective-permute-start | bytes 1179656 | tf_op jit(solution)/shard_map/ppermute | solution.py:516
  40.0 14.9 %collective-permute-done.2.x_ref = bf16[64,3072]{1,0:T(8,128)(2,1)S(1)} collective-permute-done((bf16[64,3072]{1,0:T(8,128)(2,1)}, bf16[64,3072]{1,0:T(8,128)(2,1)S(1)}, u32[]{:S(2)}, u32[]{:S(2)}) %collective-permute-start.2) | collective-permute-done | bytes 393248 | tf_op jit(solution)/shard_map/ppermute | solution.py:516
  54.8 0.7 copy-done.10
  55.6 2.1 %normalize.5.refs_3_.refs_4_ = bf16[64,3072]{1,0:T(8,128)(2,1)} custom-call(bf16[64,3072]{1,0:T(8,128)(2,1)} %copy-done.10, f32[2,3072]{1,0:T(2,128)} %mod_ref.2), custom_call_target="tpu_custom_call" | custom-call | flops 1048576 | bytes 1024 | tf_op jit(solution)/shard_map/normalize/pallas_call | solution.py:124
  57.7 2.0 %collective-permute-start.6 = (bf16[64,3072]{1,0:T(8,128)(2,1)}, bf16[64,3072]{1,0:T(8,128)(2,1)S(1)}, u32[]{:S(2)}, u32[]{:S(2)}) collective-permute-start(bf16[64,3072]{1,0:T(8,128)(2,1)} %normalize.5.refs_3_.refs_4_), channel_id=1, source_target_pairs={{0,2},{2,0},{1,3},{3,1},{4,6},{6,4},{5,7},{7,5},{8,10},{10,8},{9,1... | collective-permute-start | bytes 1179656 | tf_op jit(solution)/shard_map/ppermute | solution.py:516
  59.7 1.5 %collective-permute-start.7 = (bf16[1,768,256]{2,1,0:T(8,128)(2,1)}, bf16[1,768,256]{2,1,0:T(8,128)(2,1)S(1)}, u32[]{:S(2)}, u32[]{:S(2)}) collective-permute-start(bf16[1,768,256]{2,1,0:T(8,128)(2,1)} %collective-permute-done.1.refs_4_.refs_9_), channel_id=1, source_target_pairs={{0,16},{16,0},{1,17},{17,1},{2,18},{18,2},{3,19},{19,3},{4,20},{20... | collective-permute-start | bytes 1179656 | tf_op jit(solution)/shard_map/ppermute | solution.py:516
  61.2 6.4 %collective-permute-done.refs_2_.refs_7_ = bf16[1,768,256]{2,1,0:T(8,128)(2,1)} collective-permute-done((bf16[1,768,256]{2,1,0:T(8,128)(2,1)S(1)}, bf16[1,768,256]{2,1,0:T(8,128)(2,1)}, u32[]{:S(2)}, u32[]{:S(2)}) %collective-permute-start) | collective-permute-done | bytes 393248 | tf_op jit(solution)/shard_map/ppermute | solution.py:516
  67.6 2.0 %collective-permute-start.5 = (bf16[1,768,256]{2,1,0:T(8,128)(2,1)}, bf16[1,768,256]{2,1,0:T(8,128)(2,1)}, u32[]{:S(2)}, u32[]{:S(2)}) collective-permute-start(bf16[1,768,256]{2,1,0:T(8,128)(2,1)} %collective-permute-done.refs_2_.refs_7_), channel_id=1, source_target_pairs={{0,16},{16,0},{1,17},{17,1},{2,18},{18,2},{3,19},{19,3},{4,20},{20... | collective-permute-start | bytes 1179656 | tf_op jit(solution)/shard_map/ppermute | solution.py:516
  69.6 0.6 cut_heads.3.refs_7_
  70.3 1.0 pad_maximum_fusion.1
  71.3 0.6 copy-done.5
  71.9 2.4 %pad_maximum_fusion = bf16[256,3072]{1,0:T(8,128)(2,1)} fusion(bf16[128,3072]{1,0:T(8,128)(2,1)} %collective-permute-done.9.refs_1_.refs_2_, bf16[128,3072]{1,0:T(8,128)(2,1)S(1)} %copy-done.5), kind=kLoop, calls=%fused_computation | loop fusion | flops 3145728 | bytes 3145728 | tf_op jit(solution)/shard_map/concatenate | solution.py:552
  74.3 0.1 collective-permute-start.11
  74.4 0.1 collective-permute-start.14
  74.5 6.5 %keys_values.3.refs_12_.refs_8_ = bf16[768,256]{1,0:T(8,128)(2,1)} custom-call(s32[8]{0:T(128)} %stack.35.at_ref, bf16[768,3072]{1,0:T(8,128)(2,1)} %normalize.3.refs_0_.own_ref, bf16[1,768,256]{2,1,0:T(8,128)(2,1)} %copy-done.3, bf16[1,768,256]{2,1,0:T(8,128)(2,1)} %collective-permute-done.refs_2_.refs_7_, ...), custom_call_target="tpu_custom_call" | custom-call | flops 68719476736 | bytes 1024 | tf_op jit(solution)/shard_map/keys_values/pallas_call | solution.py:277
  81.0 0.8 collective-permute-start.15
  81.9 1.1 copy-done.8
  83.0 0.9 copy-done.9
  83.9 6.4 %keys_values.4 = (bf16[768,256]{1,0:T(8,128)(2,1)}, bf16[768,256]{1,0:T(8,128)(2,1)}) custom-call(s32[8]{0:T(128)} %stack.35.at_ref, bf16[128,3072]{1,0:T(8,128)(2,1)} %normalize.4.refs_0_.refs_1_, bf16[128,3072]{1,0:T(8,128)(2,1)} %collective-permute-done.9.refs_1_.refs_2_, bf16[256,3072]{1,0:T(8,128)(2,1)} %copy-done.8, ...), custom_call_target="tpu_custom_call" | custom-call | flops 68719476736 | bytes 1024 | tf_op jit(solution)/shard_map/keys_values/pallas_call | solution.py:277
  90.4 6.5 %collective-permute-start.13 = (bf16[768,256]{1,0:T(8,128)(2,1)}, bf16[768,256]{1,0:T(8,128)(2,1)S(1)}, u32[]{:S(2)}, u32[]{:S(2)}) collective-permute-start(bf16[768,256]{1,0:T(8,128)(2,1)} %get-tuple-element.499), channel_id=1, source_target_pairs={{0,8},{4,12},{8,0},{12,4},{1,9},{5,13},{9,1},{13,5},{2,10},{6,14},... | collective-permute-start | bytes 1179656 | tf_op jit(solution)/shard_map/ppermute | solution.py:516
  96.8 9.9 %keys_values.5 = (bf16[768,256]{1,0:T(8,128)(2,1)}, bf16[768,256]{1,0:T(8,128)(2,1)}, bf16[768,256]{1,0:T(8,128)(2,1)}) custom-call(s32[8]{0:T(128)} %stack.35.at_ref, bf16[768,3072]{1,0:T(8,128)(2,1)} %normalize.3.refs_0_.own_ref, bf16[128,3072]{1,0:T(8,128)(2,1)} %normalize.4.refs_0_.refs_1_, bf16[128,3072]{1,0:T(8,128)(2,1)} %collective-permute-done.9.refs_1_.refs_2_, ...), custom_call_target="tpu_custom_call" | custom-call | flops 68719476736 | bytes 1024 | tf_op jit(solution)/shard_map/keys_values/pallas_call | solution.py:277
  106.7 0.1 collective-permute-start.12
  106.9 0.6 copy-done.14
  107.4 20.7 %attend_pair.1 = (bf16[2,768,128]{2,1,0:T(8,128)(2,1)}, bf16[2,768,128]{2,1,0:T(8,128)(2,1)}, f32[2,768,128]{2,1,0:T(8,128)}, f32[2,768,128]{2,1,0:T(8,128)}) custom-call(s32[8]{0:T(128)} %stack.35.at_ref, f32[2,128]{1,0:T(2,128)} %see.1.limit0_ref, f32[2,128]{1,0:T(2,128)} %copy-done.14, bf16[768,3072]{1,0:T(8,128)(2,1)} %normalize.3.refs_0_.own_ref, ...), custom_call_target="tpu_custom_call" | custom-call | flops 1048576 | bytes 1024 | tf_op jit(solution)/shard_map/attend_pair/pallas_call | solution.py:402
  128.2 0.7 copy-done.17
  128.9 2.9 %attend_halo.2 = (bf16[768,128]{1,0:T(8,128)(2,1)}, bf16[768,128]{1,0:T(8,128)(2,1)}) custom-call(s32[8]{0:T(128)} %stack.35.at_ref, f32[2,128]{1,0:T(2,128)} %see.1.limit0_ref, f32[2,128]{1,0:T(2,128)} %copy-done.14, bf16[2,768,128]{2,1,0:T(8,128)(2,1)} %get-tuple-element.557.q_ref, bf16[768,256]{1,0:T(8,128)(2,1)} %copy-done.17, ...), custom_call_target="tpu_custom_call" | custom-call | flops 68719476736 | bytes 1024 | tf_op jit(solution)/shard_map/attend_halo/pallas_call | solution.py:450
  131.9 0.1 collective-permute-start.16
  132.0 0.7 copy-done.16
  132.6 2.9 %attend_halo.3 = (bf16[768,128]{1,0:T(8,128)(2,1)}, bf16[768,128]{1,0:T(8,128)(2,1)}) custom-call(s32[8]{0:T(128)} %stack.35.at_ref, f32[2,128]{1,0:T(2,128)} %see.1.limit0_ref, f32[2,128]{1,0:T(2,128)} %copy-done.14, bf16[2,768,128]{2,1,0:T(8,128)(2,1)} %get-tuple-element.557.q_ref, bf16[768,256]{1,0:T(8,128)(2,1)} %copy-done.16, ...), custom_call_target="tpu_custom_call" | custom-call | flops 68719476736 | bytes 1024 | tf_op jit(solution)/shard_map/attend_halo/pallas_call | solution.py:450
  135.6 1.3 collective-permute-start.17
  136.9 1.8 %collective-permute-done.16.refs_2_ = bf16[768,128]{1,0:T(8,128)(2,1)S(1)} collective-permute-done((bf16[768,128]{1,0:T(8,128)(2,1)}, bf16[768,128]{1,0:T(8,128)(2,1)S(1)}, u32[]{:S(2)}, u32[]{:S(2)}) %collective-permute-start.16) | collective-permute-done | bytes 196640 | tf_op jit(solution)/shard_map/ppermute | solution.py:516
  138.7 3.7 %collective-permute-done.17.refs_3_ = bf16[768,128]{1,0:T(8,128)(2,1)S(1)} collective-permute-done((bf16[768,128]{1,0:T(8,128)(2,1)}, bf16[768,128]{1,0:T(8,128)(2,1)S(1)}, u32[]{:S(2)}, u32[]{:S(2)}) %collective-permute-start.17) | collective-permute-done | bytes 196640 | tf_op jit(solution)/shard_map/ppermute | solution.py:516
  142.4 0.7 copy-done.12
  143.1 2.9 %assemble.1 = bf16[768,512]{1,0:T(8,128)(2,1)} custom-call(s32[8]{0:T(128)} %stack.35.at_ref, bf16[768,128]{1,0:T(8,128)(2,1)} %get-tuple-element.554.refs_0_, bf16[768,128]{1,0:T(8,128)(2,1)} %get-tuple-element.562.refs_1_, bf16[768,128]{1,0:T(8,128)(2,1)} %copy-done.11, bf16[768,128]{1,0:T(8,128)(2,1)} %copy-done.12), custom_call_target="tpu_custom_call" | custom-call | flops 1048576 | bytes 1024 | tf_op jit(solution)/shard_map/assemble/pallas_call | solution.py:472
  (43 shorter events, 0.1 us)
Async XLA Ops:
  0.6 6.2 %copy-start = (bf16[768,3,512]{2,0,1:T(8,128)(2,1)S(1)}, bf16[768,3,512]{2,0,1:T(8,128)(2,1)}, u32[]{:S(2)}) copy-start(bf16[768,3,512]{2,0,1:T(8,128)(2,1)} %param.8) | copy-start | bytes 7077892
  0.6 6.2 %copy-start.1 = (s32[8]{0:T(128)S(1)}, s32[8]{0:T(128)}, u32[]{:S(2)}) copy-start(s32[8]{0:T(128)} %stack.35.at_ref) | copy-start | bytes 100
  3.7 30.1 %collective-permute-start.4 = (bf16[128,3072]{1,0:T(8,128)(2,1)}, bf16[128,3072]{1,0:T(8,128)(2,1)}, u32[]{:S(2)}, u32[]{:S(2)}) collective-permute-start(bf16[128,3072]{1,0:T(8,128)(2,1)} %get-tuple-element.285), channel_id=1, source_target_pairs={{0,4},{4,0},{8,12},{12,8},{1,5},{5,1},{9,13},{13,9},{2,6},{6,2},{1... | collective-permute-start | bytes 2359304 | tf_op jit(solution)/shard_map/ppermute | solution.py:516
  8.5 13.3 %copy-start.3 = (bf16[1,768,256]{2,1,0:T(8,128)(2,1)}, bf16[1,768,256]{2,1,0:T(8,128)(2,1)S(1)}, u32[]{:S(2)}) copy-start(bf16[1,768,256]{2,1,0:T(8,128)(2,1)S(1)} %get-tuple-element.461.refs_1_.refs_6_) | copy-start | bytes 1179652
  8.5 29.9 %collective-permute-start.3 = (bf16[1,768,256]{2,1,0:T(8,128)(2,1)S(1)}, bf16[1,768,256]{2,1,0:T(8,128)(2,1)}, u32[]{:S(2)}, u32[]{:S(2)}) collective-permute-start(bf16[1,768,256]{2,1,0:T(8,128)(2,1)S(1)} %get-tuple-element.461.refs_1_.refs_6_), channel_id=1, source_target_pairs={{0,8},{4,12},{8,0},{12,4},{1,9},{5,13},{9,1},{13,5},{2,10},{6,14},... | collective-permute-start | bytes 1179656 | tf_op jit(solution)/shard_map/ppermute | solution.py:516
  11.1 43.7 %collective-permute-start.2 = (bf16[64,3072]{1,0:T(8,128)(2,1)}, bf16[64,3072]{1,0:T(8,128)(2,1)S(1)}, u32[]{:S(2)}, u32[]{:S(2)}) collective-permute-start(bf16[64,3072]{1,0:T(8,128)(2,1)} %get-tuple-element.286), channel_id=1, source_target_pairs={{0,4},{4,0},{8,12},{12,8},{1,5},{5,1},{9,13},{13,9},{2,6},{6,2},{1... | collective-permute-start | bytes 1179656 | tf_op jit(solution)/shard_map/ppermute | solution.py:516
  11.6 48.1 %collective-permute-start.1 = (bf16[1,768,256]{2,1,0:T(8,128)(2,1)S(1)}, bf16[1,768,256]{2,1,0:T(8,128)(2,1)}, u32[]{:S(2)}, u32[]{:S(2)}) collective-permute-start(bf16[1,768,256]{2,1,0:T(8,128)(2,1)S(1)} %get-tuple-element.288), channel_id=1, source_target_pairs={{0,12},{4,8},{8,4},{12,0},{1,13},{5,9},{9,5},{13,1},{2,14},{6,10},... | collective-permute-start | bytes 1179656 | tf_op jit(solution)/shard_map/ppermute | solution.py:516
  12.9 54.7 %collective-permute-start = (bf16[1,768,256]{2,1,0:T(8,128)(2,1)S(1)}, bf16[1,768,256]{2,1,0:T(8,128)(2,1)}, u32[]{:S(2)}, u32[]{:S(2)}) collective-permute-start(bf16[1,768,256]{2,1,0:T(8,128)(2,1)S(1)} %get-tuple-element.288), channel_id=1, source_target_pairs={{0,4},{4,0},{8,12},{12,8},{1,5},{5,1},{9,13},{13,9},{2,6},{6,2},{1... | collective-permute-start | bytes 1179656 | tf_op jit(solution)/shard_map/ppermute | solution.py:516
  21.8 52.6 %all-to-all-start = ((bf16[4,768,128]{2,1,0:T(8,128)(2,1)}), bf16[4,768,128]{2,1,0:T(8,128)(2,1)}, u32[]{:S(2)}, u32[]{:S(2)}) async-start(bf16[4,768,128]{2,1,0:T(8,128)(2,1)} %get-tuple-element.373), calls=%async_computation | async-start | bytes 1572864 | tf_op jit(solution)/shard_map/all_to_all | solution.py:560
  26.1 43.5 %copy-start.2 = (s32[8]{0:T(128)S(1)}, s32[8]{0:T(128)}, u32[]{:S(2)}) copy-start(s32[8]{0:T(128)} %stack.35.at_ref) | copy-start | bytes 100
  36.5 33.8 %collective-permute-start.9 = (bf16[128,3072]{1,0:T(8,128)(2,1)}, bf16[128,3072]{1,0:T(8,128)(2,1)}, u32[]{:S(2)}, u32[]{:S(2)}) collective-permute-start(bf16[128,3072]{1,0:T(8,128)(2,1)} %normalize.4.refs_0_.refs_1_), channel_id=1, source_target_pairs={{0,2},{2,0},{1,3},{3,1},{4,6},{6,4},{5,7},{7,5},{8,10},{10,8},{9,1... | collective-permute-start | bytes 2359304 | tf_op jit(solution)/shard_map/ppermute | solution.py:516
  38.5 31.8 %collective-permute-start.8 = (bf16[1,768,256]{2,1,0:T(8,128)(2,1)}, bf16[1,768,256]{2,1,0:T(8,128)(2,1)}, u32[]{:S(2)}, u32[]{:S(2)}) collective-permute-start(bf16[1,768,256]{2,1,0:T(8,128)(2,1)} %collective-permute-done.3.refs_3_.refs_8_), channel_id=1, source_target_pairs={{0,16},{16,0},{1,17},{17,1},{2,18},{18,2},{3,19},{19,3},{4,20},{20... | collective-permute-start | bytes 1179656 | tf_op jit(solution)/shard_map/ppermute | solution.py:516
  54.8 0.8 copy-start.10
  57.7 12.6 %copy-start.6 = (bf16[64,3072]{1,0:T(8,128)(2,1)S(1)}, bf16[64,3072]{1,0:T(8,128)(2,1)}, u32[]{:S(2)}) copy-start(bf16[64,3072]{1,0:T(8,128)(2,1)} %normalize.5.refs_3_.refs_4_) | copy-start | bytes 1179652
  57.7 12.6 %collective-permute-start.6 = (bf16[64,3072]{1,0:T(8,128)(2,1)}, bf16[64,3072]{1,0:T(8,128)(2,1)S(1)}, u32[]{:S(2)}, u32[]{:S(2)}) collective-permute-start(bf16[64,3072]{1,0:T(8,128)(2,1)} %normalize.5.refs_3_.refs_4_), channel_id=1, source_target_pairs={{0,2},{2,0},{1,3},{3,1},{4,6},{6,4},{5,7},{7,5},{8,10},{10,8},{9,1... | collective-permute-start | bytes 1179656 | tf_op jit(solution)/shard_map/ppermute | solution.py:516
  59.7 10.6 %collective-permute-start.7 = (bf16[1,768,256]{2,1,0:T(8,128)(2,1)}, bf16[1,768,256]{2,1,0:T(8,128)(2,1)S(1)}, u32[]{:S(2)}, u32[]{:S(2)}) collective-permute-start(bf16[1,768,256]{2,1,0:T(8,128)(2,1)} %collective-permute-done.1.refs_4_.refs_9_), channel_id=1, source_target_pairs={{0,16},{16,0},{1,17},{17,1},{2,18},{18,2},{3,19},{19,3},{4,20},{20... | collective-permute-start | bytes 1179656 | tf_op jit(solution)/shard_map/ppermute | solution.py:516
  67.6 22.8 %collective-permute-start.5 = (bf16[1,768,256]{2,1,0:T(8,128)(2,1)}, bf16[1,768,256]{2,1,0:T(8,128)(2,1)}, u32[]{:S(2)}, u32[]{:S(2)}) collective-permute-start(bf16[1,768,256]{2,1,0:T(8,128)(2,1)} %collective-permute-done.refs_2_.refs_7_), channel_id=1, source_target_pairs={{0,16},{16,0},{1,17},{17,1},{2,18},{18,2},{3,19},{19,3},{4,20},{20... | collective-permute-start | bytes 1179656 | tf_op jit(solution)/shard_map/ppermute | solution.py:516
  70.2 4.1 %copy-start.4 = (bf16[1,768,256]{2,1,0:T(8,128)(2,1)}, bf16[1,768,256]{2,1,0:T(8,128)(2,1)S(1)}, u32[]{:S(2)}) copy-start(bf16[1,768,256]{2,1,0:T(8,128)(2,1)S(1)} %cut_heads.3.refs_7_) | copy-start | bytes 1179652
  70.2 1.7 %copy-start.5 = (bf16[128,3072]{1,0:T(8,128)(2,1)S(1)}, bf16[128,3072]{1,0:T(8,128)(2,1)}, u32[]{:S(2)}) copy-start(bf16[128,3072]{1,0:T(8,128)(2,1)} %normalize.4.refs_0_.refs_1_) | copy-start | bytes 2359300
  70.3 4.0 %copy-start.15 = (bf16[1,768,256]{2,1,0:T(8,128)(2,1)}, bf16[1,768,256]{2,1,0:T(8,128)(2,1)S(1)}, u32[]{:S(2)}) copy-start(bf16[1,768,256]{2,1,0:T(8,128)(2,1)S(1)} %collective-permute-done.7.refs_10_) | copy-start | bytes 1179652
  70.3 4.0 %copy-start.7 = (bf16[64,3072]{1,0:T(8,128)(2,1)}, bf16[64,3072]{1,0:T(8,128)(2,1)S(1)}, u32[]{:S(2)}) copy-start(bf16[64,3072]{1,0:T(8,128)(2,1)S(1)} %collective-permute-done.6.refs_4_.refs_5_) | copy-start | bytes 1179652
  71.3 10.6 %collective-permute-start.10 = (bf16[128,3072]{1,0:T(8,128)(2,1)}, bf16[128,3072]{1,0:T(8,128)(2,1)S(1)}, u32[]{:S(2)}, u32[]{:S(2)}) collective-permute-start(bf16[128,3072]{1,0:T(8,128)(2,1)} %pad_maximum_fusion.1), channel_id=1, source_target_pairs={{0,1},{1,0},{2,3},{3,2},{4,5},{5,4},{6,7},{7,6},{8,9},{9,8},{10,11... | collective-permute-start | bytes 2359304 | tf_op jit(solution)/shard_map/ppermute | solution.py:516
  74.3 6.7 %copy-start.13 = (f32[2,128]{1,0:T(2,128)S(1)}, f32[2,128]{1,0:T(2,128)}, u32[]{:S(2)}) copy-start(f32[2,128]{1,0:T(2,128)} %see.1.limit0_ref) | copy-start | bytes 3076
  74.3 7.5 %collective-permute-start.11 = (bf16[256,3072]{1,0:T(8,128)(2,1)}, bf16[256,3072]{1,0:T(8,128)(2,1)S(1)}, u32[]{:S(2)}, u32[]{:S(2)}) collective-permute-start(bf16[256,3072]{1,0:T(8,128)(2,1)} %pad_maximum_fusion), channel_id=1, source_target_pairs={{0,1},{1,0},{2,3},{3,2},{4,5},{5,4},{6,7},{7,6},{8,9},{9,8},{10,11... | collective-permute-start | bytes 4718600 | tf_op jit(solution)/shard_map/ppermute | solution.py:516
  74.4 32.4 %collective-permute-start.14 = (bf16[4,768,128]{2,1,0:T(8,128)(2,1)}, bf16[4,768,128]{2,1,0:T(8,128)(2,1)}, u32[]{:S(2)}, u32[]{:S(2)}) collective-permute-start(bf16[4,768,128]{2,1,0:T(8,128)(2,1)} %all-to-all-done.refs_6_), channel_id=1, source_target_pairs={{0,16},{16,0},{1,17},{17,1},{2,18},{18,2},{3,19},{19,3},{4,20},{20... | collective-permute-start | bytes 2359304 | tf_op jit(solution)/shard_map/ppermute | solution.py:516
  81.0 25.8 %collective-permute-start.15 = (f32[2,128]{1,0:T(2,128)S(1)}, f32[2,128]{1,0:T(2,128)S(1)}, u32[]{:S(2)}, u32[]{:S(2)}) collective-permute-start(f32[2,128]{1,0:T(2,128)S(1)} %copy-done.13), channel_id=1, source_target_pairs={{0,4},{4,0},{8,12},{12,8},{1,5},{5,1},{9,13},{13,9},{2,6},{6,2},{1... | collective-permute-start | bytes 3080 | tf_op jit(solution)/shard_map/ppermute | solution.py:516
  81.9 1.1 copy-start.8
  83.0 0.9 copy-start.9
  90.4 37.8 %collective-permute-start.13 = (bf16[768,256]{1,0:T(8,128)(2,1)}, bf16[768,256]{1,0:T(8,128)(2,1)S(1)}, u32[]{:S(2)}, u32[]{:S(2)}) collective-permute-start(bf16[768,256]{1,0:T(8,128)(2,1)} %get-tuple-element.499), channel_id=1, source_target_pairs={{0,8},{4,12},{8,0},{12,4},{1,9},{5,13},{9,1},{13,5},{2,10},{6,14},... | collective-permute-start | bytes 1179656 | tf_op jit(solution)/shard_map/ppermute | solution.py:516
  106.7 25.1 %collective-permute-start.12 = (bf16[768,256]{1,0:T(8,128)(2,1)}, bf16[768,256]{1,0:T(8,128)(2,1)S(1)}, u32[]{:S(2)}, u32[]{:S(2)}) collective-permute-start(bf16[768,256]{1,0:T(8,128)(2,1)} %get-tuple-element.498), channel_id=1, source_target_pairs={{0,8},{4,12},{8,0},{12,4},{1,9},{5,13},{9,1},{13,5},{2,10},{6,14},... | collective-permute-start | bytes 1179656 | tf_op jit(solution)/shard_map/ppermute | solution.py:516
  106.8 0.6 copy-start.14
  128.2 0.7 copy-start.17
  131.9 0.7 copy-start.16
  131.9 6.8 %collective-permute-start.16 = (bf16[768,128]{1,0:T(8,128)(2,1)}, bf16[768,128]{1,0:T(8,128)(2,1)S(1)}, u32[]{:S(2)}, u32[]{:S(2)}) collective-permute-start(bf16[768,128]{1,0:T(8,128)(2,1)} %get-tuple-element.563), channel_id=1, source_target_pairs={{0,4},{4,0},{8,12},{12,8},{1,5},{5,1},{9,13},{13,9},{2,6},{6,2},{1... | collective-permute-start | bytes 589832 | tf_op jit(solution)/shard_map/ppermute | solution.py:516
  135.6 6.8 %collective-permute-start.17 = (bf16[768,128]{1,0:T(8,128)(2,1)}, bf16[768,128]{1,0:T(8,128)(2,1)S(1)}, u32[]{:S(2)}, u32[]{:S(2)}) collective-permute-start(bf16[768,128]{1,0:T(8,128)(2,1)} %get-tuple-element.564), channel_id=1, source_target_pairs={{0,4},{4,0},{8,12},{12,8},{1,5},{5,1},{9,13},{13,9},{2,6},{6,2},{1... | collective-permute-start | bytes 589832 | tf_op jit(solution)/shard_map/ppermute | solution.py:516
  138.7 3.7 %copy-start.11 = (bf16[768,128]{1,0:T(8,128)(2,1)}, bf16[768,128]{1,0:T(8,128)(2,1)S(1)}, u32[]{:S(2)}) copy-start(bf16[768,128]{1,0:T(8,128)(2,1)S(1)} %collective-permute-done.16.refs_2_) | copy-start | bytes 589828
  142.4 0.7 copy-start.12

commit v12 on v11

--- a/solution.py
+++ b/solution.py
@@ -215,7 +215,7 @@
     return value * lax.rsqrt(mean + EPS) * gain
 
 
-def keys_values(at, head, own, pieces, weights, bias, gain, own_rows=None):
+def keys_values(at, head, own, pieces, weights, bias, gain, own_rows=None, query_weights=()):
     _, rows, cols = weights[0].shape
     head_dim = gain.shape[1]
     arrays, parts = zip(*pieces) if pieces else ((), ())
@@ -227,18 +227,25 @@
     sources = [own] * (own is not None) + list(arrays)
     known = [] if own_rows is None else [own_rows]
     n_out = (own is not None) + 2 * bool(pieces)
+    queries = list(query_weights)
 
     def kernel(at_ref, *refs):
         x_sources, weight_refs = refs[: len(sources)], refs[len(sources) : len(sources) + 4]
-        b_ref, g_ref, *rest = refs[len(sources) + 4 :]
+        query_refs = refs[len(sources) + 4 : len(sources) + 4 + len(queries)]
+        b_ref, g_ref, *rest = refs[len(sources) + 4 + len(queries) :]
+        q_ref = rest[len(known) + n_out] if queries else None
         own_in, out_refs = rest[: len(known)], rest[len(known) : len(known) + n_out]
-        x_ref, w_ref, x_sems, w_sems = rest[-4:]
+        x_ref, w_ref, wq_ref, x_sems, w_sems = rest[-5:]
         z = at_ref[0]
         is_mid = (z == 1) | (z == 2)
         lanes = pl.ds(pl.multiple_of(at_ref[head] * head_dim, 128), head_dim)
         loads = [
             pltpu.make_async_copy(ref, w_ref.at[pl.ds(s, 1)], w_sems.at[s])
             for s, ref in enumerate(weight_refs)
+        ]
+        loads += [
+            pltpu.make_async_copy(ref, wq_ref.at[h], w_sems.at[4 + h])
+            for h, ref in enumerate(query_refs)
         ]
         piece_refs = x_sources[len(sources) - len(arrays) :]
         own_moves, far_moves = load_columns(
@@ -268,6 +275,20 @@
                 out_ref[here, :head_dim] = key.astype(jnp.bfloat16)
                 value = total[:, head_dim:] + b_ref[2:3, lanes]
                 out_ref[here, head_dim:] = value.astype(jnp.bfloat16)
+                if queries:
+                    total = None
+                    for s in range(4):
+                        product = jnp.dot(
+                            x_ref[columns.index(column), here, s * rows : (s + 1) * rows],
+                            jnp.concatenate([wq_ref[0, s], wq_ref[1, s]], axis=1),
+                            preferred_element_type=jnp.float32,
+                        )
+                        total = product if total is None else total + product
+                    for h in range(2):
+                        head_lanes = pl.ds(pl.multiple_of(at_ref[2 + h] * head_dim, 128), head_dim)
+                        query = total[:, h * head_dim : (h + 1) * head_dim] + b_ref[0:1, head_lanes]
+                        query = normed(query, g_ref[0:1, :])
+                        q_ref[h, column, here, :] = query.astype(jnp.bfloat16)
                 if column:
                     own_ref = own_in[0] if known else out_refs[0]
                     out_refs[-1][here, :] = jnp.where(is_mid, own_ref[here, :], out_ref[here, :])
@@ -277,20 +298,22 @@
     return pl.pallas_call(
         kernel,
         in_specs=[pl.BlockSpec(memory_space=pltpu.SMEM)]
-        + [hbm] * (len(sources) + 4)
+        + [hbm] * (len(sources) + 4 + len(queries))
         + [pl.BlockSpec()] * (2 + len(known)),
-        out_specs=[pl.BlockSpec()] * n_out,
-        out_shape=[out] * n_out,
+        out_specs=[pl.BlockSpec()] * (n_out + bool(queries)),
+        out_shape=[out] * n_out
+        + [jax.ShapeDtypeStruct((2, 2, tokens, head_dim), jnp.bfloat16)] * bool(queries),
         scratch_shapes=[
             pltpu.VMEM((len(columns), tokens, width), jnp.bfloat16),
             pltpu.VMEM((4, rows, cols), jnp.bfloat16),
+            pltpu.VMEM((2, 4, rows, head_dim) if queries else (8, 128), jnp.bfloat16),
             pltpu.SemaphoreType.DMA((moves,)),
-            pltpu.SemaphoreType.DMA((4,)),
+            pltpu.SemaphoreType.DMA((4 + len(queries),)),
         ],
         compiler_params=pltpu.CompilerParams(vmem_limit_bytes=WHOLE),
         cost_estimate=SPACE,
         name="keys_values",
-    )(at, *sources, *weights, bias, gain, *known)
+    )(at, *sources, *weights, *queries, bias, gain, *known)
 
 
 def take_rows(at, frames, sizes):
@@ -317,56 +340,21 @@
     )(at, frames)
 
 
-def attend_pair(at, limits, own, pieces, weights, bias, gain, rows):
-    tokens, width = own.shape
-    head_dim = gain.shape[1]
+def attend_pair(at, limits, queries, rows):
+    _, _, tokens, head_dim = queries.shape
     tiles = limits[0].shape[0]
     tile = tokens // tiles
-    arrays, parts = zip(*pieces)
-    step = 256
-    moves = tokens // step + sum(map(len, parts))
-    shard = weights[0].shape[1]
-
-    def kernel(at_ref, limit0_ref, limit1_ref, own_ref, *refs):
-        piece_refs, weight_refs = refs[: len(arrays)], refs[len(arrays) : len(arrays) + 2]
-        row_refs = refs[len(arrays) + 2 : len(arrays) + 6]
-        (b_ref, g_ref, edge_ref, done_ref, mixed_ref, total_ref,
-         x_ref, w_ref, q_ref, kv_ref, x_sems, w_sems) = refs[len(arrays) + 6 :]
+
+    def kernel(at_ref, limit0_ref, limit1_ref, query_ref, *refs):
+        row_refs = refs[:4]
+        edge_ref, done_ref, mixed_ref, total_ref, q_ref, kv_ref, sems = refs[4:]
         z = at_ref[0]
         is_mid = (z == 1) | (z == 2)
-        loads = [
-            pltpu.make_async_copy(ref, w_ref.at[h], w_sems.at[h])
-            for h, ref in enumerate(weight_refs)
-        ]
-        own_moves, far_moves = load_columns(at_ref, own_ref, list(zip(piece_refs, parts)), x_ref, x_sems, step)
-        late = [
-            pltpu.make_async_copy(ref, kv_ref.at[n // 2, n % 2], w_sems.at[2 + n])
-            for n, ref in enumerate(row_refs)
-        ]
-        waves = [[move] for move in own_moves] + [far_moves, late]
-        start([*loads, *waves[0]])
-        for copy in loads:
-            copy.wait()
-        for column in range(2):
-            if column:
-                start_next(waves, len(own_moves))
-            for r in range(tokens // step):
-                if not column:
-                    start_next(waves, r)
-                here = slice(r * step, (r + 1) * step)
-                total = None
-                for s in range(4):
-                    product = jnp.dot(
-                        x_ref[column, here, s * shard : (s + 1) * shard],
-                        jnp.concatenate([w_ref[0, s], w_ref[1, s]], axis=1),
-                        preferred_element_type=jnp.float32,
-                    )
-                    total = product if total is None else total + product
-                for h in range(2):
-                    lanes = pl.ds(pl.multiple_of(at_ref[2 + h] * head_dim, 128), head_dim)
-                    value = total[:, h * head_dim : (h + 1) * head_dim] + b_ref[0:1, lanes]
-                    q_ref[h, column, here, :] = normed(value, g_ref[0:1, :]).astype(jnp.bfloat16)
-        for copy in late:
+        copies = [pltpu.make_async_copy(query_ref, q_ref, sems.at[4])]
+        for n, ref in enumerate(row_refs):
+            copies.append(pltpu.make_async_copy(ref, kv_ref.at[n // 2, n % 2], sems.at[n]))
+        start(copies)
+        for copy in copies:
             copy.wait()
 
         @pl.loop(0, 2)
@@ -379,11 +367,12 @@
                     total = jnp.zeros((tile, 128), jnp.float32)
                     mixed = jnp.zeros((tile, head_dim), jnp.float32)
                     for other in range(2):
-                        limits_ref = (limit0_ref, limit1_ref)[column]
-                        seen = [limits_ref[i, (other ^ column) * tiles + t] for t in range(tiles)]
-                        total, mixed = column_step(
-                            query, kv_ref.at[h, other], tile, head_dim, seen, total, mixed
-                        )
+                        for t in range(tiles):
+                            limit = (limit0_ref, limit1_ref)[column][i, (other ^ column) * tiles + t]
+                            total, mixed = column_step(
+                                query, kv_ref.at[h, other, t * tile : (t + 1) * tile], tile,
+                                head_dim, [limit], total, mixed,
+                            )
 
                     @pl.when(is_edge)
                     def _():
@@ -401,7 +390,7 @@
     shape = (2, tokens, head_dim)
     return pl.pallas_call(
         kernel,
-        in_specs=[smem] * 3 + [hbm] * (1 + len(arrays) + 6) + [pl.BlockSpec()] * 2,
+        in_specs=[smem] * 3 + [hbm] * 5,
         out_specs=[pl.BlockSpec()] * 4,
         out_shape=[
             jax.ShapeDtypeStruct(shape, jnp.bfloat16),
@@ -410,17 +399,14 @@
             jax.ShapeDtypeStruct((2, tokens, 128), jnp.float32),
         ],
         scratch_shapes=[
-            pltpu.VMEM((2, tokens, width), jnp.bfloat16),
-            pltpu.VMEM((2, 4, shard, head_dim), jnp.bfloat16),
             pltpu.VMEM((2, 2, tokens, head_dim), jnp.bfloat16),
             pltpu.VMEM((2, 2, tokens, 2 * head_dim), jnp.bfloat16),
-            pltpu.SemaphoreType.DMA((moves,)),
-            pltpu.SemaphoreType.DMA((6,)),
+            pltpu.SemaphoreType.DMA((5,)),
         ],
         compiler_params=pltpu.CompilerParams(vmem_limit_bytes=WHOLE),
         cost_estimate=COST,
         name="attend_pair",
-    )(at, *limits, own, *arrays, *weights, *rows, bias, gain)
+    )(at, *limits, queries, *rows)
 
 
 def attend_halo(at, h, limits, query, halo, done, mixed, total):
@@ -556,17 +542,17 @@
         kept = arrive(got[which])
         return kept, to("groups", kept[0], 1)
 
+    near0, far0 = take(0)
+    two_mine, two_twin = swap(0)
+    near1, far1 = take(1)
     (q_sent[0],) = line.after(q_sent[0])
     q_got = lax.all_to_all(q_sent[0], "seq", split_axis=0, concat_axis=0, tiled=True)
     line.drop(q_sent)
-    near0, far0 = take(0)
-    two_mine, two_twin = swap(0)
-    near1, far1 = take(1)
+    far0, core0 = spread(near0, far0)
     three_mine, three_twin = swap(1)
     one_mine, one_twin = swap(2)
     (w,) = line.after(w)
     own_kv = [same, line.reached(*cut_heads(at, w, [((TWIN,), (1, 2))], SPACE))[0]]
-    far0, core0 = spread(near0, far0)
     two_twin = arrive(two_twin)
     three_twin = arrive(three_twin)
     far1, core1 = spread(near1, far1)
@@ -574,10 +560,10 @@
     q_twin = to("groups", q_mine[0], 1)
     w_mine = [own_kv[0], one_mine, two_mine, three_mine]
 
-    def kv(head, boxes, own, pieces, own_rows=None):
+    def kv(head, boxes, own, pieces, own_rows=None, query_weights=()):
         (boxes[0][0],) = line.after(boxes[0][0])
         weights = [box[0] for box in boxes]
-        return keys_values(at, head, own, pieces, weights, b_qkv, qk_gain, own_rows)
+        return keys_values(at, head, own, pieces, weights, b_qkv, qk_gain, own_rows, query_weights)
 
     own_mine = line.reached(*kv(MINE, w_mine, own_x[0][0], None))[0]
     (own_limit[0][0],) = line.after(own_limit[0][0])
@@ -600,19 +586,15 @@
     far, edge = kv(MINE, w_mine, None, column_arrays()[1], own_mine[0])
     rows_mine, halo_mine = [own_mine, *line.reached(far)], to("seq", edge, 2)
     one_twin = arrive(one_twin)
+    q_twin = arrive(q_twin)
     w_twin = [own_kv[1], one_twin, two_twin, three_twin]
-    own, far, edge = kv(TWIN, w_twin, *column_arrays())
+    own, far, edge, queries = kv(TWIN, w_twin, *column_arrays(), None, (q_mine[0], q_twin[0]))
     rows_twin, halo_twin = line.reached(own, far), to("seq", edge, 2)
-    line.drop(*w_mine, *w_twin)
+    line.drop(*w_mine, *w_twin, q_mine, q_twin, *own_x, *(box for box, _ in pieces))
     limits = own_limit + [arrive(far_limit)]
-    q_twin = arrive(q_twin)
-    parts = line.reached(
-        *attend_pair(
-            at, [b[0] for b in limits], *column_arrays(), [q_mine[0], q_twin[0]], b_qkv, qk_gain,
-            [b[0] for b in (*rows_mine, *rows_twin)],
-        )
-    )
-    line.drop(q_mine, q_twin, *own_x, *(box for box, _ in pieces), *rows_mine, *rows_twin)
+    rows = [b[0] for b in (*rows_mine, *rows_twin)]
+    parts = line.reached(*attend_pair(at, [b[0] for b in limits], queries, rows))
+    line.drop(*rows_mine, *rows_twin)
 
     def finish(h, halo):
         (halo,) = line.after(halo)

time: 147 us -> 155 us (1.054)
  waiting for transfers between devices: 34.6 us -> 51.6 us
  Pallas kernels: 71.2 us -> 65.1 us
  local copies, waits for them, and re-layouts: 6.74 us -> 4.77 us
    ppermute x18, waiting for transfers between devices: 34.6 us -> 47.8 us  [to(): lax.ppermute(value, axis, [(i, i ^ bit) for i in range(lax.axis_size(axis...]
    pallas_call x1, Pallas kernels: 20.7 us -> 12.5 us  [attend_pair(): pl.pallas_call(kernel, in_specs=[smem] * 3 + [hbm] * 5, out_specs=[pl.Blo...]
    all_to_all x1, waiting for transfers between devices: 0.01 us -> 3.81 us  [per_device(): lax.all_to_all(q_sent[0], 'seq', split_axis=0, concat_axis=0, tiled=True)]
    pallas_call x3, Pallas kernels: 22.8 us -> 24.9 us  [keys_values(): pl.pallas_call(kernel, in_specs=[pl.BlockSpec(memory_space=pltpu.SMEM)] +...]
    unnamed x36 -> x34, local copies, waits for them, and re-layouts: 6.13 us -> 4.13 us
  transfers between devices with their start and end apart: 19 -> 19, of which waited for: 5 -> 9; matrix products, arithmetic and copies ran while one was open for 2% -> 2% of each run, Pallas kernels for 45% -> 35%
where the time goes in v12:
time: 155 us; the launch traced here: 154 us
  Pallas kernels  65.1 us (42%)
  waiting for transfers between devices  51.6 us (33%)
  starting transfers between devices  30 us (19%)
  local copies, waits for them, and re-layouts  4.77 us (3%)
  other arithmetic  2.44 us (2%)
    ppermute x18, waiting for transfers between devices, to(): lax.ppermute(value, axis, [(i, i ^ bit) for i in range(lax.axis_size(axis...  47.8 us
    ppermute x18, starting transfers between devices, to(): lax.ppermute(value, axis, [(i, i ^ bit) for i in range(lax.axis_size(axis...  26.5 us
    pallas_call x3, Pallas kernels, keys_values(): pl.pallas_call(kernel, in_specs=[pl.BlockSpec(memory_space=pltpu.SMEM)] +...  24.9 us
    pallas_call x1, Pallas kernels, attend_pair(): pl.pallas_call(kernel, in_specs=[smem] * 3 + [hbm] * 5, out_specs=[pl.Blo...  12.5 us
    pallas_call x3, Pallas kernels, normalize(): pl.pallas_call(norm_kernel, grid=(tokens // rows,), in_specs=[pl.BlockSpe...  12.1 us
    pallas_call x2, Pallas kernels, attend_halo(): pl.pallas_call(kernel, grid=(1,), in_specs=[smem] * 3 + [one, fixed(halo....  5.89 us
    unnamed x34, local copies, waits for them, and re-layouts  4.13 us
    all_to_all x1, waiting for transfers between devices, per_device(): lax.all_to_all(q_sent[0], 'seq', split_axis=0, concat_axis=0, tiled=True)  3.81 us
  transfers between devices with their start and end apart: 19, of which 9 were waited for; matrix products, arithmetic and copies ran while one was open for 2% of the time, Pallas kernels for 35%

profile of v12, /device:TPU:0, one launch (start us, length us, event | category | flops | bytes accessed | tf_op | source)
XLA Modules:
  0.0 154.1 jit_solution(6072654837147857607)
XLA Ops:
  0.0 0.6 stack.35.at_ref
  0.6 3.1 %take_rows.1 = (bf16[128,3072]{1,0:T(8,128)(2,1)}, bf16[64,3072]{1,0:T(8,128)(2,1)}) custom-call(s32[8]{0:T(128)} %stack.35.at_ref, bf16[768,3072]{1,0:T(8,128)(2,1)} %x_ref.2), custom_call_target="tpu_custom_call" | custom-call | flops 1048576 | bytes 1024 | tf_op jit(solution)/shard_map/take_rows/pallas_call | solution.py:329
  3.8 3.0 %collective-permute-start.2 = (bf16[128,3072]{1,0:T(8,128)(2,1)}, bf16[128,3072]{1,0:T(8,128)(2,1)}, u32[]{:S(2)}, u32[]{:S(2)}) collective-permute-start(bf16[128,3072]{1,0:T(8,128)(2,1)} %get-tuple-element.278), channel_id=1, source_target_pairs={{0,4},{4,0},{8,12},{12,8},{1,5},{5,1},{9,13},{13,9},{2,6},{6,2},{1... | collective-permute-start | bytes 2359304 | tf_op jit(solution)/shard_map/ppermute | solution.py:502
  6.8 1.8 %cut_heads.2 = (bf16[1,768,256]{2,1,0:T(8,128)(2,1)S(1)}, bf16[1,768,256]{2,1,0:T(8,128)(2,1)S(1)}, bf16[4,768,128]{2,1,0:T(8,128)(2,1)}) custom-call(s32[8]{0:T(128)S(1)} %copy-done.1, bf16[3,768,512]{2,1,0:T(8,128)(2,1)S(1)} %bitcast.9), custom_call_target="tpu_custom_call" | custom-call | flops 1048576 | bytes 1024 | tf_op jit(solution)/shard_map/cut_heads/pallas_call | solution.py:150
  8.6 1.4 see.1.limit0_ref
  9.9 7.3 %normalize.3.refs_0_ = bf16[768,3072]{1,0:T(8,128)(2,1)} custom-call(bf16[768,3072]{1,0:T(8,128)(2,1)} %x_ref.2, f32[2,3072]{1,0:T(2,128)} %mod_ref.2), custom_call_target="tpu_custom_call" | custom-call | flops 1048576 | bytes 1024 | tf_op jit(solution)/shard_map/normalize/pallas_call | solution.py:124
  17.3 7.4 %collective-permute-done.2.x_ref = bf16[128,3072]{1,0:T(8,128)(2,1)} collective-permute-done((bf16[128,3072]{1,0:T(8,128)(2,1)}, bf16[128,3072]{1,0:T(8,128)(2,1)}, u32[]{:S(2)}, u32[]{:S(2)}) %collective-permute-start.2) | collective-permute-done | bytes 786464 | tf_op jit(solution)/shard_map/ppermute | solution.py:502
  24.6 2.6 %normalize.4.refs_0_.refs_1_ = bf16[128,3072]{1,0:T(8,128)(2,1)} custom-call(bf16[128,3072]{1,0:T(8,128)(2,1)} %collective-permute-done.2.x_ref, f32[2,3072]{1,0:T(2,128)} %mod_ref.2), custom_call_target="tpu_custom_call" | custom-call | flops 1048576 | bytes 1024 | tf_op jit(solution)/shard_map/normalize/pallas_call | solution.py:124
  27.2 1.7 %collective-permute-start.5 = (bf16[128,3072]{1,0:T(8,128)(2,1)}, bf16[128,3072]{1,0:T(8,128)(2,1)}, u32[]{:S(2)}, u32[]{:S(2)}) collective-permute-start(bf16[128,3072]{1,0:T(8,128)(2,1)} %normalize.4.refs_0_.refs_1_), channel_id=1, source_target_pairs={{0,2},{2,0},{1,3},{3,1},{4,6},{6,4},{5,7},{7,5},{8,10},{10,8},{9,1... | collective-permute-start | bytes 2359304 | tf_op jit(solution)/shard_map/ppermute | solution.py:502
  28.9 2.6 %collective-permute-start.1 = (bf16[1,768,256]{2,1,0:T(8,128)(2,1)S(1)}, bf16[1,768,256]{2,1,0:T(8,128)(2,1)}, u32[]{:S(2)}, u32[]{:S(2)}) collective-permute-start(bf16[1,768,256]{2,1,0:T(8,128)(2,1)S(1)} %get-tuple-element.459.refs_1_.refs_6_), channel_id=1, source_target_pairs={{0,8},{4,12},{8,0},{12,4},{1,9},{5,13},{9,1},{13,5},{2,10},{6,14},... | collective-permute-start | bytes 1179656 | tf_op jit(solution)/shard_map/ppermute | solution.py:502
  31.5 1.6 %collective-permute-start = (bf16[64,3072]{1,0:T(8,128)(2,1)}, bf16[64,3072]{1,0:T(8,128)(2,1)S(1)}, u32[]{:S(2)}, u32[]{:S(2)}) collective-permute-start(bf16[64,3072]{1,0:T(8,128)(2,1)} %get-tuple-element.277), channel_id=1, source_target_pairs={{0,4},{4,0},{8,12},{12,8},{1,5},{5,1},{9,13},{13,9},{2,6},{6,2},{1... | collective-permute-start | bytes 1179656 | tf_op jit(solution)/shard_map/ppermute | solution.py:502
  33.1 0.2 collective-permute-start.4
  33.3 0.7 collective-permute-start.8
  34.0 21.6 %collective-permute-done.1.refs_3_.refs_8_ = bf16[1,768,256]{2,1,0:T(8,128)(2,1)} collective-permute-done((bf16[1,768,256]{2,1,0:T(8,128)(2,1)S(1)}, bf16[1,768,256]{2,1,0:T(8,128)(2,1)}, u32[]{:S(2)}, u32[]{:S(2)}) %collective-permute-start.1) | collective-permute-done | bytes 393248 | tf_op jit(solution)/shard_map/ppermute | solution.py:502
  55.5 1.5 collective-permute-start.7
  57.0 2.2 %collective-permute-done.x_ref = bf16[64,3072]{1,0:T(8,128)(2,1)S(1)} collective-permute-done((bf16[64,3072]{1,0:T(8,128)(2,1)}, bf16[64,3072]{1,0:T(8,128)(2,1)S(1)}, u32[]{:S(2)}, u32[]{:S(2)}) %collective-permute-start) | collective-permute-done | bytes 393248 | tf_op jit(solution)/shard_map/ppermute | solution.py:502
  59.2 0.7 copy-done.8
  60.0 2.1 %normalize.5.refs_3_.refs_4_ = bf16[64,3072]{1,0:T(8,128)(2,1)} custom-call(bf16[64,3072]{1,0:T(8,128)(2,1)} %copy-done.8, f32[2,3072]{1,0:T(2,128)} %mod_ref.2), custom_call_target="tpu_custom_call" | custom-call | flops 1048576 | bytes 1024 | tf_op jit(solution)/shard_map/normalize/pallas_call | solution.py:124
  62.1 0.8 collective-permute-start.3
  62.9 3.5 %all-to-all-start = ((bf16[4,768,128]{2,1,0:T(8,128)(2,1)}), bf16[4,768,128]{2,1,0:T(8,128)(2,1)S(1)}, u32[]{:S(2)}, u32[]{:S(2)}) async-start(bf16[4,768,128]{2,1,0:T(8,128)(2,1)} %get-tuple-element.306), calls=%async_computation | async-start | bytes 1572864 | tf_op jit(solution)/shard_map/all_to_all | solution.py:549
  66.5 1.3 collective-permute-start.6
  67.7 3.0 %collective-permute-done.8.refs_2_.refs_7_ = bf16[1,768,256]{2,1,0:T(8,128)(2,1)} collective-permute-done((bf16[1,768,256]{2,1,0:T(8,128)(2,1)S(1)}, bf16[1,768,256]{2,1,0:T(8,128)(2,1)}, u32[]{:S(2)}, u32[]{:S(2)}) %collective-permute-start.8) | collective-permute-done | bytes 393248 | tf_op jit(solution)/shard_map/ppermute | solution.py:502
  70.7 1.5 collective-permute-start.10
  72.2 0.6 cut_heads.3.refs_7_
  72.9 1.4 pad_maximum_fusion
  74.3 0.1 collective-permute-start.12
  74.4 1.8 %collective-permute-done.6.refs_10_ = bf16[1,768,256]{2,1,0:T(8,128)(2,1)S(1)} collective-permute-done((bf16[1,768,256]{2,1,0:T(8,128)(2,1)}, bf16[1,768,256]{2,1,0:T(8,128)(2,1)S(1)}, u32[]{:S(2)}, u32[]{:S(2)}) %collective-permute-start.6) | collective-permute-done | bytes 393248 | tf_op jit(solution)/shard_map/ppermute | solution.py:502
  76.2 0.7 copy-done.13
  76.9 1.0 pad_maximum_fusion.1
  78.0 3.8 %all-to-all-done.refs_11_ = bf16[4,768,128]{2,1,0:T(8,128)(2,1)S(1)} async-done(((bf16[4,768,128]{2,1,0:T(8,128)(2,1)}), bf16[4,768,128]{2,1,0:T(8,128)(2,1)S(1)}, u32[]{:S(2)}, u32[]{:S(2)}) %all-to-all-start) | async-done | bytes 786464 | tf_op jit(solution)/shard_map/all_to_all | solution.py:549
  81.8 1.5 collective-permute-start.9
  83.3 6.5 %keys_values.3.refs_12_.refs_0_ = bf16[768,256]{1,0:T(8,128)(2,1)} custom-call(s32[8]{0:T(128)} %stack.35.at_ref, bf16[768,3072]{1,0:T(8,128)(2,1)} %normalize.3.refs_0_, bf16[1,768,256]{2,1,0:T(8,128)(2,1)} %copy-done.3, bf16[1,768,256]{2,1,0:T(8,128)(2,1)} %collective-permute-done.8.refs_2_.refs_7_, ...), custom_call_target="tpu_custom_call" | custom-call | flops 68719476736 | bytes 1024 | tf_op jit(solution)/shard_map/keys_values/pallas_call | solution.py:298
  89.8 1.1 collective-permute-start.15
  91.0 6.4 %keys_values.4 = (bf16[768,256]{1,0:T(8,128)(2,1)}, bf16[768,256]{1,0:T(8,128)(2,1)}) custom-call(s32[8]{0:T(128)} %stack.35.at_ref, bf16[128,3072]{1,0:T(8,128)(2,1)} %normalize.4.refs_0_.refs_1_, bf16[128,3072]{1,0:T(8,128)(2,1)} %collective-permute-done.5.refs_1_.refs_2_, bf16[256,3072]{1,0:T(8,128)(2,1)} %collective-permute-done.12.refs_2_.refs_3_, ...), custom_call_target="tpu_custom_call" | custom-call | flops 68719476736 | bytes 1024 | tf_op jit(solution)/shard_map/keys_values/pallas_call | solution.py:298
  97.4 6.8 %collective-permute-start.14 = (bf16[768,256]{1,0:T(8,128)(2,1)}, bf16[768,256]{1,0:T(8,128)(2,1)S(1)}, u32[]{:S(2)}, u32[]{:S(2)}) collective-permute-start(bf16[768,256]{1,0:T(8,128)(2,1)} %get-tuple-element.513), channel_id=1, source_target_pairs={{0,8},{4,12},{8,0},{12,4},{1,9},{5,13},{9,1},{13,5},{2,10},{6,14},... | collective-permute-start | bytes 1179656 | tf_op jit(solution)/shard_map/ppermute | solution.py:502
  104.2 12.0 %keys_values.5 = (bf16[768,256]{1,0:T(8,128)(2,1)}, bf16[768,256]{1,0:T(8,128)(2,1)}, bf16[768,256]{1,0:T(8,128)(2,1)}, bf16[2,2,768,128]{3,2,1,0:T(8,128)(2,1)}) custom-call(s32[8]{0:T(128)} %stack.35.at_ref, bf16[768,3072]{1,0:T(8,128)(2,1)} %normalize.3.refs_0_, bf16[128,3072]{1,0:T(8,128)(2,1)} %normalize.4.refs_0_.refs_1_, ...), custom_call_target="tpu_custom_call" | custom-call | flops 68719476736 | bytes 1024 | tf_op jit(solution)/shard_map/keys_values/pallas_call | solution.py:298
  116.3 0.4 copy-done.12
  116.7 12.5 %attend_pair.1 = (bf16[2,768,128]{2,1,0:T(8,128)(2,1)}, bf16[2,768,128]{2,1,0:T(8,128)(2,1)}, f32[2,768,128]{2,1,0:T(8,128)}, f32[2,768,128]{2,1,0:T(8,128)}) custom-call(s32[8]{0:T(128)} %stack.35.at_ref, f32[2,128]{1,0:T(2,128)} %see.1.limit0_ref, f32[2,128]{1,0:T(2,128)} %copy-done.12, bf16[2,2,768,128]{3,2,1,0:T(8,128)(2,1)} %get-tuple-element.521.query_ref, ...), custom_call_target="tpu_custom_call" | custom-call | flops 1048576 | bytes 1024 | tf_op jit(solution)/shard_map/attend_pair/pallas_call | solution.py:391
  129.2 0.7 copy-done.14
  130.0 2.9 %attend_halo.2 = (bf16[768,128]{1,0:T(8,128)(2,1)}, bf16[768,128]{1,0:T(8,128)(2,1)}) custom-call(s32[8]{0:T(128)} %stack.35.at_ref, f32[2,128]{1,0:T(2,128)} %see.1.limit0_ref, f32[2,128]{1,0:T(2,128)} %copy-done.12, bf16[2,768,128]{2,1,0:T(8,128)(2,1)} %get-tuple-element.541.q_ref, bf16[768,256]{1,0:T(8,128)(2,1)} %copy-done.14, ...), custom_call_target="tpu_custom_call" | custom-call | flops 68719476736 | bytes 1024 | tf_op jit(solution)/shard_map/attend_halo/pallas_call | solution.py:436
  132.9 3.3 %collective-permute-done.13.halo_ref = bf16[768,256]{1,0:T(8,128)(2,1)S(1)} collective-permute-done((bf16[768,256]{1,0:T(8,128)(2,1)}, bf16[768,256]{1,0:T(8,128)(2,1)S(1)}, u32[]{:S(2)}, u32[]{:S(2)}) %collective-permute-start.13) | collective-permute-done | bytes 393248 | tf_op jit(solution)/shard_map/ppermute | solution.py:502
  136.2 0.7 copy-done.15
  136.9 3.0 %attend_halo.3 = (bf16[768,128]{1,0:T(8,128)(2,1)}, bf16[768,128]{1,0:T(8,128)(2,1)}) custom-call(s32[8]{0:T(128)} %stack.35.at_ref, f32[2,128]{1,0:T(2,128)} %see.1.limit0_ref, f32[2,128]{1,0:T(2,128)} %copy-done.12, bf16[2,768,128]{2,1,0:T(8,128)(2,1)} %get-tuple-element.541.q_ref, bf16[768,256]{1,0:T(8,128)(2,1)} %copy-done.15, ...), custom_call_target="tpu_custom_call" | custom-call | flops 68719476736 | bytes 1024 | tf_op jit(solution)/shard_map/attend_halo/pallas_call | solution.py:436
  139.9 2.0 %collective-permute-start.16 = (bf16[768,128]{1,0:T(8,128)(2,1)S(1)}, bf16[768,128]{1,0:T(8,128)(2,1)S(1)}, u32[]{:S(2)}, u32[]{:S(2)}) collective-permute-start(bf16[768,128]{1,0:T(8,128)(2,1)S(1)} %copy-done.16), channel_id=1, source_target_pairs={{0,4},{4,0},{8,12},{12,8},{1,5},{5,1},{9,13},{13,9},{2,6},{6,2},{1... | collective-permute-start | bytes 589832 | tf_op jit(solution)/shard_map/ppermute | solution.py:502
  141.9 6.0 %collective-permute-done.17.refs_3_ = bf16[768,128]{1,0:T(8,128)(2,1)S(1)} collective-permute-done((bf16[768,128]{1,0:T(8,128)(2,1)}, bf16[768,128]{1,0:T(8,128)(2,1)S(1)}, u32[]{:S(2)}, u32[]{:S(2)}) %collective-permute-start.17) | collective-permute-done | bytes 196640 | tf_op jit(solution)/shard_map/ppermute | solution.py:502
  147.9 2.6 %collective-permute-done.16.refs_2_ = bf16[768,128]{1,0:T(8,128)(2,1)S(1)} collective-permute-done((bf16[768,128]{1,0:T(8,128)(2,1)S(1)}, bf16[768,128]{1,0:T(8,128)(2,1)S(1)}, u32[]{:S(2)}, u32[]{:S(2)}) %collective-permute-start.16) | collective-permute-done | bytes 196640 | tf_op jit(solution)/shard_map/ppermute | solution.py:502
  150.5 0.7 copy-done.10
  151.2 2.9 %assemble.1 = bf16[768,512]{1,0:T(8,128)(2,1)} custom-call(s32[8]{0:T(128)} %stack.35.at_ref, bf16[768,128]{1,0:T(8,128)(2,1)} %get-tuple-element.538.refs_0_, bf16[768,128]{1,0:T(8,128)(2,1)} %get-tuple-element.546.refs_1_, bf16[768,128]{1,0:T(8,128)(2,1)} %copy-done.10, bf16[768,128]{1,0:T(8,128)(2,1)} %copy-done.9), custom_call_target="tpu_custom_call" | custom-call | flops 1048576 | bytes 1024 | tf_op jit(solution)/shard_map/assemble/pallas_call | solution.py:458
  (41 shorter events, 0.2 us)
Async XLA Ops:
  0.6 6.2 %copy-start = (bf16[768,3,512]{2,0,1:T(8,128)(2,1)S(1)}, bf16[768,3,512]{2,0,1:T(8,128)(2,1)}, u32[]{:S(2)}) copy-start(bf16[768,3,512]{2,0,1:T(8,128)(2,1)} %param.8) | copy-start | bytes 7077892
  0.6 6.2 %copy-start.1 = (s32[8]{0:T(128)S(1)}, s32[8]{0:T(128)}, u32[]{:S(2)}) copy-start(s32[8]{0:T(128)} %stack.35.at_ref) | copy-start | bytes 100
  3.8 20.9 %collective-permute-start.2 = (bf16[128,3072]{1,0:T(8,128)(2,1)}, bf16[128,3072]{1,0:T(8,128)(2,1)}, u32[]{:S(2)}, u32[]{:S(2)}) collective-permute-start(bf16[128,3072]{1,0:T(8,128)(2,1)} %get-tuple-element.278), channel_id=1, source_target_pairs={{0,4},{4,0},{8,12},{12,8},{1,5},{5,1},{9,13},{13,9},{2,6},{6,2},{1... | collective-permute-start | bytes 2359304 | tf_op jit(solution)/shard_map/ppermute | solution.py:502
  8.6 20.4 %copy-start.3 = (bf16[1,768,256]{2,1,0:T(8,128)(2,1)}, bf16[1,768,256]{2,1,0:T(8,128)(2,1)S(1)}, u32[]{:S(2)}) copy-start(bf16[1,768,256]{2,1,0:T(8,128)(2,1)S(1)} %get-tuple-element.459.refs_1_.refs_6_) | copy-start | bytes 1179652
  27.2 45.0 %copy-start.2 = (s32[8]{0:T(128)S(1)}, s32[8]{0:T(128)}, u32[]{:S(2)}) copy-start(s32[8]{0:T(128)} %stack.35.at_ref) | copy-start | bytes 100
  27.2 39.2 %collective-permute-start.5 = (bf16[128,3072]{1,0:T(8,128)(2,1)}, bf16[128,3072]{1,0:T(8,128)(2,1)}, u32[]{:S(2)}, u32[]{:S(2)}) collective-permute-start(bf16[128,3072]{1,0:T(8,128)(2,1)} %normalize.4.refs_0_.refs_1_), channel_id=1, source_target_pairs={{0,2},{2,0},{1,3},{3,1},{4,6},{6,4},{5,7},{7,5},{8,10},{10,8},{9,1... | collective-permute-start | bytes 2359304 | tf_op jit(solution)/shard_map/ppermute | solution.py:502
  28.9 26.6 %collective-permute-start.1 = (bf16[1,768,256]{2,1,0:T(8,128)(2,1)S(1)}, bf16[1,768,256]{2,1,0:T(8,128)(2,1)}, u32[]{:S(2)}, u32[]{:S(2)}) collective-permute-start(bf16[1,768,256]{2,1,0:T(8,128)(2,1)S(1)} %get-tuple-element.459.refs_1_.refs_6_), channel_id=1, source_target_pairs={{0,8},{4,12},{8,0},{12,4},{1,9},{5,13},{9,1},{13,5},{2,10},{6,14},... | collective-permute-start | bytes 1179656 | tf_op jit(solution)/shard_map/ppermute | solution.py:502
  31.5 27.7 %collective-permute-start = (bf16[64,3072]{1,0:T(8,128)(2,1)}, bf16[64,3072]{1,0:T(8,128)(2,1)S(1)}, u32[]{:S(2)}, u32[]{:S(2)}) collective-permute-start(bf16[64,3072]{1,0:T(8,128)(2,1)} %get-tuple-element.277), channel_id=1, source_target_pairs={{0,4},{4,0},{8,12},{12,8},{1,5},{5,1},{9,13},{13,9},{2,6},{6,2},{1... | collective-permute-start | bytes 1179656 | tf_op jit(solution)/shard_map/ppermute | solution.py:502
  33.1 33.4 %collective-permute-start.4 = (bf16[1,768,256]{2,1,0:T(8,128)(2,1)S(1)}, bf16[1,768,256]{2,1,0:T(8,128)(2,1)}, u32[]{:S(2)}, u32[]{:S(2)}) collective-permute-start(bf16[1,768,256]{2,1,0:T(8,128)(2,1)S(1)} %get-tuple-element.281), channel_id=1, source_target_pairs={{0,12},{4,8},{8,4},{12,0},{1,13},{5,9},{9,5},{13,1},{2,14},{6,10},... | collective-permute-start | bytes 1179656 | tf_op jit(solution)/shard_map/ppermute | solution.py:502
  33.3 37.4 %collective-permute-start.8 = (bf16[1,768,256]{2,1,0:T(8,128)(2,1)S(1)}, bf16[1,768,256]{2,1,0:T(8,128)(2,1)}, u32[]{:S(2)}, u32[]{:S(2)}) collective-permute-start(bf16[1,768,256]{2,1,0:T(8,128)(2,1)S(1)} %get-tuple-element.281), channel_id=1, source_target_pairs={{0,4},{4,0},{8,12},{12,8},{1,5},{5,1},{9,13},{13,9},{2,6},{6,2},{1... | collective-permute-start | bytes 1179656 | tf_op jit(solution)/shard_map/ppermute | solution.py:502
  55.5 17.4 %collective-permute-start.7 = (bf16[1,768,256]{2,1,0:T(8,128)(2,1)}, bf16[1,768,256]{2,1,0:T(8,128)(2,1)}, u32[]{:S(2)}, u32[]{:S(2)}) collective-permute-start(bf16[1,768,256]{2,1,0:T(8,128)(2,1)} %collective-permute-done.1.refs_3_.refs_8_), channel_id=1, source_target_pairs={{0,16},{16,0},{1,17},{17,1},{2,18},{18,2},{3,19},{19,3},{4,20},{20... | collective-permute-start | bytes 1179656 | tf_op jit(solution)/shard_map/ppermute | solution.py:502
  59.2 0.8 copy-start.8
  62.1 14.1 %collective-permute-start.3 = (bf16[64,3072]{1,0:T(8,128)(2,1)}, bf16[64,3072]{1,0:T(8,128)(2,1)}, u32[]{:S(2)}, u32[]{:S(2)}) collective-permute-start(bf16[64,3072]{1,0:T(8,128)(2,1)} %normalize.5.refs_3_.refs_4_), channel_id=1, source_target_pairs={{0,2},{2,0},{1,3},{3,1},{4,6},{6,4},{5,7},{7,5},{8,10},{10,8},{9,1... | collective-permute-start | bytes 1179656 | tf_op jit(solution)/shard_map/ppermute | solution.py:502
  62.9 18.8 %all-to-all-start = ((bf16[4,768,128]{2,1,0:T(8,128)(2,1)}), bf16[4,768,128]{2,1,0:T(8,128)(2,1)S(1)}, u32[]{:S(2)}, u32[]{:S(2)}) async-start(bf16[4,768,128]{2,1,0:T(8,128)(2,1)} %get-tuple-element.306), calls=%async_computation | async-start | bytes 1572864 | tf_op jit(solution)/shard_map/all_to_all | solution.py:549
  66.4 6.5 %copy-start.5 = (bf16[128,3072]{1,0:T(8,128)(2,1)S(1)}, bf16[128,3072]{1,0:T(8,128)(2,1)}, u32[]{:S(2)}) copy-start(bf16[128,3072]{1,0:T(8,128)(2,1)} %normalize.4.refs_0_.refs_1_) | copy-start | bytes 2359300
  66.5 9.7 %collective-permute-start.6 = (bf16[1,768,256]{2,1,0:T(8,128)(2,1)}, bf16[1,768,256]{2,1,0:T(8,128)(2,1)S(1)}, u32[]{:S(2)}, u32[]{:S(2)}) collective-permute-start(bf16[1,768,256]{2,1,0:T(8,128)(2,1)} %collective-permute-done.4.refs_4_.refs_9_), channel_id=1, source_target_pairs={{0,16},{16,0},{1,17},{17,1},{2,18},{18,2},{3,19},{19,3},{4,20},{20... | collective-permute-start | bytes 1179656 | tf_op jit(solution)/shard_map/ppermute | solution.py:502
  70.7 26.7 %collective-permute-start.10 = (bf16[1,768,256]{2,1,0:T(8,128)(2,1)}, bf16[1,768,256]{2,1,0:T(8,128)(2,1)}, u32[]{:S(2)}, u32[]{:S(2)}) collective-permute-start(bf16[1,768,256]{2,1,0:T(8,128)(2,1)} %collective-permute-done.8.refs_2_.refs_7_), channel_id=1, source_target_pairs={{0,16},{16,0},{1,17},{17,1},{2,18},{18,2},{3,19},{19,3},{4,20},{20... | collective-permute-start | bytes 1179656 | tf_op jit(solution)/shard_map/ppermute | solution.py:502
  72.9 1.4 copy-start.4
  72.9 4.0 %copy-start.6 = (bf16[64,3072]{1,0:T(8,128)(2,1)S(1)}, bf16[64,3072]{1,0:T(8,128)(2,1)}, u32[]{:S(2)}) copy-start(bf16[64,3072]{1,0:T(8,128)(2,1)} %normalize.5.refs_3_.refs_4_) | copy-start | bytes 1179652
  74.3 16.6 %collective-permute-start.12 = (bf16[256,3072]{1,0:T(8,128)(2,1)S(1)}, bf16[256,3072]{1,0:T(8,128)(2,1)}, u32[]{:S(2)}, u32[]{:S(2)}) collective-permute-start(bf16[256,3072]{1,0:T(8,128)(2,1)S(1)} %pad_maximum_fusion), channel_id=1, source_target_pairs={{0,1},{1,0},{2,3},{3,2},{4,5},{5,4},{6,7},{7,6},{8,9},{9,8},{10,11... | collective-permute-start | bytes 4718600 | tf_op jit(solution)/shard_map/ppermute | solution.py:502
  76.2 0.8 copy-start.13
  78.0 11.8 %copy-start.11 = (f32[2,128]{1,0:T(2,128)S(1)}, f32[2,128]{1,0:T(2,128)}, u32[]{:S(2)}) copy-start(f32[2,128]{1,0:T(2,128)} %see.1.limit0_ref) | copy-start | bytes 3076
  81.8 8.0 %copy-start.7 = (bf16[4,768,128]{2,1,0:T(8,128)(2,1)}, bf16[4,768,128]{2,1,0:T(8,128)(2,1)S(1)}, u32[]{:S(2)}) copy-start(bf16[4,768,128]{2,1,0:T(8,128)(2,1)S(1)} %all-to-all-done.refs_11_) | copy-start | bytes 2359300
  81.8 15.6 %collective-permute-start.9 = (bf16[4,768,128]{2,1,0:T(8,128)(2,1)S(1)}, bf16[4,768,128]{2,1,0:T(8,128)(2,1)}, u32[]{:S(2)}, u32[]{:S(2)}) collective-permute-start(bf16[4,768,128]{2,1,0:T(8,128)(2,1)S(1)} %all-to-all-done.refs_11_), channel_id=1, source_target_pairs={{0,16},{16,0},{1,17},{17,1},{2,18},{18,2},{3,19},{19,3},{4,20},{20... | collective-permute-start | bytes 2359304 | tf_op jit(solution)/shard_map/ppermute | solution.py:502
  83.3 7.7 %collective-permute-start.11 = (bf16[128,3072]{1,0:T(8,128)(2,1)S(1)}, bf16[128,3072]{1,0:T(8,128)(2,1)}, u32[]{:S(2)}, u32[]{:S(2)}) collective-permute-start(bf16[128,3072]{1,0:T(8,128)(2,1)S(1)} %pad_maximum_fusion.1), channel_id=1, source_target_pairs={{0,1},{1,0},{2,3},{3,2},{4,5},{5,4},{6,7},{7,6},{8,9},{9,8},{10,11... | collective-permute-start | bytes 2359304 | tf_op jit(solution)/shard_map/ppermute | solution.py:502
  89.8 26.4 %collective-permute-start.15 = (f32[2,128]{1,0:T(2,128)S(1)}, f32[2,128]{1,0:T(2,128)S(1)}, u32[]{:S(2)}, u32[]{:S(2)}) collective-permute-start(f32[2,128]{1,0:T(2,128)S(1)} %copy-done.11), channel_id=1, source_target_pairs={{0,4},{4,0},{8,12},{12,8},{1,5},{5,1},{9,13},{13,9},{2,6},{6,2},{1... | collective-permute-start | bytes 3080 | tf_op jit(solution)/shard_map/ppermute | solution.py:502
  97.4 31.8 %collective-permute-start.14 = (bf16[768,256]{1,0:T(8,128)(2,1)}, bf16[768,256]{1,0:T(8,128)(2,1)S(1)}, u32[]{:S(2)}, u32[]{:S(2)}) collective-permute-start(bf16[768,256]{1,0:T(8,128)(2,1)} %get-tuple-element.513), channel_id=1, source_target_pairs={{0,8},{4,12},{8,0},{12,4},{1,9},{5,13},{9,1},{13,5},{2,10},{6,14},... | collective-permute-start | bytes 1179656 | tf_op jit(solution)/shard_map/ppermute | solution.py:502
  116.2 0.5 copy-start.12
  116.2 20.0 %collective-permute-start.13 = (bf16[768,256]{1,0:T(8,128)(2,1)}, bf16[768,256]{1,0:T(8,128)(2,1)S(1)}, u32[]{:S(2)}, u32[]{:S(2)}) collective-permute-start(bf16[768,256]{1,0:T(8,128)(2,1)} %get-tuple-element.512), channel_id=1, source_target_pairs={{0,8},{4,12},{8,0},{12,4},{1,9},{5,13},{9,1},{13,5},{2,10},{6,14},... | collective-permute-start | bytes 1179656 | tf_op jit(solution)/shard_map/ppermute | solution.py:502
  129.2 0.7 copy-start.14
  136.2 0.7 copy-start.15
  136.9 3.0 %copy-start.16 = (bf16[768,128]{1,0:T(8,128)(2,1)S(1)}, bf16[768,128]{1,0:T(8,128)(2,1)}, u32[]{:S(2)}) copy-start(bf16[768,128]{1,0:T(8,128)(2,1)} %get-tuple-element.547) | copy-start | bytes 589828
  139.9 8.0 %collective-permute-start.17 = (bf16[768,128]{1,0:T(8,128)(2,1)}, bf16[768,128]{1,0:T(8,128)(2,1)S(1)}, u32[]{:S(2)}, u32[]{:S(2)}) collective-permute-start(bf16[768,128]{1,0:T(8,128)(2,1)} %get-tuple-element.548), channel_id=1, source_target_pairs={{0,4},{4,0},{8,12},{12,8},{1,5},{5,1},{9,13},{13,9},{2,6},{6,2},{1... | collective-permute-start | bytes 589832 | tf_op jit(solution)/shard_map/ppermute | solution.py:502
  139.9 10.7 %collective-permute-start.16 = (bf16[768,128]{1,0:T(8,128)(2,1)S(1)}, bf16[768,128]{1,0:T(8,128)(2,1)S(1)}, u32[]{:S(2)}, u32[]{:S(2)}) collective-permute-start(bf16[768,128]{1,0:T(8,128)(2,1)S(1)} %copy-done.16), channel_id=1, source_target_pairs={{0,4},{4,0},{8,12},{12,8},{1,5},{5,1},{9,13},{13,9},{2,6},{6,2},{1... | collective-permute-start | bytes 589832 | tf_op jit(solution)/shard_map/ppermute | solution.py:502
  147.9 2.6 %copy-start.9 = (bf16[768,128]{1,0:T(8,128)(2,1)}, bf16[768,128]{1,0:T(8,128)(2,1)S(1)}, u32[]{:S(2)}) copy-start(bf16[768,128]{1,0:T(8,128)(2,1)S(1)} %collective-permute-done.17.refs_3_) | copy-start | bytes 589828
  150.5 0.7 copy-start.10

commit v13 on v12

--- a/solution.py
+++ b/solution.py
@@ -542,17 +542,17 @@
         kept = arrive(got[which])
         return kept, to("groups", kept[0], 1)
 
+    (q_sent[0],) = line.after(q_sent[0])
+    q_got = lax.all_to_all(q_sent[0], "seq", split_axis=0, concat_axis=0, tiled=True)
+    line.drop(q_sent)
     near0, far0 = take(0)
     two_mine, two_twin = swap(0)
     near1, far1 = take(1)
-    (q_sent[0],) = line.after(q_sent[0])
-    q_got = lax.all_to_all(q_sent[0], "seq", split_axis=0, concat_axis=0, tiled=True)
-    line.drop(q_sent)
-    far0, core0 = spread(near0, far0)
     three_mine, three_twin = swap(1)
     one_mine, one_twin = swap(2)
     (w,) = line.after(w)
     own_kv = [same, line.reached(*cut_heads(at, w, [((TWIN,), (1, 2))], SPACE))[0]]
+    far0, core0 = spread(near0, far0)
     two_twin = arrive(two_twin)
     three_twin = arrive(three_twin)
     far1, core1 = spread(near1, far1)

time: 155 us -> 148 us (0.955)
  waiting for transfers between devices: 51.6 us -> 47.4 us
  starting transfers between devices: 30 us -> 27.6 us
    all_to_all x1, waiting for transfers between devices: 3.81 us -> 0.01 us  [per_device(): lax.all_to_all(q_sent[0], 'seq', split_axis=0, concat_axis=0, tiled=True)]
    ppermute x18, starting transfers between devices: 26.5 us -> 23.4 us  [to(): lax.ppermute(value, axis, [(i, i ^ bit) for i in range(lax.axis_size(axis...]
    unnamed x34 -> x36, local copies, waits for them, and re-layouts: 4.13 us -> 5.28 us
  transfers between devices with their start and end apart: 19 -> 19, of which waited for: 9 -> 7; matrix products, arithmetic and copies ran while one was open for 2% -> 1% of each run, Pallas kernels for 35% -> 38%
where the time goes in v13:
time: 148 us
  Pallas kernels  65.1 us (44%)
  waiting for transfers between devices  47.4 us (32%)
  starting transfers between devices  27.6 us (19%)
  local copies, waits for them, and re-layouts  5.95 us (4%)
    ppermute x18, waiting for transfers between devices, to(): lax.ppermute(value, axis, [(i, i ^ bit) for i in range(lax.axis_size(axis...  47.4 us
    pallas_call x3, Pallas kernels, keys_values(): pl.pallas_call(kernel, in_specs=[pl.BlockSpec(memory_space=pltpu.SMEM)] +...  24.9 us
    ppermute x18, starting transfers between devices, to(): lax.ppermute(value, axis, [(i, i ^ bit) for i in range(lax.axis_size(axis...  23.4 us
    pallas_call x1, Pallas kernels, attend_pair(): pl.pallas_call(kernel, in_specs=[smem] * 3 + [hbm] * 5, out_specs=[pl.Blo...  12.5 us
    pallas_call x3, Pallas kernels, normalize(): pl.pallas_call(norm_kernel, grid=(tokens // rows,), in_specs=[pl.BlockSpe...  12.1 us
    pallas_call x2, Pallas kernels, attend_halo(): pl.pallas_call(kernel, grid=(1,), in_specs=[smem] * 3 + [one, fixed(halo....  5.91 us
    unnamed x36, local copies, waits for them, and re-layouts  5.28 us
    all_to_all x1, starting transfers between devices, per_device(): lax.all_to_all(q_sent[0], 'seq', split_axis=0, concat_axis=0, tiled=True)  4.19 us
  transfers between devices with their start and end apart: 19, of which 7 were waited for; matrix products, arithmetic and copies ran while one was open for 1% of the time, Pallas kernels for 38%

profile of v13, /device:TPU:0, one launch (start us, length us, event | category | flops | bytes accessed | tf_op | source)
XLA Modules:
  0.0 147.6 jit_solution(9092216081681663095)
XLA Ops:
  0.0 0.7 stack.35.at_ref
  0.7 3.1 %take_rows.1 = (bf16[128,3072]{1,0:T(8,128)(2,1)}, bf16[64,3072]{1,0:T(8,128)(2,1)}) custom-call(s32[8]{0:T(128)} %stack.35.at_ref, bf16[768,3072]{1,0:T(8,128)(2,1)} %x_ref.2), custom_call_target="tpu_custom_call" | custom-call | flops 1048576 | bytes 1024 | tf_op jit(solution)/shard_map/take_rows/pallas_call | solution.py:329
  3.8 3.0 %collective-permute-start.2 = (bf16[128,3072]{1,0:T(8,128)(2,1)}, bf16[128,3072]{1,0:T(8,128)(2,1)}, u32[]{:S(2)}, u32[]{:S(2)}) collective-permute-start(bf16[128,3072]{1,0:T(8,128)(2,1)} %get-tuple-element.271), channel_id=1, source_target_pairs={{0,4},{4,0},{8,12},{12,8},{1,5},{5,1},{9,13},{13,9},{2,6},{6,2},{1... | collective-permute-start | bytes 2359304 | tf_op jit(solution)/shard_map/ppermute | solution.py:502
  6.8 1.8 %cut_heads.2 = (bf16[1,768,256]{2,1,0:T(8,128)(2,1)S(1)}, bf16[1,768,256]{2,1,0:T(8,128)(2,1)S(1)}, bf16[4,768,128]{2,1,0:T(8,128)(2,1)}) custom-call(s32[8]{0:T(128)S(1)} %copy-done.1, bf16[3,768,512]{2,1,0:T(8,128)(2,1)S(1)} %bitcast.9), custom_call_target="tpu_custom_call" | custom-call | flops 1048576 | bytes 1024 | tf_op jit(solution)/shard_map/cut_heads/pallas_call | solution.py:150
  8.6 2.6 %collective-permute-start.1 = (bf16[1,768,256]{2,1,0:T(8,128)(2,1)S(1)}, bf16[1,768,256]{2,1,0:T(8,128)(2,1)}, u32[]{:S(2)}, u32[]{:S(2)}) collective-permute-start(bf16[1,768,256]{2,1,0:T(8,128)(2,1)S(1)} %get-tuple-element.447.refs_1_.refs_6_), channel_id=1, source_target_pairs={{0,8},{4,12},{8,0},{12,4},{1,9},{5,13},{9,1},{13,5},{2,10},{6,14},... | collective-permute-start | bytes 1179656 | tf_op jit(solution)/shard_map/ppermute | solution.py:502
  11.2 0.4 collective-permute-start
  11.6 1.3 collective-permute-start.4
  13.0 0.2 collective-permute-start.8
  13.2 1.3 see.1.limit0_ref
  14.5 7.3 %normalize.3.refs_0_ = bf16[768,3072]{1,0:T(8,128)(2,1)} custom-call(bf16[768,3072]{1,0:T(8,128)(2,1)} %x_ref.2, f32[2,3072]{1,0:T(2,128)} %mod_ref.2), custom_call_target="tpu_custom_call" | custom-call | flops 1048576 | bytes 1024 | tf_op jit(solution)/shard_map/normalize/pallas_call | solution.py:124
  21.9 4.2 %all-to-all-start = ((bf16[4,768,128]{2,1,0:T(8,128)(2,1)}), bf16[4,768,128]{2,1,0:T(8,128)(2,1)}, u32[]{:S(2)}, u32[]{:S(2)}) async-start(bf16[4,768,128]{2,1,0:T(8,128)(2,1)} %get-tuple-element.282), calls=%async_computation | async-start | bytes 1572864 | tf_op jit(solution)/shard_map/all_to_all | solution.py:546
  26.1 7.9 %collective-permute-done.2.x_ref = bf16[128,3072]{1,0:T(8,128)(2,1)} collective-permute-done((bf16[128,3072]{1,0:T(8,128)(2,1)}, bf16[128,3072]{1,0:T(8,128)(2,1)}, u32[]{:S(2)}, u32[]{:S(2)}) %collective-permute-start.2) | collective-permute-done | bytes 786464 | tf_op jit(solution)/shard_map/ppermute | solution.py:502
  33.9 2.6 %normalize.4.refs_0_.refs_1_ = bf16[128,3072]{1,0:T(8,128)(2,1)} custom-call(bf16[128,3072]{1,0:T(8,128)(2,1)} %collective-permute-done.2.x_ref, f32[2,3072]{1,0:T(2,128)} %mod_ref.2), custom_call_target="tpu_custom_call" | custom-call | flops 1048576 | bytes 1024 | tf_op jit(solution)/shard_map/normalize/pallas_call | solution.py:124
  36.5 2.0 %collective-permute-start.7 = (bf16[128,3072]{1,0:T(8,128)(2,1)}, bf16[128,3072]{1,0:T(8,128)(2,1)}, u32[]{:S(2)}, u32[]{:S(2)}) collective-permute-start(bf16[128,3072]{1,0:T(8,128)(2,1)} %normalize.4.refs_0_.refs_1_), channel_id=1, source_target_pairs={{0,2},{2,0},{1,3},{3,1},{4,6},{6,4},{5,7},{7,5},{8,10},{10,8},{9,1... | collective-permute-start | bytes 2359304 | tf_op jit(solution)/shard_map/ppermute | solution.py:502
  38.5 1.5 %collective-permute-start.6 = (bf16[1,768,256]{2,1,0:T(8,128)(2,1)}, bf16[1,768,256]{2,1,0:T(8,128)(2,1)}, u32[]{:S(2)}, u32[]{:S(2)}) collective-permute-start(bf16[1,768,256]{2,1,0:T(8,128)(2,1)} %collective-permute-done.1.refs_3_.refs_8_), channel_id=1, source_target_pairs={{0,16},{16,0},{1,17},{17,1},{2,18},{18,2},{3,19},{19,3},{4,20},{20... | collective-permute-start | bytes 1179656 | tf_op jit(solution)/shard_map/ppermute | solution.py:502
  40.0 14.9 %collective-permute-done.x_ref = bf16[64,3072]{1,0:T(8,128)(2,1)S(1)} collective-permute-done((bf16[64,3072]{1,0:T(8,128)(2,1)}, bf16[64,3072]{1,0:T(8,128)(2,1)S(1)}, u32[]{:S(2)}, u32[]{:S(2)}) %collective-permute-start) | collective-permute-done | bytes 393248 | tf_op jit(solution)/shard_map/ppermute | solution.py:502
  54.9 0.8 copy-done.7
  55.7 2.1 %normalize.5.refs_3_.refs_4_ = bf16[64,3072]{1,0:T(8,128)(2,1)} custom-call(bf16[64,3072]{1,0:T(8,128)(2,1)} %copy-done.7, f32[2,3072]{1,0:T(2,128)} %mod_ref.2), custom_call_target="tpu_custom_call" | custom-call | flops 1048576 | bytes 1024 | tf_op jit(solution)/shard_map/normalize/pallas_call | solution.py:124
  57.8 2.0 %collective-permute-start.3 = (bf16[64,3072]{1,0:T(8,128)(2,1)}, bf16[64,3072]{1,0:T(8,128)(2,1)S(1)}, u32[]{:S(2)}, u32[]{:S(2)}) collective-permute-start(bf16[64,3072]{1,0:T(8,128)(2,1)} %normalize.5.refs_3_.refs_4_), channel_id=1, source_target_pairs={{0,2},{2,0},{1,3},{3,1},{4,6},{6,4},{5,7},{7,5},{8,10},{10,8},{9,1... | collective-permute-start | bytes 1179656 | tf_op jit(solution)/shard_map/ppermute | solution.py:502
  59.8 1.5 %collective-permute-start.5 = (bf16[1,768,256]{2,1,0:T(8,128)(2,1)}, bf16[1,768,256]{2,1,0:T(8,128)(2,1)S(1)}, u32[]{:S(2)}, u32[]{:S(2)}) collective-permute-start(bf16[1,768,256]{2,1,0:T(8,128)(2,1)} %collective-permute-done.4.refs_4_.refs_9_), channel_id=1, source_target_pairs={{0,16},{16,0},{1,17},{17,1},{2,18},{18,2},{3,19},{19,3},{4,20},{20... | collective-permute-start | bytes 1179656 | tf_op jit(solution)/shard_map/ppermute | solution.py:502
  61.3 6.4 %collective-permute-done.8.refs_2_.refs_7_ = bf16[1,768,256]{2,1,0:T(8,128)(2,1)} collective-permute-done((bf16[1,768,256]{2,1,0:T(8,128)(2,1)S(1)}, bf16[1,768,256]{2,1,0:T(8,128)(2,1)}, u32[]{:S(2)}, u32[]{:S(2)}) %collective-permute-start.8) | collective-permute-done | bytes 393248 | tf_op jit(solution)/shard_map/ppermute | solution.py:502
  67.7 2.0 %collective-permute-start.10 = (bf16[1,768,256]{2,1,0:T(8,128)(2,1)}, bf16[1,768,256]{2,1,0:T(8,128)(2,1)}, u32[]{:S(2)}, u32[]{:S(2)}) collective-permute-start(bf16[1,768,256]{2,1,0:T(8,128)(2,1)} %collective-permute-done.8.refs_2_.refs_7_), channel_id=1, source_target_pairs={{0,16},{16,0},{1,17},{17,1},{2,18},{18,2},{3,19},{19,3},{4,20},{20... | collective-permute-start | bytes 1179656 | tf_op jit(solution)/shard_map/ppermute | solution.py:502
  69.7 0.6 cut_heads.3.refs_7_
  70.3 0.7 copy-done.4
  71.2 0.6 copy-done.14
  71.8 0.6 copy-done.5
  72.4 1.2 pad_maximum_fusion
  73.7 0.1 collective-permute-start.9
  73.9 0.5 collective-permute-start.11
  74.4 6.5 %keys_values.3.refs_12_.refs_0_ = bf16[768,256]{1,0:T(8,128)(2,1)} custom-call(s32[8]{0:T(128)} %stack.35.at_ref, bf16[768,3072]{1,0:T(8,128)(2,1)} %normalize.3.refs_0_, bf16[1,768,256]{2,1,0:T(8,128)(2,1)} %copy-done.3, bf16[1,768,256]{2,1,0:T(8,128)(2,1)} %collective-permute-done.8.refs_2_.refs_7_, ...), custom_call_target="tpu_custom_call" | custom-call | flops 68719476736 | bytes 1024 | tf_op jit(solution)/shard_map/keys_values/pallas_call | solution.py:298
  80.9 1.6 %collective-permute-start.15 = (f32[2,128]{1,0:T(2,128)S(1)}, f32[2,128]{1,0:T(2,128)S(1)}, u32[]{:S(2)}, u32[]{:S(2)}) collective-permute-start(f32[2,128]{1,0:T(2,128)S(1)} %copy-done.11), channel_id=1, source_target_pairs={{0,4},{4,0},{8,12},{12,8},{1,5},{5,1},{9,13},{13,9},{2,6},{6,2},{1... | collective-permute-start | bytes 3080 | tf_op jit(solution)/shard_map/ppermute | solution.py:502
  82.4 6.4 %keys_values.4 = (bf16[768,256]{1,0:T(8,128)(2,1)}, bf16[768,256]{1,0:T(8,128)(2,1)}) custom-call(s32[8]{0:T(128)} %stack.35.at_ref, bf16[128,3072]{1,0:T(8,128)(2,1)} %normalize.4.refs_0_.refs_1_, bf16[128,3072]{1,0:T(8,128)(2,1)} %collective-permute-done.7.refs_1_.refs_2_, bf16[256,3072]{1,0:T(8,128)(2,1)} %collective-permute-done.12.refs_2_.refs_3_, ...), custom_call_target="tpu_custom_call" | custom-call | flops 68719476736 | bytes 1024 | tf_op jit(solution)/shard_map/keys_values/pallas_call | solution.py:298
  88.9 5.3 %collective-permute-done.9.refs_12_ = bf16[4,768,128]{2,1,0:T(8,128)(2,1)S(1)} collective-permute-done((bf16[4,768,128]{2,1,0:T(8,128)(2,1)}, bf16[4,768,128]{2,1,0:T(8,128)(2,1)S(1)}, u32[]{:S(2)}, u32[]{:S(2)}) %collective-permute-start.9) | collective-permute-done | bytes 786464 | tf_op jit(solution)/shard_map/ppermute | solution.py:502
  94.2 0.7 collective-permute-start.14
  94.8 0.2 copy-done.13
  95.1 12.0 %keys_values.5 = (bf16[768,256]{1,0:T(8,128)(2,1)}, bf16[768,256]{1,0:T(8,128)(2,1)}, bf16[768,256]{1,0:T(8,128)(2,1)}, bf16[2,2,768,128]{3,2,1,0:T(8,128)(2,1)}) custom-call(s32[8]{0:T(128)} %stack.35.at_ref, bf16[768,3072]{1,0:T(8,128)(2,1)} %normalize.3.refs_0_, bf16[128,3072]{1,0:T(8,128)(2,1)} %normalize.4.refs_0_.refs_1_, ...), custom_call_target="tpu_custom_call" | custom-call | flops 68719476736 | bytes 1024 | tf_op jit(solution)/shard_map/keys_values/pallas_call | solution.py:298
  107.1 1.9 %collective-permute-start.13 = (bf16[768,256]{1,0:T(8,128)(2,1)}, bf16[768,256]{1,0:T(8,128)(2,1)S(1)}, u32[]{:S(2)}, u32[]{:S(2)}) collective-permute-start(bf16[768,256]{1,0:T(8,128)(2,1)} %get-tuple-element.500), channel_id=1, source_target_pairs={{0,8},{4,12},{8,0},{12,4},{1,9},{5,13},{9,1},{13,5},{2,10},{6,14},... | collective-permute-start | bytes 1179656 | tf_op jit(solution)/shard_map/ppermute | solution.py:502
  109.0 12.5 %attend_pair.1 = (bf16[2,768,128]{2,1,0:T(8,128)(2,1)}, bf16[2,768,128]{2,1,0:T(8,128)(2,1)}, f32[2,768,128]{2,1,0:T(8,128)}, f32[2,768,128]{2,1,0:T(8,128)}) custom-call(s32[8]{0:T(128)} %stack.35.at_ref, f32[2,128]{1,0:T(2,128)} %see.1.limit0_ref, f32[2,128]{1,0:T(2,128)} %copy-done.12, bf16[2,2,768,128]{3,2,1,0:T(8,128)(2,1)} %get-tuple-element.509.query_ref, ...), custom_call_target="tpu_custom_call" | custom-call | flops 1048576 | bytes 1024 | tf_op jit(solution)/shard_map/attend_pair/pallas_call | solution.py:391
  121.6 0.8 copy-done.15
  122.3 2.9 %attend_halo.2 = (bf16[768,128]{1,0:T(8,128)(2,1)}, bf16[768,128]{1,0:T(8,128)(2,1)}) custom-call(s32[8]{0:T(128)} %stack.35.at_ref, f32[2,128]{1,0:T(2,128)} %see.1.limit0_ref, f32[2,128]{1,0:T(2,128)} %copy-done.12, bf16[2,768,128]{2,1,0:T(8,128)(2,1)} %get-tuple-element.529.q_ref, bf16[768,256]{1,0:T(8,128)(2,1)} %copy-done.15, ...), custom_call_target="tpu_custom_call" | custom-call | flops 68719476736 | bytes 1024 | tf_op jit(solution)/shard_map/attend_halo/pallas_call | solution.py:436
  125.3 3.8 %collective-permute-done.13.halo_ref = bf16[768,256]{1,0:T(8,128)(2,1)S(1)} collective-permute-done((bf16[768,256]{1,0:T(8,128)(2,1)}, bf16[768,256]{1,0:T(8,128)(2,1)S(1)}, u32[]{:S(2)}, u32[]{:S(2)}) %collective-permute-start.13) | collective-permute-done | bytes 393248 | tf_op jit(solution)/shard_map/ppermute | solution.py:502
  129.0 0.8 copy-done.16
  129.8 3.0 %attend_halo.3 = (bf16[768,128]{1,0:T(8,128)(2,1)}, bf16[768,128]{1,0:T(8,128)(2,1)}) custom-call(s32[8]{0:T(128)} %stack.35.at_ref, f32[2,128]{1,0:T(2,128)} %see.1.limit0_ref, f32[2,128]{1,0:T(2,128)} %copy-done.12, bf16[2,768,128]{2,1,0:T(8,128)(2,1)} %get-tuple-element.529.q_ref, bf16[768,256]{1,0:T(8,128)(2,1)} %copy-done.16, ...), custom_call_target="tpu_custom_call" | custom-call | flops 68719476736 | bytes 1024 | tf_op jit(solution)/shard_map/attend_halo/pallas_call | solution.py:436
  132.8 2.0 %collective-permute-start.16 = (bf16[768,128]{1,0:T(8,128)(2,1)S(1)}, bf16[768,128]{1,0:T(8,128)(2,1)S(1)}, u32[]{:S(2)}, u32[]{:S(2)}) collective-permute-start(bf16[768,128]{1,0:T(8,128)(2,1)S(1)} %copy-done.17), channel_id=1, source_target_pairs={{0,4},{4,0},{8,12},{12,8},{1,5},{5,1},{9,13},{13,9},{2,6},{6,2},{1... | collective-permute-start | bytes 589832 | tf_op jit(solution)/shard_map/ppermute | solution.py:502
  134.8 5.9 %collective-permute-done.17.refs_3_ = bf16[768,128]{1,0:T(8,128)(2,1)S(1)} collective-permute-done((bf16[768,128]{1,0:T(8,128)(2,1)}, bf16[768,128]{1,0:T(8,128)(2,1)S(1)}, u32[]{:S(2)}, u32[]{:S(2)}) %collective-permute-start.17) | collective-permute-done | bytes 196640 | tf_op jit(solution)/shard_map/ppermute | solution.py:502
  140.7 3.3 %collective-permute-done.16.refs_2_ = bf16[768,128]{1,0:T(8,128)(2,1)S(1)} collective-permute-done((bf16[768,128]{1,0:T(8,128)(2,1)S(1)}, bf16[768,128]{1,0:T(8,128)(2,1)S(1)}, u32[]{:S(2)}, u32[]{:S(2)}) %collective-permute-start.16) | collective-permute-done | bytes 196640 | tf_op jit(solution)/shard_map/ppermute | solution.py:502
  144.0 0.7 copy-done.10
  144.7 2.9 %assemble.1 = bf16[768,512]{1,0:T(8,128)(2,1)} custom-call(s32[8]{0:T(128)} %stack.35.at_ref, bf16[768,128]{1,0:T(8,128)(2,1)} %get-tuple-element.526.refs_0_, bf16[768,128]{1,0:T(8,128)(2,1)} %get-tuple-element.534.refs_1_, bf16[768,128]{1,0:T(8,128)(2,1)} %copy-done.10, bf16[768,128]{1,0:T(8,128)(2,1)} %copy-done.9), custom_call_target="tpu_custom_call" | custom-call | flops 1048576 | bytes 1024 | tf_op jit(solution)/shard_map/assemble/pallas_call | solution.py:458
  (43 shorter events, 0.2 us)
Async XLA Ops:
  0.7 6.2 %copy-start = (bf16[768,3,512]{2,0,1:T(8,128)(2,1)S(1)}, bf16[768,3,512]{2,0,1:T(8,128)(2,1)}, u32[]{:S(2)}) copy-start(bf16[768,3,512]{2,0,1:T(8,128)(2,1)} %param.8) | copy-start | bytes 7077892
  0.7 6.2 %copy-start.1 = (s32[8]{0:T(128)S(1)}, s32[8]{0:T(128)}, u32[]{:S(2)}) copy-start(s32[8]{0:T(128)} %stack.35.at_ref) | copy-start | bytes 100
  3.8 30.1 %collective-permute-start.2 = (bf16[128,3072]{1,0:T(8,128)(2,1)}, bf16[128,3072]{1,0:T(8,128)(2,1)}, u32[]{:S(2)}, u32[]{:S(2)}) collective-permute-start(bf16[128,3072]{1,0:T(8,128)(2,1)} %get-tuple-element.271), channel_id=1, source_target_pairs={{0,4},{4,0},{8,12},{12,8},{1,5},{5,1},{9,13},{13,9},{2,6},{6,2},{1... | collective-permute-start | bytes 2359304 | tf_op jit(solution)/shard_map/ppermute | solution.py:502
  8.6 13.3 %copy-start.3 = (bf16[1,768,256]{2,1,0:T(8,128)(2,1)}, bf16[1,768,256]{2,1,0:T(8,128)(2,1)S(1)}, u32[]{:S(2)}) copy-start(bf16[1,768,256]{2,1,0:T(8,128)(2,1)S(1)} %get-tuple-element.447.refs_1_.refs_6_) | copy-start | bytes 1179652
  8.6 29.9 %collective-permute-start.1 = (bf16[1,768,256]{2,1,0:T(8,128)(2,1)S(1)}, bf16[1,768,256]{2,1,0:T(8,128)(2,1)}, u32[]{:S(2)}, u32[]{:S(2)}) collective-permute-start(bf16[1,768,256]{2,1,0:T(8,128)(2,1)S(1)} %get-tuple-element.447.refs_1_.refs_6_), channel_id=1, source_target_pairs={{0,8},{4,12},{8,0},{12,4},{1,9},{5,13},{9,1},{13,5},{2,10},{6,14},... | collective-permute-start | bytes 1179656 | tf_op jit(solution)/shard_map/ppermute | solution.py:502
  11.2 43.7 %collective-permute-start = (bf16[64,3072]{1,0:T(8,128)(2,1)}, bf16[64,3072]{1,0:T(8,128)(2,1)S(1)}, u32[]{:S(2)}, u32[]{:S(2)}) collective-permute-start(bf16[64,3072]{1,0:T(8,128)(2,1)} %get-tuple-element.272), channel_id=1, source_target_pairs={{0,4},{4,0},{8,12},{12,8},{1,5},{5,1},{9,13},{13,9},{2,6},{6,2},{1... | collective-permute-start | bytes 1179656 | tf_op jit(solution)/shard_map/ppermute | solution.py:502
  11.6 48.1 %collective-permute-start.4 = (bf16[1,768,256]{2,1,0:T(8,128)(2,1)S(1)}, bf16[1,768,256]{2,1,0:T(8,128)(2,1)}, u32[]{:S(2)}, u32[]{:S(2)}) collective-permute-start(bf16[1,768,256]{2,1,0:T(8,128)(2,1)S(1)} %get-tuple-element.275), channel_id=1, source_target_pairs={{0,12},{4,8},{8,4},{12,0},{1,13},{5,9},{9,5},{13,1},{2,14},{6,10},... | collective-permute-start | bytes 1179656 | tf_op jit(solution)/shard_map/ppermute | solution.py:502
  13.0 54.7 %collective-permute-start.8 = (bf16[1,768,256]{2,1,0:T(8,128)(2,1)S(1)}, bf16[1,768,256]{2,1,0:T(8,128)(2,1)}, u32[]{:S(2)}, u32[]{:S(2)}) collective-permute-start(bf16[1,768,256]{2,1,0:T(8,128)(2,1)S(1)} %get-tuple-element.275), channel_id=1, source_target_pairs={{0,4},{4,0},{8,12},{12,8},{1,5},{5,1},{9,13},{13,9},{2,6},{6,2},{1... | collective-permute-start | bytes 1179656 | tf_op jit(solution)/shard_map/ppermute | solution.py:502
  21.9 51.8 %all-to-all-start = ((bf16[4,768,128]{2,1,0:T(8,128)(2,1)}), bf16[4,768,128]{2,1,0:T(8,128)(2,1)}, u32[]{:S(2)}, u32[]{:S(2)}) async-start(bf16[4,768,128]{2,1,0:T(8,128)(2,1)} %get-tuple-element.282), calls=%async_computation | async-start | bytes 1572864 | tf_op jit(solution)/shard_map/all_to_all | solution.py:546
  26.1 43.6 %copy-start.2 = (s32[8]{0:T(128)S(1)}, s32[8]{0:T(128)}, u32[]{:S(2)}) copy-start(s32[8]{0:T(128)} %stack.35.at_ref) | copy-start | bytes 100
  36.5 34.5 %collective-permute-start.7 = (bf16[128,3072]{1,0:T(8,128)(2,1)}, bf16[128,3072]{1,0:T(8,128)(2,1)}, u32[]{:S(2)}, u32[]{:S(2)}) collective-permute-start(bf16[128,3072]{1,0:T(8,128)(2,1)} %normalize.4.refs_0_.refs_1_), channel_id=1, source_target_pairs={{0,2},{2,0},{1,3},{3,1},{4,6},{6,4},{5,7},{7,5},{8,10},{10,8},{9,1... | collective-permute-start | bytes 2359304 | tf_op jit(solution)/shard_map/ppermute | solution.py:502
  38.5 32.5 %collective-permute-start.6 = (bf16[1,768,256]{2,1,0:T(8,128)(2,1)}, bf16[1,768,256]{2,1,0:T(8,128)(2,1)}, u32[]{:S(2)}, u32[]{:S(2)}) collective-permute-start(bf16[1,768,256]{2,1,0:T(8,128)(2,1)} %collective-permute-done.1.refs_3_.refs_8_), channel_id=1, source_target_pairs={{0,16},{16,0},{1,17},{17,1},{2,18},{18,2},{3,19},{19,3},{4,20},{20... | collective-permute-start | bytes 1179656 | tf_op jit(solution)/shard_map/ppermute | solution.py:502
  54.9 0.8 copy-start.7
  57.8 13.3 %copy-start.6 = (bf16[64,3072]{1,0:T(8,128)(2,1)S(1)}, bf16[64,3072]{1,0:T(8,128)(2,1)}, u32[]{:S(2)}) copy-start(bf16[64,3072]{1,0:T(8,128)(2,1)} %normalize.5.refs_3_.refs_4_) | copy-start | bytes 1179652
  57.8 13.3 %collective-permute-start.3 = (bf16[64,3072]{1,0:T(8,128)(2,1)}, bf16[64,3072]{1,0:T(8,128)(2,1)S(1)}, u32[]{:S(2)}, u32[]{:S(2)}) collective-permute-start(bf16[64,3072]{1,0:T(8,128)(2,1)} %normalize.5.refs_3_.refs_4_), channel_id=1, source_target_pairs={{0,2},{2,0},{1,3},{3,1},{4,6},{6,4},{5,7},{7,5},{8,10},{10,8},{9,1... | collective-permute-start | bytes 1179656 | tf_op jit(solution)/shard_map/ppermute | solution.py:502
  59.8 11.3 %collective-permute-start.5 = (bf16[1,768,256]{2,1,0:T(8,128)(2,1)}, bf16[1,768,256]{2,1,0:T(8,128)(2,1)S(1)}, u32[]{:S(2)}, u32[]{:S(2)}) collective-permute-start(bf16[1,768,256]{2,1,0:T(8,128)(2,1)} %collective-permute-done.4.refs_4_.refs_9_), channel_id=1, source_target_pairs={{0,16},{16,0},{1,17},{17,1},{2,18},{18,2},{3,19},{19,3},{4,20},{20... | collective-permute-start | bytes 1179656 | tf_op jit(solution)/shard_map/ppermute | solution.py:502
  67.7 21.2 %collective-permute-start.10 = (bf16[1,768,256]{2,1,0:T(8,128)(2,1)}, bf16[1,768,256]{2,1,0:T(8,128)(2,1)}, u32[]{:S(2)}, u32[]{:S(2)}) collective-permute-start(bf16[1,768,256]{2,1,0:T(8,128)(2,1)} %collective-permute-done.8.refs_2_.refs_7_), channel_id=1, source_target_pairs={{0,16},{16,0},{1,17},{17,1},{2,18},{18,2},{3,19},{19,3},{4,20},{20... | collective-permute-start | bytes 1179656 | tf_op jit(solution)/shard_map/ppermute | solution.py:502
  70.3 0.7 copy-start.4
  71.0 1.4 copy-start.5
  71.0 0.7 copy-start.14
  71.1 2.6 %copy-start.8 = (bf16[64,3072]{1,0:T(8,128)(2,1)}, bf16[64,3072]{1,0:T(8,128)(2,1)S(1)}, u32[]{:S(2)}) copy-start(bf16[64,3072]{1,0:T(8,128)(2,1)S(1)} %collective-permute-done.3.refs_4_.refs_5_) | copy-start | bytes 1179652
  73.7 7.2 %copy-start.11 = (f32[2,128]{1,0:T(2,128)S(1)}, f32[2,128]{1,0:T(2,128)}, u32[]{:S(2)}) copy-start(f32[2,128]{1,0:T(2,128)} %see.1.limit0_ref) | copy-start | bytes 3076
  73.7 20.5 %collective-permute-start.9 = (bf16[4,768,128]{2,1,0:T(8,128)(2,1)}, bf16[4,768,128]{2,1,0:T(8,128)(2,1)S(1)}, u32[]{:S(2)}, u32[]{:S(2)}) collective-permute-start(bf16[4,768,128]{2,1,0:T(8,128)(2,1)} %all-to-all-done.refs_11_), channel_id=1, source_target_pairs={{0,16},{16,0},{1,17},{17,1},{2,18},{18,2},{3,19},{19,3},{4,20},{20... | collective-permute-start | bytes 2359304 | tf_op jit(solution)/shard_map/ppermute | solution.py:502
  73.8 8.6 %collective-permute-start.12 = (bf16[256,3072]{1,0:T(8,128)(2,1)S(1)}, bf16[256,3072]{1,0:T(8,128)(2,1)}, u32[]{:S(2)}, u32[]{:S(2)}) collective-permute-start(bf16[256,3072]{1,0:T(8,128)(2,1)S(1)} %pad_maximum_fusion), channel_id=1, source_target_pairs={{0,1},{1,0},{2,3},{3,2},{4,5},{5,4},{6,7},{7,6},{8,9},{9,8},{10,11... | collective-permute-start | bytes 4718600 | tf_op jit(solution)/shard_map/ppermute | solution.py:502
  73.9 8.6 %collective-permute-start.11 = (bf16[128,3072]{1,0:T(8,128)(2,1)S(1)}, bf16[128,3072]{1,0:T(8,128)(2,1)}, u32[]{:S(2)}, u32[]{:S(2)}) collective-permute-start(bf16[128,3072]{1,0:T(8,128)(2,1)S(1)} %pad_maximum_fusion.1), channel_id=1, source_target_pairs={{0,1},{1,0},{2,3},{3,2},{4,5},{5,4},{6,7},{7,6},{8,9},{9,8},{10,11... | collective-permute-start | bytes 2359304 | tf_op jit(solution)/shard_map/ppermute | solution.py:502
  80.9 26.2 %collective-permute-start.15 = (f32[2,128]{1,0:T(2,128)S(1)}, f32[2,128]{1,0:T(2,128)S(1)}, u32[]{:S(2)}, u32[]{:S(2)}) collective-permute-start(f32[2,128]{1,0:T(2,128)S(1)} %copy-done.11), channel_id=1, source_target_pairs={{0,4},{4,0},{8,12},{12,8},{1,5},{5,1},{9,13},{13,9},{2,6},{6,2},{1... | collective-permute-start | bytes 3080 | tf_op jit(solution)/shard_map/ppermute | solution.py:502
  94.2 0.9 copy-start.13
  94.2 27.4 %collective-permute-start.14 = (bf16[768,256]{1,0:T(8,128)(2,1)}, bf16[768,256]{1,0:T(8,128)(2,1)S(1)}, u32[]{:S(2)}, u32[]{:S(2)}) collective-permute-start(bf16[768,256]{1,0:T(8,128)(2,1)} %get-tuple-element.501), channel_id=1, source_target_pairs={{0,8},{4,12},{8,0},{12,4},{1,9},{5,13},{9,1},{13,5},{2,10},{6,14},... | collective-permute-start | bytes 1179656 | tf_op jit(solution)/shard_map/ppermute | solution.py:502
  107.1 1.9 %copy-start.12 = (f32[2,128]{1,0:T(2,128)}, f32[2,128]{1,0:T(2,128)S(1)}, u32[]{:S(2)}) copy-start(f32[2,128]{1,0:T(2,128)S(1)} %collective-permute-done.15.limit1_ref) | copy-start | bytes 3076
  107.1 21.9 %collective-permute-start.13 = (bf16[768,256]{1,0:T(8,128)(2,1)}, bf16[768,256]{1,0:T(8,128)(2,1)S(1)}, u32[]{:S(2)}, u32[]{:S(2)}) collective-permute-start(bf16[768,256]{1,0:T(8,128)(2,1)} %get-tuple-element.500), channel_id=1, source_target_pairs={{0,8},{4,12},{8,0},{12,4},{1,9},{5,13},{9,1},{13,5},{2,10},{6,14},... | collective-permute-start | bytes 1179656 | tf_op jit(solution)/shard_map/ppermute | solution.py:502
  121.5 0.8 copy-start.15
  129.0 0.8 copy-start.16
  129.8 3.0 %copy-start.17 = (bf16[768,128]{1,0:T(8,128)(2,1)S(1)}, bf16[768,128]{1,0:T(8,128)(2,1)}, u32[]{:S(2)}) copy-start(bf16[768,128]{1,0:T(8,128)(2,1)} %get-tuple-element.535) | copy-start | bytes 589828
  132.8 8.0 %collective-permute-start.17 = (bf16[768,128]{1,0:T(8,128)(2,1)}, bf16[768,128]{1,0:T(8,128)(2,1)S(1)}, u32[]{:S(2)}, u32[]{:S(2)}) collective-permute-start(bf16[768,128]{1,0:T(8,128)(2,1)} %get-tuple-element.536), channel_id=1, source_target_pairs={{0,4},{4,0},{8,12},{12,8},{1,5},{5,1},{9,13},{13,9},{2,6},{6,2},{1... | collective-permute-start | bytes 589832 | tf_op jit(solution)/shard_map/ppermute | solution.py:502
  132.8 11.2 %collective-permute-start.16 = (bf16[768,128]{1,0:T(8,128)(2,1)S(1)}, bf16[768,128]{1,0:T(8,128)(2,1)S(1)}, u32[]{:S(2)}, u32[]{:S(2)}) collective-permute-start(bf16[768,128]{1,0:T(8,128)(2,1)S(1)} %copy-done.17), channel_id=1, source_target_pairs={{0,4},{4,0},{8,12},{12,8},{1,5},{5,1},{9,13},{13,9},{2,6},{6,2},{1... | collective-permute-start | bytes 589832 | tf_op jit(solution)/shard_map/ppermute | solution.py:502
  140.7 3.3 %copy-start.9 = (bf16[768,128]{1,0:T(8,128)(2,1)}, bf16[768,128]{1,0:T(8,128)(2,1)S(1)}, u32[]{:S(2)}) copy-start(bf16[768,128]{1,0:T(8,128)(2,1)S(1)} %collective-permute-done.17.refs_3_) | copy-start | bytes 589828
  144.0 0.7 copy-start.10

commit v14 on v11

--- a/solution.py
+++ b/solution.py
@@ -379,11 +379,12 @@
                     total = jnp.zeros((tile, 128), jnp.float32)
                     mixed = jnp.zeros((tile, head_dim), jnp.float32)
                     for other in range(2):
-                        limits_ref = (limit0_ref, limit1_ref)[column]
-                        seen = [limits_ref[i, (other ^ column) * tiles + t] for t in range(tiles)]
-                        total, mixed = column_step(
-                            query, kv_ref.at[h, other], tile, head_dim, seen, total, mixed
-                        )
+                        for t in range(tiles):
+                            limit = (limit0_ref, limit1_ref)[column][i, (other ^ column) * tiles + t]
+                            total, mixed = column_step(
+                                query, kv_ref.at[h, other, t * tile : (t + 1) * tile], tile,
+                                head_dim, [limit], total, mixed,
+                            )
 
                     @pl.when(is_edge)
                     def _():
@@ -549,29 +550,27 @@
 
     def spread(near, far):
         far = arrive(far)
-        both = jnp.concatenate([near[0], far[0]], axis=0)
-        return far, to("head", both, 1)
+        (near[0],) = line.after(near[0])
+        return far, to("head", near[0], 1), to("head", far[0], 1)
 
     def swap(which):
         kept = arrive(got[which])
         return kept, to("groups", kept[0], 1)
 
+    near0, far0 = take(0)
+    two_mine, two_twin = swap(0)
+    near1, far1 = take(1)
     (q_sent[0],) = line.after(q_sent[0])
     q_got = lax.all_to_all(q_sent[0], "seq", split_axis=0, concat_axis=0, tiled=True)
     line.drop(q_sent)
-    near0, far0 = take(0)
-    two_mine, two_twin = swap(0)
-    near1, far1 = take(1)
     three_mine, three_twin = swap(1)
     one_mine, one_twin = swap(2)
     (w,) = line.after(w)
     own_kv = [same, line.reached(*cut_heads(at, w, [((TWIN,), (1, 2))], SPACE))[0]]
-    far0, core0 = spread(near0, far0)
+    far0, core0, core2 = spread(near0, far0)
     two_twin = arrive(two_twin)
     three_twin = arrive(three_twin)
-    far1, core1 = spread(near1, far1)
-    q_mine = arrive(q_got)
-    q_twin = to("groups", q_mine[0], 1)
+    far1, core1, core3 = spread(near1, far1)
     w_mine = [own_kv[0], one_mine, two_mine, three_mine]
 
     def kv(head, boxes, own, pieces, own_rows=None):
@@ -582,16 +581,17 @@
     own_mine = line.reached(*kv(MINE, w_mine, own_x[0][0], None))[0]
     (own_limit[0][0],) = line.after(own_limit[0][0])
     far_limit = to("seq", own_limit[0][0], 1)
-    core0 = arrive(core0)
-    core1 = arrive(core1)
+    core0, core1, core2, core3 = (arrive(core) for core in (core0, core1, core2, core3))
     n0, n1 = cutting[1], quarter - cutting[1]
     pieces = [
         (near0, [(0, 0, 0, n0)]),
         (far0, [(2, 0, 0, n0)]),
-        (core0, [(1, 0, 0, n0), (3, 0, n0, n0)]),
+        (core0, [(1, 0, 0, n0)]),
+        (core2, [(3, 0, 0, n0)]),
         (near1, [(0, n0, 0, n1)]),
         (far1, [(2, n0, 0, n1)]),
-        (core1, [(1, n0, 0, n1), (3, n0, n1, n1)]),
+        (core1, [(1, n0, 0, n1)]),
+        (core3, [(3, n0, 0, n1)]),
     ]
 
     def column_arrays():
@@ -599,6 +599,8 @@
 
     far, edge = kv(MINE, w_mine, None, column_arrays()[1], own_mine[0])
     rows_mine, halo_mine = [own_mine, *line.reached(far)], to("seq", edge, 2)
+    q_mine = arrive(q_got)
+    q_twin = to("groups", q_mine[0], 1)
     one_twin = arrive(one_twin)
     w_twin = [own_kv[1], one_twin, two_twin, three_twin]
     own, far, edge = kv(TWIN, w_twin, *column_arrays())

time: 147 us -> 143 us (0.973)
  other arithmetic: 3.35 us -> 0 us
    concatenate x2 -> x0, other arithmetic: 3.35 us -> none  [spread(): both = jnp.concatenate([near[0], far[0]], axis=0)]
    ppermute x18 -> x20, waiting for transfers between devices: 34.6 us -> 35.1 us  [to(): lax.ppermute(value, axis, [(i, i ^ bit) for i in range(lax.axis_size(axis...]
    ppermute x18 -> x20, starting transfers between devices: 25.6 us -> 25.2 us  [to(): lax.ppermute(value, axis, [(i, i ^ bit) for i in range(lax.axis_size(axis...]
    unnamed x36 -> x40, local copies, waits for them, and re-layouts: 6.13 us -> 6 us
  transfers between devices with their start and end apart: 19 -> 21, of which waited for: 5 -> 7; matrix products, arithmetic and copies ran while one was open for 2% -> 0% of each run, Pallas kernels for 45% -> 45%
where the time goes in v14:
time: 143 us; the launch traced here: 142 us
  Pallas kernels  69.9 us (49%)
  waiting for transfers between devices  35.1 us (25%)
  starting transfers between devices  30 us (21%)
  local copies, waits for them, and re-layouts  6.57 us (5%)
    ppermute x20, waiting for transfers between devices, to(): lax.ppermute(value, axis, [(i, i ^ bit) for i in range(lax.axis_size(axis...  35.1 us
    ppermute x20, starting transfers between devices, to(): lax.ppermute(value, axis, [(i, i ^ bit) for i in range(lax.axis_size(axis...  25.2 us
    pallas_call x3, Pallas kernels, keys_values(): pl.pallas_call(kernel, in_specs=[pl.BlockSpec(memory_space=pltpu.SMEM)] +...  22.8 us
    pallas_call x1, Pallas kernels, attend_pair(): pl.pallas_call(kernel, in_specs=[smem] * 3 + [hbm] * (1 + len(arrays) + 6...  19.4 us
    pallas_call x3, Pallas kernels, normalize(): pl.pallas_call(norm_kernel, grid=(tokens // rows,), in_specs=[pl.BlockSpe...  12 us
    unnamed x40, local copies, waits for them, and re-layouts  6 us
    pallas_call x2, Pallas kernels, attend_halo(): pl.pallas_call(kernel, grid=(1,), in_specs=[smem] * 3 + [one, fixed(halo....  5.92 us
    all_to_all x1, starting transfers between devices, per_device(): lax.all_to_all(q_sent[0], 'seq', split_axis=0, concat_axis=0, tiled=True)  4.87 us
  transfers between devices with their start and end apart: 21, of which 7 were waited for; matrix products, arithmetic and copies ran while one was open for 0% of the time, Pallas kernels for 45%

profile of v14, /device:TPU:0, one launch (start us, length us, event | category | flops | bytes accessed | tf_op | source)
XLA Modules:
  0.0 141.8 jit_solution(12102177271266206219)
XLA Ops:
  0.0 0.6 stack.35.at_ref
  0.6 3.1 %take_rows.1 = (bf16[128,3072]{1,0:T(8,128)(2,1)}, bf16[64,3072]{1,0:T(8,128)(2,1)}) custom-call(s32[8]{0:T(128)} %stack.35.at_ref, bf16[768,3072]{1,0:T(8,128)(2,1)} %x_ref.2), custom_call_target="tpu_custom_call" | custom-call | flops 1048576 | bytes 1024 | tf_op jit(solution)/shard_map/take_rows/pallas_call | solution.py:306
  3.7 3.0 %collective-permute-start.4 = (bf16[128,3072]{1,0:T(8,128)(2,1)}, bf16[128,3072]{1,0:T(8,128)(2,1)}, u32[]{:S(2)}, u32[]{:S(2)}) collective-permute-start(bf16[128,3072]{1,0:T(8,128)(2,1)} %get-tuple-element.356), channel_id=1, source_target_pairs={{0,4},{4,0},{8,12},{12,8},{1,5},{5,1},{9,13},{13,9},{2,6},{6,2},{1... | collective-permute-start | bytes 2359304 | tf_op jit(solution)/shard_map/ppermute | solution.py:517
  6.7 1.7 %cut_heads.2 = (bf16[1,768,256]{2,1,0:T(8,128)(2,1)S(1)}, bf16[1,768,256]{2,1,0:T(8,128)(2,1)S(1)}, bf16[4,768,128]{2,1,0:T(8,128)(2,1)}) custom-call(s32[8]{0:T(128)S(1)} %copy-done.1, bf16[3,768,512]{2,1,0:T(8,128)(2,1)S(1)} %bitcast.9), custom_call_target="tpu_custom_call" | custom-call | flops 1048576 | bytes 1024 | tf_op jit(solution)/shard_map/cut_heads/pallas_call | solution.py:150
  8.4 2.6 %collective-permute-start.3 = (bf16[1,768,256]{2,1,0:T(8,128)(2,1)S(1)}, bf16[1,768,256]{2,1,0:T(8,128)(2,1)}, u32[]{:S(2)}, u32[]{:S(2)}) collective-permute-start(bf16[1,768,256]{2,1,0:T(8,128)(2,1)S(1)} %get-tuple-element.578.refs_1_.refs_8_), channel_id=1, source_target_pairs={{0,8},{4,12},{8,0},{12,4},{1,9},{5,13},{9,1},{13,5},{2,10},{6,14},... | collective-permute-start | bytes 1179656 | tf_op jit(solution)/shard_map/ppermute | solution.py:517
  11.0 0.4 collective-permute-start.2
  11.5 1.3 collective-permute-start.1
  13.0 1.3 see.1.limit0_ref
  14.4 7.3 %normalize.3.refs_0_.own_ref = bf16[768,3072]{1,0:T(8,128)(2,1)} custom-call(bf16[768,3072]{1,0:T(8,128)(2,1)} %x_ref.2, f32[2,3072]{1,0:T(2,128)} %mod_ref.2), custom_call_target="tpu_custom_call" | custom-call | flops 1048576 | bytes 1024 | tf_op jit(solution)/shard_map/normalize/pallas_call | solution.py:124
  21.7 12.1 %collective-permute-done.4.x_ref = bf16[128,3072]{1,0:T(8,128)(2,1)} collective-permute-done((bf16[128,3072]{1,0:T(8,128)(2,1)}, bf16[128,3072]{1,0:T(8,128)(2,1)}, u32[]{:S(2)}, u32[]{:S(2)}) %collective-permute-start.4) | collective-permute-done | bytes 786464 | tf_op jit(solution)/shard_map/ppermute | solution.py:517
  33.8 2.6 %normalize.4.refs_0_.refs_1_ = bf16[128,3072]{1,0:T(8,128)(2,1)} custom-call(bf16[128,3072]{1,0:T(8,128)(2,1)} %collective-permute-done.4.x_ref, f32[2,3072]{1,0:T(2,128)} %mod_ref.2), custom_call_target="tpu_custom_call" | custom-call | flops 1048576 | bytes 1024 | tf_op jit(solution)/shard_map/normalize/pallas_call | solution.py:124
  36.4 2.0 %collective-permute-start.9 = (bf16[128,3072]{1,0:T(8,128)(2,1)}, bf16[128,3072]{1,0:T(8,128)(2,1)}, u32[]{:S(2)}, u32[]{:S(2)}) collective-permute-start(bf16[128,3072]{1,0:T(8,128)(2,1)} %normalize.4.refs_0_.refs_1_), channel_id=1, source_target_pairs={{0,2},{2,0},{1,3},{3,1},{4,6},{6,4},{5,7},{7,5},{8,10},{10,8},{9,1... | collective-permute-start | bytes 2359304 | tf_op jit(solution)/shard_map/ppermute | solution.py:517
  38.4 1.5 %collective-permute-start.8 = (bf16[1,768,256]{2,1,0:T(8,128)(2,1)}, bf16[1,768,256]{2,1,0:T(8,128)(2,1)}, u32[]{:S(2)}, u32[]{:S(2)}) collective-permute-start(bf16[1,768,256]{2,1,0:T(8,128)(2,1)} %collective-permute-done.3.refs_3_.refs_10_), channel_id=1, source_target_pairs={{0,16},{16,0},{1,17},{17,1},{2,18},{18,2},{3,19},{19,3},{4,20},{20... | collective-permute-start | bytes 1179656 | tf_op jit(solution)/shard_map/ppermute | solution.py:517
  39.9 2.2 %collective-permute-done.2.x_ref = bf16[64,3072]{1,0:T(8,128)(2,1)S(1)} collective-permute-done((bf16[64,3072]{1,0:T(8,128)(2,1)}, bf16[64,3072]{1,0:T(8,128)(2,1)S(1)}, u32[]{:S(2)}, u32[]{:S(2)}) %collective-permute-start.2) | collective-permute-done | bytes 393248 | tf_op jit(solution)/shard_map/ppermute | solution.py:517
  42.2 0.8 copy-done.13
  42.9 2.1 %normalize.5.refs_4_.refs_5_ = bf16[64,3072]{1,0:T(8,128)(2,1)} custom-call(bf16[64,3072]{1,0:T(8,128)(2,1)} %copy-done.13, f32[2,3072]{1,0:T(2,128)} %mod_ref.2), custom_call_target="tpu_custom_call" | custom-call | flops 1048576 | bytes 1024 | tf_op jit(solution)/shard_map/normalize/pallas_call | solution.py:124
  45.0 2.2 %collective-permute-start.6 = (bf16[64,3072]{1,0:T(8,128)(2,1)}, bf16[64,3072]{1,0:T(8,128)(2,1)S(1)}, u32[]{:S(2)}, u32[]{:S(2)}) collective-permute-start(bf16[64,3072]{1,0:T(8,128)(2,1)} %normalize.5.refs_4_.refs_5_), channel_id=1, source_target_pairs={{0,2},{2,0},{1,3},{3,1},{4,6},{6,4},{5,7},{7,5},{8,10},{10,8},{9,1... | collective-permute-start | bytes 1179656 | tf_op jit(solution)/shard_map/ppermute | solution.py:517
  47.2 6.0 %collective-permute-done.1.refs_4_.refs_11_ = bf16[1,768,256]{2,1,0:T(8,128)(2,1)} collective-permute-done((bf16[1,768,256]{2,1,0:T(8,128)(2,1)S(1)}, bf16[1,768,256]{2,1,0:T(8,128)(2,1)}, u32[]{:S(2)}, u32[]{:S(2)}) %collective-permute-start.1) | collective-permute-done | bytes 393248 | tf_op jit(solution)/shard_map/ppermute | solution.py:517
  53.2 1.5 %collective-permute-start.7 = (bf16[1,768,256]{2,1,0:T(8,128)(2,1)}, bf16[1,768,256]{2,1,0:T(8,128)(2,1)}, u32[]{:S(2)}, u32[]{:S(2)}) collective-permute-start(bf16[1,768,256]{2,1,0:T(8,128)(2,1)} %collective-permute-done.1.refs_4_.refs_11_), channel_id=1, source_target_pairs={{0,16},{16,0},{1,17},{17,1},{2,18},{18,2},{3,19},{19,3},{4,20},{20... | collective-permute-start | bytes 1179656 | tf_op jit(solution)/shard_map/ppermute | solution.py:517
  54.8 3.5 %collective-permute-done.refs_2_.refs_9_ = bf16[1,768,256]{2,1,0:T(8,128)(2,1)} collective-permute-done((bf16[1,768,256]{2,1,0:T(8,128)(2,1)S(1)}, bf16[1,768,256]{2,1,0:T(8,128)(2,1)}, u32[]{:S(2)}, u32[]{:S(2)}) %collective-permute-start) | collective-permute-done | bytes 393248 | tf_op jit(solution)/shard_map/ppermute | solution.py:517
  58.3 1.7 %collective-permute-start.5 = (bf16[1,768,256]{2,1,0:T(8,128)(2,1)}, bf16[1,768,256]{2,1,0:T(8,128)(2,1)}, u32[]{:S(2)}, u32[]{:S(2)}) collective-permute-start(bf16[1,768,256]{2,1,0:T(8,128)(2,1)} %collective-permute-done.refs_2_.refs_9_), channel_id=1, source_target_pairs={{0,16},{16,0},{1,17},{17,1},{2,18},{18,2},{3,19},{19,3},{4,20},{20... | collective-permute-start | bytes 1179656 | tf_op jit(solution)/shard_map/ppermute | solution.py:517
  60.0 4.9 %all-to-all-start = ((bf16[4,768,128]{2,1,0:T(8,128)(2,1)}), bf16[4,768,128]{2,1,0:T(8,128)(2,1)}, u32[]{:S(2)}, u32[]{:S(2)}) async-start(bf16[4,768,128]{2,1,0:T(8,128)(2,1)} %get-tuple-element.399), calls=%async_computation | async-start | bytes 1572864 | tf_op jit(solution)/shard_map/all_to_all | solution.py:564
  64.9 0.6 cut_heads.3.refs_9_
  65.5 0.7 copy-done.4
  66.3 0.5 collective-permute-start.11
  67.0 0.4 collective-permute-start.12
  67.4 6.5 %keys_values.3.refs_14_.refs_10_ = bf16[768,256]{1,0:T(8,128)(2,1)} custom-call(s32[8]{0:T(128)} %stack.35.at_ref, bf16[768,3072]{1,0:T(8,128)(2,1)} %normalize.3.refs_0_.own_ref, bf16[1,768,256]{2,1,0:T(8,128)(2,1)} %copy-done.3, bf16[1,768,256]{2,1,0:T(8,128)(2,1)} %collective-permute-done.refs_2_.refs_9_, ...), custom_call_target="tpu_custom_call" | custom-call | flops 68719476736 | bytes 1024 | tf_op jit(solution)/shard_map/keys_values/pallas_call | solution.py:277
  74.0 2.1 %collective-permute-start.17 = (f32[2,128]{1,0:T(2,128)S(1)}, f32[2,128]{1,0:T(2,128)S(1)}, u32[]{:S(2)}, u32[]{:S(2)}) collective-permute-start(f32[2,128]{1,0:T(2,128)S(1)} %copy-done.16), channel_id=1, source_target_pairs={{0,4},{4,0},{8,12},{12,8},{1,5},{5,1},{9,13},{13,9},{2,6},{6,2},{1... | collective-permute-start | bytes 3080 | tf_op jit(solution)/shard_map/ppermute | solution.py:517
  76.1 0.7 copy-done.12
  76.8 0.3 copy-done.8
  77.2 0.8 copy-done.11
  77.9 6.4 %keys_values.4 = (bf16[768,256]{1,0:T(8,128)(2,1)}, bf16[768,256]{1,0:T(8,128)(2,1)}) custom-call(s32[8]{0:T(128)} %stack.35.at_ref, bf16[128,3072]{1,0:T(8,128)(2,1)} %normalize.4.refs_0_.refs_1_, bf16[128,3072]{1,0:T(8,128)(2,1)} %collective-permute-done.9.refs_1_.refs_2_, bf16[128,3072]{1,0:T(8,128)(2,1)} %copy-done.7, bf16[128,3072]{1,0:T(8,128)(2,1)} %copy-done.8, ...), custom_call_target="tpu_custom_call" | custom-call | flops 68719476736 | bytes 1024 | tf_op jit(solution)/shard_map/keys_values/pallas_call | solution.py:277
  84.4 0.6 collective-permute-start.16
  84.9 3.0 %collective-permute-start.15 = (bf16[768,256]{1,0:T(8,128)(2,1)}, bf16[768,256]{1,0:T(8,128)(2,1)S(1)}, u32[]{:S(2)}, u32[]{:S(2)}) collective-permute-start(bf16[768,256]{1,0:T(8,128)(2,1)} %get-tuple-element.635), channel_id=1, source_target_pairs={{0,8},{4,12},{8,0},{12,4},{1,9},{5,13},{9,1},{13,5},{2,10},{6,14},... | collective-permute-start | bytes 1179656 | tf_op jit(solution)/shard_map/ppermute | solution.py:517
  87.9 9.9 %keys_values.5 = (bf16[768,256]{1,0:T(8,128)(2,1)}, bf16[768,256]{1,0:T(8,128)(2,1)}, bf16[768,256]{1,0:T(8,128)(2,1)}) custom-call(s32[8]{0:T(128)} %stack.35.at_ref, bf16[768,3072]{1,0:T(8,128)(2,1)} %normalize.3.refs_0_.own_ref, bf16[128,3072]{1,0:T(8,128)(2,1)} %normalize.4.refs_0_.refs_1_, bf16[128,3072]{1,0:T(8,128)(2,1)} %collective-permute-done.9.refs_1_.refs_2_, ...), custom_call_target="tpu_custom_call" | custom-call | flops 68719476736 | bytes 1024 | tf_op jit(solution)/shard_map/keys_values/pallas_call | solution.py:277
  97.9 6.0 %collective-permute-done.16.refs_9_ = bf16[4,768,128]{2,1,0:T(8,128)(2,1)S(1)} collective-permute-done((bf16[4,768,128]{2,1,0:T(8,128)(2,1)}, bf16[4,768,128]{2,1,0:T(8,128)(2,1)S(1)}, u32[]{:S(2)}, u32[]{:S(2)}) %collective-permute-start.16) | collective-permute-done | bytes 786464 | tf_op jit(solution)/shard_map/ppermute | solution.py:517
  103.9 0.9 copy-done.9
  104.8 19.4 %attend_pair.1 = (bf16[2,768,128]{2,1,0:T(8,128)(2,1)}, bf16[2,768,128]{2,1,0:T(8,128)(2,1)}, f32[2,768,128]{2,1,0:T(8,128)}, f32[2,768,128]{2,1,0:T(8,128)}) custom-call(s32[8]{0:T(128)} %stack.35.at_ref, f32[2,128]{1,0:T(2,128)} %see.1.limit0_ref, f32[2,128]{1,0:T(2,128)} %copy-done.17, bf16[768,3072]{1,0:T(8,128)(2,1)} %normalize.3.refs_0_.own_ref, ...), custom_call_target="tpu_custom_call" | custom-call | flops 1048576 | bytes 1024 | tf_op jit(solution)/shard_map/attend_pair/pallas_call | solution.py:403
  124.3 0.7 copy-done.18
  125.0 3.0 %attend_halo.2 = (bf16[768,128]{1,0:T(8,128)(2,1)}, bf16[768,128]{1,0:T(8,128)(2,1)}) custom-call(s32[8]{0:T(128)} %stack.35.at_ref, f32[2,128]{1,0:T(2,128)} %see.1.limit0_ref, f32[2,128]{1,0:T(2,128)} %copy-done.17, bf16[2,768,128]{2,1,0:T(8,128)(2,1)} %get-tuple-element.699.q_ref, bf16[768,256]{1,0:T(8,128)(2,1)} %copy-done.18, ...), custom_call_target="tpu_custom_call" | custom-call | flops 68719476736 | bytes 1024 | tf_op jit(solution)/shard_map/attend_halo/pallas_call | solution.py:451
  128.0 0.4 collective-permute-start.18
  128.4 0.3 copy-done.19
  128.7 2.9 %attend_halo.3 = (bf16[768,128]{1,0:T(8,128)(2,1)}, bf16[768,128]{1,0:T(8,128)(2,1)}) custom-call(s32[8]{0:T(128)} %stack.35.at_ref, f32[2,128]{1,0:T(2,128)} %see.1.limit0_ref, f32[2,128]{1,0:T(2,128)} %copy-done.17, bf16[2,768,128]{2,1,0:T(8,128)(2,1)} %get-tuple-element.699.q_ref, bf16[768,256]{1,0:T(8,128)(2,1)} %copy-done.19, ...), custom_call_target="tpu_custom_call" | custom-call | flops 68719476736 | bytes 1024 | tf_op jit(solution)/shard_map/attend_halo/pallas_call | solution.py:451
  131.7 1.3 collective-permute-start.19
  133.0 1.5 %collective-permute-done.18.refs_2_ = bf16[768,128]{1,0:T(8,128)(2,1)S(1)} collective-permute-done((bf16[768,128]{1,0:T(8,128)(2,1)}, bf16[768,128]{1,0:T(8,128)(2,1)S(1)}, u32[]{:S(2)}, u32[]{:S(2)}) %collective-permute-start.18) | collective-permute-done | bytes 196640 | tf_op jit(solution)/shard_map/ppermute | solution.py:517
  134.5 3.7 %collective-permute-done.19.refs_3_ = bf16[768,128]{1,0:T(8,128)(2,1)S(1)} collective-permute-done((bf16[768,128]{1,0:T(8,128)(2,1)}, bf16[768,128]{1,0:T(8,128)(2,1)S(1)}, u32[]{:S(2)}, u32[]{:S(2)}) %collective-permute-start.19) | collective-permute-done | bytes 196640 | tf_op jit(solution)/shard_map/ppermute | solution.py:517
  138.2 0.7 copy-done.15
  138.9 2.9 %assemble.1 = bf16[768,512]{1,0:T(8,128)(2,1)} custom-call(s32[8]{0:T(128)} %stack.35.at_ref, bf16[768,128]{1,0:T(8,128)(2,1)} %get-tuple-element.696.refs_0_, bf16[768,128]{1,0:T(8,128)(2,1)} %get-tuple-element.704.refs_1_, bf16[768,128]{1,0:T(8,128)(2,1)} %copy-done.14, bf16[768,128]{1,0:T(8,128)(2,1)} %copy-done.15), custom_call_target="tpu_custom_call" | custom-call | flops 1048576 | bytes 1024 | tf_op jit(solution)/shard_map/assemble/pallas_call | solution.py:473
  (49 shorter events, 0.6 us)
Async XLA Ops:
  0.0 6.7 %copy-start = (bf16[768,3,512]{2,0,1:T(8,128)(2,1)S(1)}, bf16[768,3,512]{2,0,1:T(8,128)(2,1)}, u32[]{:S(2)}) copy-start(bf16[768,3,512]{2,0,1:T(8,128)(2,1)} %param.8) | copy-start | bytes 7077892
  0.6 6.2 %copy-start.1 = (s32[8]{0:T(128)S(1)}, s32[8]{0:T(128)}, u32[]{:S(2)}) copy-start(s32[8]{0:T(128)} %stack.35.at_ref) | copy-start | bytes 100
  3.7 30.1 %collective-permute-start.4 = (bf16[128,3072]{1,0:T(8,128)(2,1)}, bf16[128,3072]{1,0:T(8,128)(2,1)}, u32[]{:S(2)}, u32[]{:S(2)}) collective-permute-start(bf16[128,3072]{1,0:T(8,128)(2,1)} %get-tuple-element.356), channel_id=1, source_target_pairs={{0,4},{4,0},{8,12},{12,8},{1,5},{5,1},{9,13},{13,9},{2,6},{6,2},{1... | collective-permute-start | bytes 2359304 | tf_op jit(solution)/shard_map/ppermute | solution.py:517
  8.4 13.3 %copy-start.3 = (bf16[1,768,256]{2,1,0:T(8,128)(2,1)}, bf16[1,768,256]{2,1,0:T(8,128)(2,1)S(1)}, u32[]{:S(2)}) copy-start(bf16[1,768,256]{2,1,0:T(8,128)(2,1)S(1)} %get-tuple-element.578.refs_1_.refs_8_) | copy-start | bytes 1179652
  8.4 30.0 %collective-permute-start.3 = (bf16[1,768,256]{2,1,0:T(8,128)(2,1)S(1)}, bf16[1,768,256]{2,1,0:T(8,128)(2,1)}, u32[]{:S(2)}, u32[]{:S(2)}) collective-permute-start(bf16[1,768,256]{2,1,0:T(8,128)(2,1)S(1)} %get-tuple-element.578.refs_1_.refs_8_), channel_id=1, source_target_pairs={{0,8},{4,12},{8,0},{12,4},{1,9},{5,13},{9,1},{13,5},{2,10},{6,14},... | collective-permute-start | bytes 1179656 | tf_op jit(solution)/shard_map/ppermute | solution.py:517
  11.0 31.1 %collective-permute-start.2 = (bf16[64,3072]{1,0:T(8,128)(2,1)}, bf16[64,3072]{1,0:T(8,128)(2,1)S(1)}, u32[]{:S(2)}, u32[]{:S(2)}) collective-permute-start(bf16[64,3072]{1,0:T(8,128)(2,1)} %get-tuple-element.357), channel_id=1, source_target_pairs={{0,4},{4,0},{8,12},{12,8},{1,5},{5,1},{9,13},{13,9},{2,6},{6,2},{1... | collective-permute-start | bytes 1179656 | tf_op jit(solution)/shard_map/ppermute | solution.py:517
  11.5 41.8 %collective-permute-start.1 = (bf16[1,768,256]{2,1,0:T(8,128)(2,1)S(1)}, bf16[1,768,256]{2,1,0:T(8,128)(2,1)}, u32[]{:S(2)}, u32[]{:S(2)}) collective-permute-start(bf16[1,768,256]{2,1,0:T(8,128)(2,1)S(1)} %get-tuple-element.359), channel_id=1, source_target_pairs={{0,12},{4,8},{8,4},{12,0},{1,13},{5,9},{9,5},{13,1},{2,14},{6,10},... | collective-permute-start | bytes 1179656 | tf_op jit(solution)/shard_map/ppermute | solution.py:517
  12.8 45.5 %collective-permute-start = (bf16[1,768,256]{2,1,0:T(8,128)(2,1)S(1)}, bf16[1,768,256]{2,1,0:T(8,128)(2,1)}, u32[]{:S(2)}, u32[]{:S(2)}) collective-permute-start(bf16[1,768,256]{2,1,0:T(8,128)(2,1)S(1)} %get-tuple-element.359), channel_id=1, source_target_pairs={{0,4},{4,0},{8,12},{12,8},{1,5},{5,1},{9,13},{13,9},{2,6},{6,2},{1... | collective-permute-start | bytes 1179656 | tf_op jit(solution)/shard_map/ppermute | solution.py:517
  14.4 50.5 %copy-start.2 = (s32[8]{0:T(128)S(1)}, s32[8]{0:T(128)}, u32[]{:S(2)}) copy-start(s32[8]{0:T(128)} %stack.35.at_ref) | copy-start | bytes 100
  36.4 29.8 %collective-permute-start.9 = (bf16[128,3072]{1,0:T(8,128)(2,1)}, bf16[128,3072]{1,0:T(8,128)(2,1)}, u32[]{:S(2)}, u32[]{:S(2)}) collective-permute-start(bf16[128,3072]{1,0:T(8,128)(2,1)} %normalize.4.refs_0_.refs_1_), channel_id=1, source_target_pairs={{0,2},{2,0},{1,3},{3,1},{4,6},{6,4},{5,7},{7,5},{8,10},{10,8},{9,1... | collective-permute-start | bytes 2359304 | tf_op jit(solution)/shard_map/ppermute | solution.py:517
  38.4 27.9 %collective-permute-start.8 = (bf16[1,768,256]{2,1,0:T(8,128)(2,1)}, bf16[1,768,256]{2,1,0:T(8,128)(2,1)}, u32[]{:S(2)}, u32[]{:S(2)}) collective-permute-start(bf16[1,768,256]{2,1,0:T(8,128)(2,1)} %collective-permute-done.3.refs_3_.refs_10_), channel_id=1, source_target_pairs={{0,16},{16,0},{1,17},{17,1},{2,18},{18,2},{3,19},{19,3},{4,20},{20... | collective-permute-start | bytes 1179656 | tf_op jit(solution)/shard_map/ppermute | solution.py:517
  42.2 0.8 copy-start.13
  45.0 21.8 %collective-permute-start.6 = (bf16[64,3072]{1,0:T(8,128)(2,1)}, bf16[64,3072]{1,0:T(8,128)(2,1)S(1)}, u32[]{:S(2)}, u32[]{:S(2)}) collective-permute-start(bf16[64,3072]{1,0:T(8,128)(2,1)} %normalize.5.refs_4_.refs_5_), channel_id=1, source_target_pairs={{0,2},{2,0},{1,3},{3,1},{4,6},{6,4},{5,7},{7,5},{8,10},{10,8},{9,1... | collective-permute-start | bytes 1179656 | tf_op jit(solution)/shard_map/ppermute | solution.py:517
  53.2 13.6 %collective-permute-start.7 = (bf16[1,768,256]{2,1,0:T(8,128)(2,1)}, bf16[1,768,256]{2,1,0:T(8,128)(2,1)}, u32[]{:S(2)}, u32[]{:S(2)}) collective-permute-start(bf16[1,768,256]{2,1,0:T(8,128)(2,1)} %collective-permute-done.1.refs_4_.refs_11_), channel_id=1, source_target_pairs={{0,16},{16,0},{1,17},{17,1},{2,18},{18,2},{3,19},{19,3},{4,20},{20... | collective-permute-start | bytes 1179656 | tf_op jit(solution)/shard_map/ppermute | solution.py:517
  58.3 26.6 %collective-permute-start.5 = (bf16[1,768,256]{2,1,0:T(8,128)(2,1)}, bf16[1,768,256]{2,1,0:T(8,128)(2,1)}, u32[]{:S(2)}, u32[]{:S(2)}) collective-permute-start(bf16[1,768,256]{2,1,0:T(8,128)(2,1)} %collective-permute-done.refs_2_.refs_9_), channel_id=1, source_target_pairs={{0,16},{16,0},{1,17},{17,1},{2,18},{18,2},{3,19},{19,3},{4,20},{20... | collective-permute-start | bytes 1179656 | tf_op jit(solution)/shard_map/ppermute | solution.py:517
  60.0 24.4 %all-to-all-start = ((bf16[4,768,128]{2,1,0:T(8,128)(2,1)}), bf16[4,768,128]{2,1,0:T(8,128)(2,1)}, u32[]{:S(2)}, u32[]{:S(2)}) async-start(bf16[4,768,128]{2,1,0:T(8,128)(2,1)} %get-tuple-element.399), calls=%async_computation | async-start | bytes 1572864 | tf_op jit(solution)/shard_map/all_to_all | solution.py:564
  64.8 1.4 copy-start.5
  64.9 2.1 %copy-start.6 = (bf16[64,3072]{1,0:T(8,128)(2,1)S(1)}, bf16[64,3072]{1,0:T(8,128)(2,1)}, u32[]{:S(2)}) copy-start(bf16[64,3072]{1,0:T(8,128)(2,1)} %normalize.5.refs_4_.refs_5_) | copy-start | bytes 1179652
  65.5 0.8 copy-start.4
  66.2 7.7 %copy-start.16 = (f32[2,128]{1,0:T(2,128)S(1)}, f32[2,128]{1,0:T(2,128)}, u32[]{:S(2)}) copy-start(f32[2,128]{1,0:T(2,128)} %see.1.limit0_ref) | copy-start | bytes 3076
  66.2 7.7 %collective-permute-start.13 = (bf16[128,3072]{1,0:T(8,128)(2,1)S(1)}, bf16[128,3072]{1,0:T(8,128)(2,1)S(1)}, u32[]{:S(2)}, u32[]{:S(2)}) collective-permute-start(bf16[128,3072]{1,0:T(8,128)(2,1)S(1)} %copy-done.5), channel_id=1, source_target_pairs={{0,1},{1,0},{2,3},{3,2},{4,5},{5,4},{6,7},{7,6},{8,9},{9,8},{10,11... | collective-permute-start | bytes 2359304 | tf_op jit(solution)/shard_map/ppermute | solution.py:517
  66.3 9.7 %collective-permute-start.11 = (bf16[128,3072]{1,0:T(8,128)(2,1)}, bf16[128,3072]{1,0:T(8,128)(2,1)S(1)}, u32[]{:S(2)}, u32[]{:S(2)}) collective-permute-start(bf16[128,3072]{1,0:T(8,128)(2,1)} %collective-permute-done.9.refs_1_.refs_2_), channel_id=1, source_target_pairs={{0,1},{1,0},{2,3},{3,2},{4,5},{5,4},{6,7},{7,6},{8,9},{9,8},{10,11... | collective-permute-start | bytes 2359304 | tf_op jit(solution)/shard_map/ppermute | solution.py:517
  66.8 7.1 %copy-start.10 = (bf16[64,3072]{1,0:T(8,128)(2,1)}, bf16[64,3072]{1,0:T(8,128)(2,1)S(1)}, u32[]{:S(2)}) copy-start(bf16[64,3072]{1,0:T(8,128)(2,1)S(1)} %collective-permute-done.6.refs_5_.refs_6_) | copy-start | bytes 1179652
  66.8 9.2 %collective-permute-start.10 = (bf16[64,3072]{1,0:T(8,128)(2,1)S(1)}, bf16[64,3072]{1,0:T(8,128)(2,1)S(1)}, u32[]{:S(2)}, u32[]{:S(2)}) collective-permute-start(bf16[64,3072]{1,0:T(8,128)(2,1)S(1)} %collective-permute-done.6.refs_5_.refs_6_), channel_id=1, source_target_pairs={{0,1},{1,0},{2,3},{3,2},{4,5},{5,4},{6,7},{7,6},{8,9},{9,8},{10,11... | collective-permute-start | bytes 1179656 | tf_op jit(solution)/shard_map/ppermute | solution.py:517
  67.0 9.1 %collective-permute-start.12 = (bf16[64,3072]{1,0:T(8,128)(2,1)S(1)}, bf16[64,3072]{1,0:T(8,128)(2,1)S(1)}, u32[]{:S(2)}, u32[]{:S(2)}) collective-permute-start(bf16[64,3072]{1,0:T(8,128)(2,1)S(1)} %copy-done.6), channel_id=1, source_target_pairs={{0,1},{1,0},{2,3},{3,2},{4,5},{5,4},{6,7},{7,6},{8,9},{9,8},{10,11... | collective-permute-start | bytes 1179656 | tf_op jit(solution)/shard_map/ppermute | solution.py:517
  74.0 2.1 %copy-start.7 = (bf16[128,3072]{1,0:T(8,128)(2,1)}, bf16[128,3072]{1,0:T(8,128)(2,1)S(1)}, u32[]{:S(2)}) copy-start(bf16[128,3072]{1,0:T(8,128)(2,1)S(1)} %collective-permute-done.13.refs_2_.refs_3_) | copy-start | bytes 2359300
  74.0 23.8 %collective-permute-start.17 = (f32[2,128]{1,0:T(2,128)S(1)}, f32[2,128]{1,0:T(2,128)S(1)}, u32[]{:S(2)}, u32[]{:S(2)}) collective-permute-start(f32[2,128]{1,0:T(2,128)S(1)} %copy-done.16), channel_id=1, source_target_pairs={{0,4},{4,0},{8,12},{12,8},{1,5},{5,1},{9,13},{13,9},{2,6},{6,2},{1... | collective-permute-start | bytes 3080 | tf_op jit(solution)/shard_map/ppermute | solution.py:517
  76.1 0.8 copy-start.12
  76.1 1.1 copy-start.8
  77.2 0.8 copy-start.11
  84.4 19.5 %collective-permute-start.16 = (bf16[4,768,128]{2,1,0:T(8,128)(2,1)}, bf16[4,768,128]{2,1,0:T(8,128)(2,1)S(1)}, u32[]{:S(2)}, u32[]{:S(2)}) collective-permute-start(bf16[4,768,128]{2,1,0:T(8,128)(2,1)} %all-to-all-done.refs_8_), channel_id=1, source_target_pairs={{0,16},{16,0},{1,17},{17,1},{2,18},{18,2},{3,19},{19,3},{4,20},{20... | collective-permute-start | bytes 2359304 | tf_op jit(solution)/shard_map/ppermute | solution.py:517
  84.9 39.3 %collective-permute-start.15 = (bf16[768,256]{1,0:T(8,128)(2,1)}, bf16[768,256]{1,0:T(8,128)(2,1)S(1)}, u32[]{:S(2)}, u32[]{:S(2)}) collective-permute-start(bf16[768,256]{1,0:T(8,128)(2,1)} %get-tuple-element.635), channel_id=1, source_target_pairs={{0,8},{4,12},{8,0},{12,4},{1,9},{5,13},{9,1},{13,5},{2,10},{6,14},... | collective-permute-start | bytes 1179656 | tf_op jit(solution)/shard_map/ppermute | solution.py:517
  97.8 6.1 %copy-start.17 = (f32[2,128]{1,0:T(2,128)}, f32[2,128]{1,0:T(2,128)S(1)}, u32[]{:S(2)}) copy-start(f32[2,128]{1,0:T(2,128)S(1)} %collective-permute-done.17.limit1_ref) | copy-start | bytes 3076
  97.8 30.2 %collective-permute-start.14 = (bf16[768,256]{1,0:T(8,128)(2,1)}, bf16[768,256]{1,0:T(8,128)(2,1)S(1)}, u32[]{:S(2)}, u32[]{:S(2)}) collective-permute-start(bf16[768,256]{1,0:T(8,128)(2,1)} %get-tuple-element.634), channel_id=1, source_target_pairs={{0,8},{4,12},{8,0},{12,4},{1,9},{5,13},{9,1},{13,5},{2,10},{6,14},... | collective-permute-start | bytes 1179656 | tf_op jit(solution)/shard_map/ppermute | solution.py:517
  103.9 0.9 copy-start.9
  124.2 0.7 copy-start.18
  128.0 0.7 copy-start.19
  128.0 6.5 %collective-permute-start.18 = (bf16[768,128]{1,0:T(8,128)(2,1)}, bf16[768,128]{1,0:T(8,128)(2,1)S(1)}, u32[]{:S(2)}, u32[]{:S(2)}) collective-permute-start(bf16[768,128]{1,0:T(8,128)(2,1)} %get-tuple-element.705), channel_id=1, source_target_pairs={{0,4},{4,0},{8,12},{12,8},{1,5},{5,1},{9,13},{13,9},{2,6},{6,2},{1... | collective-permute-start | bytes 589832 | tf_op jit(solution)/shard_map/ppermute | solution.py:517
  131.7 6.6 %collective-permute-start.19 = (bf16[768,128]{1,0:T(8,128)(2,1)}, bf16[768,128]{1,0:T(8,128)(2,1)S(1)}, u32[]{:S(2)}, u32[]{:S(2)}) collective-permute-start(bf16[768,128]{1,0:T(8,128)(2,1)} %get-tuple-element.706), channel_id=1, source_target_pairs={{0,4},{4,0},{8,12},{12,8},{1,5},{5,1},{9,13},{13,9},{2,6},{6,2},{1... | collective-permute-start | bytes 589832 | tf_op jit(solution)/shard_map/ppermute | solution.py:517
  134.5 3.7 %copy-start.14 = (bf16[768,128]{1,0:T(8,128)(2,1)}, bf16[768,128]{1,0:T(8,128)(2,1)S(1)}, u32[]{:S(2)}) copy-start(bf16[768,128]{1,0:T(8,128)(2,1)S(1)} %collective-permute-done.18.refs_2_) | copy-start | bytes 589828
  138.2 0.7 copy-start.15

commit v15 on v14

--- a/solution.py
+++ b/solution.py
@@ -559,12 +559,12 @@
 
     near0, far0 = take(0)
     two_mine, two_twin = swap(0)
+    one_mine, one_twin = swap(2)
     near1, far1 = take(1)
     (q_sent[0],) = line.after(q_sent[0])
     q_got = lax.all_to_all(q_sent[0], "seq", split_axis=0, concat_axis=0, tiled=True)
     line.drop(q_sent)
     three_mine, three_twin = swap(1)
-    one_mine, one_twin = swap(2)
     (w,) = line.after(w)
     own_kv = [same, line.reached(*cut_heads(at, w, [((TWIN,), (1, 2))], SPACE))[0]]
     far0, core0, core2 = spread(near0, far0)

time: 143 us -> 147 us (1.028)
  waiting for transfers between devices: 35.1 us -> 37.6 us
  starting transfers between devices: 30 us -> 31.8 us
    ppermute x20, waiting for transfers between devices: 35.1 us -> 37.6 us  [to(): lax.ppermute(value, axis, [(i, i ^ bit) for i in range(lax.axis_size(axis...]
    all_to_all x1, starting transfers between devices: 4.87 us -> 7.04 us  [per_device(): lax.all_to_all(q_sent[0], 'seq', split_axis=0, concat_axis=0, tiled=True)]
  transfers between devices with their start and end apart: 21 -> 21, of which waited for: 7 -> 7; matrix products, arithmetic and copies ran while one was open for 0% -> 0% of each run, Pallas kernels for 45% -> 44%
where the time goes in v15:
time: 147 us; the launch traced here: 146 us
  Pallas kernels  69.9 us (48%)
  waiting for transfers between devices  37.6 us (26%)
  starting transfers between devices  31.8 us (22%)
  local copies, waits for them, and re-layouts  6.58 us (4%)
    ppermute x20, waiting for transfers between devices, to(): lax.ppermute(value, axis, [(i, i ^ bit) for i in range(lax.axis_size(axis...  37.6 us
    ppermute x20, starting transfers between devices, to(): lax.ppermute(value, axis, [(i, i ^ bit) for i in range(lax.axis_size(axis...  24.7 us
    pallas_call x3, Pallas kernels, keys_values(): pl.pallas_call(kernel, in_specs=[pl.BlockSpec(memory_space=pltpu.SMEM)] +...  22.8 us
    pallas_call x1, Pallas kernels, attend_pair(): pl.pallas_call(kernel, in_specs=[smem] * 3 + [hbm] * (1 + len(arrays) + 6...  19.4 us
    pallas_call x3, Pallas kernels, normalize(): pl.pallas_call(norm_kernel, grid=(tokens // rows,), in_specs=[pl.BlockSpe...  12 us
    all_to_all x1, starting transfers between devices, per_device(): lax.all_to_all(q_sent[0], 'seq', split_axis=0, concat_axis=0, tiled=True)  7.04 us
    unnamed x40, local copies, waits for them, and re-layouts  6 us
    pallas_call x2, Pallas kernels, attend_halo(): pl.pallas_call(kernel, grid=(1,), in_specs=[smem] * 3 + [one, fixed(halo....  5.92 us
  transfers between devices with their start and end apart: 21, of which 7 were waited for; matrix products, arithmetic and copies ran while one was open for 0% of the time, Pallas kernels for 44%

profile of v15, /device:TPU:0, one launch (start us, length us, event | category | flops | bytes accessed | tf_op | source)
XLA Modules:
  0.0 146.1 jit_solution(5958714852455755638)
XLA Ops:
  0.0 0.6 stack.35.at_ref
  0.6 3.1 %take_rows.1 = (bf16[128,3072]{1,0:T(8,128)(2,1)}, bf16[64,3072]{1,0:T(8,128)(2,1)}) custom-call(s32[8]{0:T(128)} %stack.35.at_ref, bf16[768,3072]{1,0:T(8,128)(2,1)} %x_ref.2), custom_call_target="tpu_custom_call" | custom-call | flops 1048576 | bytes 1024 | tf_op jit(solution)/shard_map/take_rows/pallas_call | solution.py:306
  3.7 3.0 %collective-permute-start.2 = (bf16[128,3072]{1,0:T(8,128)(2,1)}, bf16[128,3072]{1,0:T(8,128)(2,1)}, u32[]{:S(2)}, u32[]{:S(2)}) collective-permute-start(bf16[128,3072]{1,0:T(8,128)(2,1)} %get-tuple-element.358), channel_id=1, source_target_pairs={{0,4},{4,0},{8,12},{12,8},{1,5},{5,1},{9,13},{13,9},{2,6},{6,2},{1... | collective-permute-start | bytes 2359304 | tf_op jit(solution)/shard_map/ppermute | solution.py:517
  6.7 1.7 %cut_heads.2 = (bf16[1,768,256]{2,1,0:T(8,128)(2,1)S(1)}, bf16[1,768,256]{2,1,0:T(8,128)(2,1)S(1)}, bf16[4,768,128]{2,1,0:T(8,128)(2,1)}) custom-call(s32[8]{0:T(128)S(1)} %copy-done.1, bf16[3,768,512]{2,1,0:T(8,128)(2,1)S(1)} %bitcast.9), custom_call_target="tpu_custom_call" | custom-call | flops 1048576 | bytes 1024 | tf_op jit(solution)/shard_map/cut_heads/pallas_call | solution.py:150
  8.4 2.6 %collective-permute-start.1 = (bf16[1,768,256]{2,1,0:T(8,128)(2,1)S(1)}, bf16[1,768,256]{2,1,0:T(8,128)(2,1)}, u32[]{:S(2)}, u32[]{:S(2)}) collective-permute-start(bf16[1,768,256]{2,1,0:T(8,128)(2,1)S(1)} %get-tuple-element.582.refs_1_.refs_8_), channel_id=1, source_target_pairs={{0,8},{4,12},{8,0},{12,4},{1,9},{5,13},{9,1},{13,5},{2,10},{6,14},... | collective-permute-start | bytes 1179656 | tf_op jit(solution)/shard_map/ppermute | solution.py:517
  11.0 0.4 collective-permute-start
  11.5 1.6 %collective-permute-start.4 = (bf16[64,3072]{1,0:T(8,128)(2,1)}, bf16[64,3072]{1,0:T(8,128)(2,1)S(1)}, u32[]{:S(2)}, u32[]{:S(2)}) collective-permute-start(bf16[64,3072]{1,0:T(8,128)(2,1)} %get-tuple-element.359), channel_id=1, source_target_pairs={{0,4},{4,0},{8,12},{12,8},{1,5},{5,1},{9,13},{13,9},{2,6},{6,2},{1... | collective-permute-start | bytes 1179656 | tf_op jit(solution)/shard_map/ppermute | solution.py:517
  13.0 1.3 see.1.limit0_ref
  14.4 7.3 %normalize.3.refs_0_.own_ref = bf16[768,3072]{1,0:T(8,128)(2,1)} custom-call(bf16[768,3072]{1,0:T(8,128)(2,1)} %x_ref.2, f32[2,3072]{1,0:T(2,128)} %mod_ref.2), custom_call_target="tpu_custom_call" | custom-call | flops 1048576 | bytes 1024 | tf_op jit(solution)/shard_map/normalize/pallas_call | solution.py:124
  21.7 12.1 %collective-permute-done.2.x_ref = bf16[128,3072]{1,0:T(8,128)(2,1)} collective-permute-done((bf16[128,3072]{1,0:T(8,128)(2,1)}, bf16[128,3072]{1,0:T(8,128)(2,1)}, u32[]{:S(2)}, u32[]{:S(2)}) %collective-permute-start.2) | collective-permute-done | bytes 786464 | tf_op jit(solution)/shard_map/ppermute | solution.py:517
  33.8 2.6 %normalize.4.refs_0_.refs_1_ = bf16[128,3072]{1,0:T(8,128)(2,1)} custom-call(bf16[128,3072]{1,0:T(8,128)(2,1)} %collective-permute-done.2.x_ref, f32[2,3072]{1,0:T(2,128)} %mod_ref.2), custom_call_target="tpu_custom_call" | custom-call | flops 1048576 | bytes 1024 | tf_op jit(solution)/shard_map/normalize/pallas_call | solution.py:124
  36.4 2.0 %collective-permute-start.9 = (bf16[128,3072]{1,0:T(8,128)(2,1)}, bf16[128,3072]{1,0:T(8,128)(2,1)}, u32[]{:S(2)}, u32[]{:S(2)}) collective-permute-start(bf16[128,3072]{1,0:T(8,128)(2,1)} %normalize.4.refs_0_.refs_1_), channel_id=1, source_target_pairs={{0,2},{2,0},{1,3},{3,1},{4,6},{6,4},{5,7},{7,5},{8,10},{10,8},{9,1... | collective-permute-start | bytes 2359304 | tf_op jit(solution)/shard_map/ppermute | solution.py:517
  38.4 1.5 %collective-permute-start.8 = (bf16[1,768,256]{2,1,0:T(8,128)(2,1)}, bf16[1,768,256]{2,1,0:T(8,128)(2,1)}, u32[]{:S(2)}, u32[]{:S(2)}) collective-permute-start(bf16[1,768,256]{2,1,0:T(8,128)(2,1)} %collective-permute-done.1.refs_3_.refs_10_), channel_id=1, source_target_pairs={{0,16},{16,0},{1,17},{17,1},{2,18},{18,2},{3,19},{19,3},{4,20},{20... | collective-permute-start | bytes 1179656 | tf_op jit(solution)/shard_map/ppermute | solution.py:517
  39.9 2.3 %collective-permute-done.refs_2_.refs_9_ = bf16[1,768,256]{2,1,0:T(8,128)(2,1)} collective-permute-done((bf16[1,768,256]{2,1,0:T(8,128)(2,1)S(1)}, bf16[1,768,256]{2,1,0:T(8,128)(2,1)}, u32[]{:S(2)}, u32[]{:S(2)}) %collective-permute-start) | collective-permute-done | bytes 393248 | tf_op jit(solution)/shard_map/ppermute | solution.py:517
  42.3 2.0 %collective-permute-start.3 = (bf16[1,768,256]{2,1,0:T(8,128)(2,1)}, bf16[1,768,256]{2,1,0:T(8,128)(2,1)}, u32[]{:S(2)}, u32[]{:S(2)}) collective-permute-start(bf16[1,768,256]{2,1,0:T(8,128)(2,1)} %collective-permute-done.refs_2_.refs_9_), channel_id=1, source_target_pairs={{0,16},{16,0},{1,17},{17,1},{2,18},{18,2},{3,19},{19,3},{4,20},{20... | collective-permute-start | bytes 1179656 | tf_op jit(solution)/shard_map/ppermute | solution.py:517
  44.3 6.0 %collective-permute-done.4.x_ref = bf16[64,3072]{1,0:T(8,128)(2,1)S(1)} collective-permute-done((bf16[64,3072]{1,0:T(8,128)(2,1)}, bf16[64,3072]{1,0:T(8,128)(2,1)S(1)}, u32[]{:S(2)}, u32[]{:S(2)}) %collective-permute-start.4) | collective-permute-done | bytes 393248 | tf_op jit(solution)/shard_map/ppermute | solution.py:517
  50.3 0.8 copy-done.13
  51.1 2.1 %normalize.5.refs_4_.refs_5_ = bf16[64,3072]{1,0:T(8,128)(2,1)} custom-call(bf16[64,3072]{1,0:T(8,128)(2,1)} %copy-done.13, f32[2,3072]{1,0:T(2,128)} %mod_ref.2), custom_call_target="tpu_custom_call" | custom-call | flops 1048576 | bytes 1024 | tf_op jit(solution)/shard_map/normalize/pallas_call | solution.py:124
  53.2 1.5 %collective-permute-start.5 = (bf16[64,3072]{1,0:T(8,128)(2,1)}, bf16[64,3072]{1,0:T(8,128)(2,1)S(1)}, u32[]{:S(2)}, u32[]{:S(2)}) collective-permute-start(bf16[64,3072]{1,0:T(8,128)(2,1)} %normalize.5.refs_4_.refs_5_), channel_id=1, source_target_pairs={{0,2},{2,0},{1,3},{3,1},{4,6},{6,4},{5,7},{7,5},{8,10},{10,8},{9,1... | collective-permute-start | bytes 1179656 | tf_op jit(solution)/shard_map/ppermute | solution.py:517
  54.7 5.9 %collective-permute-done.6.refs_4_.refs_11_ = bf16[1,768,256]{2,1,0:T(8,128)(2,1)} collective-permute-done((bf16[1,768,256]{2,1,0:T(8,128)(2,1)S(1)}, bf16[1,768,256]{2,1,0:T(8,128)(2,1)}, u32[]{:S(2)}, u32[]{:S(2)}) %collective-permute-start.6) | collective-permute-done | bytes 393248 | tf_op jit(solution)/shard_map/ppermute | solution.py:517
  60.5 1.5 %collective-permute-start.7 = (bf16[1,768,256]{2,1,0:T(8,128)(2,1)}, bf16[1,768,256]{2,1,0:T(8,128)(2,1)}, u32[]{:S(2)}, u32[]{:S(2)}) collective-permute-start(bf16[1,768,256]{2,1,0:T(8,128)(2,1)} %collective-permute-done.6.refs_4_.refs_11_), channel_id=1, source_target_pairs={{0,16},{16,0},{1,17},{17,1},{2,18},{18,2},{3,19},{19,3},{4,20},{20... | collective-permute-start | bytes 1179656 | tf_op jit(solution)/shard_map/ppermute | solution.py:517
  62.0 7.0 %all-to-all-start = ((bf16[4,768,128]{2,1,0:T(8,128)(2,1)}), bf16[4,768,128]{2,1,0:T(8,128)(2,1)}, u32[]{:S(2)}, u32[]{:S(2)}) async-start(bf16[4,768,128]{2,1,0:T(8,128)(2,1)} %get-tuple-element.395), calls=%async_computation | async-start | bytes 1572864 | tf_op jit(solution)/shard_map/all_to_all | solution.py:565
  69.1 0.6 cut_heads.3.refs_9_
  69.7 0.7 copy-done.4
  70.6 0.5 collective-permute-start.11
  71.2 0.4 collective-permute-start.12
  71.7 6.5 %keys_values.3.refs_14_.refs_10_ = bf16[768,256]{1,0:T(8,128)(2,1)} custom-call(s32[8]{0:T(128)} %stack.35.at_ref, bf16[768,3072]{1,0:T(8,128)(2,1)} %normalize.3.refs_0_.own_ref, bf16[1,768,256]{2,1,0:T(8,128)(2,1)} %copy-done.3, bf16[1,768,256]{2,1,0:T(8,128)(2,1)} %collective-permute-done.refs_2_.refs_9_, ...), custom_call_target="tpu_custom_call" | custom-call | flops 68719476736 | bytes 1024 | tf_op jit(solution)/shard_map/keys_values/pallas_call | solution.py:277
  78.2 2.1 %collective-permute-start.17 = (f32[2,128]{1,0:T(2,128)S(1)}, f32[2,128]{1,0:T(2,128)S(1)}, u32[]{:S(2)}, u32[]{:S(2)}) collective-permute-start(f32[2,128]{1,0:T(2,128)S(1)} %copy-done.16), channel_id=1, source_target_pairs={{0,4},{4,0},{8,12},{12,8},{1,5},{5,1},{9,13},{13,9},{2,6},{6,2},{1... | collective-permute-start | bytes 3080 | tf_op jit(solution)/shard_map/ppermute | solution.py:517
  80.3 0.7 copy-done.12
  81.1 0.3 copy-done.8
  81.4 0.8 copy-done.11
  82.2 6.4 %keys_values.4 = (bf16[768,256]{1,0:T(8,128)(2,1)}, bf16[768,256]{1,0:T(8,128)(2,1)}) custom-call(s32[8]{0:T(128)} %stack.35.at_ref, bf16[128,3072]{1,0:T(8,128)(2,1)} %normalize.4.refs_0_.refs_1_, bf16[128,3072]{1,0:T(8,128)(2,1)} %collective-permute-done.9.refs_1_.refs_2_, bf16[128,3072]{1,0:T(8,128)(2,1)} %copy-done.7, bf16[128,3072]{1,0:T(8,128)(2,1)} %copy-done.8, ...), custom_call_target="tpu_custom_call" | custom-call | flops 68719476736 | bytes 1024 | tf_op jit(solution)/shard_map/keys_values/pallas_call | solution.py:277
  88.6 0.6 collective-permute-start.16
  89.2 2.8 %collective-permute-start.15 = (bf16[768,256]{1,0:T(8,128)(2,1)}, bf16[768,256]{1,0:T(8,128)(2,1)S(1)}, u32[]{:S(2)}, u32[]{:S(2)}) collective-permute-start(bf16[768,256]{1,0:T(8,128)(2,1)} %get-tuple-element.639), channel_id=1, source_target_pairs={{0,8},{4,12},{8,0},{12,4},{1,9},{5,13},{9,1},{13,5},{2,10},{6,14},... | collective-permute-start | bytes 1179656 | tf_op jit(solution)/shard_map/ppermute | solution.py:517
  92.0 9.9 %keys_values.5 = (bf16[768,256]{1,0:T(8,128)(2,1)}, bf16[768,256]{1,0:T(8,128)(2,1)}, bf16[768,256]{1,0:T(8,128)(2,1)}) custom-call(s32[8]{0:T(128)} %stack.35.at_ref, bf16[768,3072]{1,0:T(8,128)(2,1)} %normalize.3.refs_0_.own_ref, bf16[128,3072]{1,0:T(8,128)(2,1)} %normalize.4.refs_0_.refs_1_, bf16[128,3072]{1,0:T(8,128)(2,1)} %collective-permute-done.9.refs_1_.refs_2_, ...), custom_call_target="tpu_custom_call" | custom-call | flops 68719476736 | bytes 1024 | tf_op jit(solution)/shard_map/keys_values/pallas_call | solution.py:277
  102.1 6.1 %collective-permute-done.16.refs_9_ = bf16[4,768,128]{2,1,0:T(8,128)(2,1)S(1)} collective-permute-done((bf16[4,768,128]{2,1,0:T(8,128)(2,1)}, bf16[4,768,128]{2,1,0:T(8,128)(2,1)S(1)}, u32[]{:S(2)}, u32[]{:S(2)}) %collective-permute-start.16) | collective-permute-done | bytes 786464 | tf_op jit(solution)/shard_map/ppermute | solution.py:517
  108.1 0.9 copy-done.9
  109.1 19.4 %attend_pair.1 = (bf16[2,768,128]{2,1,0:T(8,128)(2,1)}, bf16[2,768,128]{2,1,0:T(8,128)(2,1)}, f32[2,768,128]{2,1,0:T(8,128)}, f32[2,768,128]{2,1,0:T(8,128)}) custom-call(s32[8]{0:T(128)} %stack.35.at_ref, f32[2,128]{1,0:T(2,128)} %see.1.limit0_ref, f32[2,128]{1,0:T(2,128)} %copy-done.17, bf16[768,3072]{1,0:T(8,128)(2,1)} %normalize.3.refs_0_.own_ref, ...), custom_call_target="tpu_custom_call" | custom-call | flops 1048576 | bytes 1024 | tf_op jit(solution)/shard_map/attend_pair/pallas_call | solution.py:403
  128.5 0.7 copy-done.18
  129.3 3.0 %attend_halo.2 = (bf16[768,128]{1,0:T(8,128)(2,1)}, bf16[768,128]{1,0:T(8,128)(2,1)}) custom-call(s32[8]{0:T(128)} %stack.35.at_ref, f32[2,128]{1,0:T(2,128)} %see.1.limit0_ref, f32[2,128]{1,0:T(2,128)} %copy-done.17, bf16[2,768,128]{2,1,0:T(8,128)(2,1)} %get-tuple-element.703.q_ref, bf16[768,256]{1,0:T(8,128)(2,1)} %copy-done.18, ...), custom_call_target="tpu_custom_call" | custom-call | flops 68719476736 | bytes 1024 | tf_op jit(solution)/shard_map/attend_halo/pallas_call | solution.py:451
  132.2 0.4 collective-permute-start.18
  132.7 0.3 copy-done.19
  133.0 2.9 %attend_halo.3 = (bf16[768,128]{1,0:T(8,128)(2,1)}, bf16[768,128]{1,0:T(8,128)(2,1)}) custom-call(s32[8]{0:T(128)} %stack.35.at_ref, f32[2,128]{1,0:T(2,128)} %see.1.limit0_ref, f32[2,128]{1,0:T(2,128)} %copy-done.17, bf16[2,768,128]{2,1,0:T(8,128)(2,1)} %get-tuple-element.703.q_ref, bf16[768,256]{1,0:T(8,128)(2,1)} %copy-done.19, ...), custom_call_target="tpu_custom_call" | custom-call | flops 68719476736 | bytes 1024 | tf_op jit(solution)/shard_map/attend_halo/pallas_call | solution.py:451
  135.9 1.3 collective-permute-start.19
  137.3 1.5 %collective-permute-done.18.refs_2_ = bf16[768,128]{1,0:T(8,128)(2,1)S(1)} collective-permute-done((bf16[768,128]{1,0:T(8,128)(2,1)}, bf16[768,128]{1,0:T(8,128)(2,1)S(1)}, u32[]{:S(2)}, u32[]{:S(2)}) %collective-permute-start.18) | collective-permute-done | bytes 196640 | tf_op jit(solution)/shard_map/ppermute | solution.py:517
  138.8 3.7 %collective-permute-done.19.refs_3_ = bf16[768,128]{1,0:T(8,128)(2,1)S(1)} collective-permute-done((bf16[768,128]{1,0:T(8,128)(2,1)}, bf16[768,128]{1,0:T(8,128)(2,1)S(1)}, u32[]{:S(2)}, u32[]{:S(2)}) %collective-permute-start.19) | collective-permute-done | bytes 196640 | tf_op jit(solution)/shard_map/ppermute | solution.py:517
  142.5 0.7 copy-done.15
  143.2 2.9 %assemble.1 = bf16[768,512]{1,0:T(8,128)(2,1)} custom-call(s32[8]{0:T(128)} %stack.35.at_ref, bf16[768,128]{1,0:T(8,128)(2,1)} %get-tuple-element.700.refs_0_, bf16[768,128]{1,0:T(8,128)(2,1)} %get-tuple-element.708.refs_1_, bf16[768,128]{1,0:T(8,128)(2,1)} %copy-done.14, bf16[768,128]{1,0:T(8,128)(2,1)} %copy-done.15), custom_call_target="tpu_custom_call" | custom-call | flops 1048576 | bytes 1024 | tf_op jit(solution)/shard_map/assemble/pallas_call | solution.py:473
  (49 shorter events, 0.5 us)
Async XLA Ops:
  0.0 6.7 %copy-start = (bf16[768,3,512]{2,0,1:T(8,128)(2,1)S(1)}, bf16[768,3,512]{2,0,1:T(8,128)(2,1)}, u32[]{:S(2)}) copy-start(bf16[768,3,512]{2,0,1:T(8,128)(2,1)} %param.8) | copy-start | bytes 7077892
  0.6 6.2 %copy-start.1 = (s32[8]{0:T(128)S(1)}, s32[8]{0:T(128)}, u32[]{:S(2)}) copy-start(s32[8]{0:T(128)} %stack.35.at_ref) | copy-start | bytes 100
  3.7 30.1 %collective-permute-start.2 = (bf16[128,3072]{1,0:T(8,128)(2,1)}, bf16[128,3072]{1,0:T(8,128)(2,1)}, u32[]{:S(2)}, u32[]{:S(2)}) collective-permute-start(bf16[128,3072]{1,0:T(8,128)(2,1)} %get-tuple-element.358), channel_id=1, source_target_pairs={{0,4},{4,0},{8,12},{12,8},{1,5},{5,1},{9,13},{13,9},{2,6},{6,2},{1... | collective-permute-start | bytes 2359304 | tf_op jit(solution)/shard_map/ppermute | solution.py:517
  8.4 13.3 %copy-start.3 = (bf16[1,768,256]{2,1,0:T(8,128)(2,1)}, bf16[1,768,256]{2,1,0:T(8,128)(2,1)S(1)}, u32[]{:S(2)}) copy-start(bf16[1,768,256]{2,1,0:T(8,128)(2,1)S(1)} %get-tuple-element.582.refs_1_.refs_8_) | copy-start | bytes 1179652
  8.4 30.0 %collective-permute-start.1 = (bf16[1,768,256]{2,1,0:T(8,128)(2,1)S(1)}, bf16[1,768,256]{2,1,0:T(8,128)(2,1)}, u32[]{:S(2)}, u32[]{:S(2)}) collective-permute-start(bf16[1,768,256]{2,1,0:T(8,128)(2,1)S(1)} %get-tuple-element.582.refs_1_.refs_8_), channel_id=1, source_target_pairs={{0,8},{4,12},{8,0},{12,4},{1,9},{5,13},{9,1},{13,5},{2,10},{6,14},... | collective-permute-start | bytes 1179656 | tf_op jit(solution)/shard_map/ppermute | solution.py:517
  11.0 31.2 %collective-permute-start = (bf16[1,768,256]{2,1,0:T(8,128)(2,1)S(1)}, bf16[1,768,256]{2,1,0:T(8,128)(2,1)}, u32[]{:S(2)}, u32[]{:S(2)}) collective-permute-start(bf16[1,768,256]{2,1,0:T(8,128)(2,1)S(1)} %get-tuple-element.361), channel_id=1, source_target_pairs={{0,4},{4,0},{8,12},{12,8},{1,5},{5,1},{9,13},{13,9},{2,6},{6,2},{1... | collective-permute-start | bytes 1179656 | tf_op jit(solution)/shard_map/ppermute | solution.py:517
  11.5 38.8 %collective-permute-start.4 = (bf16[64,3072]{1,0:T(8,128)(2,1)}, bf16[64,3072]{1,0:T(8,128)(2,1)S(1)}, u32[]{:S(2)}, u32[]{:S(2)}) collective-permute-start(bf16[64,3072]{1,0:T(8,128)(2,1)} %get-tuple-element.359), channel_id=1, source_target_pairs={{0,4},{4,0},{8,12},{12,8},{1,5},{5,1},{9,13},{13,9},{2,6},{6,2},{1... | collective-permute-start | bytes 1179656 | tf_op jit(solution)/shard_map/ppermute | solution.py:517
  13.0 47.5 %collective-permute-start.6 = (bf16[1,768,256]{2,1,0:T(8,128)(2,1)S(1)}, bf16[1,768,256]{2,1,0:T(8,128)(2,1)}, u32[]{:S(2)}, u32[]{:S(2)}) collective-permute-start(bf16[1,768,256]{2,1,0:T(8,128)(2,1)S(1)} %get-tuple-element.361), channel_id=1, source_target_pairs={{0,12},{4,8},{8,4},{12,0},{1,13},{5,9},{9,5},{13,1},{2,14},{6,10},... | collective-permute-start | bytes 1179656 | tf_op jit(solution)/shard_map/ppermute | solution.py:517
  14.4 54.7 %copy-start.2 = (s32[8]{0:T(128)S(1)}, s32[8]{0:T(128)}, u32[]{:S(2)}) copy-start(s32[8]{0:T(128)} %stack.35.at_ref) | copy-start | bytes 100
  36.4 34.1 %collective-permute-start.9 = (bf16[128,3072]{1,0:T(8,128)(2,1)}, bf16[128,3072]{1,0:T(8,128)(2,1)}, u32[]{:S(2)}, u32[]{:S(2)}) collective-permute-start(bf16[128,3072]{1,0:T(8,128)(2,1)} %normalize.4.refs_0_.refs_1_), channel_id=1, source_target_pairs={{0,2},{2,0},{1,3},{3,1},{4,6},{6,4},{5,7},{7,5},{8,10},{10,8},{9,1... | collective-permute-start | bytes 2359304 | tf_op jit(solution)/shard_map/ppermute | solution.py:517
  38.4 32.2 %collective-permute-start.8 = (bf16[1,768,256]{2,1,0:T(8,128)(2,1)}, bf16[1,768,256]{2,1,0:T(8,128)(2,1)}, u32[]{:S(2)}, u32[]{:S(2)}) collective-permute-start(bf16[1,768,256]{2,1,0:T(8,128)(2,1)} %collective-permute-done.1.refs_3_.refs_10_), channel_id=1, source_target_pairs={{0,16},{16,0},{1,17},{17,1},{2,18},{18,2},{3,19},{19,3},{4,20},{20... | collective-permute-start | bytes 1179656 | tf_op jit(solution)/shard_map/ppermute | solution.py:517
  42.3 46.9 %collective-permute-start.3 = (bf16[1,768,256]{2,1,0:T(8,128)(2,1)}, bf16[1,768,256]{2,1,0:T(8,128)(2,1)}, u32[]{:S(2)}, u32[]{:S(2)}) collective-permute-start(bf16[1,768,256]{2,1,0:T(8,128)(2,1)} %collective-permute-done.refs_2_.refs_9_), channel_id=1, source_target_pairs={{0,16},{16,0},{1,17},{17,1},{2,18},{18,2},{3,19},{19,3},{4,20},{20... | collective-permute-start | bytes 1179656 | tf_op jit(solution)/shard_map/ppermute | solution.py:517
  50.3 0.8 copy-start.13
  53.2 17.9 %collective-permute-start.5 = (bf16[64,3072]{1,0:T(8,128)(2,1)}, bf16[64,3072]{1,0:T(8,128)(2,1)S(1)}, u32[]{:S(2)}, u32[]{:S(2)}) collective-permute-start(bf16[64,3072]{1,0:T(8,128)(2,1)} %normalize.5.refs_4_.refs_5_), channel_id=1, source_target_pairs={{0,2},{2,0},{1,3},{3,1},{4,6},{6,4},{5,7},{7,5},{8,10},{10,8},{9,1... | collective-permute-start | bytes 1179656 | tf_op jit(solution)/shard_map/ppermute | solution.py:517
  60.5 10.5 %collective-permute-start.7 = (bf16[1,768,256]{2,1,0:T(8,128)(2,1)}, bf16[1,768,256]{2,1,0:T(8,128)(2,1)}, u32[]{:S(2)}, u32[]{:S(2)}) collective-permute-start(bf16[1,768,256]{2,1,0:T(8,128)(2,1)} %collective-permute-done.6.refs_4_.refs_11_), channel_id=1, source_target_pairs={{0,16},{16,0},{1,17},{17,1},{2,18},{18,2},{3,19},{19,3},{4,20},{20... | collective-permute-start | bytes 1179656 | tf_op jit(solution)/shard_map/ppermute | solution.py:517
  62.0 26.6 %all-to-all-start = ((bf16[4,768,128]{2,1,0:T(8,128)(2,1)}), bf16[4,768,128]{2,1,0:T(8,128)(2,1)}, u32[]{:S(2)}, u32[]{:S(2)}) async-start(bf16[4,768,128]{2,1,0:T(8,128)(2,1)} %get-tuple-element.395), calls=%async_computation | async-start | bytes 1572864 | tf_op jit(solution)/shard_map/all_to_all | solution.py:565
  69.1 1.4 copy-start.5
  69.1 2.1 %copy-start.6 = (bf16[64,3072]{1,0:T(8,128)(2,1)S(1)}, bf16[64,3072]{1,0:T(8,128)(2,1)}, u32[]{:S(2)}) copy-start(bf16[64,3072]{1,0:T(8,128)(2,1)} %normalize.5.refs_4_.refs_5_) | copy-start | bytes 1179652
  69.7 0.8 copy-start.4
  70.5 7.7 %copy-start.16 = (f32[2,128]{1,0:T(2,128)S(1)}, f32[2,128]{1,0:T(2,128)}, u32[]{:S(2)}) copy-start(f32[2,128]{1,0:T(2,128)} %see.1.limit0_ref) | copy-start | bytes 3076
  70.5 7.7 %collective-permute-start.13 = (bf16[128,3072]{1,0:T(8,128)(2,1)S(1)}, bf16[128,3072]{1,0:T(8,128)(2,1)S(1)}, u32[]{:S(2)}, u32[]{:S(2)}) collective-permute-start(bf16[128,3072]{1,0:T(8,128)(2,1)S(1)} %copy-done.5), channel_id=1, source_target_pairs={{0,1},{1,0},{2,3},{3,2},{4,5},{5,4},{6,7},{7,6},{8,9},{9,8},{10,11... | collective-permute-start | bytes 2359304 | tf_op jit(solution)/shard_map/ppermute | solution.py:517
  70.6 9.7 %collective-permute-start.11 = (bf16[128,3072]{1,0:T(8,128)(2,1)}, bf16[128,3072]{1,0:T(8,128)(2,1)S(1)}, u32[]{:S(2)}, u32[]{:S(2)}) collective-permute-start(bf16[128,3072]{1,0:T(8,128)(2,1)} %collective-permute-done.9.refs_1_.refs_2_), channel_id=1, source_target_pairs={{0,1},{1,0},{2,3},{3,2},{4,5},{5,4},{6,7},{7,6},{8,9},{9,8},{10,11... | collective-permute-start | bytes 2359304 | tf_op jit(solution)/shard_map/ppermute | solution.py:517
  71.1 7.1 %copy-start.10 = (bf16[64,3072]{1,0:T(8,128)(2,1)}, bf16[64,3072]{1,0:T(8,128)(2,1)S(1)}, u32[]{:S(2)}) copy-start(bf16[64,3072]{1,0:T(8,128)(2,1)S(1)} %collective-permute-done.5.refs_5_.refs_6_) | copy-start | bytes 1179652
  71.1 9.2 %collective-permute-start.10 = (bf16[64,3072]{1,0:T(8,128)(2,1)S(1)}, bf16[64,3072]{1,0:T(8,128)(2,1)S(1)}, u32[]{:S(2)}, u32[]{:S(2)}) collective-permute-start(bf16[64,3072]{1,0:T(8,128)(2,1)S(1)} %collective-permute-done.5.refs_5_.refs_6_), channel_id=1, source_target_pairs={{0,1},{1,0},{2,3},{3,2},{4,5},{5,4},{6,7},{7,6},{8,9},{9,8},{10,11... | collective-permute-start | bytes 1179656 | tf_op jit(solution)/shard_map/ppermute | solution.py:517
  71.2 9.1 %collective-permute-start.12 = (bf16[64,3072]{1,0:T(8,128)(2,1)S(1)}, bf16[64,3072]{1,0:T(8,128)(2,1)S(1)}, u32[]{:S(2)}, u32[]{:S(2)}) collective-permute-start(bf16[64,3072]{1,0:T(8,128)(2,1)S(1)} %copy-done.6), channel_id=1, source_target_pairs={{0,1},{1,0},{2,3},{3,2},{4,5},{5,4},{6,7},{7,6},{8,9},{9,8},{10,11... | collective-permute-start | bytes 1179656 | tf_op jit(solution)/shard_map/ppermute | solution.py:517
  78.2 2.1 %copy-start.7 = (bf16[128,3072]{1,0:T(8,128)(2,1)}, bf16[128,3072]{1,0:T(8,128)(2,1)S(1)}, u32[]{:S(2)}) copy-start(bf16[128,3072]{1,0:T(8,128)(2,1)S(1)} %collective-permute-done.13.refs_2_.refs_3_) | copy-start | bytes 2359300
  78.2 23.7 %collective-permute-start.17 = (f32[2,128]{1,0:T(2,128)S(1)}, f32[2,128]{1,0:T(2,128)S(1)}, u32[]{:S(2)}, u32[]{:S(2)}) collective-permute-start(f32[2,128]{1,0:T(2,128)S(1)} %copy-done.16), channel_id=1, source_target_pairs={{0,4},{4,0},{8,12},{12,8},{1,5},{5,1},{9,13},{13,9},{2,6},{6,2},{1... | collective-permute-start | bytes 3080 | tf_op jit(solution)/shard_map/ppermute | solution.py:517
  80.3 0.8 copy-start.12
  80.3 1.1 copy-start.8
  81.4 0.8 copy-start.11
  88.6 19.5 %collective-permute-start.16 = (bf16[4,768,128]{2,1,0:T(8,128)(2,1)}, bf16[4,768,128]{2,1,0:T(8,128)(2,1)S(1)}, u32[]{:S(2)}, u32[]{:S(2)}) collective-permute-start(bf16[4,768,128]{2,1,0:T(8,128)(2,1)} %all-to-all-done.refs_8_), channel_id=1, source_target_pairs={{0,16},{16,0},{1,17},{17,1},{2,18},{18,2},{3,19},{19,3},{4,20},{20... | collective-permute-start | bytes 2359304 | tf_op jit(solution)/shard_map/ppermute | solution.py:517
  89.2 39.3 %collective-permute-start.15 = (bf16[768,256]{1,0:T(8,128)(2,1)}, bf16[768,256]{1,0:T(8,128)(2,1)S(1)}, u32[]{:S(2)}, u32[]{:S(2)}) collective-permute-start(bf16[768,256]{1,0:T(8,128)(2,1)} %get-tuple-element.639), channel_id=1, source_target_pairs={{0,8},{4,12},{8,0},{12,4},{1,9},{5,13},{9,1},{13,5},{2,10},{6,14},... | collective-permute-start | bytes 1179656 | tf_op jit(solution)/shard_map/ppermute | solution.py:517
  101.9 6.2 %copy-start.17 = (f32[2,128]{1,0:T(2,128)}, f32[2,128]{1,0:T(2,128)S(1)}, u32[]{:S(2)}) copy-start(f32[2,128]{1,0:T(2,128)S(1)} %collective-permute-done.17.limit1_ref) | copy-start | bytes 3076
  101.9 30.3 %collective-permute-start.14 = (bf16[768,256]{1,0:T(8,128)(2,1)}, bf16[768,256]{1,0:T(8,128)(2,1)S(1)}, u32[]{:S(2)}, u32[]{:S(2)}) collective-permute-start(bf16[768,256]{1,0:T(8,128)(2,1)} %get-tuple-element.638), channel_id=1, source_target_pairs={{0,8},{4,12},{8,0},{12,4},{1,9},{5,13},{9,1},{13,5},{2,10},{6,14},... | collective-permute-start | bytes 1179656 | tf_op jit(solution)/shard_map/ppermute | solution.py:517
  108.1 0.9 copy-start.9
  128.5 0.7 copy-start.18
  132.2 0.7 copy-start.19
  132.2 6.5 %collective-permute-start.18 = (bf16[768,128]{1,0:T(8,128)(2,1)}, bf16[768,128]{1,0:T(8,128)(2,1)S(1)}, u32[]{:S(2)}, u32[]{:S(2)}) collective-permute-start(bf16[768,128]{1,0:T(8,128)(2,1)} %get-tuple-element.709), channel_id=1, source_target_pairs={{0,4},{4,0},{8,12},{12,8},{1,5},{5,1},{9,13},{13,9},{2,6},{6,2},{1... | collective-permute-start | bytes 589832 | tf_op jit(solution)/shard_map/ppermute | solution.py:517
  135.9 6.6 %collective-permute-start.19 = (bf16[768,128]{1,0:T(8,128)(2,1)}, bf16[768,128]{1,0:T(8,128)(2,1)S(1)}, u32[]{:S(2)}, u32[]{:S(2)}) collective-permute-start(bf16[768,128]{1,0:T(8,128)(2,1)} %get-tuple-element.710), channel_id=1, source_target_pairs={{0,4},{4,0},{8,12},{12,8},{1,5},{5,1},{9,13},{13,9},{2,6},{6,2},{1... | collective-permute-start | bytes 589832 | tf_op jit(solution)/shard_map/ppermute | solution.py:517
  138.8 3.7 %copy-start.14 = (bf16[768,128]{1,0:T(8,128)(2,1)}, bf16[768,128]{1,0:T(8,128)(2,1)S(1)}, u32[]{:S(2)}) copy-start(bf16[768,128]{1,0:T(8,128)(2,1)S(1)} %collective-permute-done.18.refs_2_) | copy-start | bytes 589828
  142.5 0.7 copy-start.15
